TPU v7x, 128 devices: a whole 4x4x4 slice. The times are simulated.
128 devices in a mesh: req: 16 (over x, y), exp: 8 (over z, core).
Axes of the slice: x: 4, y: 4, z: 4, core: 2. Of those that a mesh axis runs over, the one named last changes fastest.
Arguments:
- hidden: bfloat16 [3072, 2048], P('req'), may hold values from -6 to 6
- gain_attn: bfloat16 [2048], replicated, may hold values from 0.099609375 to 1.8984375
- w_qkv: bfloat16 [2048, 3, 2048], P(None, None, 'exp'), may hold values from -0.125 to 0.125
- w_out: bfloat16 [2048, 2048], P('exp'), may hold values from -0.125 to 0.125
- cache_keys: bfloat16 [64, 2048, 2048], P('req', 'exp'), may hold values from -160 to 160
- cache_values: bfloat16 [64, 2048, 2048], P('req', 'exp'), may hold values from -6 to 6
- cache_lengths: int32 [64], P('req'), may hold values from 1 to 2048, as said below
- parents: int32 [64, 48], P('req'), may hold values from 0 to 46, as said below
- gain_moe: bfloat16 [2048], replicated, may hold values from 0.099609375 to 1.8984375
- w_router: bfloat16 [2048, 64], replicated, may hold values from -0.125 to 0.125
- routes: int32 [3072, 8], P(('req', 'exp')), may hold values from 0 to 63, all different within a row; in each aligned block of 24 rows (0 to 23, 24 to 47, ...) at most 6 rows name the same one
- w_gate_up: bfloat16 [128, 2048, 1024], P(('req', 'exp')), may hold values from -0.125 to 0.125
- w_down: bfloat16 [128, 512, 2048], P(('req', 'exp')), may hold values from -0.1875 to 0.1875
Outputs:
- layer_out: bfloat16 [3072, 2048], P(('req', 'exp'))
Inputs may be any that keep to these rules, and one draw needn't show every extreme that they name: `cache_lengths`: each request has 1 to 2048 live positions; some requests hold exactly 2048. `parents`: the parent of tree token t is below t; token 0 is its own parent; the last token's parent is the one before it. In each aligned block of 24 tokens no expert is named by more than 6 of the block's routes; the routes of one token differ.
All inputs are finite; a program needn't handle non-finite values.
Results may differ from a plain program's by a relative error of at most 0.017.
Values may be sent and summed in bfloat16 or wider, within the bound.
No kernel may reach another device: no remote copies, remote signals or barrier semaphores. Data moves between devices by JAX's collectives and lax.ppermute only.
A program may use at most 128 MiB of HBM per device.

v0:
```python
import jax
import jax.numpy as jnp
from jax import lax
from jax.sharding import PartitionSpec as P

HEAD_DIM = 128
EXP_SPLIT = 2


EPSILON = 1e-05
NEGATIVE = -1e30


def joined(array, axis, combine):
    everything = jax.tree.map(lambda part: lax.all_gather(part, axis), array)
    initial = jax.tree.map(lambda part: part[0], everything)

    def hop(k, so_far):
        return combine(so_far, jax.tree.map(lambda part: part[k], everything))

    return lax.fori_loop(1, lax.axis_size(axis), hop, initial)


def rms_scaled(values, gain_row):
    values = values.astype(jnp.float32)
    inverse = lax.rsqrt(jnp.mean(values * values, axis=-1, keepdims=True) + EPSILON)
    return values * inverse * gain_row.astype(jnp.float32)


def ancestor_mask(parents):
    tree_width = parents.shape[-1]
    column = jnp.arange(tree_width, dtype=jnp.int32)
    linked = (column[:, None] == column[None, :])[None, :, :] | (
        parents[:, :, None] == column[None, None, :]
    )
    closure = linked.astype(jnp.float32)
    for repeat in range(tree_width.bit_length()):
        closure = jnp.einsum("rts,rsu->rtu", closure, closure, precision=lax.Precision.HIGHEST)
        closure = jnp.minimum(closure, 1.0)
    return closure > 0.5


def per_device(
    hidden,
    gain_attn,
    w_qkv,
    w_out,
    cache_keys,
    cache_values,
    cache_lengths,
    parents,
    gain_moe,
    w_router,
    routes,
    w_gate_up,
    w_down,
):
    exp_count = lax.axis_size("exp")
    devices_all = lax.axis_size("req") * exp_count
    exp_index = lax.axis_index("exp")
    own_tokens, model_width = hidden.shape
    own_requests, tree_size = parents.shape
    page_size = cache_keys.shape[1]
    local_width = w_qkv.shape[2]
    head_size = HEAD_DIM
    all_heads = cache_keys.shape[2] // head_size
    local_heads = local_width // head_size
    score_scale = head_size ** (-0.5)
    normed = rms_scaled(hidden, gain_attn).astype(jnp.bfloat16)
    projected = jnp.dot(
        normed, w_qkv.reshape(model_width, 3 * local_width), preferred_element_type=jnp.float32
    )
    projected = projected.astype(jnp.bfloat16).reshape(own_tokens, 3, local_width)
    regrouped = lax.all_gather(projected, "exp", axis=2, tiled=True)
    regrouped = regrouped.reshape(own_requests, tree_size, 3, all_heads, head_size)
    query_rows = regrouped[:, :, 0]
    tree_keys = regrouped[:, :, 1]
    tree_values = regrouped[:, :, 2]
    old_keys = cache_keys.reshape(own_requests, page_size, all_heads, head_size)
    old_values = cache_values.reshape(own_requests, page_size, all_heads, head_size)
    positions = exp_index * page_size + jnp.arange(page_size, dtype=jnp.int32)
    usable = (positions[None, :] < cache_lengths[:, None])[:, None, None, :]
    cache_scores = (
        jnp.einsum("rthd,rphd->rthp", query_rows, old_keys, preferred_element_type=jnp.float32)
        * score_scale
    )
    cache_scores = jnp.where(usable, cache_scores, NEGATIVE)
    tree_mask = ancestor_mask(parents)[:, :, None, :] & (exp_index == exp_count - 1)
    tree_scores = (
        jnp.einsum("rthd,rshd->rths", query_rows, tree_keys, preferred_element_type=jnp.float32)
        * score_scale
    )
    tree_scores = jnp.where(tree_mask, tree_scores, NEGATIVE)
    local_high = jnp.maximum(jnp.max(cache_scores, axis=-1), jnp.max(tree_scores, axis=-1))
    cache_weights = jnp.where(usable, jnp.exp(cache_scores - local_high[..., None]), 0.0)
    tree_weights = jnp.where(tree_mask, jnp.exp(tree_scores - local_high[..., None]), 0.0)
    totals = jnp.sum(cache_weights, axis=-1) + jnp.sum(tree_weights, axis=-1)
    summed = jnp.einsum(
        "rthp,rphd->rthd",
        cache_weights.astype(jnp.bfloat16),
        old_values,
        preferred_element_type=jnp.float32,
    )
    summed = summed + jnp.einsum(
        "rths,rshd->rthd",
        tree_weights.astype(jnp.bfloat16),
        tree_values,
        preferred_element_type=jnp.float32,
    )
    totals, summed = (totals, summed)

    def combine_parts(first_part, second_part):
        highest = jnp.maximum(first_part[0], second_part[0])
        first_factor = jnp.exp(first_part[0] - highest)
        second_factor = jnp.exp(second_part[0] - highest)
        return (
            highest,
            first_part[1] * first_factor + second_part[1] * second_factor,
            first_part[2] * first_factor[..., None] + second_part[2] * second_factor[..., None],
        )

    merged = joined((local_high, totals, summed), "exp", combine_parts)
    own_totals = lax.dynamic_slice_in_dim(merged[1], exp_index * local_heads, local_heads, 2)
    own_sums = lax.dynamic_slice_in_dim(merged[2], exp_index * local_heads, local_heads, 2)
    attention = (
        (own_sums / own_totals[..., None]).astype(jnp.bfloat16).reshape(own_tokens, local_width)
    )
    tok_dev = own_tokens // exp_count
    mixed_heads = lax.psum_scatter(
        jnp.dot(attention, w_out, preferred_element_type=jnp.float32).astype(jnp.bfloat16),
        "exp",
        scatter_dimension=0,
        tiled=True,
    ).astype(jnp.float32)
    residual = (
        lax.dynamic_slice_in_dim(hidden, exp_index * tok_dev, tok_dev, 0).astype(jnp.float32)
        + mixed_heads
    )
    normed_moe = rms_scaled(residual, gain_moe).astype(jnp.bfloat16)
    logits = jnp.dot(normed_moe, w_router, preferred_element_type=jnp.float32)
    exponent = jnp.exp(logits)
    chances = exponent / jnp.sum(exponent, axis=-1, keepdims=True)
    top_count = routes.shape[1]
    experts_all = devices_all // EXP_SPLIT
    expert_ids = jnp.arange(experts_all, dtype=jnp.int32)
    chosen = routes[:, :, None] == expert_ids[None, None, :]
    picked = jnp.sum(jnp.where(chosen, chances[:, None, :], 0.0), axis=-1)
    gate_weights = picked / jnp.sum(picked, axis=-1, keepdims=True)
    capacity = max(2, tok_dev * top_count * EXP_SPLIT * 2 // devices_all)
    route_rows = tok_dev * top_count
    flat_chosen = chosen.reshape(route_rows, experts_all).astype(jnp.float32)
    row_ids = jnp.arange(route_rows, dtype=jnp.int32)
    earlier = (row_ids[:, None] > row_ids[None, :]).astype(jnp.float32)
    before = jnp.dot(earlier, flat_chosen, precision=lax.Precision.HIGHEST)
    slot_rank = jnp.sum(before * flat_chosen, axis=-1).astype(jnp.int32)
    targets = routes.reshape(-1) * capacity + slot_rank
    placing = targets[None, :] == jnp.arange(experts_all * capacity, dtype=jnp.int32)[:, None]
    spread_rows = jnp.broadcast_to(
        normed_moe[:, None, :], (tok_dev, top_count, model_width)
    ).reshape(-1, model_width)
    outgoing = jnp.dot(
        placing.astype(jnp.bfloat16), spread_rows, preferred_element_type=jnp.float32
    ).astype(jnp.bfloat16)
    gate_up_rows = w_gate_up[0]
    down_rows = w_down[0]
    group_units = down_rows.shape[0]
    doubled = jnp.broadcast_to(
        outgoing.reshape(experts_all, 1, capacity, model_width),
        (experts_all, EXP_SPLIT, capacity, model_width),
    )
    doubled = doubled.reshape(devices_all, capacity, model_width)
    arrived = lax.all_to_all(doubled, ("req", "exp"), split_axis=0, concat_axis=0, tiled=True)
    flat_rows = arrived.reshape(-1, model_width)
    both_proj = jnp.dot(flat_rows, gate_up_rows, preferred_element_type=jnp.float32)
    hidden_units = (jax.nn.silu(both_proj[:, :group_units]) * both_proj[:, group_units:]).astype(
        jnp.bfloat16
    )
    expert_out = jnp.dot(hidden_units, down_rows, preferred_element_type=jnp.float32).astype(
        jnp.bfloat16
    )
    returned = lax.all_to_all(
        expert_out.reshape(arrived.shape), ("req", "exp"), split_axis=0, concat_axis=0, tiled=True
    )
    halves = returned.reshape(experts_all, EXP_SPLIT, capacity, model_width)
    paired = jnp.sum(halves.astype(jnp.float32), axis=1).reshape(
        experts_all * capacity, model_width
    )
    weight_table = jnp.sum(
        (placing.astype(jnp.float32) * gate_weights.reshape(-1)[None, :]).reshape(
            experts_all * capacity, tok_dev, top_count
        ),
        axis=-1,
    )
    moe_out = jnp.einsum("st,sd->td", weight_table, paired, precision=lax.Precision.HIGHEST)
    return (residual + moe_out).astype(jnp.bfloat16)


def solution(mesh):
    in_specs = (
        P("req", None),
        P(),
        P(None, None, "exp"),
        P("exp", None),
        P("req", "exp", None),
        P("req", "exp", None),
        P("req"),
        P("req", None),
        P(),
        P(),
        P(("req", "exp"), None),
        P(("req", "exp"), None, None),
        P(("req", "exp"), None, None),
    )
    out_specs = P(("req", "exp"), None)
    return jax.shard_map(
        per_device, mesh=mesh, in_specs=in_specs, out_specs=out_specs, check_vma=False
    )
```

profile of v0, /device:TPU:0, one launch (start us, length us, event | category | flops | bytes accessed | tf_op | source)
XLA Modules:
  0.0 376.1 jit_solution(17572676607816973045)
XLA Ops:
  6.5 4.9 %copy.60 = bf16[2048,3,256]{0,2,1:T(8,128)(2,1)} copy(bf16[2048,3,256]{2,0,1:T(8,128)(2,1)} %param.17) | data formatting | bytes 6291456 | tf_op args[2]
  11.7 3.1 convolution_convert_fusion.3
  14.8 0.9 reshape.174
  17.4 32.8 %all-gather.6.cloned.1.call-done = bf16[192,3,2048]{2,1,0:T(4,128)(2,1)} async-done(((bf16[192,3,256]{2,1,0:T(4,128)(2,1)}), bf16[192,3,2048]{2,1,0:T(4,128)(2,1)}) %all-gather.6.cloned.1.call-update) | async-done | bytes 2359312 | tf_op jit(solution)/shard_map/all_gather | solution.py:74
  50.2 7.1 %reshape.194 = bf16[4,48,3,16,128]{4,3,2,1,0:T(8,128)(2,1)} reshape(bf16[192,3,2048]{2,1,0:T(4,128)(2,1)} %all-gather.6.cloned.1.call-done) | data formatting | bytes 4718592 | tf_op jit(solution)/shard_map/reshape | solution.py:75
  57.3 2.2 fusion.59
  60.2 1.6 bitcast_reduce_fusion
  62.6 1.5 fusion.3
  64.7 1.6 copy.69
  66.4 12.9 %all-gather = f32[32,48,16]{1,2,0:T(8,128)S(1)} all-gather(f32[4,48,16]{1,2,0:T(8,128)S(1)} %max.27), channel_id=2, replica_groups=mesh['req'=16,'exp'=8] {'exp'}, dimensions={0}, use_global_device_ids=true | all-gather | bytes 110592 | tf_op jit(solution)/shard_map/all_gather | solution.py:15
  79.3 2.3 fusion.29
  81.6 2.6 fusion.15
  84.2 13.5 %all-gather.1 = f32[32,48,16]{1,2,0:T(8,128)S(1)} all-gather(f32[4,48,16]{1,2,0:T(8,128)S(1)} %add.134), channel_id=3, replica_groups=mesh['req'=16,'exp'=8] {'exp'}, dimensions={0}, use_global_device_ids=true | all-gather | bytes 110592 | tf_op jit(solution)/shard_map/all_gather | solution.py:15
  98.3 37.6 %all-gather.8.cloned.1.call-done = f32[32,48,16,128]{3,2,1,0:T(8,128)} async-done(((f32[4,48,16,128]{3,2,1,0:T(8,128)}), f32[32,48,16,128]{3,2,1,0:T(8,128)}) %all-gather.8.cloned.1.call-update) | async-done | bytes 12582928 | tf_op jit(solution)/shard_map/all_gather | solution.py:15
  135.9 2.7 slice.40
  138.7 29.4 %while.19 = (s32[]{:T(128)}, f32[4,48,16]{1,2,0:T(8,128)S(1)}, f32[4,48,16]{1,2,0:T(8,128)S(1)}, f32[4,48,16,128]{3,2,1,0:T(8,128)}, f32[8,4,48,16]{2,3,1,0:T(8,...) while((s32[]{:T(128)}, f32[4,48,16]{1,2,0:T(8,128)S(1)}, ...), condition=%wide.region_6.7_spmd, body=%wide.region_5.6_spmd.sunk | while | flops 1198085 | bytes 4890775 | solution.py:21
  138.7 0.8 fusion.83
  139.6 3.2 fusion.84
  142.9 0.8 fusion.83
  143.8 3.2 fusion.84
  147.1 0.8 fusion.83
  148.0 3.2 fusion.84
  151.3 0.8 fusion.83
  152.2 3.2 fusion.84
  155.4 0.8 fusion.83
  156.4 3.2 fusion.84
  159.6 0.8 fusion.83
  160.6 3.2 fusion.84
  163.8 0.8 fusion.83
  164.8 3.2 fusion.84
  168.2 1.4 fusion.45
  169.6 2.5 convolution_convert_fusion.2
  172.5 31.5 %reduce-scatter.2.cloned.1.call-done = bf16[24,2048]{1,0:T(8,128)(2,1)} async-done(((bf16[192,2048]{1,0:T(8,128)(2,1)}), bf16[24,2048]{1,0:T(8,128)(2,1)}) %reduce-scatter.2.cloned.1.call-update) | async-done | bytes 98320 | tf_op jit(solution)/shard_map/reduce_scatter | solution.py:129
  204.0 1.0 multiply_reduce_fusion
  205.1 1.0 multiply_convert_fusion
  206.1 1.7 convolution_convert_fusion.1
  207.8 3.7 broadcast_in_dim.104
  211.5 2.1 broadcast_in_dim.105
  213.6 60.5 %all_to_all.10 = bf16[128,6,2048]{2,1,0:T(8,128)(2,1)} all-to-all(bf16[128,6,2048]{2,1,0:T(8,128)(2,1)S(1)} %bitcast.108), channel_id=1, replica_groups=mesh['req'=16,'exp'=8] {'req','exp'}, dimensions={0} | all-to-all | bytes 6291456 | tf_op jit(solution)/shard_map/all_to_all | solution.py:172
  274.1 6.3 %reshape.181 = bf16[768,2048]{1,0:T(8,128)(2,1)} reshape(bf16[128,6,2048]{2,1,0:T(8,128)(2,1)} %all_to_all.10) | data formatting | bytes 6291456 | tf_op jit(solution)/shard_map/reshape | solution.py:173
  280.4 6.1 %fusion.9 = f32[768,1024]{1,0:T(8,128)S(1)} fusion(bf16[768,2048]{1,0:T(8,128)(2,1)} %reshape.181, bf16[1,2048,1024]{2,1,0:T(8,128)(2,1)} %param.26), kind=kOutput, calls=%fused_computation.15 | convolution fusion | flops 3221225472 | bytes 10485760 | tf_op jit(solution)/shard_map/dot_general | solution.py:174
  286.6 3.5 convolution_convert_fusion
  290.1 6.3 %reshape.182 = bf16[128,6,2048]{2,1,0:T(8,128)(2,1)} reshape(bf16[768,2048]{1,0:T(8,128)(2,1)} %convolution_convert_fusion) | data formatting | bytes 6291456 | tf_op jit(solution)/shard_map/reshape | solution.py:182
  296.3 6.0 %all-to-all-start.1 = ((bf16[128,6,2048]{2,1,0:T(8,128)(2,1)}), bf16[128,6,2048]{2,1,0:T(8,128)(2,1)}, u32[]{:S(2)}, u32[]{:S(2)}) async-start(bf16[128,6,2048]{2,1,0:T(8,128)(2,1)} %reshape.182), calls=%async_computation.2 | async-start | bytes 8388608 | tf_op jit(solution)/shard_map/all_to_all | solution.py:181
  303.5 51.6 %all-to-all-done.1 = bf16[128,6,2048]{2,1,0:T(8,128)(2,1)} async-done(((bf16[128,6,2048]{2,1,0:T(8,128)(2,1)}), bf16[128,6,2048]{2,1,0:T(8,128)(2,1)}, u32[]{:S(2)}, u32[]{:S(2)}) %all-to-all-start.1) | async-done | bytes 3145760 | tf_op jit(solution)/shard_map/all_to_all | solution.py:181
  355.0 5.6 %convert_reduce_fusion = f32[64,6,2048]{2,1,0:T(8,128)} fusion(bf16[128,6,2048]{2,1,0:T(8,128)(2,1)} %all-to-all-done.1), kind=kLoop, calls=%fused_computation.8 | loop fusion | flops 2359296 | bytes 6291456 | tf_op jit(solution)/shard_map/reduce_sum | solution.py:185
  360.6 4.8 %reshape.183 = f32[384,2048]{1,0:T(8,128)} reshape(f32[64,6,2048]{2,1,0:T(8,128)} %convert_reduce_fusion) | data formatting | bytes 6291456 | tf_op jit(solution)/shard_map/reshape | solution.py:185
  365.4 4.1 %fusion.13 = bf16[24,2048]{1,0:T(8,128)(2,1)} fusion(f32[384,24]{0,1:T(8,128)S(1)} %select_reduce_fusion, f32[384,2048]{1,0:T(8,128)} %reshape.183, bf16[24,2048]{1,0:T(8,128)(2,1)S(1)} %copy-done.4, bf16[192,2048]{1,0:T(8,128)(2,1)S(1)} %copy-done.3, s32[]{:T(128)S(6)} %select_n.40), kind=kOutput, calls=%fused_computation.26 | convolution fusion | flops 226738176 | bytes 3477508 | tf_op jit(solution)/shard_map/st,sd->td/dot_general | solution.py:194
  (83 shorter events, 7.5 us)
Async XLA Ops:
  6.5 280.0 %copy-start = (bf16[1,512,2048]{2,1,0:T(8,128)(2,1)S(1)}, bf16[1,512,2048]{2,1,0:T(8,128)(2,1)}, u32[]{:S(2)}) copy-start(bf16[1,512,2048]{2,1,0:T(8,128)(2,1)} %param.27) | copy-start | bytes 6291460
  6.5 4.9 %copy-start.7 = (bf16[2048]{0:T(1024)(128)(2,1)S(1)}, bf16[2048]{0:T(1024)(128)(2,1)}, u32[]{:S(2)}) copy-start(bf16[2048]{0:T(1024)(128)(2,1)} %param.16) | copy-start | bytes 12292
  6.5 4.9 %copy-start.3 = (bf16[192,2048]{1,0:T(8,128)(2,1)S(1)}, bf16[192,2048]{1,0:T(8,128)(2,1)}, u32[]{:S(2)}) copy-start(bf16[192,2048]{1,0:T(8,128)(2,1)} %param.15) | copy-start | bytes 2359300
  6.5 43.6 %all-gather.6.cloned.1.call-start = ((), (), s32[]{:S(2)}) async-start(), calls=%async_computation.3 | async-start | bytes 3538944 | tf_op jit(solution)/shard_map/all_gather | solution.py:74
  11.7 4.1 %copy-start.13 = (s32[4,48]{1,0:T(4,128)S(1)}, s32[4,48]{1,0:T(4,128)}, u32[]{:S(2)}) copy-start(s32[4,48]{1,0:T(4,128)} %param.22) | copy-start | bytes 2308
  11.7 5.6 %copy-start.10 = (s32[4]{0:T(128)S(1)}, s32[4]{0:T(128)}, u32[]{:S(2)}) copy-start(s32[4]{0:T(128)} %param.21) | copy-start | bytes 52
  15.7 120.3 %all-gather.8.cloned.1.call-start = ((), (), s32[]{:S(2)}) async-start(), calls=%async_computation.5 | async-start | bytes 14155776 | tf_op jit(solution)/shard_map/all_gather | solution.py:15
  57.3 2.9 copy-start.11
  60.2 2.3 copy-start.12
  61.9 2.2 copy-start.2
  62.5 1.6 copy-start.1
  66.4 137.7 %reduce-scatter.2.cloned.1.call-start = ((), (), s32[]{:S(2)}) async-start(), calls=%async_computation.4 | async-start | bytes 884736 | tf_op jit(solution)/shard_map/reduce_scatter | solution.py:129
  97.6 0.7 copy-start.5
  168.0 4.1 %copy-start.8 = (bf16[2048]{0:T(1024)(128)(2,1)S(1)}, bf16[2048]{0:T(1024)(128)(2,1)}, u32[]{:S(2)}) copy-start(bf16[2048]{0:T(1024)(128)(2,1)} %param.23) | copy-start | bytes 12292
  168.0 4.1 %copy-start.9 = (s32[24,8]{0,1:T(8,128)S(1)}, s32[24,8]{0,1:T(8,128)}, u32[]{:S(2)}) copy-start(s32[24,8]{0,1:T(8,128)} %param.25) | copy-start | bytes 2308
  296.3 6.1 %copy-start.6 = (bf16[2048,64]{0,1:T(8,128)(2,1)S(1)}, bf16[2048,64]{0,1:T(8,128)(2,1)}, u32[]{:S(2)}) copy-start(bf16[2048,64]{0,1:T(8,128)(2,1)} %param.24) | copy-start | bytes 786436
  296.3 58.7 %all-to-all-start.1 = ((bf16[128,6,2048]{2,1,0:T(8,128)(2,1)}), bf16[128,6,2048]{2,1,0:T(8,128)(2,1)}, u32[]{:S(2)}, u32[]{:S(2)}) async-start(bf16[128,6,2048]{2,1,0:T(8,128)(2,1)} %reshape.182), calls=%async_computation.2 | async-start | bytes 8388608 | tf_op jit(solution)/shard_map/all_to_all | solution.py:181
  360.6 4.8 %copy-start.4 = (bf16[24,2048]{1,0:T(8,128)(2,1)S(1)}, bf16[24,2048]{1,0:T(8,128)(2,1)}, u32[]{:S(2)}) copy-start(bf16[24,2048]{1,0:T(8,128)(2,1)} %reduce-scatter.2.cloned.1.call-done) | copy-start | bytes 294916
Sparse Core Ops, SparseCore 0:
  15.8 34.3 all-gather.5
  66.5 69.4 all-gather.7
  172.2 31.7 reduce-scatter.1
where the time goes:
time: 378 us; the launch traced here: 376 us
  waiting for transfers between devices  154 us (41%)
  blocking collectives  86.8 us (23%)
  local copies, waits for them, and re-layouts  45.7 us (12%)
  other arithmetic  43.2 us (11%)
  matrix products  27.2 us (7%)
  between operations  13.5 us (4%)
  starting transfers between devices  6.04 us (2%)
    all_to_all x1, blocking collectives, per_device(): lax.all_to_all(doubled, ('req', 'exp'), split_axis=0, concat_axis=0, tile...  60.5 us
    all_to_all x1, waiting for transfers between devices, per_device(): lax.all_to_all(expert_out.reshape(arrived.shape), ('req', 'exp'), split_a...  51.6 us
    all_gather x1, waiting for transfers between devices, joined(): everything = jax.tree.map(lambda part: lax.all_gather(part, axis), array)  37.6 us
    all_gather x1, waiting for transfers between devices, per_device(): regrouped = lax.all_gather(projected, 'exp', axis=2, tiled=True)  32.8 us
    reduce_scatter x1, waiting for transfers between devices, per_device(): lax.psum_scatter(jnp.dot(attention, w_out, preferred_element_type=jnp.flo...  31.5 us
    all_gather x2, blocking collectives, joined(): everything = jax.tree.map(lambda part: lax.all_gather(part, axis), array)  26.3 us
    add x7, other arithmetic, combine_parts(): first_part[2] * first_factor[..., None]  22.6 us
  transfers between devices with their start and end apart: 4, of which 4 were waited for; matrix products, arithmetic and copies ran while one was open for 2% of the time, Pallas kernels for 0%

commit v1 on v0

v1 whole, which is shorter than its diff:
```python
import functools

import jax
import jax.numpy as jnp
from jax import lax
from jax.experimental import pallas as pl
from jax.experimental.pallas import tpu as pltpu
from jax.sharding import Mesh
from jax.sharding import PartitionSpec as P

HEAD_DIM = 128
EXP_SPLIT = 2
CORES = 2
CAP = 6
SLOTS = 8

EPSILON = 1e-05
NEGATIVE = -1e30
F32 = jnp.float32
BF16 = jnp.bfloat16
VMEM = pltpu.VMEM
SMEM = pltpu.SMEM


def dot(a, b):
    return jnp.dot(a, b, preferred_element_type=F32)


def dot_t(a, b):
    return lax.dot_general(a, b, (((1,), (1,)), ((), ())), preferred_element_type=F32)


def iota(shape, axis):
    return lax.broadcasted_iota(jnp.int32, shape, axis)


def call(body, out, in_spaces, scratch=(), flops=0, bytes_accessed=0, vmem=48 << 20):
    out_spec = jax.tree.map(lambda _: pl.BlockSpec(memory_space=VMEM), out)
    return pl.pallas_call(
        body,
        out_shape=out,
        in_specs=[pl.BlockSpec(memory_space=s) for s in in_spaces],
        out_specs=out_spec,
        scratch_shapes=list(scratch),
        compiler_params=pltpu.CompilerParams(vmem_limit_bytes=vmem),
        cost_estimate=pl.CostEstimate(
            flops=flops, bytes_accessed=bytes_accessed, transcendentals=0
        ),
    )


def sds(shape, dtype):
    return jax.ShapeDtypeStruct(shape, dtype)


def normed_rows(values, gain):
    inverse = lax.rsqrt(jnp.mean(values * values, axis=-1, keepdims=True) + EPSILON)
    return (values * inverse * gain).astype(BF16)


def query_kernel(x_ref, g_ref, w_ref, q_ref):
    normed = normed_rows(x_ref[...].astype(F32), g_ref[...].astype(F32))
    q_ref[...] = dot(normed, w_ref[...]).astype(BF16)


def tree_kernel(scale, x_ref, g_ref, w_ref, q_ref, up_ref, o_ref, lse_ref, turn):
    tokens, width = q_ref.shape
    normed = normed_rows(x_ref[...].astype(F32), g_ref[...].astype(F32))
    keys = dot(normed, w_ref[0]).astype(BF16)
    values = dot(normed, w_ref[1]).astype(BF16)
    row = iota((tokens, tokens), 0)
    column = iota((tokens, tokens), 1)
    reach = jnp.where((row == column) | (up_ref[...] == column), 1.0, 0.0)
    for _ in range(6):
        half = reach.astype(BF16)
        reach = jnp.minimum(dot(half, half), 1.0)
    visible = reach > 0.5
    lane = iota((tokens, 128), 1)
    stats = jnp.zeros((tokens, 128), F32)
    for h in range(width // HEAD_DIM):
        cut = slice(h * HEAD_DIM, (h + 1) * HEAD_DIM)
        scores = dot_t(q_ref[:, cut], keys[:, cut]) * scale
        scores = jnp.where(visible, scores, NEGATIVE)
        high = jnp.max(scores, axis=-1, keepdims=True)
        weights = jnp.where(visible, jnp.exp(scores - high), 0.0)
        total = jnp.sum(weights, axis=-1, keepdims=True)
        o_ref[:, cut] = dot(weights.astype(BF16), values[:, cut]) / total
        stats = jnp.where(lane == h, high + jnp.log(total), stats)
    turn[0:tokens, :] = stats
    lse_ref[...] = jnp.transpose(turn[...])[0:8, :]


def page_kernel(scale, tree, meta_ref, *refs):
    pieces = refs[:8]
    k_ref, v_ref, out_ref, q_all, turn = refs[8:]
    requests, page = k_ref.shape[0], k_ref.shape[1]
    owners = out_ref.shape[0]
    tokens = requests * tree
    heads = pieces[0].shape[1] // HEAD_DIM
    for i, piece in enumerate(pieces):
        q_all[meta_ref[8 + i]] = piece[...]
    lane = iota((tree, 128), 1)
    column = iota((tree, page), 1)
    for r in range(requests):
        rows = slice(r * tree, (r + 1) * tree)
        live = meta_ref[r]

        @pl.when(live > 0)
        def _():
            stats = jnp.zeros((tree, 128), F32)
            usable = column < live
            for e in range(owners):
                for h in range(heads):
                    at = slice((e * heads + h) * HEAD_DIM, (e * heads + h + 1) * HEAD_DIM)
                    cut = slice(h * HEAD_DIM, (h + 1) * HEAD_DIM)
                    scores = dot_t(q_all[e, rows, cut], k_ref[r, :, at]) * scale
                    scores = jnp.where(usable, scores, NEGATIVE)
                    high = jnp.max(scores, axis=-1, keepdims=True)
                    weights = jnp.exp(scores - high)
                    total = jnp.sum(weights, axis=-1, keepdims=True)
                    summed = dot(weights.astype(BF16), v_ref[r, :, at])
                    out_ref[e, rows, cut] = (summed / total).astype(BF16)
                    lse = high + jnp.log(total)
                    first = lse.astype(BF16).astype(F32)
                    second = (lse - first).astype(BF16).astype(F32)
                    third = lse - first - second
                    stats = jnp.where(lane == e * 8 + h, first, stats)
                    stats = jnp.where(lane == e * 8 + 2 + h, second, stats)
                    stats = jnp.where(lane == e * 8 + 4 + h, third, stats)
            turn[rows, :] = stats

        @pl.when(live <= 0)
        def _():
            for e in range(owners):
                out_ref[e, rows, :] = jnp.zeros((tree, heads * HEAD_DIM), BF16)
            turn[rows, :] = jnp.where(lane % 8 < 2, NEGATIVE, 0.0)

    turn[tokens:, :] = jnp.zeros((turn.shape[0] - tokens, 128), F32)
    turned = jnp.transpose(turn[...])
    for e in range(owners):
        out_ref[e, tokens:, :] = turned[e * 8 : (e + 1) * 8, :].astype(BF16)


def out_kernel(parts_ref, tree_o_ref, tree_lse_ref, w_ref, out_ref, turn):
    parts, padded, width = parts_ref.shape
    tokens = padded - 8
    heads = width // HEAD_DIM
    lses = []
    for s in range(parts):
        rows = parts_ref[s, tokens:, :].astype(F32)
        lses.append(rows[0:2] + rows[2:4] + rows[4:6])
    lses.append(tree_lse_ref[0:2, :])
    high = functools.reduce(jnp.maximum, lses)
    factors = [jnp.exp(value - high) for value in lses]
    whole = functools.reduce(lambda a, b: a + b, factors)
    for s, factor in enumerate(factors):
        turn[2 * s : 2 * s + 2, :] = factor / whole
    turned = jnp.transpose(turn[...])[0:tokens, :]
    columns = []
    for h in range(heads):
        cut = slice(h * HEAD_DIM, (h + 1) * HEAD_DIM)
        at = 2 * parts + h
        total = turned[:, at : at + 1] * tree_o_ref[:, cut]
        for s in range(parts):
            at = 2 * s + h
            total = total + turned[:, at : at + 1] * parts_ref[s, 0:tokens, cut].astype(F32)
        columns.append(total.astype(BF16))
    attention = jnp.concatenate(columns, axis=1)
    out_ref[...] = dot(attention, w_ref[...]).astype(BF16)


def expert_of_row(rows, experts):
    return jnp.where(iota((rows, experts), 0) // SLOTS == iota((rows, experts), 1), 1.0, 0.0)


def place_kernel(routes_ref, place_ref):
    top, tokens = routes_ref.shape
    chunks, rows, _ = place_ref.shape
    experts = rows // SLOTS
    named = iota((experts, tokens), 0)
    chosen = jnp.zeros((experts, tokens), F32)
    for k in range(top):
        chosen = jnp.where(routes_ref[k : k + 1, :] == named, 1.0, chosen)
    source = iota((tokens, 2 * tokens), 0)
    target = iota((tokens, 2 * tokens), 1) % tokens
    chosen = chosen.astype(BF16)
    rank = dot(chosen, jnp.where(source < target, 1.0, 0.0).astype(BF16))
    both = dot(chosen, jnp.where(source == target, 1.0, 0.0).astype(BF16))
    rank = jnp.where(both > 0.5, rank, -1.0).astype(BF16)
    spread = dot(expert_of_row(rows, experts).astype(BF16), rank)
    slot = iota((rows, 2 * tokens), 0) % SLOTS
    is_tail = iota((rows, 2 * tokens), 1) >= tokens
    for j in range(chunks):
        wanted = jnp.where(is_tail, (slot - CAP) * chunks + j, slot)
        valid = is_tail == (slot >= CAP)
        hit = valid & (spread == wanted.astype(F32))
        place_ref[j] = jnp.where(hit, 1.0, 0.0).astype(BF16)


def residual_kernel(
    meta_ref, parts_ref, x_ref, g_ref, place_ref, res_ref, normed_ref, out_ref
):
    parts, tokens, width = parts_ref.shape
    chunks = place_ref.shape[0]
    cut = width // (chunks + 1)
    start = pl.multiple_of(meta_ref[0] * tokens, 8)
    residual = parts_ref[0].astype(F32)
    for s in range(1, parts):
        residual = residual + parts_ref[s].astype(F32)
    residual = x_ref[pl.ds(start, tokens), :].astype(F32) + residual
    res_ref[...] = residual
    inverse = lax.rsqrt(jnp.mean(residual * residual, axis=-1, keepdims=True) + EPSILON)
    normed = residual * inverse * g_ref[...].astype(F32)
    normed_ref[...] = normed.astype(BF16)
    tail = normed[:, chunks * cut :]
    for j in range(chunks):
        pair = jnp.concatenate([normed[:, j * cut : (j + 1) * cut], tail], axis=0).astype(BF16)
        out_ref[:, j * cut : (j + 1) * cut] = dot(place_ref[j], pair).astype(BF16)


def gate_kernel(normed_ref, router_ref, routes_ref, table_ref):
    tokens, top = routes_ref.shape
    experts = router_ref.shape[0]
    chunks, _, rows = table_ref.shape
    logits = dot_t(normed_ref[...], router_ref[...])
    exponent = jnp.exp(logits)
    chances = exponent / jnp.sum(exponent, axis=-1, keepdims=True)
    named = iota((tokens, experts), 1)
    chosen = jnp.zeros((tokens, experts), F32)
    for k in range(top):
        chosen = jnp.where(routes_ref[:, k : k + 1] == named, 1.0, chosen)
    picked = chances * chosen
    gates = picked / jnp.sum(picked, axis=-1, keepdims=True)
    earlier = jnp.where(iota((tokens, tokens), 0) > iota((tokens, tokens), 1), 1.0, 0.0)
    rank = dot(earlier.astype(BF16), chosen.astype(BF16))
    rank = jnp.where(chosen > 0.5, rank, -1.0).astype(BF16)
    first = gates.astype(BF16)
    second = (gates - first.astype(F32)).astype(BF16)
    home = iota((experts, rows), 0) == iota((experts, rows), 1) // SLOTS
    home = jnp.where(home, 1.0, 0.0).astype(BF16)
    rank, first, second = dot(rank, home), dot(first, home), dot(second, home)
    slot = iota((tokens, rows), 1) % SLOTS
    main = (slot < CAP) & (rank == slot.astype(F32))
    for j in range(chunks):
        tail = (slot >= CAP) & (rank == ((slot - CAP) * chunks + j).astype(F32))
        table_ref[j] = jnp.concatenate(
            [
                jnp.where(main, first, 0.0),
                jnp.where(main, second, 0.0),
                jnp.where(tail, first, 0.0),
                jnp.where(tail, second, 0.0),
            ],
            axis=0,
        ).astype(BF16)


def expert_kernel(block, x_ref, gate_up_ref, down_ref, out_ref):
    rows, packed = x_ref.shape
    width, both = gate_up_ref.shape
    units = both // 2
    cut = width - packed
    chunks = packed // cut
    a = iota((block, block), 0)
    b = iota((block, block), 1)
    same = a // SLOTS == b // SLOTS
    slot_a, slot_b = a % SLOTS, b % SLOTS
    unpack, pack = [], []
    for k in range(chunks):
        hit = same & (slot_a < CAP) & (slot_b >= CAP) & (slot_a == (slot_b - CAP) * chunks + k)
        unpack.append(jnp.where(hit, 1.0, 0.0).astype(BF16))
        hit = same & (slot_b < CAP) & (slot_a >= CAP) & (slot_b == (slot_a - CAP) * chunks + k)
        pack.append(jnp.where(hit, 1.0, 0.0).astype(BF16))
    is_tail = iota((block, cut), 0) % SLOTS >= CAP
    for at in range(0, rows, block):
        span = slice(at, at + block)
        tail = dot(unpack[0], x_ref[span, 0:cut])
        for k in range(1, chunks):
            tail = tail + dot(unpack[k], x_ref[span, k * cut : (k + 1) * cut])
        up = dot(x_ref[span, :], gate_up_ref[0:packed, :])
        up = up + dot(tail.astype(BF16), gate_up_ref[packed:, :])
        gate = up[:, :units]
        hidden = (gate / (1.0 + jnp.exp(-gate)) * up[:, units:]).astype(BF16)
        last = dot(hidden, down_ref[:, packed:]).astype(BF16)
        for k in range(chunks):
            main = dot(hidden, down_ref[:, k * cut : (k + 1) * cut])
            out_ref[span, k * cut : (k + 1) * cut] = jnp.where(
                is_tail, dot(pack[k], last), main
            ).astype(BF16)


def final_kernel(back_ref, table_ref, res_ref, out_ref):
    tokens, width = res_ref.shape
    chunks = table_ref.shape[0]
    cut = width // (chunks + 1)
    tail = res_ref[:, chunks * cut :]
    for j in range(chunks):
        span = slice(j * cut, (j + 1) * cut)
        sums = dot(table_ref[j], back_ref[:, span])
        main = sums[0:tokens] + sums[tokens : 2 * tokens]
        out_ref[:, span] = (res_ref[:, span] + main).astype(BF16)
        tail = tail + (sums[2 * tokens : 3 * tokens] + sums[3 * tokens :])
    out_ref[:, chunks * cut :] = tail.astype(BF16)


def per_device(
    hidden,
    gain_attn,
    w_qkv,
    w_out,
    cache_keys,
    cache_values,
    cache_lengths,
    parents,
    gain_moe,
    w_router,
    routes,
    w_gate_up,
    w_down,
):
    z_count = lax.axis_size("z")
    exp_count = z_count * CORES
    z_index = lax.axis_index("z")
    core = lax.axis_index("core")
    exp_index = z_index * CORES + core
    tokens, width = hidden.shape
    requests, tree = parents.shape
    page = cache_keys.shape[1]
    local_width = w_qkv.shape[2]
    scale = HEAD_DIM ** (-0.5)
    own = tokens // exp_count
    experts = w_router.shape[1]
    packed = width * CAP // SLOTS
    chunks = packed // (width - packed)
    padded = tokens + 8

    gain_a = gain_attn.reshape(1, width)
    gain_m = gain_moe.reshape(1, width)
    w_three = jnp.transpose(w_qkv, (1, 0, 2))

    query = call(
        query_kernel,
        sds((tokens, local_width), BF16),
        [VMEM] * 3,
        flops=2 * tokens * width * local_width,
        bytes_accessed=2 * width * (tokens + local_width),
    )(hidden, gain_a, w_three[0])

    def over_z(value, step):
        return lax.ppermute(value, "z", [(i, (i + step) % z_count) for i in range(z_count)])

    def over_core(value):
        return lax.ppermute(value, "core", [(0, 1), (1, 0)])

    pieces = [query] + [over_z(query, step) for step in range(1, z_count)]
    owners = [((z_index - step) % z_count) * CORES + core for step in range(z_count)]
    pieces = pieces + [over_core(piece) for piece in pieces]
    owners = owners + [owner + 1 - 2 * core for owner in owners]

    up = (parents + tree * jnp.arange(requests, dtype=jnp.int32)[:, None]).reshape(tokens, 1)
    tree_o, tree_lse = call(
        functools.partial(tree_kernel, scale),
        (sds((tokens, local_width), F32), sds((8, 256), F32)),
        [VMEM] * 5,
        [pltpu.VMEM((256, 128), F32)],
        flops=4 * tokens * width * local_width,
        bytes_accessed=2 * width * (tokens + 2 * local_width),
    )(hidden, gain_a, w_three[1:], query, up)

    place = call(
        place_kernel,
        sds((chunks, experts * SLOTS, 2 * own), BF16),
        [VMEM],
        flops=1 << 22,
        bytes_accessed=1 << 18,
    )(routes.T)

    meta = jnp.concatenate(
        [
            cache_lengths - exp_index * page,
            jnp.zeros((8 - requests,), jnp.int32),
            jnp.stack(owners).astype(jnp.int32),
        ]
    )
    partial = call(
        functools.partial(page_kernel, scale, tree),
        sds((exp_count, padded, local_width), BF16),
        [SMEM] + [VMEM] * 10,
        [pltpu.VMEM((exp_count, tokens, local_width), BF16), pltpu.VMEM((256, 128), F32)],
        flops=4 * tokens * page * width,
        bytes_accessed=4 * requests * page * width,
    )(meta, *pieces, cache_keys, cache_values)
    arrived = lax.all_to_all(
        partial.reshape(exp_count * padded, local_width),
        ("z", "core"),
        split_axis=0,
        concat_axis=0,
        tiled=True,
    ).reshape(exp_count, padded, local_width)
    mixed = call(
        out_kernel,
        sds((tokens, width), BF16),
        [VMEM] * 4,
        [pltpu.VMEM((128, 256), F32)],
        flops=2 * tokens * width * local_width,
        bytes_accessed=2 * width * (tokens + local_width),
    )(arrived, tree_o, tree_lse, w_out)
    mixed = lax.all_to_all(
        mixed, ("z", "core"), split_axis=0, concat_axis=0, tiled=True
    ).reshape(exp_count, own, width)

    residual, normed, outgoing = call(
        residual_kernel,
        (
            sds((own, width), F32),
            sds((own, width), BF16),
            sds((experts * SLOTS, packed), BF16),
        ),
        [SMEM] + [VMEM] * 4,
        flops=1 << 27,
        bytes_accessed=1 << 22,
    )(exp_index.reshape(1).astype(jnp.int32), mixed, hidden, gain_m, place)
    rows = lax.all_to_all(
        outgoing.reshape(experts, SLOTS, packed),
        ("req", "z"),
        split_axis=0,
        concat_axis=0,
        tiled=True,
    ).reshape(experts * SLOTS, packed)
    table = call(
        gate_kernel,
        sds((chunks, 4 * own, experts * SLOTS), BF16),
        [VMEM] * 3,
        flops=1 << 24,
        bytes_accessed=1 << 19,
    )(normed, w_router.T, routes)

    expert = call(
        functools.partial(expert_kernel, 256),
        sds((experts * SLOTS, packed), BF16),
        [VMEM] * 3,
        flops=6 * experts * SLOTS * width * w_down.shape[1],
        bytes_accessed=6 * width * w_down.shape[1],
    )
    theirs = over_core(rows)
    mine_out = expert(rows, w_gate_up[0], w_down[0])
    their_out = expert(theirs, w_gate_up[0], w_down[0])
    other_out = over_core(their_out)
    summed = (mine_out.astype(F32) + other_out.astype(F32)).astype(BF16)
    back = lax.all_to_all(
        summed.reshape(experts, SLOTS, packed),
        ("req", "z"),
        split_axis=0,
        concat_axis=0,
        tiled=True,
    ).reshape(experts * SLOTS, packed)
    return call(
        final_kernel,
        sds((own, width), BF16),
        [VMEM] * 3,
        flops=1 << 27,
        bytes_accessed=1 << 22,
    )(back, table, residual)


def solution(mesh):
    req_count, exp_count = mesh.devices.shape
    split = Mesh(
        mesh.devices.reshape(req_count, exp_count // CORES, CORES), ("req", "z", "core")
    )
    exp = ("z", "core")
    everywhere = ("req", "z", "core")
    in_specs = (
        P("req", None),
        P(),
        P(None, None, exp),
        P(exp, None),
        P("req", exp, None),
        P("req", exp, None),
        P("req"),
        P("req", None),
        P(),
        P(),
        P(everywhere, None),
        P(everywhere, None, None),
        P(everywhere, None, None),
    )
    return jax.shard_map(
        per_device,
        mesh=split,
        in_specs=in_specs,
        out_specs=P(everywhere, None),
        check_vma=False,
    )
```

time: 378 us -> 158 us (0.42)
  waiting for transfers between devices: 154 us -> 54 us
  blocking collectives: 86.8 us -> 32.7 us
  Pallas kernels: 0 us -> 41.6 us
  other arithmetic: 43.2 us -> 1.64 us
  local copies, waits for them, and re-layouts: 45.7 us -> 6.9 us
  matrix products: 27.2 us -> 0 us
  starting transfers between devices: 6.04 us -> 20.2 us
  between operations: 13.5 us -> 0.19 us
    all_gather x2 -> x0, waiting for transfers between devices: 70.4 us -> none  [the longest x1 37.6 us: joined(): everything = jax.tree.map(lambda part: lax.all_gather(part, axis), array)]
    pallas_call x0 -> x10, Pallas kernels: none -> 41.6 us  [the longest x1 19.5 us: per_device(): call(functools.partial(page_kernel, scale, tree), sds((exp_count, padded,...]
    reduce_scatter x1 -> x0, waiting for transfers between devices: 31.5 us -> none  [per_device(): lax.psum_scatter(jnp.dot(attention, w_out, preferred_element_type=jnp.flo...]
    add x18 -> x1, other arithmetic: 28.2 us -> 0.07 us  [per_device(): parents + tree * jnp.arange(requests, dtype=jnp.int32)[:, None]]
    all_to_all x1, blocking collectives: 60.5 us -> 32.7 us  [per_device(): lax.all_to_all(outgoing.reshape(experts, SLOTS, packed), ('req', 'z'), sp...]
    dot_general x18 -> x0, matrix products: 27.2 us -> none  [the longest x1 6.12 us: per_device(): jnp.dot(flat_rows, gate_up_rows, preferred_element_type=jnp.float32)]
    all_gather x2 -> x0, blocking collectives: 26.3 us -> none  [joined(): everything = jax.tree.map(lambda part: lax.all_gather(part, axis), array)]
    reshape x5 -> x3, local copies, waits for them, and re-layouts: 25.3 us -> 0.13 us  [the longest x1 0.12 us: per_device(): (parents + tree * jnp.arange(requests, dtype=jnp.int32)[:, None]).reshape...]
  transfers between devices with their start and end apart: 4 -> 12, of which waited for: 4 -> 8; matrix products, arithmetic and copies ran while one was open for 2% -> 1% of each run, Pallas kernels for 0% -> 6%
where the time goes in v1:
time: 158 us; the launch traced here: 157 us
  waiting for transfers between devices  54 us (34%)
  Pallas kernels  41.6 us (26%)
  blocking collectives  32.7 us (21%)
  starting transfers between devices  20.2 us (13%)
  local copies, waits for them, and re-layouts  6.9 us (4%)
  other arithmetic  1.64 us (1%)
    all_to_all x1, blocking collectives, per_device(): lax.all_to_all(outgoing.reshape(experts, SLOTS, packed), ('req', 'z'), sp...  32.7 us
    all_to_all x1, waiting for transfers between devices, per_device(): lax.all_to_all(summed.reshape(experts, SLOTS, packed), ('req', 'z'), spli...  24.2 us
    pallas_call x1, Pallas kernels, per_device(): call(functools.partial(page_kernel, scale, tree), sds((exp_count, padded,...  19.5 us
    all_to_all x1, waiting for transfers between devices, per_device(): lax.all_to_all(mixed, ('z', 'core'), split_axis=0, concat_axis=0, tiled=T...  12.6 us
    all_to_all x1, waiting for transfers between devices, per_device(): lax.all_to_all(partial.reshape(exp_count * padded, local_width), ('z', 'c...  9.57 us
    pallas_call x1, Pallas kernels, per_device(): their_out = expert(theirs, w_gate_up[0], w_down[0])  6.79 us
    pallas_call x1, Pallas kernels, per_device(): mine_out = expert(rows, w_gate_up[0], w_down[0])  6.78 us
    ppermute x3, starting transfers between devices, over_z(): lax.ppermute(value, 'z', [(i, (i + step) % z_count) for i in range(z_coun...  6.65 us
  transfers between devices with their start and end apart: 12, of which 8 were waited for; matrix products, arithmetic and copies ran while one was open for 1% of the time, Pallas kernels for 6%

profile of v1, /device:TPU:0, one launch (start us, length us, event | category | flops | bytes accessed | tf_op | source)
XLA Modules:
  0.0 157.2 jit_solution(18240559741907655791)
XLA Ops:
  0.0 1.4 slice_bitcast_fusion.w_ref
  1.4 0.1 copy-done
  1.5 0.6 shard_map.127.refs_0_.q_ref
  2.1 2.1 %collective-permute-start = (bf16[192,256]{1,0:T(8,128)(2,1)S(1)}, bf16[192,256]{1,0:T(8,128)(2,1)S(1)}, u32[]{:S(2)}, u32[]{:S(2)}) collective-permute-start(bf16[192,256]{1,0:T(8,128)(2,1)S(1)} %shard_map.127.refs_0_.q_ref), channel_id=1, source_target_pairs={{0,2},{2,4},{4,6},{6,0},{1,3},{3,5},{5,7},{7,1},{8,10},{10,12},{12... | collective-permute-start | bytes 294920 | tf_op jit(solution)/shard_map/ppermute | solution.py:349
  4.1 3.6 %collective-permute-start.1 = (bf16[192,256]{1,0:T(8,128)(2,1)S(1)}, bf16[192,256]{1,0:T(8,128)(2,1)S(1)}, u32[]{:S(2)}, u32[]{:S(2)}) collective-permute-start(bf16[192,256]{1,0:T(8,128)(2,1)S(1)} %shard_map.127.refs_0_.q_ref), channel_id=1, source_target_pairs={{0,4},{2,6},{4,0},{6,2},{1,5},{3,7},{5,1},{7,3},{8,12},{10,14},{12... | collective-permute-start | bytes 294920 | tf_op jit(solution)/shard_map/ppermute | solution.py:349
  7.7 1.0 collective-permute-start.2
  8.7 0.0 collective-permute-start.3
  8.7 0.3 collective-permute-done.refs_1_
  9.1 0.2 collective-permute-start.4
  9.2 3.1 %collective-permute-done.1.refs_2_ = bf16[192,256]{1,0:T(8,128)(2,1)S(1)} collective-permute-done((bf16[192,256]{1,0:T(8,128)(2,1)S(1)}, bf16[192,256]{1,0:T(8,128)(2,1)S(1)}, u32[]{:S(2)}, u32[]{:S(2)}) %collective-permute-start.1) | collective-permute-done | bytes 98336 | tf_op jit(solution)/shard_map/ppermute | solution.py:349
  12.3 0.0 collective-permute-start.5
  12.3 0.0 collective-permute-done.2.refs_3_
  12.4 0.5 collective-permute-start.6
  12.9 0.1 concatenate.3.meta_ref
  13.0 0.0 collective-permute-done.3.refs_4_
  13.0 0.0 collective-permute-done.4.refs_5_
  13.0 0.7 collective-permute-done.5.refs_6_
  13.6 0.2 collective-permute-done.6.refs_7_
  13.8 2.2 %copy-done.1 = bf16[4,256,2048]{2,1,0:T(8,128)(2,1)S(1)} copy-done((bf16[4,256,2048]{2,1,0:T(8,128)(2,1)S(1)}, bf16[4,256,2048]{2,1,0:T(8,128)(2,1)}, u32[]{:S(2)}) %copy-start.1) | copy-done | bytes 4194328
  16.0 19.5 %shard_map.128 = bf16[8,200,256]{2,1,0:T(8,128)(2,1)} custom-call(s32[16]{0:T(128)S(1)} %concatenate.3.meta_ref, bf16[192,256]{1,0:T(8,128)(2,1)S(1)} %shard_map.127.refs_0_.q_ref, bf16[192,256]{1,0:T(8,128)(2,1)S(1)} %collective-permute-done.refs_1_, bf16[192,256]{1,0:T(8,128)(2,1)S(1)} %collective-permute-done.1.refs_2_, ...), custom_call_target="tpu_custom_call" | custom-call | flops 402653184 | bytes 8388608 | tf_op jit(solution)/shard_map/pallas_call | solution.py:384
  35.5 4.2 %all-to-all-start = ((bf16[8,200,256]{2,1,0:T(8,128)(2,1)}), bf16[8,200,256]{2,1,0:T(8,128)(2,1)}, u32[]{:S(2)}, u32[]{:S(2)}) async-start(bf16[8,200,256]{2,1,0:T(8,128)(2,1)} %shard_map.128), calls=%async_computation | async-start | bytes 1638400 | tf_op jit(solution)/shard_map/all_to_all | solution.py:392
  39.7 0.0 copy-start.8
  39.7 1.7 %slice.9.w_ref = bf16[2,2048,256]{2,1,0:T(8,128)(2,1)S(1)} slice(bf16[3,2048,256]{2,1,0:T(8,128)(2,1)} %bitcast.31), slice={[1:3], [0:2048], [0:256]} | slice | bytes 4194304 | tf_op jit(solution)/shard_map/slice | solution.py:367
  41.4 0.0 copy-done.8
  41.5 0.1 broadcast_add_fusion
  41.5 0.1 reshape.47.up_ref
  41.7 2.0 %shard_map.129 = (f32[192,256]{1,0:T(8,128)S(1)}, f32[8,256]{1,0:T(8,128)S(1)}) custom-call(bf16[192,2048]{1,0:T(8,128)(2,1)S(1)} %copy-done, bf16[1,2048]{1,0:T(2,128)(2,1)S(1)} %reshape.40.g_ref, bf16[2,2048,256]{2,1,0:T(8,128)(2,1)S(1)} %slice.9.w_ref, bf16[192,256]{1,0:T(8,128)(2,1)S(1)} %shard_map.127.refs_0_.q_ref, s32[192,1]{1,0:T(8,128)S(1)} %reshape.47.up_ref), custom_call_target="tpu_custom_call" | custom-call | flops 402653184 | bytes 2883584 | tf_op jit(solution)/shard_map/pallas_call | solution.py:360
  43.6 9.6 %all-to-all-done.parts_ref = bf16[8,200,256]{2,1,0:T(8,128)(2,1)} async-done(((bf16[8,200,256]{2,1,0:T(8,128)(2,1)}), bf16[8,200,256]{2,1,0:T(8,128)(2,1)}, u32[]{:S(2)}, u32[]{:S(2)}) %all-to-all-start) | async-done | bytes 819232 | tf_op jit(solution)/shard_map/all_to_all | solution.py:392
  53.2 1.2 copy-done.2
  54.4 3.2 %shard_map.130 = bf16[192,2048]{1,0:T(8,128)(2,1)} custom-call(bf16[8,200,256]{2,1,0:T(8,128)(2,1)} %all-to-all-done.parts_ref, f32[192,256]{1,0:T(8,128)S(1)} %get-tuple-element.10.tree_o_ref, f32[8,256]{1,0:T(8,128)S(1)} %get-tuple-element.11.tree_lse_ref, bf16[256,2048]{1,0:T(8,128)(2,1)S(1)} %copy-done.2), custom_call_target="tpu_custom_call" | custom-call | flops 201326592 | bytes 1835008 | tf_op jit(solution)/shard_map/pallas_call | solution.py:399
  57.6 3.5 %all-to-all-start.1 = ((bf16[8,24,2048]{2,1,0:T(8,128)(2,1)}), bf16[8,24,2048]{2,1,0:T(8,128)(2,1)S(1)}, u32[]{:S(2)}, u32[]{:S(2)}) async-start(bf16[8,24,2048]{2,1,0:T(8,128)(2,1)} %bitcast.11), calls=%async_computation.1 | async-start | bytes 1572864 | tf_op jit(solution)/shard_map/all_to_all | solution.py:407
  61.2 0.4 shard_map.131.place_ref
  61.6 12.6 %all-to-all-done.1.parts_ref = bf16[8,24,2048]{2,1,0:T(8,128)(2,1)S(1)} async-done(((bf16[8,24,2048]{2,1,0:T(8,128)(2,1)}), bf16[8,24,2048]{2,1,0:T(8,128)(2,1)S(1)}, u32[]{:S(2)}, u32[]{:S(2)}) %all-to-all-start.1) | async-done | bytes 786464 | tf_op jit(solution)/shard_map/all_to_all | solution.py:407
  74.2 0.8 shard_map.132
  75.0 0.0 copy-start.5
  75.0 32.7 %all_to_all.25 = bf16[64,8,1536]{2,1,0:T(8,128)(2,1)S(1)} all-to-all(bf16[64,8,1536]{2,1,0:T(8,128)(2,1)S(1)} %bitcast.25), channel_id=1, replica_groups=mesh['req'=16,'z'=4,'core'=2] {'req','z'}, dimensions={0} | all-to-all | bytes 3145728 | tf_op jit(solution)/shard_map/all_to_all | solution.py:422
  107.7 0.0 collective-permute-start.7
  107.7 3.4 %collective-permute-done.7.x_ref = bf16[512,1536]{1,0:T(8,128)(2,1)S(1)} collective-permute-done((bf16[512,1536]{1,0:T(8,128)(2,1)S(1)}, bf16[512,1536]{1,0:T(8,128)(2,1)S(1)}, u32[]{:S(2)}, u32[]{:S(2)}) %collective-permute-start.7) | collective-permute-done | bytes 1572896 | tf_op jit(solution)/shard_map/ppermute | solution.py:352
  111.1 6.8 %shard_map.134 = bf16[512,1536]{1,0:T(8,128)(2,1)S(1)} custom-call(bf16[512,1536]{1,0:T(8,128)(2,1)S(1)} %collective-permute-done.7.x_ref, bf16[2048,1024]{1,0:T(8,128)(2,1)} %bitcast.32, bf16[512,2048]{1,0:T(8,128)(2,1)S(1)} %bitcast.28), custom_call_target="tpu_custom_call" | custom-call | flops 3221225472 | bytes 6291456 | tf_op jit(solution)/shard_map/pallas_call | solution.py:446
  117.9 0.2 collective-permute-start.8
  118.1 6.8 %shard_map.133 = bf16[512,1536]{1,0:T(8,128)(2,1)S(1)} custom-call(bf16[512,1536]{1,0:T(8,128)(2,1)S(1)} %bitcast.24, bf16[2048,1024]{1,0:T(8,128)(2,1)} %bitcast.33, bf16[512,2048]{1,0:T(8,128)(2,1)S(1)} %bitcast.29), custom_call_target="tpu_custom_call" | custom-call | flops 3221225472 | bytes 6291456 | tf_op jit(solution)/shard_map/pallas_call | solution.py:445
  124.9 0.0 collective-permute-done.8
  124.9 1.6 fusion
  126.5 4.9 %all-to-all-start.3 = ((bf16[64,8,1536]{2,1,0:T(8,128)(2,1)}), bf16[64,8,1536]{2,1,0:T(8,128)(2,1)S(1)}, u32[]{:S(2)}, u32[]{:S(2)}) async-start(bf16[64,8,1536]{2,1,0:T(8,128)(2,1)} %fusion), calls=%async_computation.3 | async-start | bytes 3145728 | tf_op jit(solution)/shard_map/all_to_all | solution.py:449
  131.4 0.1 copy.16.routes_ref
  131.4 0.6 shard_map.135.table_ref
  132.0 24.2 %all-to-all-done.3 = bf16[64,8,1536]{2,1,0:T(8,128)(2,1)S(1)} async-done(((bf16[64,8,1536]{2,1,0:T(8,128)(2,1)}), bf16[64,8,1536]{2,1,0:T(8,128)(2,1)S(1)}, u32[]{:S(2)}, u32[]{:S(2)}) %all-to-all-start.3) | async-done | bytes 1572896 | tf_op jit(solution)/shard_map/all_to_all | solution.py:449
  156.2 1.0 shard_map.136
  (19 shorter events, 0.0 us)
Async XLA Ops:
  0.0 1.4 copy-start.6
  0.0 1.5 copy-start
  0.0 12.9 %copy-start.9 = (s32[4]{0:T(128)S(1)}, s32[4]{0:T(128)}, u32[]{:S(2)}) copy-start(s32[4]{0:T(128)} %param.19) | copy-start | bytes 52
  2.1 7.0 %collective-permute-start = (bf16[192,256]{1,0:T(8,128)(2,1)S(1)}, bf16[192,256]{1,0:T(8,128)(2,1)S(1)}, u32[]{:S(2)}, u32[]{:S(2)}) collective-permute-start(bf16[192,256]{1,0:T(8,128)(2,1)S(1)} %shard_map.127.refs_0_.q_ref), channel_id=1, source_target_pairs={{0,2},{2,4},{4,6},{6,0},{1,3},{3,5},{5,7},{7,1},{8,10},{10,12},{12... | collective-permute-start | bytes 294920 | tf_op jit(solution)/shard_map/ppermute | solution.py:349
  4.1 8.2 %collective-permute-start.1 = (bf16[192,256]{1,0:T(8,128)(2,1)S(1)}, bf16[192,256]{1,0:T(8,128)(2,1)S(1)}, u32[]{:S(2)}, u32[]{:S(2)}) collective-permute-start(bf16[192,256]{1,0:T(8,128)(2,1)S(1)} %shard_map.127.refs_0_.q_ref), channel_id=1, source_target_pairs={{0,4},{2,6},{4,0},{6,2},{1,5},{3,7},{5,1},{7,3},{8,12},{10,14},{12... | collective-permute-start | bytes 294920 | tf_op jit(solution)/shard_map/ppermute | solution.py:349
  7.7 4.6 %collective-permute-start.2 = (bf16[192,256]{1,0:T(8,128)(2,1)S(1)}, bf16[192,256]{1,0:T(8,128)(2,1)S(1)}, u32[]{:S(2)}, u32[]{:S(2)}) collective-permute-start(bf16[192,256]{1,0:T(8,128)(2,1)S(1)} %shard_map.127.refs_0_.q_ref), channel_id=1, source_target_pairs={{0,6},{2,0},{4,2},{6,4},{1,7},{3,1},{5,3},{7,5},{8,14},{10,8},{12,... | collective-permute-start | bytes 294920 | tf_op jit(solution)/shard_map/ppermute | solution.py:349
  8.7 4.2 %collective-permute-start.3 = (bf16[192,256]{1,0:T(8,128)(2,1)S(1)}, bf16[192,256]{1,0:T(8,128)(2,1)S(1)}, u32[]{:S(2)}, u32[]{:S(2)}) collective-permute-start(bf16[192,256]{1,0:T(8,128)(2,1)S(1)} %shard_map.127.refs_0_.q_ref), channel_id=1, source_target_pairs={{0,1},{1,0},{2,3},{3,2},{4,5},{5,4},{6,7},{7,6},{8,9},{9,8},{10,11... | collective-permute-start | bytes 294920 | tf_op jit(solution)/shard_map/ppermute | solution.py:352
  9.1 3.9 %collective-permute-start.4 = (bf16[192,256]{1,0:T(8,128)(2,1)S(1)}, bf16[192,256]{1,0:T(8,128)(2,1)S(1)}, u32[]{:S(2)}, u32[]{:S(2)}) collective-permute-start(bf16[192,256]{1,0:T(8,128)(2,1)S(1)} %collective-permute-done.refs_1_), channel_id=1, source_target_pairs={{0,1},{1,0},{2,3},{3,2},{4,5},{5,4},{6,7},{7,6},{8,9},{9,8},{10,11... | collective-permute-start | bytes 294920 | tf_op jit(solution)/shard_map/ppermute | solution.py:352
  12.3 1.3 collective-permute-start.5
  12.4 1.5 collective-permute-start.6
  13.8 2.2 %copy-start.1 = (bf16[4,256,2048]{2,1,0:T(8,128)(2,1)S(1)}, bf16[4,256,2048]{2,1,0:T(8,128)(2,1)}, u32[]{:S(2)}) copy-start(bf16[4,256,2048]{2,1,0:T(8,128)(2,1)} %refs_8_.1) | copy-start | bytes 12582916
  35.5 17.7 %all-to-all-start = ((bf16[8,200,256]{2,1,0:T(8,128)(2,1)}), bf16[8,200,256]{2,1,0:T(8,128)(2,1)}, u32[]{:S(2)}, u32[]{:S(2)}) async-start(bf16[8,200,256]{2,1,0:T(8,128)(2,1)} %shard_map.128), calls=%async_computation | async-start | bytes 1638400 | tf_op jit(solution)/shard_map/all_to_all | solution.py:392
  39.7 1.8 %copy-start.8 = (s32[4,48]{1,0:T(4,128)S(1)}, s32[4,48]{1,0:T(4,128)}, u32[]{:S(2)}) copy-start(s32[4,48]{1,0:T(4,128)} %param.20) | copy-start | bytes 2308
  53.2 1.2 copy-start.2
  54.4 6.7 %copy-start.7 = (bf16[2048]{0:T(1024)(128)(2,1)S(1)}, bf16[2048]{0:T(1024)(128)(2,1)}, u32[]{:S(2)}) copy-start(bf16[2048]{0:T(1024)(128)(2,1)} %param.21) | copy-start | bytes 12292
  54.4 6.8 %copy-start.4 = (s32[24,8]{0,1:T(8,128)S(1)}, s32[24,8]{0,1:T(8,128)}, u32[]{:S(2)}) copy-start(s32[24,8]{0,1:T(8,128)} %param.23) | copy-start | bytes 2308
  57.6 16.6 %all-to-all-start.1 = ((bf16[8,24,2048]{2,1,0:T(8,128)(2,1)}), bf16[8,24,2048]{2,1,0:T(8,128)(2,1)S(1)}, u32[]{:S(2)}, u32[]{:S(2)}) async-start(bf16[8,24,2048]{2,1,0:T(8,128)(2,1)} %bitcast.11), calls=%async_computation.1 | async-start | bytes 1572864 | tf_op jit(solution)/shard_map/all_to_all | solution.py:407
  75.0 36.1 %copy-start.5 = (bf16[1,512,2048]{2,1,0:T(8,128)(2,1)S(1)}, bf16[1,512,2048]{2,1,0:T(8,128)(2,1)}, u32[]{:S(2)}) copy-start(bf16[1,512,2048]{2,1,0:T(8,128)(2,1)} %param.25) | copy-start | bytes 6291460
  107.7 3.4 %collective-permute-start.7 = (bf16[512,1536]{1,0:T(8,128)(2,1)S(1)}, bf16[512,1536]{1,0:T(8,128)(2,1)S(1)}, u32[]{:S(2)}, u32[]{:S(2)}) collective-permute-start(bf16[512,1536]{1,0:T(8,128)(2,1)S(1)} %bitcast.23), channel_id=1, source_target_pairs={{0,1},{1,0},{2,3},{3,2},{4,5},{5,4},{6,7},{7,6},{8,9},{9,8},{10,11... | collective-permute-start | bytes 4718600 | tf_op jit(solution)/shard_map/ppermute | solution.py:352
  117.9 7.0 %collective-permute-start.8 = (bf16[512,1536]{1,0:T(8,128)(2,1)S(1)}, bf16[512,1536]{1,0:T(8,128)(2,1)S(1)}, u32[]{:S(2)}, u32[]{:S(2)}) collective-permute-start(bf16[512,1536]{1,0:T(8,128)(2,1)S(1)} %shard_map.134), channel_id=1, source_target_pairs={{0,1},{1,0},{2,3},{3,2},{4,5},{5,4},{6,7},{7,6},{8,9},{9,8},{10,11... | collective-permute-start | bytes 4718600 | tf_op jit(solution)/shard_map/ppermute | solution.py:352
  126.5 5.0 %copy-start.3 = (bf16[2048,64]{0,1:T(8,128)(2,1)S(1)}, bf16[2048,64]{0,1:T(8,128)(2,1)}, u32[]{:S(2)}) copy-start(bf16[2048,64]{0,1:T(8,128)(2,1)} %param.22) | copy-start | bytes 786436
  126.5 29.7 %all-to-all-start.3 = ((bf16[64,8,1536]{2,1,0:T(8,128)(2,1)}), bf16[64,8,1536]{2,1,0:T(8,128)(2,1)S(1)}, u32[]{:S(2)}, u32[]{:S(2)}) async-start(bf16[64,8,1536]{2,1,0:T(8,128)(2,1)} %fusion), calls=%async_computation.3 | async-start | bytes 3145728 | tf_op jit(solution)/shard_map/all_to_all | solution.py:449

commit v2 on v1

--- a/solution.py
+++ b/solution.py
@@ -20,6 +20,7 @@
 BF16 = jnp.bfloat16
 VMEM = pltpu.VMEM
 SMEM = pltpu.SMEM
+HBM = pltpu.HBM
 
 
 def dot(a, b):
@@ -34,7 +35,7 @@
     return lax.broadcasted_iota(jnp.int32, shape, axis)
 
 
-def call(body, out, in_spaces, scratch=(), flops=0, bytes_accessed=0, vmem=48 << 20):
+def call(body, out, in_spaces, scratch=(), flops=0, bytes_accessed=0, vmem=10 << 20):
     out_spec = jax.tree.map(lambda _: pl.BlockSpec(memory_space=VMEM), out)
     return pl.pallas_call(
         body,
@@ -58,15 +59,30 @@
     return (values * inverse * gain).astype(BF16)
 
 
-def query_kernel(x_ref, g_ref, w_ref, q_ref):
+def query_kernel(x_hbm, g_ref, w_hbm, q_ref, x_ref, w_ref, sems):
+    x_copy = pltpu.make_async_copy(x_hbm, x_ref, sems.at[0])
+    w_copy = pltpu.make_async_copy(w_hbm.at[0], w_ref, sems.at[1])
+    x_copy.start()
+    w_copy.start()
+    x_copy.wait()
     normed = normed_rows(x_ref[...].astype(F32), g_ref[...].astype(F32))
+    w_copy.wait()
     q_ref[...] = dot(normed, w_ref[...]).astype(BF16)
 
 
-def tree_kernel(scale, x_ref, g_ref, w_ref, q_ref, up_ref, o_ref, lse_ref, turn):
+def tree_kernel(
+    scale, x_ref, g_ref, w_hbm, q_ref, up_ref, o_ref, lse_ref, turn, w_ref, sems
+):
     tokens, width = q_ref.shape
+    w_copies = [
+        pltpu.make_async_copy(w_hbm.at[i + 1], w_ref.at[i], sems.at[i]) for i in range(2)
+    ]
+    for w_copy in w_copies:
+        w_copy.start()
     normed = normed_rows(x_ref[...].astype(F32), g_ref[...].astype(F32))
+    w_copies[0].wait()
     keys = dot(normed, w_ref[0]).astype(BF16)
+    w_copies[1].wait()
     values = dot(normed, w_ref[1]).astype(BF16)
     row = iota((tokens, tokens), 0)
     column = iota((tokens, tokens), 1)
@@ -90,64 +106,132 @@
     lse_ref[...] = jnp.transpose(turn[...])[0:8, :]
 
 
-def page_kernel(scale, tree, meta_ref, *refs):
-    pieces = refs[:8]
-    k_ref, v_ref, out_ref, q_all, turn = refs[8:]
-    requests, page = k_ref.shape[0], k_ref.shape[1]
-    owners = out_ref.shape[0]
-    tokens = requests * tree
-    heads = pieces[0].shape[1] // HEAD_DIM
-    for i, piece in enumerate(pieces):
-        q_all[meta_ref[8 + i]] = piece[...]
+def page_kernel(scale, tree, kept, meta_ref, *refs):
+    pieces, (k_hbm, v_hbm) = refs[:4], refs[4:6]
+    outs = refs[7:-5] if kept else refs[6:-5]
+    s_all, p_all, k_ref, v_ref, sems = refs[-5:]
+    out_ref = outs[0]
+    requests, page = k_hbm.shape[0], k_hbm.shape[1]
+    width = pieces[0].shape[1]
+    pair = 2 * tree
     lane = iota((tree, 128), 1)
-    column = iota((tree, page), 1)
+    wide = iota((tree, width), 1) < HEAD_DIM
+    first_at = 8 if kept else 12
+
+    def copies(r, which):
+        source, target = (k_hbm, k_ref) if which == 0 else (v_hbm, v_ref)
+        found = []
+        for i in range(len(pieces)):
+            at = pl.ds(pl.multiple_of(meta_ref[first_at + i], width), width)
+            found.append(
+                pltpu.make_async_copy(
+                    source.at[r, :, at], target.at[r, i], sems.at[which, r, i]
+                )
+            )
+        return found
+
+    for r in range(requests):
+
+        @pl.when(meta_ref[r] > 0)
+        def _():
+            for which in range(2):
+                for copy in copies(r, which):
+                    copy.start()
+
     for r in range(requests):
         rows = slice(r * tree, (r + 1) * tree)
         live = meta_ref[r]
 
         @pl.when(live > 0)
         def _():
+            for copy in copies(r, 0):
+                copy.wait()
+            for i, piece in enumerate(pieces):
+                query = piece[rows, :]
+                zero = jnp.zeros_like(query)
+                both = jnp.concatenate(
+                    [jnp.where(wide, query, zero), jnp.where(wide, zero, query)], axis=0
+                )
+                s_all[i * pair : (i + 1) * pair, :] = dot_t(both, k_ref[r, i])
+            scores = s_all[...] * scale
+            scores = jnp.where(iota(scores.shape, 1) < live, scores, NEGATIVE)
+            high = jnp.max(scores, axis=-1, keepdims=True)
+            weights = jnp.exp(scores - high)
+            total = jnp.sum(weights, axis=-1, keepdims=True)
+            p_all[...] = weights.astype(BF16)
+            inverse = 1.0 / total
+            lse = high + jnp.log(total)
+            first = lse.astype(BF16).astype(F32)
+            second = (lse - first).astype(BF16).astype(F32)
+            third = lse - first - second
             stats = jnp.zeros((tree, 128), F32)
-            usable = column < live
-            for e in range(owners):
-                for h in range(heads):
-                    at = slice((e * heads + h) * HEAD_DIM, (e * heads + h + 1) * HEAD_DIM)
+            for copy in copies(r, 1):
+                copy.wait()
+            for i in range(len(pieces)):
+                summed = dot(p_all[i * pair : (i + 1) * pair, :], v_ref[r, i])
+                for h in range(2):
+                    own = slice(i * pair + h * tree, i * pair + (h + 1) * tree)
                     cut = slice(h * HEAD_DIM, (h + 1) * HEAD_DIM)
-                    scores = dot_t(q_all[e, rows, cut], k_ref[r, :, at]) * scale
-                    scores = jnp.where(usable, scores, NEGATIVE)
-                    high = jnp.max(scores, axis=-1, keepdims=True)
-                    weights = jnp.exp(scores - high)
-                    total = jnp.sum(weights, axis=-1, keepdims=True)
-                    summed = dot(weights.astype(BF16), v_ref[r, :, at])
-                    out_ref[e, rows, cut] = (summed / total).astype(BF16)
-                    lse = high + jnp.log(total)
-                    first = lse.astype(BF16).astype(F32)
-                    second = (lse - first).astype(BF16).astype(F32)
-                    third = lse - first - second
-                    stats = jnp.where(lane == e * 8 + h, first, stats)
-                    stats = jnp.where(lane == e * 8 + 2 + h, second, stats)
-                    stats = jnp.where(lane == e * 8 + 4 + h, third, stats)
-            turn[rows, :] = stats
+                    value = summed[h * tree : (h + 1) * tree, cut] * inverse[own]
+                    out_ref[2 * i + h, rows, :] = value.astype(out_ref.dtype)
+                    if kept:
+                        stats = jnp.where(lane == i * 8 + h, lse[own], stats)
+                    else:
+                        for j, part in enumerate((first, second, third)):
+                            stats = jnp.where(lane == i * 8 + 2 * j + h, part[own], stats)
+            if kept:
+                outs[1][rows, :] = stats
+            else:
+                out_ref[8, rows, :] = stats.astype(BF16)
 
         @pl.when(live <= 0)
         def _():
-            for e in range(owners):
-                out_ref[e, rows, :] = jnp.zeros((tree, heads * HEAD_DIM), BF16)
-            turn[rows, :] = jnp.where(lane % 8 < 2, NEGATIVE, 0.0)
-
+            for i in range(8):
+                out_ref[i, rows, :] = jnp.zeros((tree, HEAD_DIM), out_ref.dtype)
+            empty = jnp.where(lane % 8 < 2, NEGATIVE, 0.0)
+            if kept:
+                outs[1][rows, :] = empty
+            else:
+                out_ref[8, rows, :] = empty.astype(BF16)
+
+
+def merge_kernel(other_ref, kept_ref, lse_ref, *refs):
+    outs, turn = refs[:-1], refs[-1]
+    tokens = lse_ref.shape[0]
+    sent = other_ref[8].astype(F32)
+    other = sent + pltpu.roll(sent, 126, 1) + pltpu.roll(sent, 124, 1)
+    kept = lse_ref[...]
+    high = jnp.maximum(other, kept)
+    other, kept = jnp.exp(other - high), jnp.exp(kept - high)
+    whole = other + kept
+    inverse = 1.0 / whole
+    other, kept = other * inverse, kept * inverse
+    lse = jnp.where(iota(high.shape, 1) % 8 < 2, high + jnp.log(whole), 0.0)
+    first = lse.astype(BF16).astype(F32)
+    second = (lse - first).astype(BF16).astype(F32)
+    third = lse - first - second
+    turn[0:tokens, :] = first + pltpu.roll(second, 2, 1) + pltpu.roll(third, 4, 1)
     turn[tokens:, :] = jnp.zeros((turn.shape[0] - tokens, 128), F32)
     turned = jnp.transpose(turn[...])
-    for e in range(owners):
-        out_ref[e, tokens:, :] = turned[e * 8 : (e + 1) * 8, :].astype(BF16)
-
-
-def out_kernel(parts_ref, tree_o_ref, tree_lse_ref, w_ref, out_ref, turn):
-    parts, padded, width = parts_ref.shape
+    for i, out_ref in enumerate(outs):
+        for h in range(2):
+            at = i * 8 + h
+            value = other[:, at : at + 1] * other_ref[2 * i + h].astype(F32)
+            value = value + kept[:, at : at + 1] * kept_ref[2 * i + h]
+            out_ref[0:tokens, h * HEAD_DIM : (h + 1) * HEAD_DIM] = value.astype(BF16)
+        out_ref[tokens:, :] = turned[i * 8 : (i + 1) * 8, :].astype(BF16)
+
+
+def out_kernel(meta_ref, *refs):
+    parts = refs[:4]
+    tree_o_ref, tree_lse_ref, w_ref, theirs_ref, ours_ref, turn, mixed = refs[4:]
+    padded, width = parts[0].shape
     tokens = padded - 8
     heads = width // HEAD_DIM
+    own = ours_ref.shape[0] // 4
     lses = []
-    for s in range(parts):
-        rows = parts_ref[s, tokens:, :].astype(F32)
+    for part in parts:
+        rows = part[tokens:, :].astype(F32)
         lses.append(rows[0:2] + rows[2:4] + rows[4:6])
     lses.append(tree_lse_ref[0:2, :])
     high = functools.reduce(jnp.maximum, lses)
@@ -156,17 +240,30 @@
     for s, factor in enumerate(factors):
         turn[2 * s : 2 * s + 2, :] = factor / whole
     turned = jnp.transpose(turn[...])[0:tokens, :]
-    columns = []
     for h in range(heads):
         cut = slice(h * HEAD_DIM, (h + 1) * HEAD_DIM)
-        at = 2 * parts + h
+        at = 2 * len(parts) + h
         total = turned[:, at : at + 1] * tree_o_ref[:, cut]
-        for s in range(parts):
+        for s, part in enumerate(parts):
             at = 2 * s + h
-            total = total + turned[:, at : at + 1] * parts_ref[s, 0:tokens, cut].astype(F32)
-        columns.append(total.astype(BF16))
-    attention = jnp.concatenate(columns, axis=1)
-    out_ref[...] = dot(attention, w_ref[...]).astype(BF16)
+            total = total + turned[:, at : at + 1] * part[0:tokens, cut].astype(F32)
+        mixed[:, cut] = total
+
+    def rows_of(first_at):
+        rows = [
+            mixed[pl.ds(pl.multiple_of(meta_ref[first_at + i], 8), own), :] for i in range(4)
+        ]
+        return jnp.concatenate(rows, axis=0).astype(BF16)
+
+    theirs_ref[...] = dot(rows_of(20), w_ref[...]).astype(BF16)
+    ours_ref[...] = dot(rows_of(16), w_ref[...])
+
+
+def fold_kernel(ours_ref, theirs_ref, *outs):
+    own = outs[0].shape[0]
+    for i, out_ref in enumerate(outs):
+        rows = slice(i * own, (i + 1) * own)
+        out_ref[...] = (ours_ref[rows, :] + theirs_ref[rows, :].astype(F32)).astype(out_ref.dtype)
 
 
 def expert_of_row(rows, experts):
@@ -197,17 +294,16 @@
         place_ref[j] = jnp.where(hit, 1.0, 0.0).astype(BF16)
 
 
-def residual_kernel(
-    meta_ref, parts_ref, x_ref, g_ref, place_ref, res_ref, normed_ref, out_ref
-):
-    parts, tokens, width = parts_ref.shape
+def residual_kernel(meta_ref, *refs):
+    parts = refs[:4]
+    x_ref, g_ref, place_ref, res_ref, normed_ref, out_ref = refs[4:]
+    tokens, width = parts[0].shape
     chunks = place_ref.shape[0]
     cut = width // (chunks + 1)
-    start = pl.multiple_of(meta_ref[0] * tokens, 8)
-    residual = parts_ref[0].astype(F32)
-    for s in range(1, parts):
-        residual = residual + parts_ref[s].astype(F32)
-    residual = x_ref[pl.ds(start, tokens), :].astype(F32) + residual
+    start = pl.multiple_of(meta_ref[16], 8)
+    residual = x_ref[pl.ds(start, tokens), :].astype(F32)
+    for part in parts:
+        residual = residual + part[...].astype(F32)
     res_ref[...] = residual
     inverse = lax.rsqrt(jnp.mean(residual * residual, axis=-1, keepdims=True) + EPSILON)
     normed = residual * inverse * g_ref[...].astype(F32)
@@ -254,8 +350,9 @@
         ).astype(BF16)
 
 
-def expert_kernel(block, x_ref, gate_up_ref, down_ref, out_ref):
-    rows, packed = x_ref.shape
+def expert_kernel(first_row, x_ref, gate_up_ref, down_ref, *refs):
+    out_ref = refs[-1]
+    block, packed = out_ref.shape
     width, both = gate_up_ref.shape
     units = both // 2
     cut = width - packed
@@ -271,21 +368,30 @@
         hit = same & (slot_b < CAP) & (slot_a >= CAP) & (slot_b == (slot_a - CAP) * chunks + k)
         pack.append(jnp.where(hit, 1.0, 0.0).astype(BF16))
     is_tail = iota((block, cut), 0) % SLOTS >= CAP
-    for at in range(0, rows, block):
-        span = slice(at, at + block)
-        tail = dot(unpack[0], x_ref[span, 0:cut])
-        for k in range(1, chunks):
-            tail = tail + dot(unpack[k], x_ref[span, k * cut : (k + 1) * cut])
-        up = dot(x_ref[span, :], gate_up_ref[0:packed, :])
-        up = up + dot(tail.astype(BF16), gate_up_ref[packed:, :])
-        gate = up[:, :units]
-        hidden = (gate / (1.0 + jnp.exp(-gate)) * up[:, units:]).astype(BF16)
-        last = dot(hidden, down_ref[:, packed:]).astype(BF16)
-        for k in range(chunks):
-            main = dot(hidden, down_ref[:, k * cut : (k + 1) * cut])
-            out_ref[span, k * cut : (k + 1) * cut] = jnp.where(
-                is_tail, dot(pack[k], last), main
-            ).astype(BF16)
+    span = slice(first_row, first_row + block)
+    tail = dot(unpack[0], x_ref[span, 0:cut])
+    for k in range(1, chunks):
+        tail = tail + dot(unpack[k], x_ref[span, k * cut : (k + 1) * cut])
+    up = dot(x_ref[span, :], gate_up_ref[0:packed, :])
+    up = up + dot(tail.astype(BF16), gate_up_ref[packed:, :])
+    gate = up[:, :units]
+    hidden = (gate / (1.0 + jnp.exp(-gate)) * up[:, units:]).astype(BF16)
+    last = dot(hidden, down_ref[:, packed:]).astype(BF16)
+    for k in range(chunks):
+        main = dot(hidden, down_ref[:, k * cut : (k + 1) * cut])
+        out_ref[:, k * cut : (k + 1) * cut] = jnp.where(
+            is_tail, dot(pack[k], last), main
+        ).astype(BF16)
+
+
+def add_kernel(*refs):
+    out_ref = refs[-1]
+    at = 0
+    for first, second in zip(refs[0:-1:2], refs[1:-1:2]):
+        rows = first.shape[0]
+        total = first[...].astype(F32) + second[...].astype(F32)
+        out_ref[at : at + rows, :] = total.astype(BF16)
+        at += rows
 
 
 def final_kernel(back_ref, table_ref, res_ref, out_ref):
@@ -335,15 +441,22 @@
 
     gain_a = gain_attn.reshape(1, width)
     gain_m = gain_moe.reshape(1, width)
-    w_three = jnp.transpose(w_qkv, (1, 0, 2))
+    w_three = pltpu.with_memory_space_constraint(jnp.transpose(w_qkv, (1, 0, 2)), HBM)
+    cache_keys = pltpu.with_memory_space_constraint(cache_keys, HBM)
+    cache_values = pltpu.with_memory_space_constraint(cache_values, HBM)
 
     query = call(
         query_kernel,
         sds((tokens, local_width), BF16),
-        [VMEM] * 3,
+        [HBM, VMEM, HBM],
+        [
+            pltpu.VMEM((tokens, width), BF16),
+            pltpu.VMEM((width, local_width), BF16),
+            pltpu.SemaphoreType.DMA((2,)),
+        ],
         flops=2 * tokens * width * local_width,
         bytes_accessed=2 * width * (tokens + local_width),
-    )(hidden, gain_a, w_three[0])
+    )(pltpu.with_memory_space_constraint(hidden, HBM), gain_a, w_three)
 
     def over_z(value, step):
         return lax.ppermute(value, "z", [(i, (i + step) % z_count) for i in range(z_count)])
@@ -351,20 +464,33 @@
     def over_core(value):
         return lax.ppermute(value, "core", [(0, 1), (1, 0)])
 
-    pieces = [query] + [over_z(query, step) for step in range(1, z_count)]
-    owners = [((z_index - step) % z_count) * CORES + core for step in range(z_count)]
-    pieces = pieces + [over_core(piece) for piece in pieces]
-    owners = owners + [owner + 1 - 2 * core for owner in owners]
+    steps = range(1, z_count)
+    pieces = [query] + [over_z(query, step) for step in steps]
+    other_pieces = [over_core(piece) for piece in pieces]
+    homes = jnp.bitwise_and(z_index - jnp.arange(z_count), z_count - 1) * CORES
+    homes = jnp.stack([homes + core, homes + 1 - core])
+    meta = jnp.concatenate(
+        [
+            cache_lengths - exp_index * page,
+            jnp.zeros((8 - requests,), jnp.int32),
+            (homes * local_width).reshape(-1),
+            (homes * own).reshape(-1),
+        ]
+    ).astype(jnp.int32)
 
     up = (parents + tree * jnp.arange(requests, dtype=jnp.int32)[:, None]).reshape(tokens, 1)
     tree_o, tree_lse = call(
         functools.partial(tree_kernel, scale),
         (sds((tokens, local_width), F32), sds((8, 256), F32)),
-        [VMEM] * 5,
-        [pltpu.VMEM((256, 128), F32)],
+        [VMEM, VMEM, HBM, VMEM, VMEM],
+        [
+            pltpu.VMEM((256, 128), F32),
+            pltpu.VMEM((2, width, local_width), BF16),
+            pltpu.SemaphoreType.DMA((2,)),
+        ],
         flops=4 * tokens * width * local_width,
         bytes_accessed=2 * width * (tokens + 2 * local_width),
-    )(hidden, gain_a, w_three[1:], query, up)
+    )(hidden, gain_a, w_three, query, up)
 
     place = call(
         place_kernel,
@@ -374,39 +500,56 @@
         bytes_accessed=1 << 18,
     )(routes.T)
 
-    meta = jnp.concatenate(
-        [
-            cache_lengths - exp_index * page,
-            jnp.zeros((8 - requests,), jnp.int32),
-            jnp.stack(owners).astype(jnp.int32),
-        ]
-    )
-    partial = call(
-        functools.partial(page_kernel, scale, tree),
-        sds((exp_count, padded, local_width), BF16),
-        [SMEM] + [VMEM] * 10,
-        [pltpu.VMEM((exp_count, tokens, local_width), BF16), pltpu.VMEM((256, 128), F32)],
-        flops=4 * tokens * page * width,
-        bytes_accessed=4 * requests * page * width,
-    )(meta, *pieces, cache_keys, cache_values)
-    arrived = lax.all_to_all(
-        partial.reshape(exp_count * padded, local_width),
-        ("z", "core"),
-        split_axis=0,
-        concat_axis=0,
-        tiled=True,
-    ).reshape(exp_count, padded, local_width)
-    mixed = call(
+    scratch = [
+        pltpu.VMEM((z_count * 2 * tree, page), F32),
+        pltpu.VMEM((z_count * 2 * tree, page), BF16),
+        pltpu.VMEM((requests, z_count, page, local_width), BF16),
+        pltpu.VMEM((requests, z_count, page, local_width), BF16),
+        pltpu.SemaphoreType.DMA((2, requests, z_count)),
+    ]
+    heads = 2 * z_count
+    for_other = call(
+        functools.partial(page_kernel, scale, tree, False),
+        sds((heads + 1, tokens, HEAD_DIM), BF16),
+        [SMEM] + [VMEM] * 4 + [HBM] * 2,
+        scratch,
+        flops=2 * tokens * page * width,
+        bytes_accessed=2 * requests * page * width,
+        vmem=20 << 20,
+    )(meta, *other_pieces, cache_keys, cache_values)
+    from_other = over_core(for_other)
+    kept, kept_lse = call(
+        functools.partial(page_kernel, scale, tree, True),
+        (sds((heads, tokens, HEAD_DIM), F32), sds((tokens, 128), F32)),
+        [SMEM] + [VMEM] * 4 + [HBM] * 2 + [pl.ANY],
+        scratch,
+        flops=2 * tokens * page * width,
+        bytes_accessed=2 * requests * page * width,
+        vmem=20 << 20,
+    )(meta, *pieces, cache_keys, cache_values, for_other)
+    merged = call(
+        merge_kernel,
+        tuple(sds((padded, local_width), BF16) for _ in range(z_count)),
+        [VMEM] * 3,
+        [pltpu.VMEM((256, 128), F32)],
+        bytes_accessed=1 << 20,
+    )(from_other, kept, kept_lse)
+    arrived = [merged[0]] + [over_z(merged[step], -step) for step in steps]
+    theirs, ours = call(
         out_kernel,
-        sds((tokens, width), BF16),
-        [VMEM] * 4,
-        [pltpu.VMEM((128, 256), F32)],
+        (sds((z_count * own, width), BF16), sds((z_count * own, width), F32)),
+        [SMEM] + [VMEM] * 7,
+        [pltpu.VMEM((128, 256), F32), pltpu.VMEM((tokens, local_width), F32)],
         flops=2 * tokens * width * local_width,
         bytes_accessed=2 * width * (tokens + local_width),
-    )(arrived, tree_o, tree_lse, w_out)
-    mixed = lax.all_to_all(
-        mixed, ("z", "core"), split_axis=0, concat_axis=0, tiled=True
-    ).reshape(exp_count, own, width)
+    )(meta, *arrived, tree_o, tree_lse, w_out)
+    folded = call(
+        fold_kernel,
+        tuple(sds((own, width), BF16 if step else F32) for step in range(z_count)),
+        [VMEM] * 2,
+        bytes_accessed=1 << 20,
+    )(ours, over_core(theirs))
+    mixed = [folded[0]] + [over_z(folded[step], -step) for step in steps]
 
     residual, normed, outgoing = call(
         residual_kernel,
@@ -415,10 +558,10 @@
             sds((own, width), BF16),
             sds((experts * SLOTS, packed), BF16),
         ),
-        [SMEM] + [VMEM] * 4,
+        [SMEM] + [VMEM] * 7,
         flops=1 << 27,
         bytes_accessed=1 << 22,
-    )(exp_index.reshape(1).astype(jnp.int32), mixed, hidden, gain_m, place)
+    )(meta, *mixed, hidden, gain_m, place)
     rows = lax.all_to_all(
         outgoing.reshape(experts, SLOTS, packed),
         ("req", "z"),
@@ -434,18 +577,30 @@
         bytes_accessed=1 << 19,
     )(normed, w_router.T, routes)
 
-    expert = call(
-        functools.partial(expert_kernel, 256),
+    block = experts * SLOTS // 2
+
+    def expert(values, half, after=None):
+        extra = [] if after is None else [after]
+        return call(
+            functools.partial(expert_kernel, half * block),
+            sds((block, packed), BF16),
+            [VMEM] * 3 + [pl.ANY] * len(extra),
+            flops=6 * block * width * w_down.shape[1],
+            bytes_accessed=6 * width * w_down.shape[1],
+            vmem=20 << 20,
+        )(values, w_gate_up[0], w_down[0], *extra)
+
+    theirs = over_core(rows)
+    mine_0 = expert(rows, 0)
+    theirs_0 = expert(theirs, 0, mine_0)
+    theirs_1 = expert(theirs, 1, theirs_0)
+    mine_1 = expert(rows, 1, theirs_1)
+    summed = call(
+        add_kernel,
         sds((experts * SLOTS, packed), BF16),
-        [VMEM] * 3,
-        flops=6 * experts * SLOTS * width * w_down.shape[1],
-        bytes_accessed=6 * width * w_down.shape[1],
-    )
-    theirs = over_core(rows)
-    mine_out = expert(rows, w_gate_up[0], w_down[0])
-    their_out = expert(theirs, w_gate_up[0], w_down[0])
-    other_out = over_core(their_out)
-    summed = (mine_out.astype(F32) + other_out.astype(F32)).astype(BF16)
+        [VMEM] * 4,
+        bytes_accessed=1 << 22,
+    )(mine_0, over_core(theirs_0), mine_1, over_core(theirs_1))
     back = lax.all_to_all(
         summed.reshape(experts, SLOTS, packed),
         ("req", "z"),

time: 158 us -> 124 us (0.78)
  waiting for transfers between devices: 54 us -> 39.4 us
  Pallas kernels: 41.6 us -> 31.8 us
  local copies, waits for them, and re-layouts: 6.9 us -> 1.11 us
    all_to_all x2 -> x0, waiting for transfers between devices: 22.2 us -> none  [the longest x1 12.6 us: per_device(): lax.all_to_all(mixed, ('z', 'core'), split_axis=0, concat_axis=0, tiled=T...]
    pallas_call x5 -> x11, Pallas kernels: 36.8 us -> 25 us  [the longest x4 9.63 us: expert(): call(functools.partial(expert_kernel, half * block), sds((block, packed),...]
    ppermute x3 -> x9, waiting for transfers between devices: 3.44 us -> 11.3 us  [over_z(): lax.ppermute(value, 'z', [(i, (i + step) % z_count) for i in range(z_coun...]
    all_to_all x2 -> x0, starting transfers between devices: 7.75 us -> none  [the longest x1 4.21 us: per_device(): lax.all_to_all(partial.reshape(exp_count * padded, local_width), ('z', 'c...]
    ppermute x3 -> x9, starting transfers between devices: 6.65 us -> 12.6 us  [over_z(): lax.ppermute(value, 'z', [(i, (i + step) % z_count) for i in range(z_coun...]
    unnamed x21 -> x19, local copies, waits for them, and re-layouts: 3.58 us -> 0.12 us
    slice x1 -> x0, local copies, waits for them, and re-layouts: 1.73 us -> none  [per_device(): w_three[1:]]
    ppermute x6 -> x9, waiting for transfers between devices: 4.25 us -> 4.03 us  [over_core(): return lax.ppermute(value, 'core', [(0, 1), (1, 0)])]
  transfers between devices with their start and end apart: 12 -> 19, of which waited for: 8 -> 12; matrix products, arithmetic and copies ran while one was open for 1% -> 0% of each run, Pallas kernels for 6% -> 11%
where the time goes in v2:
time: 124 us
  waiting for transfers between devices  39.4 us (32%)
  blocking collectives  32.1 us (26%)
  Pallas kernels  31.8 us (26%)
  starting transfers between devices  19.2 us (15%)
    all_to_all x1, blocking collectives, per_device(): lax.all_to_all(outgoing.reshape(experts, SLOTS, packed), ('req', 'z'), sp...  32.1 us
    all_to_all x1, waiting for transfers between devices, per_device(): lax.all_to_all(summed.reshape(experts, SLOTS, packed), ('req', 'z'), spli...  24.1 us
    ppermute x9, starting transfers between devices, over_z(): lax.ppermute(value, 'z', [(i, (i + step) % z_count) for i in range(z_coun...  12.6 us
    ppermute x9, waiting for transfers between devices, over_z(): lax.ppermute(value, 'z', [(i, (i + step) % z_count) for i in range(z_coun...  11.3 us
    pallas_call x4, Pallas kernels, expert(): call(functools.partial(expert_kernel, half * block), sds((block, packed),...  9.63 us
    pallas_call x1, Pallas kernels, per_device(): call(functools.partial(page_kernel, scale, tree, False), sds((heads + 1,...  4.89 us
    all_to_all x1, starting transfers between devices, per_device(): lax.all_to_all(summed.reshape(experts, SLOTS, packed), ('req', 'z'), spli...  4.88 us
    pallas_call x1, Pallas kernels, per_device(): call(functools.partial(page_kernel, scale, tree, True), (sds((heads, toke...  4.81 us
  transfers between devices with their start and end apart: 19, of which 12 were waited for; matrix products, arithmetic and copies ran while one was open for 0% of the time, Pallas kernels for 11%

profile of v2, /device:TPU:0, one launch (start us, length us, event | category | flops | bytes accessed | tf_op | source)
XLA Modules:
  0.0 124.1 jit_solution(18297923033567211241)
XLA Ops:
  0.0 0.7 reshape.57.g_ref
  0.7 1.9 %shard_map.127.refs_0_.q_ref = bf16[192,256]{1,0:T(8,128)(2,1)S(1)} custom-call(bf16[192,2048]{1,0:T(8,128)(2,1)} %refs_4_.5, bf16[1,2048]{1,0:T(2,128)(2,1)S(1)} %reshape.57.g_ref, bf16[3,2048,256]{2,1,0:T(8,128)(2,1)} %bitcast.24), custom_call_target="tpu_custom_call" | custom-call | flops 201326592 | bytes 1835008 | tf_op jit(solution)/shard_map/pallas_call | solution.py:448
  2.6 2.1 %collective-permute-start.1 = (bf16[192,256]{1,0:T(8,128)(2,1)S(1)}, bf16[192,256]{1,0:T(8,128)(2,1)S(1)}, u32[]{:S(2)}, u32[]{:S(2)}) collective-permute-start(bf16[192,256]{1,0:T(8,128)(2,1)S(1)} %shard_map.127.refs_0_.q_ref), channel_id=1, source_target_pairs={{0,2},{2,4},{4,6},{6,0},{1,3},{3,5},{5,7},{7,1},{8,10},{10,12},{12... | collective-permute-start | bytes 294920 | tf_op jit(solution)/shard_map/ppermute | solution.py:462
  4.7 3.6 %collective-permute-start.3 = (bf16[192,256]{1,0:T(8,128)(2,1)S(1)}, bf16[192,256]{1,0:T(8,128)(2,1)S(1)}, u32[]{:S(2)}, u32[]{:S(2)}) collective-permute-start(bf16[192,256]{1,0:T(8,128)(2,1)S(1)} %shard_map.127.refs_0_.q_ref), channel_id=1, source_target_pairs={{0,4},{2,6},{4,0},{6,2},{1,5},{3,7},{5,1},{7,3},{8,12},{10,14},{12... | collective-permute-start | bytes 294920 | tf_op jit(solution)/shard_map/ppermute | solution.py:462
  8.2 1.0 collective-permute-start.5
  9.3 0.1 mul.46
  9.4 0.1 mul.48
  9.5 0.1 collective-permute-done.1.refs_1_
  9.6 0.4 collective-permute-start.2
  10.0 2.9 %collective-permute-done.3.refs_2_ = bf16[192,256]{1,0:T(8,128)(2,1)S(1)} collective-permute-done((bf16[192,256]{1,0:T(8,128)(2,1)S(1)}, bf16[192,256]{1,0:T(8,128)(2,1)S(1)}, u32[]{:S(2)}, u32[]{:S(2)}) %collective-permute-start.3) | collective-permute-done | bytes 98336 | tf_op jit(solution)/shard_map/ppermute | solution.py:462
  12.9 0.5 collective-permute-start.6
  13.4 0.1 pad_add_fusion.1.meta_ref
  13.5 0.7 collective-permute-done.4.refs_2_
  14.2 0.2 collective-permute-done.6.refs_3_
  14.3 4.9 %shard_map.128.refs_6_ = bf16[9,192,128]{2,1,0:T(8,128)(2,1)S(1)} custom-call(s32[24]{0:T(128)S(1)} %pad_add_fusion.1.meta_ref, bf16[192,256]{1,0:T(8,128)(2,1)S(1)} %collective-permute-done.refs_0_, bf16[192,256]{1,0:T(8,128)(2,1)S(1)} %collective-permute-done.2.refs_1_, bf16[192,256]{1,0:T(8,128)(2,1)S(1)} %collective-permute-done.4.refs_2_, ...), custom_call_target="tpu_custom_call" | custom-call | flops 201326592 | bytes 4194304 | tf_op jit(solution)/shard_map/pallas_call | solution.py:511
  19.2 0.1 collective-permute-start.7
  19.3 4.8 %shard_map.129 = (f32[8,192,128]{2,1,0:T(8,128)S(1)}, f32[192,128]{1,0:T(8,128)S(1)}) custom-call(s32[24]{0:T(128)S(1)} %pad_add_fusion.1.meta_ref, bf16[192,256]{1,0:T(8,128)(2,1)S(1)} %shard_map.127.refs_0_.q_ref, bf16[192,256]{1,0:T(8,128)(2,1)S(1)} %collective-permute-done.1.refs_1_, bf16[192,256]{1,0:T(8,128)(2,1)S(1)} %collective-permute-done.3.refs_2_, ...), custom_call_target="tpu_custom_call" | custom-call | flops 201326592 | bytes 4194304 | tf_op jit(solution)/shard_map/pallas_call | solution.py:521
  24.2 0.7 shard_map.130
  25.0 3.2 %collective-permute-start.8 = (bf16[200,256]{1,0:T(8,128)(2,1)S(1)}, bf16[200,256]{1,0:T(8,128)(2,1)S(1)}, u32[]{:S(2)}, u32[]{:S(2)}) collective-permute-start(bf16[200,256]{1,0:T(8,128)(2,1)S(1)} %get-tuple-element.25), channel_id=1, source_target_pairs={{0,6},{2,0},{4,2},{6,4},{1,7},{3,1},{5,3},{7,5},{8,14},{10,8},{12,... | collective-permute-start | bytes 307208 | tf_op jit(solution)/shard_map/ppermute | solution.py:462
  28.3 0.1 reshape.64.up_ref
  28.4 3.5 %shard_map.131 = (f32[192,256]{1,0:T(8,128)S(1)}, f32[8,256]{1,0:T(8,128)S(1)}) custom-call(bf16[192,2048]{1,0:T(8,128)(2,1)S(1)} %copy-done.2, bf16[1,2048]{1,0:T(2,128)(2,1)S(1)} %reshape.57.g_ref, bf16[3,2048,256]{2,1,0:T(8,128)(2,1)} %bitcast.25, bf16[192,256]{1,0:T(8,128)(2,1)S(1)} %shard_map.127.refs_0_.q_ref, s32[192,1]{1,0:T(8,128)S(1)} %reshape.64.up_ref), custom_call_target="tpu_custom_call" | custom-call | flops 402653184 | bytes 2883584 | tf_op jit(solution)/shard_map/pallas_call | solution.py:482
  32.0 2.4 %collective-permute-done.9.refs_2_ = bf16[200,256]{1,0:T(8,128)(2,1)S(1)} collective-permute-done((bf16[200,256]{1,0:T(8,128)(2,1)S(1)}, bf16[200,256]{1,0:T(8,128)(2,1)S(1)}, u32[]{:S(2)}, u32[]{:S(2)}) %collective-permute-start.9) | collective-permute-done | bytes 102432 | tf_op jit(solution)/shard_map/ppermute | solution.py:462
  34.4 1.5 %shard_map.132 = (bf16[96,2048]{1,0:T(8,128)(2,1)S(1)}, f32[96,2048]{1,0:T(8,128)S(1)}) custom-call(s32[24]{0:T(128)S(1)} %pad_add_fusion.1.meta_ref, bf16[200,256]{1,0:T(8,128)(2,1)S(1)} %get-tuple-element.24.refs_0_, bf16[200,256]{1,0:T(8,128)(2,1)S(1)} %collective-permute-done.8.refs_1_, bf16[200,256]{1,0:T(8,128)(2,1)S(1)} %collective-permute-done.9.refs_2_, ...), custom_call_target="tpu_custom_call" | custom-call | flops 201326592 | bytes 1835008 | tf_op jit(solution)/shard_map/pallas_call | solution.py:538
  35.8 0.1 collective-permute-start.11
  35.9 1.7 %collective-permute-done.11.theirs_ref = bf16[96,2048]{1,0:T(8,128)(2,1)S(1)} collective-permute-done((bf16[96,2048]{1,0:T(8,128)(2,1)S(1)}, bf16[96,2048]{1,0:T(8,128)(2,1)S(1)}, u32[]{:S(2)}, u32[]{:S(2)}) %collective-permute-start.11) | collective-permute-done | bytes 393248 | tf_op jit(solution)/shard_map/ppermute | solution.py:465
  37.6 0.1 shard_map.133
  37.7 0.9 collective-permute-start.12
  38.6 0.7 collective-permute-start.13
  39.3 1.1 collective-permute-start.14
  40.4 0.4 shard_map.134.refs_6_
  40.9 2.6 %collective-permute-done.12.refs_1_ = bf16[24,2048]{1,0:T(8,128)(2,1)S(1)} collective-permute-done((bf16[24,2048]{1,0:T(8,128)(2,1)S(1)}, bf16[24,2048]{1,0:T(8,128)(2,1)S(1)}, u32[]{:S(2)}, u32[]{:S(2)}) %collective-permute-start.12) | collective-permute-done | bytes 98336 | tf_op jit(solution)/shard_map/ppermute | solution.py:462
  43.4 2.0 %collective-permute-done.13.refs_2_ = bf16[24,2048]{1,0:T(8,128)(2,1)S(1)} collective-permute-done((bf16[24,2048]{1,0:T(8,128)(2,1)S(1)}, bf16[24,2048]{1,0:T(8,128)(2,1)S(1)}, u32[]{:S(2)}, u32[]{:S(2)}) %collective-permute-start.13) | collective-permute-done | bytes 98336 | tf_op jit(solution)/shard_map/ppermute | solution.py:462
  45.4 1.3 %collective-permute-done.14.refs_3_ = bf16[24,2048]{1,0:T(8,128)(2,1)S(1)} collective-permute-done((bf16[24,2048]{1,0:T(8,128)(2,1)S(1)}, bf16[24,2048]{1,0:T(8,128)(2,1)S(1)}, u32[]{:S(2)}, u32[]{:S(2)}) %collective-permute-start.14) | collective-permute-done | bytes 98336 | tf_op jit(solution)/shard_map/ppermute | solution.py:462
  46.8 1.2 %shard_map.135 = (f32[24,2048]{1,0:T(8,128)S(1)}, bf16[24,2048]{1,0:T(8,128)(2,1)S(1)}, bf16[512,1536]{1,0:T(8,128)(2,1)S(1)}) custom-call(s32[24]{0:T(128)S(1)} %pad_add_fusion.1.meta_ref, f32[24,2048]{1,0:T(8,128)S(1)} %get-tuple-element.32.refs_0_, bf16[24,2048]{1,0:T(8,128)(2,1)S(1)} %collective-permute-done.12.refs_1_, ...), custom_call_target="tpu_custom_call" | custom-call | flops 134217728 | bytes 4194304 | tf_op jit(solution)/shard_map/pallas_call | solution.py:554
  48.0 32.1 %all_to_all.10 = bf16[64,8,1536]{2,1,0:T(8,128)(2,1)S(1)} all-to-all(bf16[64,8,1536]{2,1,0:T(8,128)(2,1)S(1)} %bitcast.21), channel_id=1, replica_groups=mesh['req'=16,'z'=4,'core'=2] {'req','z'}, dimensions={0} | all-to-all | bytes 3145728 | tf_op jit(solution)/shard_map/all_to_all | solution.py:565
  80.2 2.4 %shard_map.136.refs_0_ = bf16[256,1536]{1,0:T(8,128)(2,1)S(1)} custom-call(bf16[512,1536]{1,0:T(8,128)(2,1)S(1)} %bitcast.18, bf16[2048,1024]{1,0:T(8,128)(2,1)S(1)} %bitcast.9, bf16[512,2048]{1,0:T(8,128)(2,1)S(1)} %bitcast.13), custom_call_target="tpu_custom_call" | custom-call | flops 1610612736 | bytes 6291456 | tf_op jit(solution)/shard_map/pallas_call | solution.py:584
  82.6 1.0 collective-permute-done.15.x_ref
  83.6 2.4 %shard_map.137.refs_0_ = bf16[256,1536]{1,0:T(8,128)(2,1)S(1)} custom-call(bf16[512,1536]{1,0:T(8,128)(2,1)S(1)} %collective-permute-done.15.x_ref, bf16[2048,1024]{1,0:T(8,128)(2,1)S(1)} %bitcast.10, bf16[512,2048]{1,0:T(8,128)(2,1)S(1)} %bitcast.14, bf16[256,1536]{1,0:T(8,128)(2,1)S(1)} %shard_map.136.refs_0_), custom_call_target="tpu_custom_call" | custom-call | flops 1610612736 | bytes 6291456 | tf_op jit(solution)/shard_map/pallas_call | solution.py:584
  86.0 2.4 %shard_map.138.refs_0_ = bf16[256,1536]{1,0:T(8,128)(2,1)S(1)} custom-call(bf16[512,1536]{1,0:T(8,128)(2,1)S(1)} %collective-permute-done.15.x_ref, bf16[2048,1024]{1,0:T(8,128)(2,1)S(1)} %bitcast.11, bf16[512,2048]{1,0:T(8,128)(2,1)S(1)} %bitcast.15, bf16[256,1536]{1,0:T(8,128)(2,1)S(1)} %shard_map.137.refs_0_), custom_call_target="tpu_custom_call" | custom-call | flops 1610612736 | bytes 6291456 | tf_op jit(solution)/shard_map/pallas_call | solution.py:584
  88.4 0.2 collective-permute-start.17
  88.6 0.4 collective-permute-start.16
  89.0 2.4 %shard_map.139.refs_2_ = bf16[256,1536]{1,0:T(8,128)(2,1)S(1)} custom-call(bf16[512,1536]{1,0:T(8,128)(2,1)S(1)} %bitcast.19, bf16[2048,1024]{1,0:T(8,128)(2,1)S(1)} %bitcast.12, bf16[512,2048]{1,0:T(8,128)(2,1)S(1)} %bitcast.16, bf16[256,1536]{1,0:T(8,128)(2,1)S(1)} %shard_map.138.refs_0_), custom_call_target="tpu_custom_call" | custom-call | flops 1610612736 | bytes 6291456 | tf_op jit(solution)/shard_map/pallas_call | solution.py:584
  91.4 0.5 collective-permute-done.16.refs_1_
  91.9 1.5 %shard_map.140 = bf16[512,1536]{1,0:T(8,128)(2,1)} custom-call(bf16[256,1536]{1,0:T(8,128)(2,1)S(1)} %shard_map.136.refs_0_, bf16[256,1536]{1,0:T(8,128)(2,1)S(1)} %collective-permute-done.16.refs_1_, bf16[256,1536]{1,0:T(8,128)(2,1)S(1)} %shard_map.139.refs_2_, bf16[256,1536]{1,0:T(8,128)(2,1)S(1)} %collective-permute-done.17.refs_3_), custom_call_target="tpu_custom_call" | custom-call | bytes 4194304 | tf_op jit(solution)/shard_map/pallas_call | solution.py:598
  93.4 4.9 %all-to-all-start.1 = ((bf16[64,8,1536]{2,1,0:T(8,128)(2,1)}), bf16[64,8,1536]{2,1,0:T(8,128)(2,1)S(1)}, u32[]{:S(2)}, u32[]{:S(2)}) async-start(bf16[64,8,1536]{2,1,0:T(8,128)(2,1)} %bitcast.6), calls=%async_computation.1 | async-start | bytes 3145728 | tf_op jit(solution)/shard_map/all_to_all | solution.py:604
  98.4 0.6 shard_map.141.table_ref
  99.0 24.1 %all-to-all-done.1 = bf16[64,8,1536]{2,1,0:T(8,128)(2,1)S(1)} async-done(((bf16[64,8,1536]{2,1,0:T(8,128)(2,1)}), bf16[64,8,1536]{2,1,0:T(8,128)(2,1)S(1)}, u32[]{:S(2)}, u32[]{:S(2)}) %all-to-all-start.1) | async-done | bytes 1572896 | tf_op jit(solution)/shard_map/all_to_all | solution.py:604
  123.1 1.0 shard_map.142
  (38 shorter events, 0.3 us)
Async XLA Ops:
  0.0 9.3 %copy-start.8 = (s32[4]{0:T(128)S(1)}, s32[4]{0:T(128)}, u32[]{:S(2)}) copy-start(s32[4]{0:T(128)} %param.19) | copy-start | bytes 52
  2.6 7.0 %collective-permute-start.1 = (bf16[192,256]{1,0:T(8,128)(2,1)S(1)}, bf16[192,256]{1,0:T(8,128)(2,1)S(1)}, u32[]{:S(2)}, u32[]{:S(2)}) collective-permute-start(bf16[192,256]{1,0:T(8,128)(2,1)S(1)} %shard_map.127.refs_0_.q_ref), channel_id=1, source_target_pairs={{0,2},{2,4},{4,6},{6,0},{1,3},{3,5},{5,7},{7,1},{8,10},{10,12},{12... | collective-permute-start | bytes 294920 | tf_op jit(solution)/shard_map/ppermute | solution.py:462
  4.7 8.2 %collective-permute-start.3 = (bf16[192,256]{1,0:T(8,128)(2,1)S(1)}, bf16[192,256]{1,0:T(8,128)(2,1)S(1)}, u32[]{:S(2)}, u32[]{:S(2)}) collective-permute-start(bf16[192,256]{1,0:T(8,128)(2,1)S(1)} %shard_map.127.refs_0_.q_ref), channel_id=1, source_target_pairs={{0,4},{2,6},{4,0},{6,2},{1,5},{3,7},{5,1},{7,3},{8,12},{10,14},{12... | collective-permute-start | bytes 294920 | tf_op jit(solution)/shard_map/ppermute | solution.py:462
  8.2 4.6 %collective-permute-start.5 = (bf16[192,256]{1,0:T(8,128)(2,1)S(1)}, bf16[192,256]{1,0:T(8,128)(2,1)S(1)}, u32[]{:S(2)}, u32[]{:S(2)}) collective-permute-start(bf16[192,256]{1,0:T(8,128)(2,1)S(1)} %shard_map.127.refs_0_.q_ref), channel_id=1, source_target_pairs={{0,6},{2,0},{4,2},{6,4},{1,7},{3,1},{5,3},{7,5},{8,14},{10,8},{12,... | collective-permute-start | bytes 294920 | tf_op jit(solution)/shard_map/ppermute | solution.py:462
  9.2 4.2 %collective-permute-start = (bf16[192,256]{1,0:T(8,128)(2,1)S(1)}, bf16[192,256]{1,0:T(8,128)(2,1)S(1)}, u32[]{:S(2)}, u32[]{:S(2)}) collective-permute-start(bf16[192,256]{1,0:T(8,128)(2,1)S(1)} %shard_map.127.refs_0_.q_ref), channel_id=1, source_target_pairs={{0,1},{1,0},{2,3},{3,2},{4,5},{5,4},{6,7},{7,6},{8,9},{9,8},{10,11... | collective-permute-start | bytes 294920 | tf_op jit(solution)/shard_map/ppermute | solution.py:465
  9.6 3.9 %collective-permute-start.2 = (bf16[192,256]{1,0:T(8,128)(2,1)S(1)}, bf16[192,256]{1,0:T(8,128)(2,1)S(1)}, u32[]{:S(2)}, u32[]{:S(2)}) collective-permute-start(bf16[192,256]{1,0:T(8,128)(2,1)S(1)} %collective-permute-done.1.refs_1_), channel_id=1, source_target_pairs={{0,1},{1,0},{2,3},{3,2},{4,5},{5,4},{6,7},{7,6},{8,9},{9,8},{10,11... | collective-permute-start | bytes 294920 | tf_op jit(solution)/shard_map/ppermute | solution.py:465
  12.9 1.3 %collective-permute-start.4 = (bf16[192,256]{1,0:T(8,128)(2,1)S(1)}, bf16[192,256]{1,0:T(8,128)(2,1)S(1)}, u32[]{:S(2)}, u32[]{:S(2)}) collective-permute-start(bf16[192,256]{1,0:T(8,128)(2,1)S(1)} %collective-permute-done.3.refs_2_), channel_id=1, source_target_pairs={{0,1},{1,0},{2,3},{3,2},{4,5},{5,4},{6,7},{7,6},{8,9},{9,8},{10,11... | collective-permute-start | bytes 294920 | tf_op jit(solution)/shard_map/ppermute | solution.py:465
  12.9 1.5 %collective-permute-start.6 = (bf16[192,256]{1,0:T(8,128)(2,1)S(1)}, bf16[192,256]{1,0:T(8,128)(2,1)S(1)}, u32[]{:S(2)}, u32[]{:S(2)}) collective-permute-start(bf16[192,256]{1,0:T(8,128)(2,1)S(1)} %collective-permute-done.5.refs_3_), channel_id=1, source_target_pairs={{0,1},{1,0},{2,3},{3,2},{4,5},{5,4},{6,7},{7,6},{8,9},{9,8},{10,11... | collective-permute-start | bytes 294920 | tf_op jit(solution)/shard_map/ppermute | solution.py:465
  19.2 4.9 %collective-permute-start.7 = (bf16[9,192,128]{2,1,0:T(8,128)(2,1)S(1)}, bf16[9,192,128]{2,1,0:T(8,128)(2,1)S(1)}, u32[]{:S(2)}, u32[]{:S(2)}) collective-permute-start(bf16[9,192,128]{2,1,0:T(8,128)(2,1)S(1)} %shard_map.128.refs_6_), channel_id=1, source_target_pairs={{0,1},{1,0},{2,3},{3,2},{4,5},{5,4},{6,7},{7,6},{8,9},{9,8},{10,11... | collective-permute-start | bytes 1327112 | tf_op jit(solution)/shard_map/ppermute | solution.py:465
  19.3 8.9 %copy-start.7 = (s32[4,48]{1,0:T(4,128)S(1)}, s32[4,48]{1,0:T(4,128)}, u32[]{:S(2)}) copy-start(s32[4,48]{1,0:T(4,128)} %param.20) | copy-start | bytes 2308
  19.3 9.1 %copy-start.2 = (bf16[192,2048]{1,0:T(8,128)(2,1)S(1)}, bf16[192,2048]{1,0:T(8,128)(2,1)}, u32[]{:S(2)}) copy-start(bf16[192,2048]{1,0:T(8,128)(2,1)} %refs_4_.5) | copy-start | bytes 2359300
  24.9 7.1 %collective-permute-start.10 = (bf16[200,256]{1,0:T(8,128)(2,1)S(1)}, bf16[200,256]{1,0:T(8,128)(2,1)S(1)}, u32[]{:S(2)}, u32[]{:S(2)}) collective-permute-start(bf16[200,256]{1,0:T(8,128)(2,1)S(1)} %get-tuple-element.27), channel_id=1, source_target_pairs={{0,2},{2,4},{4,6},{6,0},{1,3},{3,5},{5,7},{7,1},{8,10},{10,12},{12... | collective-permute-start | bytes 307208 | tf_op jit(solution)/shard_map/ppermute | solution.py:462
  25.0 7.0 %collective-permute-start.8 = (bf16[200,256]{1,0:T(8,128)(2,1)S(1)}, bf16[200,256]{1,0:T(8,128)(2,1)S(1)}, u32[]{:S(2)}, u32[]{:S(2)}) collective-permute-start(bf16[200,256]{1,0:T(8,128)(2,1)S(1)} %get-tuple-element.25), channel_id=1, source_target_pairs={{0,6},{2,0},{4,2},{6,4},{1,7},{3,1},{5,3},{7,5},{8,14},{10,8},{12,... | collective-permute-start | bytes 307208 | tf_op jit(solution)/shard_map/ppermute | solution.py:462
  28.2 6.2 %collective-permute-start.9 = (bf16[200,256]{1,0:T(8,128)(2,1)S(1)}, bf16[200,256]{1,0:T(8,128)(2,1)S(1)}, u32[]{:S(2)}, u32[]{:S(2)}) collective-permute-start(bf16[200,256]{1,0:T(8,128)(2,1)S(1)} %get-tuple-element.26), channel_id=1, source_target_pairs={{0,4},{2,6},{4,0},{6,2},{1,5},{3,7},{5,1},{7,3},{8,12},{10,14},{12... | collective-permute-start | bytes 307208 | tf_op jit(solution)/shard_map/ppermute | solution.py:462
  28.3 6.1 %copy-start.3 = (bf16[256,2048]{1,0:T(8,128)(2,1)S(1)}, bf16[256,2048]{1,0:T(8,128)(2,1)}, u32[]{:S(2)}) copy-start(bf16[256,2048]{1,0:T(8,128)(2,1)} %refs_6_.1) | copy-start | bytes 3145732
  31.9 8.5 %copy-start.6 = (bf16[2048]{0:T(1024)(128)(2,1)S(1)}, bf16[2048]{0:T(1024)(128)(2,1)}, u32[]{:S(2)}) copy-start(bf16[2048]{0:T(1024)(128)(2,1)} %param.21) | copy-start | bytes 12292
  32.0 8.5 %copy-start.5 = (s32[24,8]{0,1:T(8,128)S(1)}, s32[24,8]{0,1:T(8,128)}, u32[]{:S(2)}) copy-start(s32[24,8]{0,1:T(8,128)} %param.23) | copy-start | bytes 2308
  35.8 1.8 %collective-permute-start.11 = (bf16[96,2048]{1,0:T(8,128)(2,1)S(1)}, bf16[96,2048]{1,0:T(8,128)(2,1)S(1)}, u32[]{:S(2)}, u32[]{:S(2)}) collective-permute-start(bf16[96,2048]{1,0:T(8,128)(2,1)S(1)} %get-tuple-element.31), channel_id=1, source_target_pairs={{0,1},{1,0},{2,3},{3,2},{4,5},{5,4},{6,7},{7,6},{8,9},{9,8},{10,11... | collective-permute-start | bytes 1179656 | tf_op jit(solution)/shard_map/ppermute | solution.py:465
  37.6 42.5 %copy-start.1 = (bf16[1,512,2048]{2,1,0:T(8,128)(2,1)S(1)}, bf16[1,512,2048]{2,1,0:T(8,128)(2,1)}, u32[]{:S(2)}) copy-start(bf16[1,512,2048]{2,1,0:T(8,128)(2,1)} %param.25) | copy-start | bytes 6291460
  37.7 5.7 %collective-permute-start.12 = (bf16[24,2048]{1,0:T(8,128)(2,1)S(1)}, bf16[24,2048]{1,0:T(8,128)(2,1)S(1)}, u32[]{:S(2)}, u32[]{:S(2)}) collective-permute-start(bf16[24,2048]{1,0:T(8,128)(2,1)S(1)} %get-tuple-element.33), channel_id=1, source_target_pairs={{0,6},{2,0},{4,2},{6,4},{1,7},{3,1},{5,3},{7,5},{8,14},{10,8},{12,... | collective-permute-start | bytes 294920 | tf_op jit(solution)/shard_map/ppermute | solution.py:462
  38.6 6.8 %collective-permute-start.13 = (bf16[24,2048]{1,0:T(8,128)(2,1)S(1)}, bf16[24,2048]{1,0:T(8,128)(2,1)S(1)}, u32[]{:S(2)}, u32[]{:S(2)}) collective-permute-start(bf16[24,2048]{1,0:T(8,128)(2,1)S(1)} %get-tuple-element.34), channel_id=1, source_target_pairs={{0,4},{2,6},{4,0},{6,2},{1,5},{3,7},{5,1},{7,3},{8,12},{10,14},{12... | collective-permute-start | bytes 294920 | tf_op jit(solution)/shard_map/ppermute | solution.py:462
  39.3 7.5 %collective-permute-start.14 = (bf16[24,2048]{1,0:T(8,128)(2,1)S(1)}, bf16[24,2048]{1,0:T(8,128)(2,1)S(1)}, u32[]{:S(2)}, u32[]{:S(2)}) collective-permute-start(bf16[24,2048]{1,0:T(8,128)(2,1)S(1)} %get-tuple-element.35), channel_id=1, source_target_pairs={{0,2},{2,4},{4,6},{6,0},{1,3},{3,5},{5,7},{7,1},{8,10},{10,12},{12... | collective-permute-start | bytes 294920 | tf_op jit(solution)/shard_map/ppermute | solution.py:462
  46.8 33.4 %copy-start = (bf16[1,2048,1024]{2,1,0:T(8,128)(2,1)S(1)}, bf16[1,2048,1024]{2,1,0:T(8,128)(2,1)}, u32[]{:S(2)}) copy-start(bf16[1,2048,1024]{2,1,0:T(8,128)(2,1)} %param.24) | copy-start | bytes 12582916
  80.2 3.4 %collective-permute-start.15 = (bf16[512,1536]{1,0:T(8,128)(2,1)S(1)}, bf16[512,1536]{1,0:T(8,128)(2,1)S(1)}, u32[]{:S(2)}, u32[]{:S(2)}) collective-permute-start(bf16[512,1536]{1,0:T(8,128)(2,1)S(1)} %bitcast.17), channel_id=1, source_target_pairs={{0,1},{1,0},{2,3},{3,2},{4,5},{5,4},{6,7},{7,6},{8,9},{9,8},{10,11... | collective-permute-start | bytes 4718600 | tf_op jit(solution)/shard_map/ppermute | solution.py:465
  88.4 3.0 %collective-permute-start.17 = (bf16[256,1536]{1,0:T(8,128)(2,1)S(1)}, bf16[256,1536]{1,0:T(8,128)(2,1)S(1)}, u32[]{:S(2)}, u32[]{:S(2)}) collective-permute-start(bf16[256,1536]{1,0:T(8,128)(2,1)S(1)} %shard_map.138.refs_0_), channel_id=1, source_target_pairs={{0,1},{1,0},{2,3},{3,2},{4,5},{5,4},{6,7},{7,6},{8,9},{9,8},{10,11... | collective-permute-start | bytes 2359304 | tf_op jit(solution)/shard_map/ppermute | solution.py:465
  88.6 3.3 %collective-permute-start.16 = (bf16[256,1536]{1,0:T(8,128)(2,1)S(1)}, bf16[256,1536]{1,0:T(8,128)(2,1)S(1)}, u32[]{:S(2)}, u32[]{:S(2)}) collective-permute-start(bf16[256,1536]{1,0:T(8,128)(2,1)S(1)} %shard_map.137.refs_0_), channel_id=1, source_target_pairs={{0,1},{1,0},{2,3},{3,2},{4,5},{5,4},{6,7},{7,6},{8,9},{9,8},{10,11... | collective-permute-start | bytes 2359304 | tf_op jit(solution)/shard_map/ppermute | solution.py:465
  93.4 5.0 %copy-start.4 = (bf16[2048,64]{0,1:T(8,128)(2,1)S(1)}, bf16[2048,64]{0,1:T(8,128)(2,1)}, u32[]{:S(2)}) copy-start(bf16[2048,64]{0,1:T(8,128)(2,1)} %param.22) | copy-start | bytes 786436
  93.4 29.6 %all-to-all-start.1 = ((bf16[64,8,1536]{2,1,0:T(8,128)(2,1)}), bf16[64,8,1536]{2,1,0:T(8,128)(2,1)S(1)}, u32[]{:S(2)}, u32[]{:S(2)}) async-start(bf16[64,8,1536]{2,1,0:T(8,128)(2,1)} %bitcast.6), calls=%async_computation.1 | async-start | bytes 3145728 | tf_op jit(solution)/shard_map/all_to_all | solution.py:604

commit v3 on v2

--- a/solution.py
+++ b/solution.py
@@ -35,7 +35,7 @@
     return lax.broadcasted_iota(jnp.int32, shape, axis)
 
 
-def call(body, out, in_spaces, scratch=(), flops=0, bytes_accessed=0, vmem=10 << 20):
+def call(body, out, in_spaces, scratch=(), flops=0, bytes_accessed=0, vmem=10 << 20, aliases={}):
     out_spec = jax.tree.map(lambda _: pl.BlockSpec(memory_space=VMEM), out)
     return pl.pallas_call(
         body,
@@ -43,6 +43,7 @@
         in_specs=[pl.BlockSpec(memory_space=s) for s in in_spaces],
         out_specs=out_spec,
         scratch_shapes=list(scratch),
+        input_output_aliases=aliases,
         compiler_params=pltpu.CompilerParams(vmem_limit_bytes=vmem),
         cost_estimate=pl.CostEstimate(
             flops=flops, bytes_accessed=bytes_accessed, transcendentals=0
@@ -65,21 +66,24 @@
     x_copy.start()
     w_copy.start()
     x_copy.wait()
-    normed = normed_rows(x_ref[...].astype(F32), g_ref[...].astype(F32))
+    normed = normed_rows(x_ref[...].astype(F32), g_ref[...].astype(F32).reshape(1, -1))
     w_copy.wait()
     q_ref[...] = dot(normed, w_ref[...]).astype(BF16)
 
 
-def tree_kernel(
-    scale, x_ref, g_ref, w_hbm, q_ref, up_ref, o_ref, lse_ref, turn, w_ref, sems
-):
+def tree_kernel(scale, x_ref, g_ref, w_hbm, q_ref, up_ref, k_hbm, v_hbm, *refs):
+    o_ref, lse_ref, k_ref, v_ref, turn, w_ref, sems = refs
     tokens, width = q_ref.shape
     w_copies = [
         pltpu.make_async_copy(w_hbm.at[i + 1], w_ref.at[i], sems.at[i]) for i in range(2)
     ]
     for w_copy in w_copies:
         w_copy.start()
-    normed = normed_rows(x_ref[...].astype(F32), g_ref[...].astype(F32))
+    k_copy = pltpu.make_async_copy(k_hbm, k_ref, sems.at[2])
+    v_copy = pltpu.make_async_copy(v_hbm, v_ref, sems.at[3])
+    k_copy.start()
+    v_copy.start()
+    normed = normed_rows(x_ref[...].astype(F32), g_ref[...].astype(F32).reshape(1, -1))
     w_copies[0].wait()
     keys = dot(normed, w_ref[0]).astype(BF16)
     w_copies[1].wait()
@@ -104,39 +108,24 @@
         stats = jnp.where(lane == h, high + jnp.log(total), stats)
     turn[0:tokens, :] = stats
     lse_ref[...] = jnp.transpose(turn[...])[0:8, :]
+    k_copy.wait()
+    v_copy.wait()
 
 
 def page_kernel(scale, tree, kept, meta_ref, *refs):
-    pieces, (k_hbm, v_hbm) = refs[:4], refs[4:6]
-    outs = refs[7:-5] if kept else refs[6:-5]
-    s_all, p_all, k_ref, v_ref, sems = refs[-5:]
+    pieces, (k_ref, v_ref) = refs[:4], refs[4:6]
+    outs = refs[7:-2] if kept else refs[6:-2]
+    s_all, p_all = refs[-2:]
     out_ref = outs[0]
-    requests, page = k_hbm.shape[0], k_hbm.shape[1]
+    requests, page = k_ref.shape[0], k_ref.shape[1]
     width = pieces[0].shape[1]
     pair = 2 * tree
     lane = iota((tree, 128), 1)
     wide = iota((tree, width), 1) < HEAD_DIM
     first_at = 8 if kept else 12
 
-    def copies(r, which):
-        source, target = (k_hbm, k_ref) if which == 0 else (v_hbm, v_ref)
-        found = []
-        for i in range(len(pieces)):
-            at = pl.ds(pl.multiple_of(meta_ref[first_at + i], width), width)
-            found.append(
-                pltpu.make_async_copy(
-                    source.at[r, :, at], target.at[r, i], sems.at[which, r, i]
-                )
-            )
-        return found
-
-    for r in range(requests):
-
-        @pl.when(meta_ref[r] > 0)
-        def _():
-            for which in range(2):
-                for copy in copies(r, which):
-                    copy.start()
+    def columns(i):
+        return pl.ds(pl.multiple_of(meta_ref[first_at + i], width), width)
 
     for r in range(requests):
         rows = slice(r * tree, (r + 1) * tree)
@@ -144,15 +133,13 @@
 
         @pl.when(live > 0)
         def _():
-            for copy in copies(r, 0):
-                copy.wait()
             for i, piece in enumerate(pieces):
                 query = piece[rows, :]
                 zero = jnp.zeros_like(query)
                 both = jnp.concatenate(
                     [jnp.where(wide, query, zero), jnp.where(wide, zero, query)], axis=0
                 )
-                s_all[i * pair : (i + 1) * pair, :] = dot_t(both, k_ref[r, i])
+                s_all[i * pair : (i + 1) * pair, :] = dot_t(both, k_ref[r, :, columns(i)])
             scores = s_all[...] * scale
             scores = jnp.where(iota(scores.shape, 1) < live, scores, NEGATIVE)
             high = jnp.max(scores, axis=-1, keepdims=True)
@@ -165,10 +152,8 @@
             second = (lse - first).astype(BF16).astype(F32)
             third = lse - first - second
             stats = jnp.zeros((tree, 128), F32)
-            for copy in copies(r, 1):
-                copy.wait()
             for i in range(len(pieces)):
-                summed = dot(p_all[i * pair : (i + 1) * pair, :], v_ref[r, i])
+                summed = dot(p_all[i * pair : (i + 1) * pair, :], v_ref[r, :, columns(i)])
                 for h in range(2):
                     own = slice(i * pair + h * tree, i * pair + (h + 1) * tree)
                     cut = slice(h * HEAD_DIM, (h + 1) * HEAD_DIM)
@@ -270,7 +255,24 @@
     return jnp.where(iota((rows, experts), 0) // SLOTS == iota((rows, experts), 1), 1.0, 0.0)
 
 
-def place_kernel(routes_ref, place_ref):
+def place_kernel(routes_ref, after_ref, up_hbm, down_hbm, *refs):
+    place_ref, pack_ref, up_ref, down_ref, sems = refs
+    del after_ref
+    up_copy = pltpu.make_async_copy(up_hbm, up_ref, sems.at[0])
+    down_copy = pltpu.make_async_copy(down_hbm, down_ref, sems.at[1])
+    up_copy.start()
+    down_copy.start()
+    block = pack_ref.shape[1]
+    a = iota((block, block), 0)
+    b = iota((block, block), 1)
+    same = a // SLOTS == b // SLOTS
+    slot_a, slot_b = a % SLOTS, b % SLOTS
+    chunks = place_ref.shape[0]
+    for k in range(chunks):
+        hit = same & (slot_a < CAP) & (slot_b >= CAP) & (slot_a == (slot_b - CAP) * chunks + k)
+        pack_ref[k] = jnp.where(hit, 1.0, 0.0).astype(BF16)
+        hit = same & (slot_b < CAP) & (slot_a >= CAP) & (slot_b == (slot_a - CAP) * chunks + k)
+        pack_ref[chunks + k] = jnp.where(hit, 1.0, 0.0).astype(BF16)
     top, tokens = routes_ref.shape
     chunks, rows, _ = place_ref.shape
     experts = rows // SLOTS
@@ -292,6 +294,8 @@
         valid = is_tail == (slot >= CAP)
         hit = valid & (spread == wanted.astype(F32))
         place_ref[j] = jnp.where(hit, 1.0, 0.0).astype(BF16)
+    up_copy.wait()
+    down_copy.wait()
 
 
 def residual_kernel(meta_ref, *refs):
@@ -306,7 +310,7 @@
         residual = residual + part[...].astype(F32)
     res_ref[...] = residual
     inverse = lax.rsqrt(jnp.mean(residual * residual, axis=-1, keepdims=True) + EPSILON)
-    normed = residual * inverse * g_ref[...].astype(F32)
+    normed = residual * inverse * g_ref[...].astype(F32).reshape(1, -1)
     normed_ref[...] = normed.astype(BF16)
     tail = normed[:, chunks * cut :]
     for j in range(chunks):
@@ -314,17 +318,20 @@
         out_ref[:, j * cut : (j + 1) * cut] = dot(place_ref[j], pair).astype(BF16)
 
 
-def gate_kernel(normed_ref, router_ref, routes_ref, table_ref):
-    tokens, top = routes_ref.shape
+def gate_kernel(normed_ref, router_ref, routes_ref, after_ref, table_ref):
+    del after_ref
+    top, tokens = routes_ref.shape
     experts = router_ref.shape[0]
     chunks, _, rows = table_ref.shape
     logits = dot_t(normed_ref[...], router_ref[...])
     exponent = jnp.exp(logits)
     chances = exponent / jnp.sum(exponent, axis=-1, keepdims=True)
-    named = iota((tokens, experts), 1)
-    chosen = jnp.zeros((tokens, experts), F32)
+    named = iota((experts, tokens), 0)
+    chosen = jnp.zeros((experts, tokens), F32)
     for k in range(top):
-        chosen = jnp.where(routes_ref[:, k : k + 1] == named, 1.0, chosen)
+        chosen = jnp.where(routes_ref[k : k + 1, :] == named, 1.0, chosen)
+    same = jnp.where(iota((tokens, tokens), 0) == iota((tokens, tokens), 1), 1.0, 0.0)
+    chosen = dot_t(same.astype(BF16), chosen.astype(BF16))
     picked = chances * chosen
     gates = picked / jnp.sum(picked, axis=-1, keepdims=True)
     earlier = jnp.where(iota((tokens, tokens), 0) > iota((tokens, tokens), 1), 1.0, 0.0)
@@ -350,23 +357,16 @@
         ).astype(BF16)
 
 
-def expert_kernel(first_row, x_ref, gate_up_ref, down_ref, *refs):
+def expert_kernel(first_row, x_ref, gate_up_ref, down_ref, pack_ref, *refs):
     out_ref = refs[-1]
-    block, packed = out_ref.shape
+    block = pack_ref.shape[1]
+    packed = x_ref.shape[1]
     width, both = gate_up_ref.shape
     units = both // 2
     cut = width - packed
     chunks = packed // cut
-    a = iota((block, block), 0)
-    b = iota((block, block), 1)
-    same = a // SLOTS == b // SLOTS
-    slot_a, slot_b = a % SLOTS, b % SLOTS
-    unpack, pack = [], []
-    for k in range(chunks):
-        hit = same & (slot_a < CAP) & (slot_b >= CAP) & (slot_a == (slot_b - CAP) * chunks + k)
-        unpack.append(jnp.where(hit, 1.0, 0.0).astype(BF16))
-        hit = same & (slot_b < CAP) & (slot_a >= CAP) & (slot_b == (slot_a - CAP) * chunks + k)
-        pack.append(jnp.where(hit, 1.0, 0.0).astype(BF16))
+    unpack = [pack_ref[k] for k in range(chunks)]
+    pack = [pack_ref[chunks + k] for k in range(chunks)]
     is_tail = iota((block, cut), 0) % SLOTS >= CAP
     span = slice(first_row, first_row + block)
     tail = dot(unpack[0], x_ref[span, 0:cut])
@@ -377,21 +377,23 @@
     gate = up[:, :units]
     hidden = (gate / (1.0 + jnp.exp(-gate)) * up[:, units:]).astype(BF16)
     last = dot(hidden, down_ref[:, packed:]).astype(BF16)
+    last_call = out_ref.shape[0] > block
+    if last_call:
+        own_ref, other_ref = refs[0], refs[1]
+        total = own_ref[...].astype(F32) + other_ref[...].astype(F32)
+        out_ref[0:block, :] = total.astype(BF16)
+    at = block if last_call else 0
     for k in range(chunks):
         main = dot(hidden, down_ref[:, k * cut : (k + 1) * cut])
-        out_ref[:, k * cut : (k + 1) * cut] = jnp.where(
+        out_ref[at : at + block, k * cut : (k + 1) * cut] = jnp.where(
             is_tail, dot(pack[k], last), main
         ).astype(BF16)
 
 
-def add_kernel(*refs):
-    out_ref = refs[-1]
-    at = 0
-    for first, second in zip(refs[0:-1:2], refs[1:-1:2]):
-        rows = first.shape[0]
-        total = first[...].astype(F32) + second[...].astype(F32)
-        out_ref[at : at + rows, :] = total.astype(BF16)
-        at += rows
+def add_kernel(values_ref, other_ref, out_ref):
+    at = out_ref.shape[0] - other_ref.shape[0]
+    total = values_ref[at:, :].astype(F32) + other_ref[...].astype(F32)
+    out_ref[at:, :] = total.astype(BF16)
 
 
 def final_kernel(back_ref, table_ref, res_ref, out_ref):
@@ -439,8 +441,6 @@
     chunks = packed // (width - packed)
     padded = tokens + 8
 
-    gain_a = gain_attn.reshape(1, width)
-    gain_m = gain_moe.reshape(1, width)
     w_three = pltpu.with_memory_space_constraint(jnp.transpose(w_qkv, (1, 0, 2)), HBM)
     cache_keys = pltpu.with_memory_space_constraint(cache_keys, HBM)
     cache_values = pltpu.with_memory_space_constraint(cache_values, HBM)
@@ -456,7 +456,7 @@
         ],
         flops=2 * tokens * width * local_width,
         bytes_accessed=2 * width * (tokens + local_width),
-    )(pltpu.with_memory_space_constraint(hidden, HBM), gain_a, w_three)
+    )(pltpu.with_memory_space_constraint(hidden, HBM), gain_attn, w_three)
 
     def over_z(value, step):
         return lax.ppermute(value, "z", [(i, (i + step) % z_count) for i in range(z_count)])
@@ -479,54 +479,49 @@
     ).astype(jnp.int32)
 
     up = (parents + tree * jnp.arange(requests, dtype=jnp.int32)[:, None]).reshape(tokens, 1)
-    tree_o, tree_lse = call(
+    tree_o, tree_lse, keys, values = call(
         functools.partial(tree_kernel, scale),
-        (sds((tokens, local_width), F32), sds((8, 256), F32)),
-        [VMEM, VMEM, HBM, VMEM, VMEM],
+        (
+            sds((tokens, local_width), F32),
+            sds((8, 256), F32),
+            sds(cache_keys.shape, BF16),
+            sds(cache_values.shape, BF16),
+        ),
+        [VMEM, VMEM, HBM, VMEM, VMEM, HBM, HBM],
         [
             pltpu.VMEM((256, 128), F32),
             pltpu.VMEM((2, width, local_width), BF16),
-            pltpu.SemaphoreType.DMA((2,)),
+            pltpu.SemaphoreType.DMA((4,)),
         ],
         flops=4 * tokens * width * local_width,
-        bytes_accessed=2 * width * (tokens + 2 * local_width),
-    )(hidden, gain_a, w_three, query, up)
-
-    place = call(
-        place_kernel,
-        sds((chunks, experts * SLOTS, 2 * own), BF16),
-        [VMEM],
-        flops=1 << 22,
-        bytes_accessed=1 << 18,
-    )(routes.T)
+        bytes_accessed=4 * requests * page * width,
+        vmem=16 << 20,
+    )(hidden, gain_attn, w_three, query, up, cache_keys, cache_values)
 
     scratch = [
         pltpu.VMEM((z_count * 2 * tree, page), F32),
         pltpu.VMEM((z_count * 2 * tree, page), BF16),
-        pltpu.VMEM((requests, z_count, page, local_width), BF16),
-        pltpu.VMEM((requests, z_count, page, local_width), BF16),
-        pltpu.SemaphoreType.DMA((2, requests, z_count)),
     ]
     heads = 2 * z_count
     for_other = call(
         functools.partial(page_kernel, scale, tree, False),
         sds((heads + 1, tokens, HEAD_DIM), BF16),
-        [SMEM] + [VMEM] * 4 + [HBM] * 2,
+        [SMEM] + [VMEM] * 6,
         scratch,
         flops=2 * tokens * page * width,
         bytes_accessed=2 * requests * page * width,
         vmem=20 << 20,
-    )(meta, *other_pieces, cache_keys, cache_values)
+    )(meta, *other_pieces, keys, values)
     from_other = over_core(for_other)
     kept, kept_lse = call(
         functools.partial(page_kernel, scale, tree, True),
         (sds((heads, tokens, HEAD_DIM), F32), sds((tokens, 128), F32)),
-        [SMEM] + [VMEM] * 4 + [HBM] * 2 + [pl.ANY],
+        [SMEM] + [VMEM] * 6 + [pl.ANY],
         scratch,
         flops=2 * tokens * page * width,
         bytes_accessed=2 * requests * page * width,
         vmem=20 << 20,
-    )(meta, *pieces, cache_keys, cache_values, for_other)
+    )(meta, *pieces, keys, values, for_other)
     merged = call(
         merge_kernel,
         tuple(sds((padded, local_width), BF16) for _ in range(z_count)),
@@ -535,6 +530,26 @@
         bytes_accessed=1 << 20,
     )(from_other, kept, kept_lse)
     arrived = [merged[0]] + [over_z(merged[step], -step) for step in steps]
+    block = experts * SLOTS // 2
+    place, pack, gate_up, down = call(
+        place_kernel,
+        (
+            sds((chunks, experts * SLOTS, 2 * own), BF16),
+            sds((2 * chunks, block, block), BF16),
+            sds(w_gate_up.shape[1:], BF16),
+            sds(w_down.shape[1:], BF16),
+        ),
+        [VMEM, pl.ANY, HBM, HBM],
+        [pltpu.SemaphoreType.DMA((2,))],
+        flops=1 << 24,
+        bytes_accessed=1 << 23,
+        vmem=16 << 20,
+    )(
+        routes.T,
+        merged[0],
+        pltpu.with_memory_space_constraint(w_gate_up[0], HBM),
+        pltpu.with_memory_space_constraint(w_down[0], HBM),
+    )
     theirs, ours = call(
         out_kernel,
         (sds((z_count * own, width), BF16), sds((z_count * own, width), F32)),
@@ -561,7 +576,7 @@
         [SMEM] + [VMEM] * 7,
         flops=1 << 27,
         bytes_accessed=1 << 22,
-    )(meta, *mixed, hidden, gain_m, place)
+    )(meta, *mixed, hidden, gain_moe, place)
     rows = lax.all_to_all(
         outgoing.reshape(experts, SLOTS, packed),
         ("req", "z"),
@@ -569,38 +584,38 @@
         concat_axis=0,
         tiled=True,
     ).reshape(experts * SLOTS, packed)
+
+    def expert(values, half, extra, extra_spaces, out_rows):
+        return call(
+            functools.partial(expert_kernel, half * block),
+            sds((out_rows, packed), BF16),
+            [VMEM] * 4 + extra_spaces,
+            flops=6 * block * width * w_down.shape[1],
+            bytes_accessed=6 * width * w_down.shape[1],
+            vmem=20 << 20,
+        )(values, gate_up, down, pack, *extra)
+
+    theirs = over_core(rows)
+    mine_0 = expert(rows, 0, [], [], block)
     table = call(
         gate_kernel,
         sds((chunks, 4 * own, experts * SLOTS), BF16),
-        [VMEM] * 3,
+        [VMEM] * 3 + [pl.ANY],
         flops=1 << 24,
         bytes_accessed=1 << 19,
-    )(normed, w_router.T, routes)
-
-    block = experts * SLOTS // 2
-
-    def expert(values, half, after=None):
-        extra = [] if after is None else [after]
-        return call(
-            functools.partial(expert_kernel, half * block),
-            sds((block, packed), BF16),
-            [VMEM] * 3 + [pl.ANY] * len(extra),
-            flops=6 * block * width * w_down.shape[1],
-            bytes_accessed=6 * width * w_down.shape[1],
-            vmem=20 << 20,
-        )(values, w_gate_up[0], w_down[0], *extra)
-
-    theirs = over_core(rows)
-    mine_0 = expert(rows, 0)
-    theirs_0 = expert(theirs, 0, mine_0)
-    theirs_1 = expert(theirs, 1, theirs_0)
-    mine_1 = expert(rows, 1, theirs_1)
+    )(normed, w_router.T, routes.T, mine_0)
+    theirs_0 = expert(theirs, 0, [table], [pl.ANY], block)
+    theirs_1 = expert(theirs, 1, [theirs_0], [pl.ANY], block)
+    summed = expert(
+        rows, 1, [mine_0, over_core(theirs_0), theirs_1], [VMEM, VMEM, pl.ANY], 2 * block
+    )
     summed = call(
         add_kernel,
-        sds((experts * SLOTS, packed), BF16),
-        [VMEM] * 4,
-        bytes_accessed=1 << 22,
-    )(mine_0, over_core(theirs_0), mine_1, over_core(theirs_1))
+        sds((2 * block, packed), BF16),
+        [VMEM] * 2,
+        bytes_accessed=1 << 21,
+        aliases={0: 0},
+    )(summed, over_core(theirs_1))
     back = lax.all_to_all(
         summed.reshape(experts, SLOTS, packed),
         ("req", "z"),

time: 124 us -> 120 us (0.968)
  blocking collectives: 32.1 us -> 61.1 us
  waiting for transfers between devices: 39.4 us -> 13.4 us
  starting transfers between devices: 19.2 us -> 14 us
  Pallas kernels: 31.8 us -> 30 us
    all_to_all x0 -> x1, blocking collectives: none -> 29 us  [per_device(): lax.all_to_all(summed.reshape(experts, SLOTS, packed), ('req', 'z'), spli...]
    all_to_all x1 -> x0, waiting for transfers between devices: 24.1 us -> none  [per_device(): lax.all_to_all(summed.reshape(experts, SLOTS, packed), ('req', 'z'), spli...]
    all_to_all x1 -> x0, starting transfers between devices: 4.88 us -> none  [per_device(): lax.all_to_all(summed.reshape(experts, SLOTS, packed), ('req', 'z'), spli...]
    pallas_call x1, Pallas kernels: 4.89 us -> 2.75 us  [per_device(): call(functools.partial(page_kernel, scale, tree, False), sds((heads + 1,...]
    pallas_call x1, Pallas kernels: 4.81 us -> 2.72 us  [per_device(): call(functools.partial(page_kernel, scale, tree, True), (sds((heads, toke...]
    pallas_call x6, Pallas kernels: 11.6 us -> 13.3 us  [the longest x4 9.76 us: expert(): call(functools.partial(expert_kernel, half * block), sds((out_rows, packe...]
  transfers between devices with their start and end apart: 19 -> 18, of which waited for: 12 -> 11; matrix products, arithmetic and copies ran while one was open for 0% -> 0% of each run, Pallas kernels for 11% -> 15%
where the time goes in v3:
time: 120 us
  blocking collectives  61.1 us (51%)
  Pallas kernels  30 us (25%)
  starting transfers between devices  14 us (12%)
  waiting for transfers between devices  13.4 us (11%)
    all_to_all x1, blocking collectives, per_device(): lax.all_to_all(outgoing.reshape(experts, SLOTS, packed), ('req', 'z'), sp...  32.1 us
    all_to_all x1, blocking collectives, per_device(): lax.all_to_all(summed.reshape(experts, SLOTS, packed), ('req', 'z'), spli...  29 us
    ppermute x9, starting transfers between devices, over_z(): lax.ppermute(value, 'z', [(i, (i + step) % z_count) for i in range(z_coun...  12.1 us
    ppermute x9, waiting for transfers between devices, over_z(): lax.ppermute(value, 'z', [(i, (i + step) % z_count) for i in range(z_coun...  10.4 us
    pallas_call x4, Pallas kernels, expert(): call(functools.partial(expert_kernel, half * block), sds((out_rows, packe...  9.76 us
    pallas_call x1, Pallas kernels, per_device(): call(functools.partial(tree_kernel, scale), (sds((tokens, local_width), F...  4.24 us
    ppermute x9, waiting for transfers between devices, over_core(): return lax.ppermute(value, 'core', [(0, 1), (1, 0)])  3.05 us
    pallas_call x1, Pallas kernels, per_device(): call(place_kernel, (sds((chunks, experts * SLOTS, 2 * own), BF16), sds((2...  2.9 us
  transfers between devices with their start and end apart: 18, of which 11 were waited for; matrix products, arithmetic and copies ran while one was open for 0% of the time, Pallas kernels for 15%

profile of v3, /device:TPU:0, one launch (start us, length us, event | category | flops | bytes accessed | tf_op | source)
XLA Modules:
  0.0 120.0 jit_solution(6838513780844825527)
XLA Ops:
  0.0 0.8 copy-done.3
  0.8 1.9 %shard_map.127.q_ref.refs_0_ = bf16[192,256]{1,0:T(8,128)(2,1)S(1)} custom-call(bf16[192,2048]{1,0:T(8,128)(2,1)} %refs_4_.1, bf16[2048]{0:T(1024)(128)(2,1)S(1)} %copy-done.3, bf16[3,2048,256]{2,1,0:T(8,128)(2,1)} %bitcast.18), custom_call_target="tpu_custom_call" | custom-call | flops 201326592 | bytes 1835008 | tf_op jit(solution)/shard_map/pallas_call | solution.py:448
  2.7 2.1 %collective-permute-start.1 = (bf16[192,256]{1,0:T(8,128)(2,1)S(1)}, bf16[192,256]{1,0:T(8,128)(2,1)S(1)}, u32[]{:S(2)}, u32[]{:S(2)}) collective-permute-start(bf16[192,256]{1,0:T(8,128)(2,1)S(1)} %shard_map.127.q_ref.refs_0_), channel_id=1, source_target_pairs={{0,2},{2,4},{4,6},{6,0},{1,3},{3,5},{5,7},{7,1},{8,10},{10,12},{12... | collective-permute-start | bytes 294920 | tf_op jit(solution)/shard_map/ppermute | solution.py:462
  4.7 3.6 %collective-permute-start.3 = (bf16[192,256]{1,0:T(8,128)(2,1)S(1)}, bf16[192,256]{1,0:T(8,128)(2,1)S(1)}, u32[]{:S(2)}, u32[]{:S(2)}) collective-permute-start(bf16[192,256]{1,0:T(8,128)(2,1)S(1)} %shard_map.127.q_ref.refs_0_), channel_id=1, source_target_pairs={{0,4},{2,6},{4,0},{6,2},{1,5},{3,7},{5,1},{7,3},{8,12},{10,14},{12... | collective-permute-start | bytes 294920 | tf_op jit(solution)/shard_map/ppermute | solution.py:462
  8.3 1.0 collective-permute-start.5
  9.5 0.1 mul.46
  9.5 0.1 mul.48
  9.6 0.1 reshape.56.up_ref
  9.8 4.2 %shard_map.128 = (f32[192,256]{1,0:T(8,128)S(1)}, f32[8,256]{1,0:T(8,128)S(1)}, bf16[4,256,2048]{2,1,0:T(8,128)(2,1)S(1)}, bf16[4,256,2048]{2,1,0:T(8,128)(2,1)S(1)}) custom-call(bf16[192,2048]{1,0:T(8,128)(2,1)S(1)} %copy-done, bf16[2048]{0:T(1024)(128)(2,1)S(1)} %copy-done.4, bf16[3,2048,256]{2,1,0:T(8,128)(2,1)} %bitcast.19, ...), custom_call_target="tpu_custom_call" | custom-call | flops 402653184 | bytes 8388608 | tf_op jit(solution)/shard_map/pallas_call | solution.py:482
  14.0 0.6 collective-permute-start.2
  14.6 0.1 collective-permute-start.4
  14.7 0.4 collective-permute-start.6
  15.1 0.1 pad_add_fusion.1.meta_ref
  15.2 0.3 collective-permute-done.2.refs_1_
  15.6 0.4 collective-permute-done.4.refs_2_
  15.9 0.2 collective-permute-done.6.refs_3_
  16.1 2.8 %shard_map.129.refs_6_ = bf16[9,192,128]{2,1,0:T(8,128)(2,1)S(1)} custom-call(s32[24]{0:T(128)S(1)} %pad_add_fusion.1.meta_ref, bf16[192,256]{1,0:T(8,128)(2,1)S(1)} %collective-permute-done.refs_0_, bf16[192,256]{1,0:T(8,128)(2,1)S(1)} %collective-permute-done.2.refs_1_, bf16[192,256]{1,0:T(8,128)(2,1)S(1)} %collective-permute-done.4.refs_2_, ...), custom_call_target="tpu_custom_call" | custom-call | flops 201326592 | bytes 4194304 | tf_op jit(solution)/shard_map/pallas_call | solution.py:506
  18.8 0.1 collective-permute-start.7
  18.9 2.7 %shard_map.130 = (f32[8,192,128]{2,1,0:T(8,128)S(1)}, f32[192,128]{1,0:T(8,128)S(1)}) custom-call(s32[24]{0:T(128)S(1)} %pad_add_fusion.1.meta_ref, bf16[192,256]{1,0:T(8,128)(2,1)S(1)} %shard_map.127.q_ref.refs_0_, bf16[192,256]{1,0:T(8,128)(2,1)S(1)} %collective-permute-done.1.refs_1_, bf16[192,256]{1,0:T(8,128)(2,1)S(1)} %collective-permute-done.3.refs_2_, ...), custom_call_target="tpu_custom_call" | custom-call | flops 201326592 | bytes 4194304 | tf_op jit(solution)/shard_map/pallas_call | solution.py:516
  21.7 0.7 shard_map.131
  22.5 3.2 %collective-permute-start.8 = (bf16[200,256]{1,0:T(8,128)(2,1)S(1)}, bf16[200,256]{1,0:T(8,128)(2,1)S(1)}, u32[]{:S(2)}, u32[]{:S(2)}) collective-permute-start(bf16[200,256]{1,0:T(8,128)(2,1)S(1)} %get-tuple-element.33), channel_id=1, source_target_pairs={{0,6},{2,0},{4,2},{6,4},{1,7},{3,1},{5,3},{7,5},{8,14},{10,8},{12,... | collective-permute-start | bytes 307208 | tf_op jit(solution)/shard_map/ppermute | solution.py:462
  25.7 2.6 %collective-permute-done.10.refs_3_ = bf16[200,256]{1,0:T(8,128)(2,1)S(1)} collective-permute-done((bf16[200,256]{1,0:T(8,128)(2,1)S(1)}, bf16[200,256]{1,0:T(8,128)(2,1)S(1)}, u32[]{:S(2)}, u32[]{:S(2)}) %collective-permute-start.10) | collective-permute-done | bytes 102432 | tf_op jit(solution)/shard_map/ppermute | solution.py:462
  28.4 0.8 collective-permute-done.8.refs_1_
  29.2 2.7 %collective-permute-done.9.refs_2_ = bf16[200,256]{1,0:T(8,128)(2,1)S(1)} collective-permute-done((bf16[200,256]{1,0:T(8,128)(2,1)S(1)}, bf16[200,256]{1,0:T(8,128)(2,1)S(1)}, u32[]{:S(2)}, u32[]{:S(2)}) %collective-permute-start.9) | collective-permute-done | bytes 102432 | tf_op jit(solution)/shard_map/ppermute | solution.py:462
  31.9 1.5 %shard_map.132 = (bf16[96,2048]{1,0:T(8,128)(2,1)S(1)}, f32[96,2048]{1,0:T(8,128)S(1)}) custom-call(s32[24]{0:T(128)S(1)} %pad_add_fusion.1.meta_ref, bf16[200,256]{1,0:T(8,128)(2,1)S(1)} %get-tuple-element.32.refs_0_.after_ref, bf16[200,256]{1,0:T(8,128)(2,1)S(1)} %collective-permute-done.8.refs_1_, bf16[200,256]{1,0:T(8,128)(2,1)S(1)} %collective-permute-done.9.refs_2_, ...), custom_call_target="tpu_custom_call" | custom-call | flops 201326592 | bytes 1835008 | tf_op jit(solution)/shard_map/pallas_call | solution.py:553
  33.4 0.1 collective-permute-start.11
  33.4 1.7 %collective-permute-done.11.theirs_ref = bf16[96,2048]{1,0:T(8,128)(2,1)S(1)} collective-permute-done((bf16[96,2048]{1,0:T(8,128)(2,1)S(1)}, bf16[96,2048]{1,0:T(8,128)(2,1)S(1)}, u32[]{:S(2)}, u32[]{:S(2)}) %collective-permute-start.11) | collective-permute-done | bytes 393248 | tf_op jit(solution)/shard_map/ppermute | solution.py:465
  35.1 0.1 shard_map.133
  35.2 1.0 collective-permute-start.12
  36.3 0.1 collective-permute-start.13
  36.4 1.0 collective-permute-start.14
  37.4 2.9 %shard_map.134 = (bf16[3,512,48]{2,1,0:T(8,128)(2,1)S(1)}, bf16[6,256,256]{2,1,0:T(8,128)(2,1)S(1)}, bf16[2048,1024]{1,0:T(8,128)(2,1)S(1)}, bf16[512,2048]{1,0:T(8,128)(2,1)S(1)}) custom-call(s32[8,24]{1,0:T(8,128)S(1)} %bitcast.16, bf16[200,256]{1,0:T(8,128)(2,1)S(1)} %get-tuple-element.32.refs_0_.after_ref, bf16[2048,1024]{1,0:T(8,128)(2,1)} %bitcast.20, ...), custom_call_target="tpu_custom_call" | custom-call | flops 16777216 | bytes 8388608 | tf_op jit(solution)/shard_map/pallas_call | solution.py:534
  40.3 0.7 collective-permute-done.12.refs_1_
  41.0 2.2 %collective-permute-done.13.refs_2_ = bf16[24,2048]{1,0:T(8,128)(2,1)S(1)} collective-permute-done((bf16[24,2048]{1,0:T(8,128)(2,1)S(1)}, bf16[24,2048]{1,0:T(8,128)(2,1)S(1)}, u32[]{:S(2)}, u32[]{:S(2)}) %collective-permute-start.13) | collective-permute-done | bytes 98336 | tf_op jit(solution)/shard_map/ppermute | solution.py:462
  43.2 1.3 %collective-permute-done.14.refs_3_ = bf16[24,2048]{1,0:T(8,128)(2,1)S(1)} collective-permute-done((bf16[24,2048]{1,0:T(8,128)(2,1)S(1)}, bf16[24,2048]{1,0:T(8,128)(2,1)S(1)}, u32[]{:S(2)}, u32[]{:S(2)}) %collective-permute-start.14) | collective-permute-done | bytes 98336 | tf_op jit(solution)/shard_map/ppermute | solution.py:462
  44.4 1.2 %shard_map.135 = (f32[24,2048]{1,0:T(8,128)S(1)}, bf16[24,2048]{1,0:T(8,128)(2,1)S(1)}, bf16[512,1536]{1,0:T(8,128)(2,1)S(1)}) custom-call(s32[24]{0:T(128)S(1)} %pad_add_fusion.1.meta_ref, f32[24,2048]{1,0:T(8,128)S(1)} %get-tuple-element.40.refs_0_, bf16[24,2048]{1,0:T(8,128)(2,1)S(1)} %collective-permute-done.12.refs_1_, ...), custom_call_target="tpu_custom_call" | custom-call | flops 134217728 | bytes 4194304 | tf_op jit(solution)/shard_map/pallas_call | solution.py:569
  45.7 32.1 %all_to_all.10 = bf16[64,8,1536]{2,1,0:T(8,128)(2,1)S(1)} all-to-all(bf16[64,8,1536]{2,1,0:T(8,128)(2,1)S(1)} %bitcast.14), channel_id=1, replica_groups=mesh['req'=16,'z'=4,'core'=2] {'req','z'}, dimensions={0} | all-to-all | bytes 3145728 | tf_op jit(solution)/shard_map/all_to_all | solution.py:580
  77.8 2.4 %shard_map.136.after_ref.refs_0_ = bf16[256,1536]{1,0:T(8,128)(2,1)S(1)} custom-call(bf16[512,1536]{1,0:T(8,128)(2,1)S(1)} %bitcast.10, bf16[2048,1024]{1,0:T(8,128)(2,1)S(1)} %get-tuple-element.46.gate_up_ref, bf16[512,2048]{1,0:T(8,128)(2,1)S(1)} %get-tuple-element.47.down_ref, bf16[6,256,256]{2,1,0:T(8,128)(2,1)S(1)} %get-tuple-element.48.pack_ref), custom_call_target="tpu_custom_call" | custom-call | flops 1610612736 | bytes 6291456 | tf_op jit(solution)/shard_map/pallas_call | solution.py:589
  80.2 0.6 shard_map.137.refs_0_.table_ref
  80.8 0.5 collective-permute-done.15.x_ref
  81.2 2.4 %shard_map.138.refs_0_ = bf16[256,1536]{1,0:T(8,128)(2,1)S(1)} custom-call(bf16[512,1536]{1,0:T(8,128)(2,1)S(1)} %collective-permute-done.15.x_ref, bf16[2048,1024]{1,0:T(8,128)(2,1)S(1)} %get-tuple-element.46.gate_up_ref, bf16[512,2048]{1,0:T(8,128)(2,1)S(1)} %get-tuple-element.47.down_ref, bf16[6,256,256]{2,1,0:T(8,128)(2,1)S(1)} %get-tuple-element.48.pack_ref, ...), custom_call_target="tpu_custom_call" | custom-call | flops 1610612736 | bytes 6291456 | tf_op jit(solution)/shard_map/pallas_call | solution.py:589
  83.6 0.2 collective-permute-start.16
  83.8 2.3 %shard_map.139.refs_2_ = bf16[256,1536]{1,0:T(8,128)(2,1)S(1)} custom-call(bf16[512,1536]{1,0:T(8,128)(2,1)S(1)} %collective-permute-done.15.x_ref, bf16[2048,1024]{1,0:T(8,128)(2,1)S(1)} %get-tuple-element.46.gate_up_ref, bf16[512,2048]{1,0:T(8,128)(2,1)S(1)} %get-tuple-element.47.down_ref, bf16[6,256,256]{2,1,0:T(8,128)(2,1)S(1)} %get-tuple-element.48.pack_ref, ...), custom_call_target="tpu_custom_call" | custom-call | flops 1610612736 | bytes 6291456 | tf_op jit(solution)/shard_map/pallas_call | solution.py:589
  86.2 0.5 collective-permute-start.17
  86.6 2.7 %shard_map.140.values_ref = bf16[512,1536]{1,0:T(8,128)(2,1)S(1)} custom-call(bf16[512,1536]{1,0:T(8,128)(2,1)S(1)} %bitcast.11, bf16[2048,1024]{1,0:T(8,128)(2,1)S(1)} %get-tuple-element.46.gate_up_ref, bf16[512,2048]{1,0:T(8,128)(2,1)S(1)} %get-tuple-element.47.down_ref, bf16[6,256,256]{2,1,0:T(8,128)(2,1)S(1)} %get-tuple-element.48.pack_ref, ...), custom_call_target="tpu_custom_call" | custom-call | flops 1610612736 | bytes 6291456 | tf_op jit(solution)/shard_map/pallas_call | solution.py:589
  89.4 0.6 shard_map.141
  90.0 29.0 %all_to_all.11 = bf16[64,8,1536]{2,1,0:T(8,128)(2,1)S(1)} all-to-all(bf16[64,8,1536]{2,1,0:T(8,128)(2,1)S(1)} %bitcast.12), channel_id=1, replica_groups=mesh['req'=16,'z'=4,'core'=2] {'req','z'}, dimensions={0} | all-to-all | bytes 3145728 | tf_op jit(solution)/shard_map/all_to_all | solution.py:619
  119.0 1.0 shard_map.142
  (34 shorter events, 0.2 us)
Async XLA Ops:
  0.0 9.7 %copy-start = (bf16[192,2048]{1,0:T(8,128)(2,1)S(1)}, bf16[192,2048]{1,0:T(8,128)(2,1)}, u32[]{:S(2)}) copy-start(bf16[192,2048]{1,0:T(8,128)(2,1)} %refs_4_.1) | copy-start | bytes 2359300
  0.0 0.8 copy-start.3
  0.8 8.6 %copy-start.8 = (s32[4]{0:T(128)S(1)}, s32[4]{0:T(128)}, u32[]{:S(2)}) copy-start(s32[4]{0:T(128)} %param.19) | copy-start | bytes 52
  0.8 8.6 %copy-start.7 = (s32[4,48]{1,0:T(4,128)S(1)}, s32[4,48]{1,0:T(4,128)}, u32[]{:S(2)}) copy-start(s32[4,48]{1,0:T(4,128)} %param.20) | copy-start | bytes 2308
  0.8 9.0 %copy-start.4 = (bf16[2048]{0:T(1024)(128)(2,1)S(1)}, bf16[2048]{0:T(1024)(128)(2,1)}, u32[]{:S(2)}) copy-start(bf16[2048]{0:T(1024)(128)(2,1)} %g_ref.3) | copy-start | bytes 12292
  2.7 11.4 %collective-permute-start.1 = (bf16[192,256]{1,0:T(8,128)(2,1)S(1)}, bf16[192,256]{1,0:T(8,128)(2,1)S(1)}, u32[]{:S(2)}, u32[]{:S(2)}) collective-permute-start(bf16[192,256]{1,0:T(8,128)(2,1)S(1)} %shard_map.127.q_ref.refs_0_), channel_id=1, source_target_pairs={{0,2},{2,4},{4,6},{6,0},{1,3},{3,5},{5,7},{7,1},{8,10},{10,12},{12... | collective-permute-start | bytes 294920 | tf_op jit(solution)/shard_map/ppermute | solution.py:462
  4.7 9.9 %collective-permute-start.3 = (bf16[192,256]{1,0:T(8,128)(2,1)S(1)}, bf16[192,256]{1,0:T(8,128)(2,1)S(1)}, u32[]{:S(2)}, u32[]{:S(2)}) collective-permute-start(bf16[192,256]{1,0:T(8,128)(2,1)S(1)} %shard_map.127.q_ref.refs_0_), channel_id=1, source_target_pairs={{0,4},{2,6},{4,0},{6,2},{1,5},{3,7},{5,1},{7,3},{8,12},{10,14},{12... | collective-permute-start | bytes 294920 | tf_op jit(solution)/shard_map/ppermute | solution.py:462
  8.3 6.4 %collective-permute-start.5 = (bf16[192,256]{1,0:T(8,128)(2,1)S(1)}, bf16[192,256]{1,0:T(8,128)(2,1)S(1)}, u32[]{:S(2)}, u32[]{:S(2)}) collective-permute-start(bf16[192,256]{1,0:T(8,128)(2,1)S(1)} %shard_map.127.q_ref.refs_0_), channel_id=1, source_target_pairs={{0,6},{2,0},{4,2},{6,4},{1,7},{3,1},{5,3},{7,5},{8,14},{10,8},{12,... | collective-permute-start | bytes 294920 | tf_op jit(solution)/shard_map/ppermute | solution.py:462
  9.3 5.9 %collective-permute-start = (bf16[192,256]{1,0:T(8,128)(2,1)S(1)}, bf16[192,256]{1,0:T(8,128)(2,1)S(1)}, u32[]{:S(2)}, u32[]{:S(2)}) collective-permute-start(bf16[192,256]{1,0:T(8,128)(2,1)S(1)} %shard_map.127.q_ref.refs_0_), channel_id=1, source_target_pairs={{0,1},{1,0},{2,3},{3,2},{4,5},{5,4},{6,7},{7,6},{8,9},{9,8},{10,11... | collective-permute-start | bytes 294920 | tf_op jit(solution)/shard_map/ppermute | solution.py:465
  14.0 1.5 %collective-permute-start.2 = (bf16[192,256]{1,0:T(8,128)(2,1)S(1)}, bf16[192,256]{1,0:T(8,128)(2,1)S(1)}, u32[]{:S(2)}, u32[]{:S(2)}) collective-permute-start(bf16[192,256]{1,0:T(8,128)(2,1)S(1)} %collective-permute-done.1.refs_1_), channel_id=1, source_target_pairs={{0,1},{1,0},{2,3},{3,2},{4,5},{5,4},{6,7},{7,6},{8,9},{9,8},{10,11... | collective-permute-start | bytes 294920 | tf_op jit(solution)/shard_map/ppermute | solution.py:465
  14.6 1.3 %collective-permute-start.4 = (bf16[192,256]{1,0:T(8,128)(2,1)S(1)}, bf16[192,256]{1,0:T(8,128)(2,1)S(1)}, u32[]{:S(2)}, u32[]{:S(2)}) collective-permute-start(bf16[192,256]{1,0:T(8,128)(2,1)S(1)} %collective-permute-done.3.refs_2_), channel_id=1, source_target_pairs={{0,1},{1,0},{2,3},{3,2},{4,5},{5,4},{6,7},{7,6},{8,9},{9,8},{10,11... | collective-permute-start | bytes 294920 | tf_op jit(solution)/shard_map/ppermute | solution.py:465
  14.7 1.4 %collective-permute-start.6 = (bf16[192,256]{1,0:T(8,128)(2,1)S(1)}, bf16[192,256]{1,0:T(8,128)(2,1)S(1)}, u32[]{:S(2)}, u32[]{:S(2)}) collective-permute-start(bf16[192,256]{1,0:T(8,128)(2,1)S(1)} %collective-permute-done.5.refs_3_), channel_id=1, source_target_pairs={{0,1},{1,0},{2,3},{3,2},{4,5},{5,4},{6,7},{7,6},{8,9},{9,8},{10,11... | collective-permute-start | bytes 294920 | tf_op jit(solution)/shard_map/ppermute | solution.py:465
  18.8 13.1 %copy-start.1 = (bf16[256,2048]{1,0:T(8,128)(2,1)S(1)}, bf16[256,2048]{1,0:T(8,128)(2,1)}, u32[]{:S(2)}) copy-start(bf16[256,2048]{1,0:T(8,128)(2,1)} %refs_6_.1) | copy-start | bytes 3145732
  18.8 2.8 %collective-permute-start.7 = (bf16[9,192,128]{2,1,0:T(8,128)(2,1)S(1)}, bf16[9,192,128]{2,1,0:T(8,128)(2,1)S(1)}, u32[]{:S(2)}, u32[]{:S(2)}) collective-permute-start(bf16[9,192,128]{2,1,0:T(8,128)(2,1)S(1)} %shard_map.129.refs_6_), channel_id=1, source_target_pairs={{0,1},{1,0},{2,3},{3,2},{4,5},{5,4},{6,7},{7,6},{8,9},{9,8},{10,11... | collective-permute-start | bytes 1327112 | tf_op jit(solution)/shard_map/ppermute | solution.py:465
  21.7 15.7 %copy-start.5 = (s32[24,8]{0,1:T(8,128)S(1)}, s32[24,8]{0,1:T(8,128)}, u32[]{:S(2)}) copy-start(s32[24,8]{0,1:T(8,128)} %param.23) | copy-start | bytes 2308
  22.4 5.9 %collective-permute-start.10 = (bf16[200,256]{1,0:T(8,128)(2,1)S(1)}, bf16[200,256]{1,0:T(8,128)(2,1)S(1)}, u32[]{:S(2)}, u32[]{:S(2)}) collective-permute-start(bf16[200,256]{1,0:T(8,128)(2,1)S(1)} %get-tuple-element.35), channel_id=1, source_target_pairs={{0,2},{2,4},{4,6},{6,0},{1,3},{3,5},{5,7},{7,1},{8,10},{10,12},{12... | collective-permute-start | bytes 307208 | tf_op jit(solution)/shard_map/ppermute | solution.py:462
  22.5 6.7 %collective-permute-start.8 = (bf16[200,256]{1,0:T(8,128)(2,1)S(1)}, bf16[200,256]{1,0:T(8,128)(2,1)S(1)}, u32[]{:S(2)}, u32[]{:S(2)}) collective-permute-start(bf16[200,256]{1,0:T(8,128)(2,1)S(1)} %get-tuple-element.33), channel_id=1, source_target_pairs={{0,6},{2,0},{4,2},{6,4},{1,7},{3,1},{5,3},{7,5},{8,14},{10,8},{12,... | collective-permute-start | bytes 307208 | tf_op jit(solution)/shard_map/ppermute | solution.py:462
  25.7 6.2 %collective-permute-start.9 = (bf16[200,256]{1,0:T(8,128)(2,1)S(1)}, bf16[200,256]{1,0:T(8,128)(2,1)S(1)}, u32[]{:S(2)}, u32[]{:S(2)}) collective-permute-start(bf16[200,256]{1,0:T(8,128)(2,1)S(1)} %get-tuple-element.34), channel_id=1, source_target_pairs={{0,4},{2,6},{4,0},{6,2},{1,5},{3,7},{5,1},{7,3},{8,12},{10,14},{12... | collective-permute-start | bytes 307208 | tf_op jit(solution)/shard_map/ppermute | solution.py:462
  33.4 1.8 %collective-permute-start.11 = (bf16[96,2048]{1,0:T(8,128)(2,1)S(1)}, bf16[96,2048]{1,0:T(8,128)(2,1)S(1)}, u32[]{:S(2)}, u32[]{:S(2)}) collective-permute-start(bf16[96,2048]{1,0:T(8,128)(2,1)S(1)} %get-tuple-element.39), channel_id=1, source_target_pairs={{0,1},{1,0},{2,3},{3,2},{4,5},{5,4},{6,7},{7,6},{8,9},{9,8},{10,11... | collective-permute-start | bytes 1179656 | tf_op jit(solution)/shard_map/ppermute | solution.py:465
  35.2 5.7 %collective-permute-start.12 = (bf16[24,2048]{1,0:T(8,128)(2,1)S(1)}, bf16[24,2048]{1,0:T(8,128)(2,1)S(1)}, u32[]{:S(2)}, u32[]{:S(2)}) collective-permute-start(bf16[24,2048]{1,0:T(8,128)(2,1)S(1)} %get-tuple-element.41), channel_id=1, source_target_pairs={{0,6},{2,0},{4,2},{6,4},{1,7},{3,1},{5,3},{7,5},{8,14},{10,8},{12,... | collective-permute-start | bytes 294920 | tf_op jit(solution)/shard_map/ppermute | solution.py:462
  36.3 6.9 %collective-permute-start.13 = (bf16[24,2048]{1,0:T(8,128)(2,1)S(1)}, bf16[24,2048]{1,0:T(8,128)(2,1)S(1)}, u32[]{:S(2)}, u32[]{:S(2)}) collective-permute-start(bf16[24,2048]{1,0:T(8,128)(2,1)S(1)} %get-tuple-element.42), channel_id=1, source_target_pairs={{0,4},{2,6},{4,0},{6,2},{1,5},{3,7},{5,1},{7,3},{8,12},{10,14},{12... | collective-permute-start | bytes 294920 | tf_op jit(solution)/shard_map/ppermute | solution.py:462
  36.4 8.1 %collective-permute-start.14 = (bf16[24,2048]{1,0:T(8,128)(2,1)S(1)}, bf16[24,2048]{1,0:T(8,128)(2,1)S(1)}, u32[]{:S(2)}, u32[]{:S(2)}) collective-permute-start(bf16[24,2048]{1,0:T(8,128)(2,1)S(1)} %get-tuple-element.43), channel_id=1, source_target_pairs={{0,2},{2,4},{4,6},{6,0},{1,3},{3,5},{5,7},{7,1},{8,10},{10,12},{12... | collective-permute-start | bytes 294920 | tf_op jit(solution)/shard_map/ppermute | solution.py:462
  37.3 7.1 %copy-start.6 = (bf16[2048]{0:T(1024)(128)(2,1)S(1)}, bf16[2048]{0:T(1024)(128)(2,1)}, u32[]{:S(2)}) copy-start(bf16[2048]{0:T(1024)(128)(2,1)} %refs_5_.1) | copy-start | bytes 12292
  77.8 3.4 %collective-permute-start.15 = (bf16[512,1536]{1,0:T(8,128)(2,1)S(1)}, bf16[512,1536]{1,0:T(8,128)(2,1)S(1)}, u32[]{:S(2)}, u32[]{:S(2)}) collective-permute-start(bf16[512,1536]{1,0:T(8,128)(2,1)S(1)} %bitcast.9), channel_id=1, source_target_pairs={{0,1},{1,0},{2,3},{3,2},{4,5},{5,4},{6,7},{7,6},{8,9},{9,8},{10,11... | collective-permute-start | bytes 4718600 | tf_op jit(solution)/shard_map/ppermute | solution.py:465
  77.8 2.4 %copy-start.2 = (bf16[2048,64]{0,1:T(8,128)(2,1)S(1)}, bf16[2048,64]{0,1:T(8,128)(2,1)}, u32[]{:S(2)}) copy-start(bf16[2048,64]{0,1:T(8,128)(2,1)} %param.22) | copy-start | bytes 786436
  83.6 3.0 %collective-permute-start.16 = (bf16[256,1536]{1,0:T(8,128)(2,1)S(1)}, bf16[256,1536]{1,0:T(8,128)(2,1)S(1)}, u32[]{:S(2)}, u32[]{:S(2)}) collective-permute-start(bf16[256,1536]{1,0:T(8,128)(2,1)S(1)} %shard_map.138.refs_0_), channel_id=1, source_target_pairs={{0,1},{1,0},{2,3},{3,2},{4,5},{5,4},{6,7},{7,6},{8,9},{9,8},{10,11... | collective-permute-start | bytes 2359304 | tf_op jit(solution)/shard_map/ppermute | solution.py:465
  86.2 3.2 %collective-permute-start.17 = (bf16[256,1536]{1,0:T(8,128)(2,1)S(1)}, bf16[256,1536]{1,0:T(8,128)(2,1)S(1)}, u32[]{:S(2)}, u32[]{:S(2)}) collective-permute-start(bf16[256,1536]{1,0:T(8,128)(2,1)S(1)} %shard_map.139.refs_2_), channel_id=1, source_target_pairs={{0,1},{1,0},{2,3},{3,2},{4,5},{5,4},{6,7},{7,6},{8,9},{9,8},{10,11... | collective-permute-start | bytes 2359304 | tf_op jit(solution)/shard_map/ppermute | solution.py:465

commit v4 on v3

--- a/solution.py
+++ b/solution.py
@@ -60,41 +60,56 @@
     return (values * inverse * gain).astype(BF16)
 
 
-def query_kernel(x_hbm, g_ref, w_hbm, q_ref, x_ref, w_ref, sems):
+def query_kernel(x_hbm, g_hbm, w_hbm, q_ref, x_ref, g_ref, w_ref, sems):
     x_copy = pltpu.make_async_copy(x_hbm, x_ref, sems.at[0])
     w_copy = pltpu.make_async_copy(w_hbm.at[0], w_ref, sems.at[1])
+    g_copy = pltpu.make_async_copy(g_hbm, g_ref, sems.at[2])
     x_copy.start()
+    g_copy.start()
     w_copy.start()
+    g_copy.wait()
     x_copy.wait()
     normed = normed_rows(x_ref[...].astype(F32), g_ref[...].astype(F32).reshape(1, -1))
     w_copy.wait()
     q_ref[...] = dot(normed, w_ref[...]).astype(BF16)
 
 
-def tree_kernel(scale, x_ref, g_ref, w_hbm, q_ref, up_ref, k_hbm, v_hbm, *refs):
-    o_ref, lse_ref, k_ref, v_ref, turn, w_ref, sems = refs
+def load_kernel(k_hbm, v_hbm, after_ref, k_ref, v_ref, sems):
+    del after_ref
+    k_copy = pltpu.make_async_copy(k_hbm, k_ref, sems.at[0])
+    v_copy = pltpu.make_async_copy(v_hbm, v_ref, sems.at[1])
+    k_copy.start()
+    v_copy.start()
+    k_copy.wait()
+    v_copy.wait()
+
+
+def tree_kernel(scale, x_ref, g_ref, w_hbm, q_ref, up_ref, *refs):
+    o_ref, lse_ref, turn, w_ref, sems = refs
     tokens, width = q_ref.shape
     w_copies = [
         pltpu.make_async_copy(w_hbm.at[i + 1], w_ref.at[i], sems.at[i]) for i in range(2)
     ]
     for w_copy in w_copies:
         w_copy.start()
-    k_copy = pltpu.make_async_copy(k_hbm, k_ref, sems.at[2])
-    v_copy = pltpu.make_async_copy(v_hbm, v_ref, sems.at[3])
-    k_copy.start()
-    v_copy.start()
     normed = normed_rows(x_ref[...].astype(F32), g_ref[...].astype(F32).reshape(1, -1))
     w_copies[0].wait()
     keys = dot(normed, w_ref[0]).astype(BF16)
     w_copies[1].wait()
     values = dot(normed, w_ref[1]).astype(BF16)
+    requests, tree = up_ref.shape
+    spread = iota((tree, tokens), 0) == iota((tree, tokens), 1) % tree
+    wide = dot(up_ref[...].astype(BF16), jnp.where(spread, 1.0, 0.0).astype(BF16))
+    home = iota((requests, tokens), 1) // tree
+    wide = jnp.where(iota((requests, tokens), 0) == home, wide + (home * tree).astype(F32), 0.0)
+    parent = jnp.sum(wide, axis=0, keepdims=True)
     row = iota((tokens, tokens), 0)
-    column = iota((tokens, tokens), 1)
-    reach = jnp.where((row == column) | (up_ref[...] == column), 1.0, 0.0)
+    same = row == iota((tokens, tokens), 1)
+    reach = jnp.where(same | (row.astype(F32) == parent), 1.0, 0.0)
     for _ in range(6):
         half = reach.astype(BF16)
         reach = jnp.minimum(dot(half, half), 1.0)
-    visible = reach > 0.5
+    visible = dot_t(jnp.where(same, 1.0, 0.0).astype(BF16), reach.astype(BF16)) > 0.5
     lane = iota((tokens, 128), 1)
     stats = jnp.zeros((tokens, 128), F32)
     for h in range(width // HEAD_DIM):
@@ -108,8 +123,6 @@
         stats = jnp.where(lane == h, high + jnp.log(total), stats)
     turn[0:tokens, :] = stats
     lse_ref[...] = jnp.transpose(turn[...])[0:8, :]
-    k_copy.wait()
-    v_copy.wait()
 
 
 def page_kernel(scale, tree, kept, meta_ref, *refs):
@@ -255,24 +268,36 @@
     return jnp.where(iota((rows, experts), 0) // SLOTS == iota((rows, experts), 1), 1.0, 0.0)
 
 
-def place_kernel(routes_ref, after_ref, up_hbm, down_hbm, *refs):
-    place_ref, pack_ref, up_ref, down_ref, sems = refs
+def window_kernel(scale, tree_inputs, routes_ref, up_hbm, down_hbm, after_ref, *refs):
+    tree_refs, place_refs, (up_ref, down_ref), scratch = refs[:2], refs[2:5], refs[5:7], refs[7:]
     del after_ref
-    up_copy = pltpu.make_async_copy(up_hbm, up_ref, sems.at[0])
-    down_copy = pltpu.make_async_copy(down_hbm, down_ref, sems.at[1])
+    up_copy = pltpu.make_async_copy(up_hbm, up_ref, scratch[3].at[0])
+    down_copy = pltpu.make_async_copy(down_hbm, down_ref, scratch[3].at[1])
     up_copy.start()
     down_copy.start()
-    block = pack_ref.shape[1]
-    a = iota((block, block), 0)
-    b = iota((block, block), 1)
-    same = a // SLOTS == b // SLOTS
-    slot_a, slot_b = a % SLOTS, b % SLOTS
+    tree_kernel(scale, *tree_inputs, *tree_refs, *scratch[:3])
+    place_kernel(routes_ref, *place_refs)
+    up_copy.wait()
+    down_copy.wait()
+
+
+def place_kernel(routes_ref, place_ref, gather_ref, scatter_ref):
     chunks = place_ref.shape[0]
+    _, real, block = gather_ref.shape
+    row, column = iota((real, block), 0), iota((real, block), 1)
+    base, slot = row // CAP * SLOTS, row % CAP
+    gather_ref[0] = jnp.where(column == base + slot, 1.0, 0.0).astype(BF16)
     for k in range(chunks):
-        hit = same & (slot_a < CAP) & (slot_b >= CAP) & (slot_a == (slot_b - CAP) * chunks + k)
-        pack_ref[k] = jnp.where(hit, 1.0, 0.0).astype(BF16)
-        hit = same & (slot_b < CAP) & (slot_a >= CAP) & (slot_b == (slot_a - CAP) * chunks + k)
-        pack_ref[chunks + k] = jnp.where(hit, 1.0, 0.0).astype(BF16)
+        hit = (column == base + CAP + slot // chunks) & (slot % chunks == k)
+        gather_ref[1 + k] = jnp.where(hit, 1.0, 0.0).astype(BF16)
+    row, column = iota((block, 2 * real), 0), iota((block, 2 * real), 1)
+    is_tail = column >= real
+    column = column - jnp.where(is_tail, real, 0)
+    base, slot = column // CAP * SLOTS, column % CAP
+    for k in range(chunks):
+        main = (row == base + slot) & jnp.logical_not(is_tail)
+        tail = (row == base + CAP + slot // chunks) & (slot % chunks == k) & is_tail
+        scatter_ref[k] = jnp.where(main | tail, 1.0, 0.0).astype(BF16)
     top, tokens = routes_ref.shape
     chunks, rows, _ = place_ref.shape
     experts = rows // SLOTS
@@ -294,8 +319,6 @@
         valid = is_tail == (slot >= CAP)
         hit = valid & (spread == wanted.astype(F32))
         place_ref[j] = jnp.where(hit, 1.0, 0.0).astype(BF16)
-    up_copy.wait()
-    down_copy.wait()
 
 
 def residual_kernel(meta_ref, *refs):
@@ -318,8 +341,7 @@
         out_ref[:, j * cut : (j + 1) * cut] = dot(place_ref[j], pair).astype(BF16)
 
 
-def gate_kernel(normed_ref, router_ref, routes_ref, after_ref, table_ref):
-    del after_ref
+def gate_kernel(normed_ref, router_ref, routes_ref, table_ref):
     top, tokens = routes_ref.shape
     experts = router_ref.shape[0]
     chunks, _, rows = table_ref.shape
@@ -357,43 +379,62 @@
         ).astype(BF16)
 
 
-def expert_kernel(first_row, x_ref, gate_up_ref, down_ref, pack_ref, *refs):
-    out_ref = refs[-1]
-    block = pack_ref.shape[1]
-    packed = x_ref.shape[1]
-    width, both = gate_up_ref.shape
+def expert_kernel(
+    x_ref,
+    up_ref,
+    down_ref,
+    other_up_ref,
+    other_down_ref,
+    gather_ref,
+    scatter_ref,
+    normed_ref,
+    router_ref,
+    routes_ref,
+    out_ref,
+    table_ref,
+):
+    gate_kernel(normed_ref, router_ref, routes_ref, table_ref)
+    rows, packed = x_ref.shape
+    width, both = up_ref.shape
     units = both // 2
     cut = width - packed
     chunks = packed // cut
-    unpack = [pack_ref[k] for k in range(chunks)]
-    pack = [pack_ref[chunks + k] for k in range(chunks)]
-    is_tail = iota((block, cut), 0) % SLOTS >= CAP
-    span = slice(first_row, first_row + block)
-    tail = dot(unpack[0], x_ref[span, 0:cut])
-    for k in range(1, chunks):
-        tail = tail + dot(unpack[k], x_ref[span, k * cut : (k + 1) * cut])
-    up = dot(x_ref[span, :], gate_up_ref[0:packed, :])
-    up = up + dot(tail.astype(BF16), gate_up_ref[packed:, :])
-    gate = up[:, :units]
-    hidden = (gate / (1.0 + jnp.exp(-gate)) * up[:, units:]).astype(BF16)
-    last = dot(hidden, down_ref[:, packed:]).astype(BF16)
-    last_call = out_ref.shape[0] > block
-    if last_call:
-        own_ref, other_ref = refs[0], refs[1]
-        total = own_ref[...].astype(F32) + other_ref[...].astype(F32)
-        out_ref[0:block, :] = total.astype(BF16)
-    at = block if last_call else 0
+    _, real, block = gather_ref.shape
+    mains, tails = [], []
+    for at in range(0, rows, block):
+        span = slice(at, at + block)
+        mains.append(dot(gather_ref[0], x_ref[span, :]).astype(BF16))
+        tail = dot(gather_ref[1], x_ref[span, 0:cut])
+        for k in range(1, chunks):
+            tail = tail + dot(gather_ref[1 + k], x_ref[span, k * cut : (k + 1) * cut])
+        tails.append(tail.astype(BF16))
+    main, tail = jnp.concatenate(mains, axis=0), jnp.concatenate(tails, axis=0)
+    hidden = []
+    for weights in (up_ref, other_up_ref):
+        parts = []
+        for at in range(0, units, units // 2):
+            gate_cut = slice(at, at + units // 2)
+            up_cut = slice(units + at, units + at + units // 2)
+            gate = dot(main, weights[0:packed, gate_cut]) + dot(tail, weights[packed:, gate_cut])
+            up = dot(main, weights[0:packed, up_cut]) + dot(tail, weights[packed:, up_cut])
+            parts.append((gate / (1.0 + jnp.exp(-gate)) * up).astype(BF16))
+        hidden.append(jnp.concatenate(parts, axis=1))
+
+    def result(columns):
+        first = dot(hidden[0], down_ref[:, columns]).astype(BF16).astype(F32)
+        second = dot(hidden[1], other_down_ref[:, columns]).astype(BF16).astype(F32)
+        return (first + second).astype(BF16)
+
+    last = result(slice(packed, width))
     for k in range(chunks):
-        main = dot(hidden, down_ref[:, k * cut : (k + 1) * cut])
-        out_ref[at : at + block, k * cut : (k + 1) * cut] = jnp.where(
-            is_tail, dot(pack[k], last), main
-        ).astype(BF16)
-
-
-def add_kernel(values_ref, other_ref, out_ref):
-    at = out_ref.shape[0] - other_ref.shape[0]
-    total = values_ref[at:, :].astype(F32) + other_ref[...].astype(F32)
-    out_ref[at:, :] = total.astype(BF16)
+        columns = slice(k * cut, (k + 1) * cut)
+        value = result(columns)
+        for i in range(rows // block):
+            own = slice(i * real, (i + 1) * real)
+            pair = jnp.concatenate([value[own], last[own]], axis=0)
+            out_ref[i * block : (i + 1) * block, columns] = dot(scatter_ref[k], pair).astype(
+                BF16
+            )
 
 
 def final_kernel(back_ref, table_ref, res_ref, out_ref):
@@ -448,15 +489,20 @@
     query = call(
         query_kernel,
         sds((tokens, local_width), BF16),
-        [HBM, VMEM, HBM],
+        [HBM, HBM, HBM],
         [
             pltpu.VMEM((tokens, width), BF16),
+            pltpu.VMEM((width,), BF16),
             pltpu.VMEM((width, local_width), BF16),
-            pltpu.SemaphoreType.DMA((2,)),
+            pltpu.SemaphoreType.DMA((3,)),
         ],
         flops=2 * tokens * width * local_width,
         bytes_accessed=2 * width * (tokens + local_width),
-    )(pltpu.with_memory_space_constraint(hidden, HBM), gain_attn, w_three)
+    )(
+        pltpu.with_memory_space_constraint(hidden, HBM),
+        pltpu.with_memory_space_constraint(gain_attn, HBM),
+        w_three,
+    )
 
     def over_z(value, step):
         return lax.ppermute(value, "z", [(i, (i + step) % z_count) for i in range(z_count)])
@@ -478,25 +524,14 @@
         ]
     ).astype(jnp.int32)
 
-    up = (parents + tree * jnp.arange(requests, dtype=jnp.int32)[:, None]).reshape(tokens, 1)
-    tree_o, tree_lse, keys, values = call(
-        functools.partial(tree_kernel, scale),
-        (
-            sds((tokens, local_width), F32),
-            sds((8, 256), F32),
-            sds(cache_keys.shape, BF16),
-            sds(cache_values.shape, BF16),
-        ),
-        [VMEM, VMEM, HBM, VMEM, VMEM, HBM, HBM],
-        [
-            pltpu.VMEM((256, 128), F32),
-            pltpu.VMEM((2, width, local_width), BF16),
-            pltpu.SemaphoreType.DMA((4,)),
-        ],
-        flops=4 * tokens * width * local_width,
+    keys, values = call(
+        load_kernel,
+        (sds(cache_keys.shape, BF16), sds(cache_values.shape, BF16)),
+        [HBM, HBM, pl.ANY],
+        [pltpu.SemaphoreType.DMA((2,))],
         bytes_accessed=4 * requests * page * width,
         vmem=16 << 20,
-    )(hidden, gain_attn, w_three, query, up, cache_keys, cache_values)
+    )(cache_keys, cache_values, query)
 
     scratch = [
         pltpu.VMEM((z_count * 2 * tree, page), F32),
@@ -530,26 +565,46 @@
         bytes_accessed=1 << 20,
     )(from_other, kept, kept_lse)
     arrived = [merged[0]] + [over_z(merged[step], -step) for step in steps]
+
     block = experts * SLOTS // 2
-    place, pack, gate_up, down = call(
-        place_kernel,
+    real = block // SLOTS * CAP
+
+    def body(x_ref, g_ref, w_hbm, q_ref, up_ref, *refs):
+        window_kernel(scale, (x_ref, g_ref, w_hbm, q_ref, up_ref), *refs)
+
+    tree_o, tree_lse, place, gather, scatter, gate_up, down = call(
+        body,
         (
+            sds((tokens, local_width), F32),
+            sds((8, 256), F32),
             sds((chunks, experts * SLOTS, 2 * own), BF16),
-            sds((2 * chunks, block, block), BF16),
+            sds((1 + chunks, real, block), BF16),
+            sds((chunks, block, 2 * real), BF16),
             sds(w_gate_up.shape[1:], BF16),
             sds(w_down.shape[1:], BF16),
         ),
-        [VMEM, pl.ANY, HBM, HBM],
-        [pltpu.SemaphoreType.DMA((2,))],
-        flops=1 << 24,
-        bytes_accessed=1 << 23,
-        vmem=16 << 20,
+        [VMEM, VMEM, HBM, VMEM, VMEM, VMEM, HBM, HBM, pl.ANY],
+        [
+            pltpu.VMEM((256, 128), F32),
+            pltpu.VMEM((2, width, local_width), BF16),
+            pltpu.SemaphoreType.DMA((2,)),
+            pltpu.SemaphoreType.DMA((2,)),
+        ],
+        flops=4 * tokens * width * local_width,
+        bytes_accessed=2 * width * (tokens + 2 * local_width) + (1 << 23),
+        vmem=24 << 20,
     )(
+        hidden,
+        gain_attn,
+        w_three,
+        query,
+        parents,
         routes.T,
-        merged[0],
         pltpu.with_memory_space_constraint(w_gate_up[0], HBM),
         pltpu.with_memory_space_constraint(w_down[0], HBM),
+        merged[0],
     )
+
     theirs, ours = call(
         out_kernel,
         (sds((z_count * own, width), BF16), sds((z_count * own, width), F32)),
@@ -564,7 +619,11 @@
         [VMEM] * 2,
         bytes_accessed=1 << 20,
     )(ours, over_core(theirs))
-    mixed = [folded[0]] + [over_z(folded[step], -step) for step in steps]
+    first_fold, far_up, far_down = lax.optimization_barrier(
+        (folded[0], w_gate_up[0], w_down[0])
+    )
+    other_gate_up, other_down = over_core(far_up), over_core(far_down)
+    mixed = [first_fold] + [over_z(folded[step], -step) for step in steps]
 
     residual, normed, outgoing = call(
         residual_kernel,
@@ -585,37 +644,28 @@
         tiled=True,
     ).reshape(experts * SLOTS, packed)
 
-    def expert(values, half, extra, extra_spaces, out_rows):
-        return call(
-            functools.partial(expert_kernel, half * block),
-            sds((out_rows, packed), BF16),
-            [VMEM] * 4 + extra_spaces,
-            flops=6 * block * width * w_down.shape[1],
-            bytes_accessed=6 * width * w_down.shape[1],
-            vmem=20 << 20,
-        )(values, gate_up, down, pack, *extra)
-
-    theirs = over_core(rows)
-    mine_0 = expert(rows, 0, [], [], block)
-    table = call(
-        gate_kernel,
-        sds((chunks, 4 * own, experts * SLOTS), BF16),
-        [VMEM] * 3 + [pl.ANY],
-        flops=1 << 24,
-        bytes_accessed=1 << 19,
-    )(normed, w_router.T, routes.T, mine_0)
-    theirs_0 = expert(theirs, 0, [table], [pl.ANY], block)
-    theirs_1 = expert(theirs, 1, [theirs_0], [pl.ANY], block)
-    summed = expert(
-        rows, 1, [mine_0, over_core(theirs_0), theirs_1], [VMEM, VMEM, pl.ANY], 2 * block
+    summed, table = call(
+        expert_kernel,
+        (
+            sds((experts * SLOTS, packed), BF16),
+            sds((chunks, 4 * own, experts * SLOTS), BF16),
+        ),
+        [VMEM] * 10,
+        flops=12 * experts * CAP * width * w_down.shape[1],
+        bytes_accessed=12 * width * w_down.shape[1],
+        vmem=24 << 20,
+    )(
+        rows,
+        gate_up,
+        down,
+        other_gate_up,
+        other_down,
+        gather,
+        scatter,
+        normed,
+        w_router.T,
+        routes.T,
     )
-    summed = call(
-        add_kernel,
-        sds((2 * block, packed), BF16),
-        [VMEM] * 2,
-        bytes_accessed=1 << 21,
-        aliases={0: 0},
-    )(summed, over_core(theirs_1))
     back = lax.all_to_all(
         summed.reshape(experts, SLOTS, packed),
         ("req", "z"),

time: 120 us -> 116 us (0.967)
  waiting for transfers between devices: 13.4 us -> 10.4 us
    ppermute x9, waiting for transfers between devices: 10.4 us -> 7.42 us  [over_z(): lax.ppermute(value, 'z', [(i, (i + step) % z_count) for i in range(z_coun...]
    pallas_call x9 -> x4, Pallas kernels: 20 us -> 18.8 us  [the longest x1 7.37 us: per_device(): call(expert_kernel, (sds((experts * SLOTS, packed), BF16), sds((chunks, 4...]
    ppermute x9 -> x8, waiting for transfers between devices: 3.05 us -> 2.93 us  [over_core(): return lax.ppermute(value, 'core', [(0, 1), (1, 0)])]
  transfers between devices with their start and end apart: 18 -> 17, of which waited for: 11 -> 7; matrix products, arithmetic and copies ran while one was open for 0% -> 0% of each run, Pallas kernels for 15% -> 12%
where the time goes in v4:
time: 116 us
  blocking collectives  61.5 us (53%)
  Pallas kernels  28.8 us (25%)
  starting transfers between devices  14.6 us (13%)
  waiting for transfers between devices  10.4 us (9%)
    all_to_all x1, blocking collectives, per_device(): lax.all_to_all(outgoing.reshape(experts, SLOTS, packed), ('req', 'z'), sp...  33.2 us
    all_to_all x1, blocking collectives, per_device(): lax.all_to_all(summed.reshape(experts, SLOTS, packed), ('req', 'z'), spli...  28.3 us
    ppermute x9, starting transfers between devices, over_z(): lax.ppermute(value, 'z', [(i, (i + step) % z_count) for i in range(z_coun...  13.1 us
    ppermute x9, waiting for transfers between devices, over_z(): lax.ppermute(value, 'z', [(i, (i + step) % z_count) for i in range(z_coun...  7.42 us
    pallas_call x1, Pallas kernels, per_device(): call(expert_kernel, (sds((experts * SLOTS, packed), BF16), sds((chunks, 4...  7.37 us
    pallas_call x1, Pallas kernels, per_device(): call(body, (sds((tokens, local_width), F32), sds((8, 256), F32), sds((chu...  6.01 us
    pallas_call x1, Pallas kernels, per_device(): call(load_kernel, (sds(cache_keys.shape, BF16), sds(cache_values.shape, B...  3.48 us
    ppermute x8, waiting for transfers between devices, over_core(): return lax.ppermute(value, 'core', [(0, 1), (1, 0)])  2.93 us
  transfers between devices with their start and end apart: 17, of which 7 were waited for; matrix products, arithmetic and copies ran while one was open for 0% of the time, Pallas kernels for 12%

profile of v4, /device:TPU:0, one launch (start us, length us, event | category | flops | bytes accessed | tf_op | source)
XLA Modules:
  0.0 115.9 jit_solution(4383629942770433559)
XLA Ops:
  0.0 1.9 %shard_map.127.after_ref.refs_0_.q_ref = bf16[192,256]{1,0:T(8,128)(2,1)S(1)} custom-call(bf16[192,2048]{1,0:T(8,128)(2,1)} %refs_4_.1, bf16[2048]{0:T(1024)(128)(2,1)} %g_ref.1, bf16[3,2048,256]{2,1,0:T(8,128)(2,1)} %bitcast.16), custom_call_target="tpu_custom_call" | custom-call | flops 201326592 | bytes 1835008 | tf_op jit(solution)/shard_map/pallas_call | solution.py:489
  1.9 4.2 %collective-permute-start.5 = (bf16[192,256]{1,0:T(8,128)(2,1)S(1)}, bf16[192,256]{1,0:T(8,128)(2,1)S(1)}, u32[]{:S(2)}, u32[]{:S(2)}) collective-permute-start(bf16[192,256]{1,0:T(8,128)(2,1)S(1)} %shard_map.127.after_ref.refs_0_.q_ref), channel_id=1, source_target_pairs={{0,6},{2,0},{4,2},{6,4},{1,7},{3,1},{5,3},{7,5},{8,14},{10,8},{12,... | collective-permute-start | bytes 294920 | tf_op jit(solution)/shard_map/ppermute | solution.py:508
  6.1 1.3 %collective-permute-start.1 = (bf16[192,256]{1,0:T(8,128)(2,1)S(1)}, bf16[192,256]{1,0:T(8,128)(2,1)S(1)}, u32[]{:S(2)}, u32[]{:S(2)}) collective-permute-start(bf16[192,256]{1,0:T(8,128)(2,1)S(1)} %shard_map.127.after_ref.refs_0_.q_ref), channel_id=1, source_target_pairs={{0,2},{2,4},{4,6},{6,0},{1,3},{3,5},{5,7},{7,1},{8,10},{10,12},{12... | collective-permute-start | bytes 294920 | tf_op jit(solution)/shard_map/ppermute | solution.py:508
  7.4 0.1 mul.38
  7.5 0.1 mul.40
  7.6 3.5 %shard_map.128 = (bf16[4,256,2048]{2,1,0:T(8,128)(2,1)S(1)}, bf16[4,256,2048]{2,1,0:T(8,128)(2,1)S(1)}) custom-call(bf16[4,256,2048]{2,1,0:T(8,128)(2,1)} %k_hbm.1, bf16[4,256,2048]{2,1,0:T(8,128)(2,1)} %v_hbm.1, bf16[192,256]{1,0:T(8,128)(2,1)S(1)} %shard_map.127.after_ref.refs_0_.q_ref), custom_call_target="tpu_custom_call" | custom-call | bytes 8388608 | tf_op jit(solution)/shard_map/pallas_call | solution.py:527
  11.1 0.0 collective-permute-done.5.refs_3_
  11.1 0.6 collective-permute-start.6
  11.7 1.3 %collective-permute-done.3.refs_2_ = bf16[192,256]{1,0:T(8,128)(2,1)S(1)} collective-permute-done((bf16[192,256]{1,0:T(8,128)(2,1)S(1)}, bf16[192,256]{1,0:T(8,128)(2,1)S(1)}, u32[]{:S(2)}, u32[]{:S(2)}) %collective-permute-start.3) | collective-permute-done | bytes 98336 | tf_op jit(solution)/shard_map/ppermute | solution.py:508
  13.0 0.0 collective-permute-start.4
  13.0 0.7 collective-permute-done.1.refs_1_
  13.7 0.1 pad_add_fusion.1.meta_ref
  13.8 0.5 collective-permute-done.4.refs_2_
  14.3 0.7 collective-permute-done.2.refs_1_
  15.0 2.7 %shard_map.129.refs_6_ = bf16[9,192,128]{2,1,0:T(8,128)(2,1)S(1)} custom-call(s32[24]{0:T(128)S(1)} %pad_add_fusion.1.meta_ref, bf16[192,256]{1,0:T(8,128)(2,1)S(1)} %collective-permute-done.refs_0_, bf16[192,256]{1,0:T(8,128)(2,1)S(1)} %collective-permute-done.2.refs_1_, bf16[192,256]{1,0:T(8,128)(2,1)S(1)} %collective-permute-done.4.refs_2_, ...), custom_call_target="tpu_custom_call" | custom-call | flops 201326592 | bytes 4194304 | tf_op jit(solution)/shard_map/pallas_call | solution.py:541
  17.7 0.0 copy-start
  17.7 0.0 copy-start.2
  17.8 0.0 copy-start.4
  17.8 0.0 copy-start.5
  17.8 0.1 collective-permute-start.7
  17.9 2.7 %shard_map.130 = (f32[8,192,128]{2,1,0:T(8,128)S(1)}, f32[192,128]{1,0:T(8,128)S(1)}) custom-call(s32[24]{0:T(128)S(1)} %pad_add_fusion.1.meta_ref, bf16[192,256]{1,0:T(8,128)(2,1)S(1)} %shard_map.127.after_ref.refs_0_.q_ref, bf16[192,256]{1,0:T(8,128)(2,1)S(1)} %collective-permute-done.1.refs_1_, bf16[192,256]{1,0:T(8,128)(2,1)S(1)} %collective-permute-done.3.refs_2_, ...), custom_call_target="tpu_custom_call" | custom-call | flops 201326592 | bytes 4194304 | tf_op jit(solution)/shard_map/pallas_call | solution.py:551
  20.6 0.7 shard_map.131
  21.3 0.1 collective-permute-start.8
  21.4 0.1 collective-permute-start.9
  21.5 1.9 %collective-permute-start.10 = (bf16[200,256]{1,0:T(8,128)(2,1)S(1)}, bf16[200,256]{1,0:T(8,128)(2,1)S(1)}, u32[]{:S(2)}, u32[]{:S(2)}) collective-permute-start(bf16[200,256]{1,0:T(8,128)(2,1)S(1)} %get-tuple-element.41), channel_id=1, source_target_pairs={{0,2},{2,4},{4,6},{6,0},{1,3},{3,5},{5,7},{7,1},{8,10},{10,12},{12... | collective-permute-start | bytes 307208 | tf_op jit(solution)/shard_map/ppermute | solution.py:508
  23.4 0.0 copy-start.1
  23.5 0.0 copy-start.7
  23.5 0.0 copy-start.8
  23.5 0.0 copy-start.3
  23.5 6.0 %shard_map.132 = (f32[192,256]{1,0:T(8,128)S(1)}, f32[8,256]{1,0:T(8,128)S(1)}, bf16[3,512,48]{2,1,0:T(8,128)(2,1)S(1)}, bf16[4,192,256]{2,1,0:T(8,128)(2,1)S(1)...) custom-call(bf16[192,2048]{1,0:T(8,128)(2,1)S(1)} %copy-done, ...), custom_call_target="tpu_custom_call" | custom-call | flops 402653184 | bytes 11272192 | tf_op jit(solution)/shard_map/pallas_call | solution.py:575
  29.5 0.0 collective-permute-done.8.refs_1_
  29.6 1.5 %shard_map.133 = (bf16[96,2048]{1,0:T(8,128)(2,1)S(1)}, f32[96,2048]{1,0:T(8,128)S(1)}) custom-call(s32[24]{0:T(128)S(1)} %pad_add_fusion.1.meta_ref, bf16[200,256]{1,0:T(8,128)(2,1)S(1)} %get-tuple-element.38.refs_3_.refs_0_, bf16[200,256]{1,0:T(8,128)(2,1)S(1)} %collective-permute-done.8.refs_1_, bf16[200,256]{1,0:T(8,128)(2,1)S(1)} %collective-permute-done.9.refs_2_, ...), custom_call_target="tpu_custom_call" | custom-call | flops 201326592 | bytes 1835008 | tf_op jit(solution)/shard_map/pallas_call | solution.py:608
  31.0 0.0 copy-start.6
  31.1 0.1 collective-permute-start.11
  31.2 1.7 %collective-permute-done.11.theirs_ref = bf16[96,2048]{1,0:T(8,128)(2,1)S(1)} collective-permute-done((bf16[96,2048]{1,0:T(8,128)(2,1)S(1)}, bf16[96,2048]{1,0:T(8,128)(2,1)S(1)}, u32[]{:S(2)}, u32[]{:S(2)}) %collective-permute-start.11) | collective-permute-done | bytes 393248 | tf_op jit(solution)/shard_map/ppermute | solution.py:511
  32.9 0.1 shard_map.134
  33.0 0.4 collective-permute-start.15
  33.4 0.4 collective-permute-start.16
  33.7 2.7 %collective-permute-start.12 = (bf16[24,2048]{1,0:T(8,128)(2,1)S(1)}, bf16[24,2048]{1,0:T(8,128)(2,1)S(1)}, u32[]{:S(2)}, u32[]{:S(2)}) collective-permute-start(bf16[24,2048]{1,0:T(8,128)(2,1)S(1)} %get-tuple-element.48), channel_id=1, source_target_pairs={{0,6},{2,0},{4,2},{6,4},{1,7},{3,1},{5,3},{7,5},{8,14},{10,8},{12,... | collective-permute-start | bytes 294920 | tf_op jit(solution)/shard_map/ppermute | solution.py:508
  36.4 1.4 %collective-permute-start.13 = (bf16[24,2048]{1,0:T(8,128)(2,1)S(1)}, bf16[24,2048]{1,0:T(8,128)(2,1)S(1)}, u32[]{:S(2)}, u32[]{:S(2)}) collective-permute-start(bf16[24,2048]{1,0:T(8,128)(2,1)S(1)} %get-tuple-element.49), channel_id=1, source_target_pairs={{0,4},{2,6},{4,0},{6,2},{1,5},{3,7},{5,1},{7,3},{8,12},{10,14},{12... | collective-permute-start | bytes 294920 | tf_op jit(solution)/shard_map/ppermute | solution.py:508
  37.9 1.4 %collective-permute-start.14 = (bf16[24,2048]{1,0:T(8,128)(2,1)S(1)}, bf16[24,2048]{1,0:T(8,128)(2,1)S(1)}, u32[]{:S(2)}, u32[]{:S(2)}) collective-permute-start(bf16[24,2048]{1,0:T(8,128)(2,1)S(1)} %get-tuple-element.50), channel_id=1, source_target_pairs={{0,2},{2,4},{4,6},{6,0},{1,3},{3,5},{5,7},{7,1},{8,10},{10,12},{12... | collective-permute-start | bytes 294920 | tf_op jit(solution)/shard_map/ppermute | solution.py:508
  39.3 4.4 %collective-permute-done.13.refs_2_ = bf16[24,2048]{1,0:T(8,128)(2,1)S(1)} collective-permute-done((bf16[24,2048]{1,0:T(8,128)(2,1)S(1)}, bf16[24,2048]{1,0:T(8,128)(2,1)S(1)}, u32[]{:S(2)}, u32[]{:S(2)}) %collective-permute-start.13) | collective-permute-done | bytes 98336 | tf_op jit(solution)/shard_map/ppermute | solution.py:508
  43.6 1.0 collective-permute-done.14.refs_3_
  44.7 1.2 %shard_map.135 = (f32[24,2048]{1,0:T(8,128)S(1)}, bf16[24,2048]{1,0:T(8,128)(2,1)S(1)}, bf16[512,1536]{1,0:T(8,128)(2,1)S(1)}) custom-call(s32[24]{0:T(128)S(1)} %pad_add_fusion.1.meta_ref, f32[24,2048]{1,0:T(8,128)S(1)} %get-tuple-element.47.refs_0_, bf16[24,2048]{1,0:T(8,128)(2,1)S(1)} %collective-permute-done.12.refs_1_, ...), custom_call_target="tpu_custom_call" | custom-call | flops 134217728 | bytes 4194304 | tf_op jit(solution)/shard_map/pallas_call | solution.py:628
  45.9 33.2 %all_to_all.10 = bf16[64,8,1536]{2,1,0:T(8,128)(2,1)S(1)} all-to-all(bf16[64,8,1536]{2,1,0:T(8,128)(2,1)S(1)} %bitcast.12), channel_id=1, replica_groups=mesh['req'=16,'z'=4,'core'=2] {'req','z'}, dimensions={0} | all-to-all | bytes 3145728 | tf_op jit(solution)/shard_map/all_to_all | solution.py:639
  79.2 7.4 %shard_map.136 = (bf16[512,1536]{1,0:T(8,128)(2,1)S(1)}, bf16[3,96,512]{2,1,0:T(8,128)(2,1)S(1)}) custom-call(bf16[512,1536]{1,0:T(8,128)(2,1)S(1)} %bitcast.10, bf16[2048,1024]{1,0:T(8,128)(2,1)S(1)} %get-tuple-element.53.up_ref, bf16[512,2048]{1,0:T(8,128)(2,1)S(1)} %get-tuple-element.54.down_ref, ...), custom_call_target="tpu_custom_call" | custom-call | flops 4831838208 | bytes 12582912 | tf_op jit(solution)/shard_map/pallas_call | solution.py:647
  86.6 28.3 %all_to_all.11 = bf16[64,8,1536]{2,1,0:T(8,128)(2,1)S(1)} all-to-all(bf16[64,8,1536]{2,1,0:T(8,128)(2,1)S(1)} %bitcast.11), channel_id=1, replica_groups=mesh['req'=16,'z'=4,'core'=2] {'req','z'}, dimensions={0} | all-to-all | bytes 3145728 | tf_op jit(solution)/shard_map/all_to_all | solution.py:669
  114.9 1.0 shard_map.137
  (26 shorter events, 0.1 us)
Async XLA Ops:
  0.0 7.4 %copy-start.9 = (s32[4]{0:T(128)S(1)}, s32[4]{0:T(128)}, u32[]{:S(2)}) copy-start(s32[4]{0:T(128)} %param.19) | copy-start | bytes 52
  1.9 9.2 %collective-permute-start.5 = (bf16[192,256]{1,0:T(8,128)(2,1)S(1)}, bf16[192,256]{1,0:T(8,128)(2,1)S(1)}, u32[]{:S(2)}, u32[]{:S(2)}) collective-permute-start(bf16[192,256]{1,0:T(8,128)(2,1)S(1)} %shard_map.127.after_ref.refs_0_.q_ref), channel_id=1, source_target_pairs={{0,6},{2,0},{4,2},{6,4},{1,7},{3,1},{5,3},{7,5},{8,14},{10,8},{12,... | collective-permute-start | bytes 294920 | tf_op jit(solution)/shard_map/ppermute | solution.py:508
  6.1 6.9 %collective-permute-start.3 = (bf16[192,256]{1,0:T(8,128)(2,1)S(1)}, bf16[192,256]{1,0:T(8,128)(2,1)S(1)}, u32[]{:S(2)}, u32[]{:S(2)}) collective-permute-start(bf16[192,256]{1,0:T(8,128)(2,1)S(1)} %shard_map.127.after_ref.refs_0_.q_ref), channel_id=1, source_target_pairs={{0,4},{2,6},{4,0},{6,2},{1,5},{3,7},{5,1},{7,3},{8,12},{10,14},{12... | collective-permute-start | bytes 294920 | tf_op jit(solution)/shard_map/ppermute | solution.py:508
  6.1 7.6 %collective-permute-start.1 = (bf16[192,256]{1,0:T(8,128)(2,1)S(1)}, bf16[192,256]{1,0:T(8,128)(2,1)S(1)}, u32[]{:S(2)}, u32[]{:S(2)}) collective-permute-start(bf16[192,256]{1,0:T(8,128)(2,1)S(1)} %shard_map.127.after_ref.refs_0_.q_ref), channel_id=1, source_target_pairs={{0,2},{2,4},{4,6},{6,0},{1,3},{3,5},{5,7},{7,1},{8,10},{10,12},{12... | collective-permute-start | bytes 294920 | tf_op jit(solution)/shard_map/ppermute | solution.py:508
  7.4 6.4 %collective-permute-start = (bf16[192,256]{1,0:T(8,128)(2,1)S(1)}, bf16[192,256]{1,0:T(8,128)(2,1)S(1)}, u32[]{:S(2)}, u32[]{:S(2)}) collective-permute-start(bf16[192,256]{1,0:T(8,128)(2,1)S(1)} %shard_map.127.after_ref.refs_0_.q_ref), channel_id=1, source_target_pairs={{0,1},{1,0},{2,3},{3,2},{4,5},{5,4},{6,7},{7,6},{8,9},{9,8},{10,11... | collective-permute-start | bytes 294920 | tf_op jit(solution)/shard_map/ppermute | solution.py:511
  11.1 2.7 %collective-permute-start.6 = (bf16[192,256]{1,0:T(8,128)(2,1)S(1)}, bf16[192,256]{1,0:T(8,128)(2,1)S(1)}, u32[]{:S(2)}, u32[]{:S(2)}) collective-permute-start(bf16[192,256]{1,0:T(8,128)(2,1)S(1)} %collective-permute-done.5.refs_3_), channel_id=1, source_target_pairs={{0,1},{1,0},{2,3},{3,2},{4,5},{5,4},{6,7},{7,6},{8,9},{9,8},{10,11... | collective-permute-start | bytes 294920 | tf_op jit(solution)/shard_map/ppermute | solution.py:511
  13.0 1.3 %collective-permute-start.4 = (bf16[192,256]{1,0:T(8,128)(2,1)S(1)}, bf16[192,256]{1,0:T(8,128)(2,1)S(1)}, u32[]{:S(2)}, u32[]{:S(2)}) collective-permute-start(bf16[192,256]{1,0:T(8,128)(2,1)S(1)} %collective-permute-done.3.refs_2_), channel_id=1, source_target_pairs={{0,1},{1,0},{2,3},{3,2},{4,5},{5,4},{6,7},{7,6},{8,9},{9,8},{10,11... | collective-permute-start | bytes 294920 | tf_op jit(solution)/shard_map/ppermute | solution.py:511
  13.7 1.3 %collective-permute-start.2 = (bf16[192,256]{1,0:T(8,128)(2,1)S(1)}, bf16[192,256]{1,0:T(8,128)(2,1)S(1)}, u32[]{:S(2)}, u32[]{:S(2)}) collective-permute-start(bf16[192,256]{1,0:T(8,128)(2,1)S(1)} %collective-permute-done.1.refs_1_), channel_id=1, source_target_pairs={{0,1},{1,0},{2,3},{3,2},{4,5},{5,4},{6,7},{7,6},{8,9},{9,8},{10,11... | collective-permute-start | bytes 294920 | tf_op jit(solution)/shard_map/ppermute | solution.py:511
  17.7 5.7 %copy-start = (bf16[192,2048]{1,0:T(8,128)(2,1)S(1)}, bf16[192,2048]{1,0:T(8,128)(2,1)}, u32[]{:S(2)}) copy-start(bf16[192,2048]{1,0:T(8,128)(2,1)} %refs_4_.1) | copy-start | bytes 2359300
  17.7 5.7 %copy-start.2 = (bf16[2048]{0:T(1024)(128)(2,1)S(1)}, bf16[2048]{0:T(1024)(128)(2,1)}, u32[]{:S(2)}) copy-start(bf16[2048]{0:T(1024)(128)(2,1)} %g_ref.1) | copy-start | bytes 12292
  17.8 5.7 %copy-start.4 = (s32[24,8]{0,1:T(8,128)S(1)}, s32[24,8]{0,1:T(8,128)}, u32[]{:S(2)}) copy-start(s32[24,8]{0,1:T(8,128)} %param.23) | copy-start | bytes 2308
  17.8 5.7 %copy-start.5 = (s32[4,48]{1,0:T(4,128)S(1)}, s32[4,48]{1,0:T(4,128)}, u32[]{:S(2)}) copy-start(s32[4,48]{1,0:T(4,128)} %up_ref.1) | copy-start | bytes 2308
  17.8 2.8 %collective-permute-start.7 = (bf16[9,192,128]{2,1,0:T(8,128)(2,1)S(1)}, bf16[9,192,128]{2,1,0:T(8,128)(2,1)S(1)}, u32[]{:S(2)}, u32[]{:S(2)}) collective-permute-start(bf16[9,192,128]{2,1,0:T(8,128)(2,1)S(1)} %shard_map.129.refs_6_), channel_id=1, source_target_pairs={{0,1},{1,0},{2,3},{3,2},{4,5},{5,4},{6,7},{7,6},{8,9},{9,8},{10,11... | collective-permute-start | bytes 1327112 | tf_op jit(solution)/shard_map/ppermute | solution.py:511
  21.3 8.2 %collective-permute-start.8 = (bf16[200,256]{1,0:T(8,128)(2,1)S(1)}, bf16[200,256]{1,0:T(8,128)(2,1)S(1)}, u32[]{:S(2)}, u32[]{:S(2)}) collective-permute-start(bf16[200,256]{1,0:T(8,128)(2,1)S(1)} %get-tuple-element.39), channel_id=1, source_target_pairs={{0,6},{2,0},{4,2},{6,4},{1,7},{3,1},{5,3},{7,5},{8,14},{10,8},{12,... | collective-permute-start | bytes 307208 | tf_op jit(solution)/shard_map/ppermute | solution.py:508
  21.4 8.1 %collective-permute-start.9 = (bf16[200,256]{1,0:T(8,128)(2,1)S(1)}, bf16[200,256]{1,0:T(8,128)(2,1)S(1)}, u32[]{:S(2)}, u32[]{:S(2)}) collective-permute-start(bf16[200,256]{1,0:T(8,128)(2,1)S(1)} %get-tuple-element.40), channel_id=1, source_target_pairs={{0,4},{2,6},{4,0},{6,2},{1,5},{3,7},{5,1},{7,3},{8,12},{10,14},{12... | collective-permute-start | bytes 307208 | tf_op jit(solution)/shard_map/ppermute | solution.py:508
  21.5 8.0 %collective-permute-start.10 = (bf16[200,256]{1,0:T(8,128)(2,1)S(1)}, bf16[200,256]{1,0:T(8,128)(2,1)S(1)}, u32[]{:S(2)}, u32[]{:S(2)}) collective-permute-start(bf16[200,256]{1,0:T(8,128)(2,1)S(1)} %get-tuple-element.41), channel_id=1, source_target_pairs={{0,2},{2,4},{4,6},{6,0},{1,3},{3,5},{5,7},{7,1},{8,10},{10,12},{12... | collective-permute-start | bytes 307208 | tf_op jit(solution)/shard_map/ppermute | solution.py:508
  23.4 6.1 %copy-start.1 = (bf16[256,2048]{1,0:T(8,128)(2,1)S(1)}, bf16[256,2048]{1,0:T(8,128)(2,1)}, u32[]{:S(2)}) copy-start(bf16[256,2048]{1,0:T(8,128)(2,1)} %refs_6_.1) | copy-start | bytes 3145732
  23.5 9.5 %copy-start.7 = (bf16[1,2048,1024]{2,1,0:T(8,128)(2,1)S(1)}, bf16[1,2048,1024]{2,1,0:T(8,128)(2,1)}, u32[]{:S(2)}) copy-start(bf16[1,2048,1024]{2,1,0:T(8,128)(2,1)} %param.24) | copy-start | bytes 12582916
  23.5 9.9 %copy-start.8 = (bf16[1,512,2048]{2,1,0:T(8,128)(2,1)S(1)}, bf16[1,512,2048]{2,1,0:T(8,128)(2,1)}, u32[]{:S(2)}) copy-start(bf16[1,512,2048]{2,1,0:T(8,128)(2,1)} %param.25) | copy-start | bytes 6291460
  23.5 21.2 %copy-start.3 = (bf16[2048]{0:T(1024)(128)(2,1)S(1)}, bf16[2048]{0:T(1024)(128)(2,1)}, u32[]{:S(2)}) copy-start(bf16[2048]{0:T(1024)(128)(2,1)} %refs_5_.1) | copy-start | bytes 12292
  31.0 48.1 %copy-start.6 = (bf16[2048,64]{0,1:T(8,128)(2,1)S(1)}, bf16[2048,64]{0,1:T(8,128)(2,1)}, u32[]{:S(2)}) copy-start(bf16[2048,64]{0,1:T(8,128)(2,1)} %param.22) | copy-start | bytes 786436
  31.1 1.8 %collective-permute-start.11 = (bf16[96,2048]{1,0:T(8,128)(2,1)S(1)}, bf16[96,2048]{1,0:T(8,128)(2,1)S(1)}, u32[]{:S(2)}, u32[]{:S(2)}) collective-permute-start(bf16[96,2048]{1,0:T(8,128)(2,1)S(1)} %get-tuple-element.45), channel_id=1, source_target_pairs={{0,1},{1,0},{2,3},{3,2},{4,5},{5,4},{6,7},{7,6},{8,9},{9,8},{10,11... | collective-permute-start | bytes 1179656 | tf_op jit(solution)/shard_map/ppermute | solution.py:511
  33.0 46.2 %collective-permute-start.15 = (bf16[2048,1024]{1,0:T(8,128)(2,1)S(1)}, bf16[2048,1024]{1,0:T(8,128)(2,1)S(1)}, u32[]{:S(2)}, u32[]{:S(2)}) collective-permute-start(bf16[2048,1024]{1,0:T(8,128)(2,1)S(1)} %bitcast.19), channel_id=1, source_target_pairs={{0,1},{1,0},{2,3},{3,2},{4,5},{5,4},{6,7},{7,6},{8,9},{9,8},{10,11... | collective-permute-start | bytes 12582920 | tf_op jit(solution)/shard_map/ppermute | solution.py:511
  33.4 45.8 %collective-permute-start.16 = (bf16[512,2048]{1,0:T(8,128)(2,1)S(1)}, bf16[512,2048]{1,0:T(8,128)(2,1)S(1)}, u32[]{:S(2)}, u32[]{:S(2)}) collective-permute-start(bf16[512,2048]{1,0:T(8,128)(2,1)S(1)} %bitcast.21), channel_id=1, source_target_pairs={{0,1},{1,0},{2,3},{3,2},{4,5},{5,4},{6,7},{7,6},{8,9},{9,8},{10,11... | collective-permute-start | bytes 6291464 | tf_op jit(solution)/shard_map/ppermute | solution.py:511
  33.7 5.6 %collective-permute-start.12 = (bf16[24,2048]{1,0:T(8,128)(2,1)S(1)}, bf16[24,2048]{1,0:T(8,128)(2,1)S(1)}, u32[]{:S(2)}, u32[]{:S(2)}) collective-permute-start(bf16[24,2048]{1,0:T(8,128)(2,1)S(1)} %get-tuple-element.48), channel_id=1, source_target_pairs={{0,6},{2,0},{4,2},{6,4},{1,7},{3,1},{5,3},{7,5},{8,14},{10,8},{12,... | collective-permute-start | bytes 294920 | tf_op jit(solution)/shard_map/ppermute | solution.py:508
  36.4 7.2 %collective-permute-start.13 = (bf16[24,2048]{1,0:T(8,128)(2,1)S(1)}, bf16[24,2048]{1,0:T(8,128)(2,1)S(1)}, u32[]{:S(2)}, u32[]{:S(2)}) collective-permute-start(bf16[24,2048]{1,0:T(8,128)(2,1)S(1)} %get-tuple-element.49), channel_id=1, source_target_pairs={{0,4},{2,6},{4,0},{6,2},{1,5},{3,7},{5,1},{7,3},{8,12},{10,14},{12... | collective-permute-start | bytes 294920 | tf_op jit(solution)/shard_map/ppermute | solution.py:508
  37.9 6.8 %collective-permute-start.14 = (bf16[24,2048]{1,0:T(8,128)(2,1)S(1)}, bf16[24,2048]{1,0:T(8,128)(2,1)S(1)}, u32[]{:S(2)}, u32[]{:S(2)}) collective-permute-start(bf16[24,2048]{1,0:T(8,128)(2,1)S(1)} %get-tuple-element.50), channel_id=1, source_target_pairs={{0,2},{2,4},{4,6},{6,0},{1,3},{3,5},{5,7},{7,1},{8,10},{10,12},{12... | collective-permute-start | bytes 294920 | tf_op jit(solution)/shard_map/ppermute | solution.py:508

commit v5 on v4

--- a/solution.py
+++ b/solution.py
@@ -74,18 +74,16 @@
     q_ref[...] = dot(normed, w_ref[...]).astype(BF16)
 
 
-def load_kernel(k_hbm, v_hbm, after_ref, k_ref, v_ref, sems):
+def load_kernel(k_hbm, after_ref, k_ref, sem):
     del after_ref
-    k_copy = pltpu.make_async_copy(k_hbm, k_ref, sems.at[0])
-    v_copy = pltpu.make_async_copy(v_hbm, v_ref, sems.at[1])
+    k_copy = pltpu.make_async_copy(k_hbm, k_ref, sem)
     k_copy.start()
-    v_copy.start()
     k_copy.wait()
-    v_copy.wait()
-
-
-def tree_kernel(scale, x_ref, g_ref, w_hbm, q_ref, up_ref, *refs):
+
+
+def tree_kernel(scale, x_ref, g_ref, w_hbm, q_ref, up_ref, after_ref, *refs):
     o_ref, lse_ref, turn, w_ref, sems = refs
+    del after_ref
     tokens, width = q_ref.shape
     w_copies = [
         pltpu.make_async_copy(w_hbm.at[i + 1], w_ref.at[i], sems.at[i]) for i in range(2)
@@ -127,9 +125,17 @@
 
 def page_kernel(scale, tree, kept, meta_ref, *refs):
     pieces, (k_ref, v_ref) = refs[:4], refs[4:6]
-    outs = refs[7:-2] if kept else refs[6:-2]
-    s_all, p_all = refs[-2:]
+    outs = refs[7:-2] if kept else refs[6:-3]
+    s_all, p_all = refs[-2:] if kept else refs[-3:-1]
     out_ref = outs[0]
+    if not kept:
+        v_hbm, v_ref, sems = v_ref, outs[1], refs[-1]
+        loads = [
+            pltpu.make_async_copy(v_hbm.at[r], v_ref.at[r], sems.at[r])
+            for r in range(v_hbm.shape[0])
+        ]
+        for load in loads:
+            load.start()
     requests, page = k_ref.shape[0], k_ref.shape[1]
     width = pieces[0].shape[1]
     pair = 2 * tree
@@ -143,6 +149,8 @@
     for r in range(requests):
         rows = slice(r * tree, (r + 1) * tree)
         live = meta_ref[r]
+        if not kept:
+            loads[r].wait()
 
         @pl.when(live > 0)
         def _():
@@ -268,17 +276,26 @@
     return jnp.where(iota((rows, experts), 0) // SLOTS == iota((rows, experts), 1), 1.0, 0.0)
 
 
-def window_kernel(scale, tree_inputs, routes_ref, up_hbm, down_hbm, after_ref, *refs):
-    tree_refs, place_refs, (up_ref, down_ref), scratch = refs[:2], refs[2:5], refs[5:7], refs[7:]
+def table_kernel(routes_ref, up_hbm, down_hbm, after_ref, *refs):
+    place_refs, (weights_ref, sems) = refs[:3], refs[3:]
     del after_ref
-    up_copy = pltpu.make_async_copy(up_hbm, up_ref, scratch[3].at[0])
-    down_copy = pltpu.make_async_copy(down_hbm, down_ref, scratch[3].at[1])
-    up_copy.start()
-    down_copy.start()
-    tree_kernel(scale, *tree_inputs, *tree_refs, *scratch[:3])
+    depth, both = up_hbm.shape
+    units = down_hbm.shape[0]
+    copies = [pltpu.make_async_copy(up_hbm, weights_ref.at[0:depth], sems.at[0])]
+    for i in range(down_hbm.shape[1] // both):
+        at = depth + i * units
+        copies.append(
+            pltpu.make_async_copy(
+                down_hbm.at[:, i * both : (i + 1) * both],
+                weights_ref.at[at : at + units],
+                sems.at[1 + i],
+            )
+        )
+    for copy in copies:
+        copy.start()
     place_kernel(routes_ref, *place_refs)
-    up_copy.wait()
-    down_copy.wait()
+    for copy in copies:
+        copy.wait()
 
 
 def place_kernel(routes_ref, place_ref, gather_ref, scatter_ref):
@@ -381,10 +398,8 @@
 
 def expert_kernel(
     x_ref,
-    up_ref,
-    down_ref,
-    other_up_ref,
-    other_down_ref,
+    weights_ref,
+    other_ref,
     gather_ref,
     scatter_ref,
     normed_ref,
@@ -395,7 +410,8 @@
 ):
     gate_kernel(normed_ref, router_ref, routes_ref, table_ref)
     rows, packed = x_ref.shape
-    width, both = up_ref.shape
+    width = normed_ref.shape[1]
+    both = weights_ref.shape[1]
     units = both // 2
     cut = width - packed
     chunks = packed // cut
@@ -410,25 +426,27 @@
         tails.append(tail.astype(BF16))
     main, tail = jnp.concatenate(mains, axis=0), jnp.concatenate(tails, axis=0)
     hidden = []
-    for weights in (up_ref, other_up_ref):
+    for weights in (weights_ref, other_ref):
         parts = []
         for at in range(0, units, units // 2):
             gate_cut = slice(at, at + units // 2)
             up_cut = slice(units + at, units + at + units // 2)
-            gate = dot(main, weights[0:packed, gate_cut]) + dot(tail, weights[packed:, gate_cut])
-            up = dot(main, weights[0:packed, up_cut]) + dot(tail, weights[packed:, up_cut])
+            gate = dot(main, weights[0:packed, gate_cut]) + dot(tail, weights[packed:width, gate_cut])
+            up = dot(main, weights[0:packed, up_cut]) + dot(tail, weights[packed:width, up_cut])
             parts.append((gate / (1.0 + jnp.exp(-gate)) * up).astype(BF16))
         hidden.append(jnp.concatenate(parts, axis=1))
 
-    def result(columns):
-        first = dot(hidden[0], down_ref[:, columns]).astype(BF16).astype(F32)
-        second = dot(hidden[1], other_down_ref[:, columns]).astype(BF16).astype(F32)
+    def result(k):
+        at = width + k * cut // both * units
+        rows, columns = slice(at, at + units), slice(k * cut % both, k * cut % both + cut)
+        first = dot(hidden[0], weights_ref[rows, columns]).astype(BF16).astype(F32)
+        second = dot(hidden[1], other_ref[rows, columns]).astype(BF16).astype(F32)
         return (first + second).astype(BF16)
 
-    last = result(slice(packed, width))
+    last = result(chunks)
     for k in range(chunks):
         columns = slice(k * cut, (k + 1) * cut)
-        value = result(columns)
+        value = result(k)
         for i in range(rows // block):
             own = slice(i * real, (i + 1) * real)
             pair = jnp.concatenate([value[own], last[own]], axis=0)
@@ -524,29 +542,28 @@
         ]
     ).astype(jnp.int32)
 
-    keys, values = call(
+    keys = call(
         load_kernel,
-        (sds(cache_keys.shape, BF16), sds(cache_values.shape, BF16)),
-        [HBM, HBM, pl.ANY],
-        [pltpu.SemaphoreType.DMA((2,))],
-        bytes_accessed=4 * requests * page * width,
-        vmem=16 << 20,
-    )(cache_keys, cache_values, query)
+        sds(cache_keys.shape, BF16),
+        [HBM, pl.ANY],
+        [pltpu.SemaphoreType.DMA],
+        bytes_accessed=2 * requests * page * width,
+    )(cache_keys, query)
 
     scratch = [
         pltpu.VMEM((z_count * 2 * tree, page), F32),
         pltpu.VMEM((z_count * 2 * tree, page), BF16),
     ]
     heads = 2 * z_count
-    for_other = call(
+    for_other, values = call(
         functools.partial(page_kernel, scale, tree, False),
-        sds((heads + 1, tokens, HEAD_DIM), BF16),
-        [SMEM] + [VMEM] * 6,
-        scratch,
+        (sds((heads + 1, tokens, HEAD_DIM), BF16), sds(cache_values.shape, BF16)),
+        [SMEM] + [VMEM] * 5 + [HBM],
+        scratch + [pltpu.SemaphoreType.DMA((requests,))],
         flops=2 * tokens * page * width,
         bytes_accessed=2 * requests * page * width,
         vmem=20 << 20,
-    )(meta, *other_pieces, keys, values)
+    )(meta, *other_pieces, keys, cache_values)
     from_other = over_core(for_other)
     kept, kept_lse = call(
         functools.partial(page_kernel, scale, tree, True),
@@ -566,45 +583,18 @@
     )(from_other, kept, kept_lse)
     arrived = [merged[0]] + [over_z(merged[step], -step) for step in steps]
 
-    block = experts * SLOTS // 2
-    real = block // SLOTS * CAP
-
-    def body(x_ref, g_ref, w_hbm, q_ref, up_ref, *refs):
-        window_kernel(scale, (x_ref, g_ref, w_hbm, q_ref, up_ref), *refs)
-
-    tree_o, tree_lse, place, gather, scatter, gate_up, down = call(
-        body,
-        (
-            sds((tokens, local_width), F32),
-            sds((8, 256), F32),
-            sds((chunks, experts * SLOTS, 2 * own), BF16),
-            sds((1 + chunks, real, block), BF16),
-            sds((chunks, block, 2 * real), BF16),
-            sds(w_gate_up.shape[1:], BF16),
-            sds(w_down.shape[1:], BF16),
-        ),
-        [VMEM, VMEM, HBM, VMEM, VMEM, VMEM, HBM, HBM, pl.ANY],
+    tree_o, tree_lse = call(
+        functools.partial(tree_kernel, scale),
+        (sds((tokens, local_width), F32), sds((8, 256), F32)),
+        [VMEM, VMEM, HBM, VMEM, VMEM, pl.ANY],
         [
             pltpu.VMEM((256, 128), F32),
             pltpu.VMEM((2, width, local_width), BF16),
             pltpu.SemaphoreType.DMA((2,)),
-            pltpu.SemaphoreType.DMA((2,)),
         ],
         flops=4 * tokens * width * local_width,
-        bytes_accessed=2 * width * (tokens + 2 * local_width) + (1 << 23),
-        vmem=24 << 20,
-    )(
-        hidden,
-        gain_attn,
-        w_three,
-        query,
-        parents,
-        routes.T,
-        pltpu.with_memory_space_constraint(w_gate_up[0], HBM),
-        pltpu.with_memory_space_constraint(w_down[0], HBM),
-        merged[0],
-    )
-
+        bytes_accessed=2 * width * (tokens + 2 * local_width),
+    )(hidden, gain_attn, w_three, query, parents, merged[0])
     theirs, ours = call(
         out_kernel,
         (sds((z_count * own, width), BF16), sds((z_count * own, width), F32)),
@@ -619,11 +609,31 @@
         [VMEM] * 2,
         bytes_accessed=1 << 20,
     )(ours, over_core(theirs))
-    first_fold, far_up, far_down = lax.optimization_barrier(
-        (folded[0], w_gate_up[0], w_down[0])
+    mixed = [folded[0]] + [over_z(folded[step], -step) for step in steps]
+    block = experts * SLOTS // 2
+    real = block // SLOTS * CAP
+    weight_rows = width + width * w_down.shape[1] // w_gate_up.shape[2]
+    place, gather, scatter, weights = call(
+        table_kernel,
+        (
+            sds((chunks, experts * SLOTS, 2 * own), BF16),
+            sds((1 + chunks, real, block), BF16),
+            sds((chunks, block, 2 * real), BF16),
+            sds((weight_rows, w_gate_up.shape[2]), BF16),
+        ),
+        [VMEM, HBM, HBM, pl.ANY],
+        [pltpu.SemaphoreType.DMA((1 + width // w_gate_up.shape[2],))],
+        flops=1 << 24,
+        bytes_accessed=1 << 23,
+        vmem=16 << 20,
+    )(
+        routes.T,
+        pltpu.with_memory_space_constraint(w_gate_up[0], HBM),
+        pltpu.with_memory_space_constraint(w_down[0], HBM),
+        folded[0],
     )
-    other_gate_up, other_down = over_core(far_up), over_core(far_down)
-    mixed = [first_fold] + [over_z(folded[step], -step) for step in steps]
+    *mixed, weights = lax.optimization_barrier((*mixed, weights))
+    other_weights = over_core(weights)
 
     residual, normed, outgoing = call(
         residual_kernel,
@@ -650,16 +660,14 @@
             sds((experts * SLOTS, packed), BF16),
             sds((chunks, 4 * own, experts * SLOTS), BF16),
         ),
-        [VMEM] * 10,
+        [VMEM] * 8,
         flops=12 * experts * CAP * width * w_down.shape[1],
         bytes_accessed=12 * width * w_down.shape[1],
         vmem=24 << 20,
     )(
         rows,
-        gate_up,
-        down,
-        other_gate_up,
-        other_down,
+        weights,
+        other_weights,
         gather,
         scatter,
         normed,

time: 116 us -> 115 us (level)
  starting transfers between devices: 14.6 us -> 12 us
    ppermute x9, starting transfers between devices: 13.1 us -> 11.2 us  [over_z(): lax.ppermute(value, 'z', [(i, (i + step) % z_count) for i in range(z_coun...]
    pallas_call x3 -> x4, Pallas kernels: 12.2 us -> 13.3 us  [the longest x1 4 us: per_device(): call(functools.partial(page_kernel, scale, tree, False), (sds((heads + 1,...]
    ppermute x8 -> x7, waiting for transfers between devices: 2.93 us -> 2.93 us  [over_core(): return lax.ppermute(value, 'core', [(0, 1), (1, 0)])]
  transfers between devices with their start and end apart: 17 -> 16, of which waited for: 7 -> 9; matrix products, arithmetic and copies ran while one was open for 0% -> 1% of each run, Pallas kernels for 12% -> 12%
where the time goes in v5:
time: 115 us
  blocking collectives  61.7 us (54%)
  Pallas kernels  29.8 us (26%)
  starting transfers between devices  12 us (10%)
  waiting for transfers between devices  10.3 us (9%)
    all_to_all x1, blocking collectives, per_device(): lax.all_to_all(outgoing.reshape(experts, SLOTS, packed), ('req', 'z'), sp...  33.1 us
    all_to_all x1, blocking collectives, per_device(): lax.all_to_all(summed.reshape(experts, SLOTS, packed), ('req', 'z'), spli...  28.7 us
    ppermute x9, starting transfers between devices, over_z(): lax.ppermute(value, 'z', [(i, (i + step) % z_count) for i in range(z_coun...  11.2 us
    ppermute x9, waiting for transfers between devices, over_z(): lax.ppermute(value, 'z', [(i, (i + step) % z_count) for i in range(z_coun...  7.41 us
    pallas_call x1, Pallas kernels, per_device(): call(expert_kernel, (sds((experts * SLOTS, packed), BF16), sds((chunks, 4...  7.35 us
    pallas_call x1, Pallas kernels, per_device(): call(functools.partial(page_kernel, scale, tree, False), (sds((heads + 1,...  4 us
    pallas_call x1, Pallas kernels, per_device(): call(functools.partial(tree_kernel, scale), (sds((tokens, local_width), F...  3.83 us
    pallas_call x1, Pallas kernels, per_device(): call(table_kernel, (sds((chunks, experts * SLOTS, 2 * own), BF16), sds((1...  3.24 us
  transfers between devices with their start and end apart: 16, of which 9 were waited for; matrix products, arithmetic and copies ran while one was open for 1% of the time, Pallas kernels for 12%

profile of v5, /device:TPU:0, one launch (start us, length us, event | category | flops | bytes accessed | tf_op | source)
XLA Modules:
  0.0 115.1 jit_solution(12025139975816064442)
XLA Ops:
  0.0 1.9 %shard_map.127.after_ref.refs_0_.q_ref = bf16[192,256]{1,0:T(8,128)(2,1)S(1)} custom-call(bf16[192,2048]{1,0:T(8,128)(2,1)} %refs_4_.1, bf16[2048]{0:T(1024)(128)(2,1)} %g_ref.1, bf16[3,2048,256]{2,1,0:T(8,128)(2,1)} %bitcast.16), custom_call_target="tpu_custom_call" | custom-call | flops 201326592 | bytes 1835008 | tf_op jit(solution)/shard_map/pallas_call | solution.py:507
  1.9 4.2 %collective-permute-start.5 = (bf16[192,256]{1,0:T(8,128)(2,1)S(1)}, bf16[192,256]{1,0:T(8,128)(2,1)S(1)}, u32[]{:S(2)}, u32[]{:S(2)}) collective-permute-start(bf16[192,256]{1,0:T(8,128)(2,1)S(1)} %shard_map.127.after_ref.refs_0_.q_ref), channel_id=1, source_target_pairs={{0,6},{2,0},{4,2},{6,4},{1,7},{3,1},{5,3},{7,5},{8,14},{10,8},{12,... | collective-permute-start | bytes 294920 | tf_op jit(solution)/shard_map/ppermute | solution.py:526
  6.1 0.0 collective-permute-start.3
  6.1 1.3 %collective-permute-start.1 = (bf16[192,256]{1,0:T(8,128)(2,1)S(1)}, bf16[192,256]{1,0:T(8,128)(2,1)S(1)}, u32[]{:S(2)}, u32[]{:S(2)}) collective-permute-start(bf16[192,256]{1,0:T(8,128)(2,1)S(1)} %shard_map.127.after_ref.refs_0_.q_ref), channel_id=1, source_target_pairs={{0,2},{2,4},{4,6},{6,0},{1,3},{3,5},{5,7},{7,1},{8,10},{10,12},{12... | collective-permute-start | bytes 294920 | tf_op jit(solution)/shard_map/ppermute | solution.py:526
  7.3 0.0 collective-permute-start
  7.4 0.7 broadcast_subtract_fusion
  8.0 0.1 mul.38
  8.1 0.1 mul.40
  8.2 2.2 %shard_map.128.refs_4_ = bf16[4,256,2048]{2,1,0:T(8,128)(2,1)S(1)} custom-call(bf16[4,256,2048]{2,1,0:T(8,128)(2,1)} %k_hbm.1, bf16[192,256]{1,0:T(8,128)(2,1)S(1)} %shard_map.127.after_ref.refs_0_.q_ref), custom_call_target="tpu_custom_call" | custom-call | bytes 4194304 | tf_op jit(solution)/shard_map/pallas_call | solution.py:545
  10.4 0.0 collective-permute-done.5.refs_3_
  10.4 0.6 collective-permute-start.6
  11.0 2.0 %collective-permute-done.3.refs_2_ = bf16[192,256]{1,0:T(8,128)(2,1)S(1)} collective-permute-done((bf16[192,256]{1,0:T(8,128)(2,1)S(1)}, bf16[192,256]{1,0:T(8,128)(2,1)S(1)}, u32[]{:S(2)}, u32[]{:S(2)}) %collective-permute-start.3) | collective-permute-done | bytes 98336 | tf_op jit(solution)/shard_map/ppermute | solution.py:526
  13.0 0.0 collective-permute-start.4
  13.0 0.7 collective-permute-done.1.refs_1_
  13.7 0.1 pad_add_fusion.1.meta_ref
  13.7 0.5 collective-permute-done.4.refs_2_
  14.3 0.7 collective-permute-done.2.refs_1_
  15.0 4.0 %shard_map.129 = (bf16[9,192,128]{2,1,0:T(8,128)(2,1)S(1)}, bf16[4,256,2048]{2,1,0:T(8,128)(2,1)S(1)}) custom-call(s32[24]{0:T(128)S(1)} %pad_add_fusion.1.meta_ref, bf16[192,256]{1,0:T(8,128)(2,1)S(1)} %collective-permute-done.refs_0_, bf16[192,256]{1,0:T(8,128)(2,1)S(1)} %collective-permute-done.2.refs_1_, ...), custom_call_target="tpu_custom_call" | custom-call | flops 201326592 | bytes 4194304 | tf_op jit(solution)/shard_map/pallas_call | solution.py:558
  19.0 0.1 collective-permute-start.7
  19.1 0.0 copy-start
  19.1 0.0 copy-start.2
  19.1 0.0 copy-start.5
  19.1 2.7 %shard_map.130 = (f32[8,192,128]{2,1,0:T(8,128)S(1)}, f32[192,128]{1,0:T(8,128)S(1)}) custom-call(s32[24]{0:T(128)S(1)} %pad_add_fusion.1.meta_ref, bf16[192,256]{1,0:T(8,128)(2,1)S(1)} %shard_map.127.after_ref.refs_0_.q_ref, bf16[192,256]{1,0:T(8,128)(2,1)S(1)} %collective-permute-done.1.refs_1_, bf16[192,256]{1,0:T(8,128)(2,1)S(1)} %collective-permute-done.3.refs_2_, ...), custom_call_target="tpu_custom_call" | custom-call | flops 201326592 | bytes 4194304 | tf_op jit(solution)/shard_map/pallas_call | solution.py:568
  21.8 0.0 copy-start.1
  21.9 0.0 copy-start.4
  21.9 0.7 shard_map.131
  22.6 0.1 collective-permute-start.8
  22.7 0.1 collective-permute-start.9
  22.8 1.9 %collective-permute-start.10 = (bf16[200,256]{1,0:T(8,128)(2,1)S(1)}, bf16[200,256]{1,0:T(8,128)(2,1)S(1)}, u32[]{:S(2)}, u32[]{:S(2)}) collective-permute-start(bf16[200,256]{1,0:T(8,128)(2,1)S(1)} %get-tuple-element.42), channel_id=1, source_target_pairs={{0,2},{2,4},{4,6},{6,0},{1,3},{3,5},{5,7},{7,1},{8,10},{10,12},{12... | collective-permute-start | bytes 307208 | tf_op jit(solution)/shard_map/ppermute | solution.py:526
  24.7 3.8 %shard_map.132 = (f32[192,256]{1,0:T(8,128)S(1)}, f32[8,256]{1,0:T(8,128)S(1)}) custom-call(bf16[192,2048]{1,0:T(8,128)(2,1)S(1)} %copy-done, bf16[2048]{0:T(1024)(128)(2,1)S(1)} %copy-done.2, bf16[3,2048,256]{2,1,0:T(8,128)(2,1)} %bitcast.17, bf16[192,256]{1,0:T(8,128)(2,1)S(1)} %shard_map.127.after_ref.refs_0_.q_ref, s32[4,48]{1,0:T(4,128)S(1)} %copy-done.5, ...), custom_call_target="tpu_custom_call" | custom-call | flops 402653184 | bytes 2883584 | tf_op jit(solution)/shard_map/pallas_call | solution.py:586
  28.5 1.4 %collective-permute-done.9.refs_2_ = bf16[200,256]{1,0:T(8,128)(2,1)S(1)} collective-permute-done((bf16[200,256]{1,0:T(8,128)(2,1)S(1)}, bf16[200,256]{1,0:T(8,128)(2,1)S(1)}, u32[]{:S(2)}, u32[]{:S(2)}) %collective-permute-start.9) | collective-permute-done | bytes 102432 | tf_op jit(solution)/shard_map/ppermute | solution.py:526
  29.9 0.6 collective-permute-done.10.refs_3_
  30.5 1.5 %shard_map.133 = (bf16[96,2048]{1,0:T(8,128)(2,1)S(1)}, f32[96,2048]{1,0:T(8,128)S(1)}) custom-call(s32[24]{0:T(128)S(1)} %pad_add_fusion.1.meta_ref, bf16[200,256]{1,0:T(8,128)(2,1)S(1)} %get-tuple-element.39.after_ref.refs_0_, bf16[200,256]{1,0:T(8,128)(2,1)S(1)} %collective-permute-done.8.refs_1_, bf16[200,256]{1,0:T(8,128)(2,1)S(1)} %collective-permute-done.9.refs_2_, ...), custom_call_target="tpu_custom_call" | custom-call | flops 201326592 | bytes 1835008 | tf_op jit(solution)/shard_map/pallas_call | solution.py:598
  32.0 0.0 copy-start.3
  32.0 0.1 collective-permute-start.11
  32.1 1.7 %collective-permute-done.11.theirs_ref = bf16[96,2048]{1,0:T(8,128)(2,1)S(1)} collective-permute-done((bf16[96,2048]{1,0:T(8,128)(2,1)S(1)}, bf16[96,2048]{1,0:T(8,128)(2,1)S(1)}, u32[]{:S(2)}, u32[]{:S(2)}) %collective-permute-start.11) | collective-permute-done | bytes 393248 | tf_op jit(solution)/shard_map/ppermute | solution.py:529
  33.8 0.1 shard_map.134
  33.9 1.6 %collective-permute-start.12 = (bf16[24,2048]{1,0:T(8,128)(2,1)S(1)}, bf16[24,2048]{1,0:T(8,128)(2,1)S(1)}, u32[]{:S(2)}, u32[]{:S(2)}) collective-permute-start(bf16[24,2048]{1,0:T(8,128)(2,1)S(1)} %get-tuple-element.48), channel_id=1, source_target_pairs={{0,6},{2,0},{4,2},{6,4},{1,7},{3,1},{5,3},{7,5},{8,14},{10,8},{12,... | collective-permute-start | bytes 294920 | tf_op jit(solution)/shard_map/ppermute | solution.py:526
  35.5 0.9 collective-permute-start.13
  36.4 1.2 %collective-permute-start.14 = (bf16[24,2048]{1,0:T(8,128)(2,1)S(1)}, bf16[24,2048]{1,0:T(8,128)(2,1)S(1)}, u32[]{:S(2)}, u32[]{:S(2)}) collective-permute-start(bf16[24,2048]{1,0:T(8,128)(2,1)S(1)} %get-tuple-element.50), channel_id=1, source_target_pairs={{0,2},{2,4},{4,6},{6,0},{1,3},{3,5},{5,7},{7,1},{8,10},{10,12},{12... | collective-permute-start | bytes 294920 | tf_op jit(solution)/shard_map/ppermute | solution.py:526
  37.6 3.2 %shard_map.135 = (bf16[3,512,48]{2,1,0:T(8,128)(2,1)S(1)}, bf16[4,192,256]{2,1,0:T(8,128)(2,1)S(1)}, bf16[3,256,384]{2,1,0:T(8,128)(2,1)S(1)}, bf16[3072,1024]{1,0:T(8,128)(2,1)S(1)}) custom-call(s32[8,24]{1,0:T(8,128)S(1)} %bitcast.13, bf16[2048,1024]{1,0:T(8,128)(2,1)} %bitcast.18, bf16[512,2048]{1,0:T(8,128)(2,1)} %bitcast.19, ...), custom_call_target="tpu_custom_call" | custom-call | flops 16777216 | bytes 8388608 | tf_op jit(solution)/shard_map/pallas_call | solution.py:616
  40.9 1.7 %collective-permute-done.13.refs_2_ = bf16[24,2048]{1,0:T(8,128)(2,1)S(1)} collective-permute-done((bf16[24,2048]{1,0:T(8,128)(2,1)S(1)}, bf16[24,2048]{1,0:T(8,128)(2,1)S(1)}, u32[]{:S(2)}, u32[]{:S(2)}) %collective-permute-start.13) | collective-permute-done | bytes 98336 | tf_op jit(solution)/shard_map/ppermute | solution.py:526
  42.6 1.0 collective-permute-done.14.refs_3_
  43.7 1.2 %shard_map.136 = (f32[24,2048]{1,0:T(8,128)S(1)}, bf16[24,2048]{1,0:T(8,128)(2,1)S(1)}, bf16[512,1536]{1,0:T(8,128)(2,1)S(1)}) custom-call(s32[24]{0:T(128)S(1)} %pad_add_fusion.1.meta_ref, f32[24,2048]{1,0:T(8,128)S(1)} %get-tuple-element.52.after_ref.refs_0_, bf16[24,2048]{1,0:T(8,128)(2,1)S(1)} %collective-permute-done.12.refs_1_, ...), custom_call_target="tpu_custom_call" | custom-call | flops 134217728 | bytes 4194304 | tf_op jit(solution)/shard_map/pallas_call | solution.py:638
  44.9 33.1 %all_to_all.10 = bf16[64,8,1536]{2,1,0:T(8,128)(2,1)S(1)} all-to-all(bf16[64,8,1536]{2,1,0:T(8,128)(2,1)S(1)} %bitcast.11), channel_id=1, replica_groups=mesh['req'=16,'z'=4,'core'=2] {'req','z'}, dimensions={0} | all-to-all | bytes 3145728 | tf_op jit(solution)/shard_map/all_to_all | solution.py:649
  78.0 7.4 %shard_map.137 = (bf16[512,1536]{1,0:T(8,128)(2,1)S(1)}, bf16[3,96,512]{2,1,0:T(8,128)(2,1)S(1)}) custom-call(bf16[512,1536]{1,0:T(8,128)(2,1)S(1)} %bitcast.10, bf16[3072,1024]{1,0:T(8,128)(2,1)S(1)} %get-tuple-element.58.weights_ref, bf16[3072,1024]{1,0:T(8,128)(2,1)S(1)} %collective-permute-done.15.other_ref, ...), custom_call_target="tpu_custom_call" | custom-call | flops 4831838208 | bytes 12582912 | tf_op jit(solution)/shard_map/pallas_call | solution.py:657
  85.4 28.7 %all_to_all.11 = bf16[64,8,1536]{2,1,0:T(8,128)(2,1)S(1)} all-to-all(bf16[64,8,1536]{2,1,0:T(8,128)(2,1)S(1)} %bitcast.12), channel_id=1, replica_groups=mesh['req'=16,'z'=4,'core'=2] {'req','z'}, dimensions={0} | all-to-all | bytes 3145728 | tf_op jit(solution)/shard_map/all_to_all | solution.py:677
  114.0 1.0 shard_map.138
  (19 shorter events, 0.1 us)
Async XLA Ops:
  1.9 8.5 %collective-permute-start.5 = (bf16[192,256]{1,0:T(8,128)(2,1)S(1)}, bf16[192,256]{1,0:T(8,128)(2,1)S(1)}, u32[]{:S(2)}, u32[]{:S(2)}) collective-permute-start(bf16[192,256]{1,0:T(8,128)(2,1)S(1)} %shard_map.127.after_ref.refs_0_.q_ref), channel_id=1, source_target_pairs={{0,6},{2,0},{4,2},{6,4},{1,7},{3,1},{5,3},{7,5},{8,14},{10,8},{12,... | collective-permute-start | bytes 294920 | tf_op jit(solution)/shard_map/ppermute | solution.py:526
  6.1 6.9 %collective-permute-start.3 = (bf16[192,256]{1,0:T(8,128)(2,1)S(1)}, bf16[192,256]{1,0:T(8,128)(2,1)S(1)}, u32[]{:S(2)}, u32[]{:S(2)}) collective-permute-start(bf16[192,256]{1,0:T(8,128)(2,1)S(1)} %shard_map.127.after_ref.refs_0_.q_ref), channel_id=1, source_target_pairs={{0,4},{2,6},{4,0},{6,2},{1,5},{3,7},{5,1},{7,3},{8,12},{10,14},{12... | collective-permute-start | bytes 294920 | tf_op jit(solution)/shard_map/ppermute | solution.py:526
  6.1 7.6 %collective-permute-start.1 = (bf16[192,256]{1,0:T(8,128)(2,1)S(1)}, bf16[192,256]{1,0:T(8,128)(2,1)S(1)}, u32[]{:S(2)}, u32[]{:S(2)}) collective-permute-start(bf16[192,256]{1,0:T(8,128)(2,1)S(1)} %shard_map.127.after_ref.refs_0_.q_ref), channel_id=1, source_target_pairs={{0,2},{2,4},{4,6},{6,0},{1,3},{3,5},{5,7},{7,1},{8,10},{10,12},{12... | collective-permute-start | bytes 294920 | tf_op jit(solution)/shard_map/ppermute | solution.py:526
  7.3 6.4 %collective-permute-start = (bf16[192,256]{1,0:T(8,128)(2,1)S(1)}, bf16[192,256]{1,0:T(8,128)(2,1)S(1)}, u32[]{:S(2)}, u32[]{:S(2)}) collective-permute-start(bf16[192,256]{1,0:T(8,128)(2,1)S(1)} %shard_map.127.after_ref.refs_0_.q_ref), channel_id=1, source_target_pairs={{0,1},{1,0},{2,3},{3,2},{4,5},{5,4},{6,7},{7,6},{8,9},{9,8},{10,11... | collective-permute-start | bytes 294920 | tf_op jit(solution)/shard_map/ppermute | solution.py:529
  10.4 3.3 %collective-permute-start.6 = (bf16[192,256]{1,0:T(8,128)(2,1)S(1)}, bf16[192,256]{1,0:T(8,128)(2,1)S(1)}, u32[]{:S(2)}, u32[]{:S(2)}) collective-permute-start(bf16[192,256]{1,0:T(8,128)(2,1)S(1)} %collective-permute-done.5.refs_3_), channel_id=1, source_target_pairs={{0,1},{1,0},{2,3},{3,2},{4,5},{5,4},{6,7},{7,6},{8,9},{9,8},{10,11... | collective-permute-start | bytes 294920 | tf_op jit(solution)/shard_map/ppermute | solution.py:529
  13.0 1.3 %collective-permute-start.4 = (bf16[192,256]{1,0:T(8,128)(2,1)S(1)}, bf16[192,256]{1,0:T(8,128)(2,1)S(1)}, u32[]{:S(2)}, u32[]{:S(2)}) collective-permute-start(bf16[192,256]{1,0:T(8,128)(2,1)S(1)} %collective-permute-done.3.refs_2_), channel_id=1, source_target_pairs={{0,1},{1,0},{2,3},{3,2},{4,5},{5,4},{6,7},{7,6},{8,9},{9,8},{10,11... | collective-permute-start | bytes 294920 | tf_op jit(solution)/shard_map/ppermute | solution.py:529
  13.7 1.3 %collective-permute-start.2 = (bf16[192,256]{1,0:T(8,128)(2,1)S(1)}, bf16[192,256]{1,0:T(8,128)(2,1)S(1)}, u32[]{:S(2)}, u32[]{:S(2)}) collective-permute-start(bf16[192,256]{1,0:T(8,128)(2,1)S(1)} %collective-permute-done.1.refs_1_), channel_id=1, source_target_pairs={{0,1},{1,0},{2,3},{3,2},{4,5},{5,4},{6,7},{7,6},{8,9},{9,8},{10,11... | collective-permute-start | bytes 294920 | tf_op jit(solution)/shard_map/ppermute | solution.py:529
  19.0 2.9 %collective-permute-start.7 = (bf16[9,192,128]{2,1,0:T(8,128)(2,1)S(1)}, bf16[9,192,128]{2,1,0:T(8,128)(2,1)S(1)}, u32[]{:S(2)}, u32[]{:S(2)}) collective-permute-start(bf16[9,192,128]{2,1,0:T(8,128)(2,1)S(1)} %get-tuple-element.35.refs_6_), channel_id=1, source_target_pairs={{0,1},{1,0},{2,3},{3,2},{4,5},{5,4},{6,7},{7,6},{8,9},{9,8},{10,11... | collective-permute-start | bytes 1327112 | tf_op jit(solution)/shard_map/ppermute | solution.py:529
  19.1 5.6 %copy-start = (bf16[192,2048]{1,0:T(8,128)(2,1)S(1)}, bf16[192,2048]{1,0:T(8,128)(2,1)}, u32[]{:S(2)}) copy-start(bf16[192,2048]{1,0:T(8,128)(2,1)} %refs_4_.1) | copy-start | bytes 2359300
  19.1 5.6 %copy-start.2 = (bf16[2048]{0:T(1024)(128)(2,1)S(1)}, bf16[2048]{0:T(1024)(128)(2,1)}, u32[]{:S(2)}) copy-start(bf16[2048]{0:T(1024)(128)(2,1)} %g_ref.1) | copy-start | bytes 12292
  19.1 5.6 %copy-start.5 = (s32[4,48]{1,0:T(4,128)S(1)}, s32[4,48]{1,0:T(4,128)}, u32[]{:S(2)}) copy-start(s32[4,48]{1,0:T(4,128)} %up_ref.1) | copy-start | bytes 2308
  21.8 8.7 %copy-start.1 = (bf16[256,2048]{1,0:T(8,128)(2,1)S(1)}, bf16[256,2048]{1,0:T(8,128)(2,1)}, u32[]{:S(2)}) copy-start(bf16[256,2048]{1,0:T(8,128)(2,1)} %refs_6_.1) | copy-start | bytes 3145732
  21.9 15.7 %copy-start.4 = (s32[24,8]{0,1:T(8,128)S(1)}, s32[24,8]{0,1:T(8,128)}, u32[]{:S(2)}) copy-start(s32[24,8]{0,1:T(8,128)} %param.23) | copy-start | bytes 2308
  22.6 5.9 %collective-permute-start.8 = (bf16[200,256]{1,0:T(8,128)(2,1)S(1)}, bf16[200,256]{1,0:T(8,128)(2,1)S(1)}, u32[]{:S(2)}, u32[]{:S(2)}) collective-permute-start(bf16[200,256]{1,0:T(8,128)(2,1)S(1)} %get-tuple-element.40), channel_id=1, source_target_pairs={{0,6},{2,0},{4,2},{6,4},{1,7},{3,1},{5,3},{7,5},{8,14},{10,8},{12,... | collective-permute-start | bytes 307208 | tf_op jit(solution)/shard_map/ppermute | solution.py:526
  22.7 7.2 %collective-permute-start.9 = (bf16[200,256]{1,0:T(8,128)(2,1)S(1)}, bf16[200,256]{1,0:T(8,128)(2,1)S(1)}, u32[]{:S(2)}, u32[]{:S(2)}) collective-permute-start(bf16[200,256]{1,0:T(8,128)(2,1)S(1)} %get-tuple-element.41), channel_id=1, source_target_pairs={{0,4},{2,6},{4,0},{6,2},{1,5},{3,7},{5,1},{7,3},{8,12},{10,14},{12... | collective-permute-start | bytes 307208 | tf_op jit(solution)/shard_map/ppermute | solution.py:526
  22.8 7.7 %collective-permute-start.10 = (bf16[200,256]{1,0:T(8,128)(2,1)S(1)}, bf16[200,256]{1,0:T(8,128)(2,1)S(1)}, u32[]{:S(2)}, u32[]{:S(2)}) collective-permute-start(bf16[200,256]{1,0:T(8,128)(2,1)S(1)} %get-tuple-element.42), channel_id=1, source_target_pairs={{0,2},{2,4},{4,6},{6,0},{1,3},{3,5},{5,7},{7,1},{8,10},{10,12},{12... | collective-permute-start | bytes 307208 | tf_op jit(solution)/shard_map/ppermute | solution.py:526
  32.0 11.7 %copy-start.3 = (bf16[2048]{0:T(1024)(128)(2,1)S(1)}, bf16[2048]{0:T(1024)(128)(2,1)}, u32[]{:S(2)}) copy-start(bf16[2048]{0:T(1024)(128)(2,1)} %refs_5_.3) | copy-start | bytes 12292
  32.0 1.8 %collective-permute-start.11 = (bf16[96,2048]{1,0:T(8,128)(2,1)S(1)}, bf16[96,2048]{1,0:T(8,128)(2,1)S(1)}, u32[]{:S(2)}, u32[]{:S(2)}) collective-permute-start(bf16[96,2048]{1,0:T(8,128)(2,1)S(1)} %get-tuple-element.46), channel_id=1, source_target_pairs={{0,1},{1,0},{2,3},{3,2},{4,5},{5,4},{6,7},{7,6},{8,9},{9,8},{10,11... | collective-permute-start | bytes 1179656 | tf_op jit(solution)/shard_map/ppermute | solution.py:529
  33.9 7.0 %collective-permute-start.12 = (bf16[24,2048]{1,0:T(8,128)(2,1)S(1)}, bf16[24,2048]{1,0:T(8,128)(2,1)S(1)}, u32[]{:S(2)}, u32[]{:S(2)}) collective-permute-start(bf16[24,2048]{1,0:T(8,128)(2,1)S(1)} %get-tuple-element.48), channel_id=1, source_target_pairs={{0,6},{2,0},{4,2},{6,4},{1,7},{3,1},{5,3},{7,5},{8,14},{10,8},{12,... | collective-permute-start | bytes 294920 | tf_op jit(solution)/shard_map/ppermute | solution.py:526
  35.5 7.1 %collective-permute-start.13 = (bf16[24,2048]{1,0:T(8,128)(2,1)S(1)}, bf16[24,2048]{1,0:T(8,128)(2,1)S(1)}, u32[]{:S(2)}, u32[]{:S(2)}) collective-permute-start(bf16[24,2048]{1,0:T(8,128)(2,1)S(1)} %get-tuple-element.49), channel_id=1, source_target_pairs={{0,4},{2,6},{4,0},{6,2},{1,5},{3,7},{5,1},{7,3},{8,12},{10,14},{12... | collective-permute-start | bytes 294920 | tf_op jit(solution)/shard_map/ppermute | solution.py:526
  36.4 7.3 %collective-permute-start.14 = (bf16[24,2048]{1,0:T(8,128)(2,1)S(1)}, bf16[24,2048]{1,0:T(8,128)(2,1)S(1)}, u32[]{:S(2)}, u32[]{:S(2)}) collective-permute-start(bf16[24,2048]{1,0:T(8,128)(2,1)S(1)} %get-tuple-element.50), channel_id=1, source_target_pairs={{0,2},{2,4},{4,6},{6,0},{1,3},{3,5},{5,7},{7,1},{8,10},{10,12},{12... | collective-permute-start | bytes 294920 | tf_op jit(solution)/shard_map/ppermute | solution.py:526
  37.6 40.4 %copy-start.6 = (bf16[2048,64]{0,1:T(8,128)(2,1)S(1)}, bf16[2048,64]{0,1:T(8,128)(2,1)}, u32[]{:S(2)}) copy-start(bf16[2048,64]{0,1:T(8,128)(2,1)} %param.22) | copy-start | bytes 786436
  43.7 34.3 %collective-permute-start.15 = (bf16[3072,1024]{1,0:T(8,128)(2,1)S(1)}, bf16[3072,1024]{1,0:T(8,128)(2,1)S(1)}, u32[]{:S(2)}, u32[]{:S(2)}) collective-permute-start(bf16[3072,1024]{1,0:T(8,128)(2,1)S(1)} %get-tuple-element.58.weights_ref), channel_id=1, source_target_pairs={{0,1},{1,0},{2,3},{3,2},{4,5},{5,4},{6,7},{7,6},{8,9},{9,8},{10,11... | collective-permute-start | bytes 18874376 | tf_op jit(solution)/shard_map/ppermute | solution.py:529

commit v6 on v5

--- a/solution.py
+++ b/solution.py
@@ -55,30 +55,51 @@
     return jax.ShapeDtypeStruct(shape, dtype)
 
 
+def homes(count, other):
+    z, core = lax.axis_index("z"), lax.axis_index("core")
+    core = 1 - core if other else core
+    return [lax.rem(z + count - i, count) * CORES + core for i in range(count)]
+
+
 def normed_rows(values, gain):
     inverse = lax.rsqrt(jnp.mean(values * values, axis=-1, keepdims=True) + EPSILON)
     return (values * inverse * gain).astype(BF16)
 
 
 def query_kernel(x_hbm, g_hbm, w_hbm, q_ref, x_ref, g_ref, w_ref, sems):
-    x_copy = pltpu.make_async_copy(x_hbm, x_ref, sems.at[0])
-    w_copy = pltpu.make_async_copy(w_hbm.at[0], w_ref, sems.at[1])
-    g_copy = pltpu.make_async_copy(g_hbm, g_ref, sems.at[2])
-    x_copy.start()
+    half = x_ref.shape[0] // 2
+    rows = [slice(0, half), slice(half, 2 * half)]
+    g_copy = pltpu.make_async_copy(g_hbm, g_ref, sems.at[0])
+    x_copies = [
+        pltpu.make_async_copy(x_hbm.at[rows[i]], x_ref.at[rows[i]], sems.at[1 + i])
+        for i in range(2)
+    ]
+    w_copy = pltpu.make_async_copy(w_hbm.at[0], w_ref, sems.at[3])
     g_copy.start()
+    for copy in x_copies:
+        copy.start()
     w_copy.start()
     g_copy.wait()
-    x_copy.wait()
-    normed = normed_rows(x_ref[...].astype(F32), g_ref[...].astype(F32).reshape(1, -1))
+    gain = g_ref[...].astype(F32).reshape(1, -1)
+    normed = []
+    for copy, cut in zip(x_copies, rows):
+        copy.wait()
+        normed.append(normed_rows(x_ref[cut, :].astype(F32), gain))
     w_copy.wait()
-    q_ref[...] = dot(normed, w_ref[...]).astype(BF16)
-
-
-def load_kernel(k_hbm, after_ref, k_ref, sem):
+    for values, cut in zip(normed, rows):
+        q_ref[cut, :] = dot(values, w_ref[...]).astype(BF16)
+
+
+def load_kernel(k_hbm, v_hbm, after_ref, k_ref, v_ref, sems):
     del after_ref
-    k_copy = pltpu.make_async_copy(k_hbm, k_ref, sem)
-    k_copy.start()
-    k_copy.wait()
+    copies = [
+        pltpu.make_async_copy(k_hbm, k_ref, sems.at[0]),
+        pltpu.make_async_copy(v_hbm, v_ref, sems.at[1]),
+    ]
+    for copy in copies:
+        copy.start()
+    for copy in copies:
+        copy.wait()
 
 
 def tree_kernel(scale, x_ref, g_ref, w_hbm, q_ref, up_ref, after_ref, *refs):
@@ -123,34 +144,25 @@
     lse_ref[...] = jnp.transpose(turn[...])[0:8, :]
 
 
-def page_kernel(scale, tree, kept, meta_ref, *refs):
+def page_kernel(scale, tree, kept, lengths_ref, *refs):
     pieces, (k_ref, v_ref) = refs[:4], refs[4:6]
-    outs = refs[7:-2] if kept else refs[6:-3]
-    s_all, p_all = refs[-2:] if kept else refs[-3:-1]
+    outs = refs[7:-2] if kept else refs[6:-2]
+    s_all, p_all = refs[-2:]
     out_ref = outs[0]
-    if not kept:
-        v_hbm, v_ref, sems = v_ref, outs[1], refs[-1]
-        loads = [
-            pltpu.make_async_copy(v_hbm.at[r], v_ref.at[r], sems.at[r])
-            for r in range(v_hbm.shape[0])
-        ]
-        for load in loads:
-            load.start()
     requests, page = k_ref.shape[0], k_ref.shape[1]
     width = pieces[0].shape[1]
     pair = 2 * tree
     lane = iota((tree, 128), 1)
     wide = iota((tree, width), 1) < HEAD_DIM
-    first_at = 8 if kept else 12
+    owners = homes(len(pieces), not kept)
+    start = (lax.axis_index("z") * CORES + lax.axis_index("core")) * page
 
     def columns(i):
-        return pl.ds(pl.multiple_of(meta_ref[first_at + i], width), width)
+        return pl.ds(pl.multiple_of(owners[i] * width, width), width)
 
     for r in range(requests):
         rows = slice(r * tree, (r + 1) * tree)
-        live = meta_ref[r]
-        if not kept:
-            loads[r].wait()
+        live = lengths_ref[r] - start
 
         @pl.when(live > 0)
         def _():
@@ -228,7 +240,7 @@
         out_ref[tokens:, :] = turned[i * 8 : (i + 1) * 8, :].astype(BF16)
 
 
-def out_kernel(meta_ref, *refs):
+def out_kernel(*refs):
     parts = refs[:4]
     tree_o_ref, tree_lse_ref, w_ref, theirs_ref, ours_ref, turn, mixed = refs[4:]
     padded, width = parts[0].shape
@@ -255,14 +267,15 @@
             total = total + turned[:, at : at + 1] * part[0:tokens, cut].astype(F32)
         mixed[:, cut] = total
 
-    def rows_of(first_at):
+    def rows_of(other):
         rows = [
-            mixed[pl.ds(pl.multiple_of(meta_ref[first_at + i], 8), own), :] for i in range(4)
+            mixed[pl.ds(pl.multiple_of(owner * own, 8), own), :]
+            for owner in homes(len(parts), other)
         ]
         return jnp.concatenate(rows, axis=0).astype(BF16)
 
-    theirs_ref[...] = dot(rows_of(20), w_ref[...]).astype(BF16)
-    ours_ref[...] = dot(rows_of(16), w_ref[...])
+    theirs_ref[...] = dot(rows_of(True), w_ref[...]).astype(BF16)
+    ours_ref[...] = dot(rows_of(False), w_ref[...])
 
 
 def fold_kernel(ours_ref, theirs_ref, *outs):
@@ -338,13 +351,13 @@
         place_ref[j] = jnp.where(hit, 1.0, 0.0).astype(BF16)
 
 
-def residual_kernel(meta_ref, *refs):
+def residual_kernel(*refs):
     parts = refs[:4]
     x_ref, g_ref, place_ref, res_ref, normed_ref, out_ref = refs[4:]
     tokens, width = parts[0].shape
     chunks = place_ref.shape[0]
     cut = width // (chunks + 1)
-    start = pl.multiple_of(meta_ref[16], 8)
+    start = pl.multiple_of(homes(len(parts), False)[0] * tokens, 8)
     residual = x_ref[pl.ds(start, tokens), :].astype(F32)
     for part in parts:
         residual = residual + part[...].astype(F32)
@@ -486,9 +499,6 @@
 ):
     z_count = lax.axis_size("z")
     exp_count = z_count * CORES
-    z_index = lax.axis_index("z")
-    core = lax.axis_index("core")
-    exp_index = z_index * CORES + core
     tokens, width = hidden.shape
     requests, tree = parents.shape
     page = cache_keys.shape[1]
@@ -512,7 +522,7 @@
             pltpu.VMEM((tokens, width), BF16),
             pltpu.VMEM((width,), BF16),
             pltpu.VMEM((width, local_width), BF16),
-            pltpu.SemaphoreType.DMA((3,)),
+            pltpu.SemaphoreType.DMA((4,)),
         ],
         flops=2 * tokens * width * local_width,
         bytes_accessed=2 * width * (tokens + local_width),
@@ -530,40 +540,31 @@
 
     steps = range(1, z_count)
     pieces = [query] + [over_z(query, step) for step in steps]
+    keys, values = call(
+        load_kernel,
+        (sds(cache_keys.shape, BF16), sds(cache_values.shape, BF16)),
+        [HBM, HBM, pl.ANY],
+        [pltpu.SemaphoreType.DMA((2,))],
+        bytes_accessed=4 * requests * page * width,
+        vmem=16 << 20,
+    )(cache_keys, cache_values, query)
+    pieces[1:], keys = lax.optimization_barrier((pieces[1:], keys))
     other_pieces = [over_core(piece) for piece in pieces]
-    homes = jnp.bitwise_and(z_index - jnp.arange(z_count), z_count - 1) * CORES
-    homes = jnp.stack([homes + core, homes + 1 - core])
-    meta = jnp.concatenate(
-        [
-            cache_lengths - exp_index * page,
-            jnp.zeros((8 - requests,), jnp.int32),
-            (homes * local_width).reshape(-1),
-            (homes * own).reshape(-1),
-        ]
-    ).astype(jnp.int32)
-
-    keys = call(
-        load_kernel,
-        sds(cache_keys.shape, BF16),
-        [HBM, pl.ANY],
-        [pltpu.SemaphoreType.DMA],
-        bytes_accessed=2 * requests * page * width,
-    )(cache_keys, query)
 
     scratch = [
         pltpu.VMEM((z_count * 2 * tree, page), F32),
         pltpu.VMEM((z_count * 2 * tree, page), BF16),
     ]
     heads = 2 * z_count
-    for_other, values = call(
+    for_other = call(
         functools.partial(page_kernel, scale, tree, False),
-        (sds((heads + 1, tokens, HEAD_DIM), BF16), sds(cache_values.shape, BF16)),
-        [SMEM] + [VMEM] * 5 + [HBM],
-        scratch + [pltpu.SemaphoreType.DMA((requests,))],
+        sds((heads + 1, tokens, HEAD_DIM), BF16),
+        [SMEM] + [VMEM] * 6,
+        scratch,
         flops=2 * tokens * page * width,
         bytes_accessed=2 * requests * page * width,
         vmem=20 << 20,
-    )(meta, *other_pieces, keys, cache_values)
+    )(cache_lengths, *other_pieces, keys, values)
     from_other = over_core(for_other)
     kept, kept_lse = call(
         functools.partial(page_kernel, scale, tree, True),
@@ -573,7 +574,7 @@
         flops=2 * tokens * page * width,
         bytes_accessed=2 * requests * page * width,
         vmem=20 << 20,
-    )(meta, *pieces, keys, values, for_other)
+    )(cache_lengths, *pieces, keys, values, for_other)
     merged = call(
         merge_kernel,
         tuple(sds((padded, local_width), BF16) for _ in range(z_count)),
@@ -598,11 +599,11 @@
     theirs, ours = call(
         out_kernel,
         (sds((z_count * own, width), BF16), sds((z_count * own, width), F32)),
-        [SMEM] + [VMEM] * 7,
+        [VMEM] * 7,
         [pltpu.VMEM((128, 256), F32), pltpu.VMEM((tokens, local_width), F32)],
         flops=2 * tokens * width * local_width,
         bytes_accessed=2 * width * (tokens + local_width),
-    )(meta, *arrived, tree_o, tree_lse, w_out)
+    )(*arrived, tree_o, tree_lse, w_out)
     folded = call(
         fold_kernel,
         tuple(sds((own, width), BF16 if step else F32) for step in range(z_count)),
@@ -642,10 +643,10 @@
             sds((own, width), BF16),
             sds((experts * SLOTS, packed), BF16),
         ),
-        [SMEM] + [VMEM] * 7,
+        [VMEM] * 7,
         flops=1 << 27,
         bytes_accessed=1 << 22,
-    )(meta, *mixed, hidden, gain_moe, place)
+    )(*mixed, hidden, gain_moe, place)
     rows = lax.all_to_all(
         outgoing.reshape(experts, SLOTS, packed),
         ("req", "z"),

time: 115 us -> 114 us (level)
  transfers between devices with their start and end apart: 16 -> 16, of which waited for: 9 -> 10; matrix products, arithmetic and copies ran while one was open for 1% -> 0% of each run, Pallas kernels for 12% -> 12%
where the time goes in v6:
time: 114 us; the launch traced here: 113 us
  blocking collectives  61.7 us (54%)
  Pallas kernels  28.9 us (25%)
  starting transfers between devices  11.9 us (10%)
  waiting for transfers between devices  10.6 us (9%)
    all_to_all x1, blocking collectives, per_device(): lax.all_to_all(outgoing.reshape(experts, SLOTS, packed), ('req', 'z'), sp...  33.1 us
    all_to_all x1, blocking collectives, per_device(): lax.all_to_all(summed.reshape(experts, SLOTS, packed), ('req', 'z'), spli...  28.6 us
    ppermute x9, starting transfers between devices, over_z(): lax.ppermute(value, 'z', [(i, (i + step) % z_count) for i in range(z_coun...  11.2 us
    ppermute x9, waiting for transfers between devices, over_z(): lax.ppermute(value, 'z', [(i, (i + step) % z_count) for i in range(z_coun...  7.55 us
    pallas_call x1, Pallas kernels, per_device(): call(expert_kernel, (sds((experts * SLOTS, packed), BF16), sds((chunks, 4...  7.35 us
    pallas_call x1, Pallas kernels, per_device(): call(functools.partial(tree_kernel, scale), (sds((tokens, local_width), F...  3.83 us
    pallas_call x1, Pallas kernels, per_device(): call(load_kernel, (sds(cache_keys.shape, BF16), sds(cache_values.shape, B...  3.48 us
    pallas_call x1, Pallas kernels, per_device(): call(table_kernel, (sds((chunks, experts * SLOTS, 2 * own), BF16), sds((1...  3.24 us
  transfers between devices with their start and end apart: 16, of which 10 were waited for; matrix products, arithmetic and copies ran while one was open for 0% of the time, Pallas kernels for 12%

profile of v6, /device:TPU:0, one launch (start us, length us, event | category | flops | bytes accessed | tf_op | source)
XLA Modules:
  0.0 113.3 jit_solution(9310343268465222652)
XLA Ops:
  0.0 2.0 %shard_map.127.after_ref.refs_0_.q_ref = bf16[192,256]{1,0:T(8,128)(2,1)S(1)} custom-call(bf16[192,2048]{1,0:T(8,128)(2,1)} %refs_4_.1, bf16[2048]{0:T(1024)(128)(2,1)} %g_ref.1, bf16[3,2048,256]{2,1,0:T(8,128)(2,1)} %bitcast.16), custom_call_target="tpu_custom_call" | custom-call | flops 201326592 | bytes 1835008 | tf_op jit(solution)/shard_map/pallas_call | solution.py:517
  2.0 0.0 copy-start.6
  2.0 4.2 %collective-permute-start.3 = (bf16[192,256]{1,0:T(8,128)(2,1)S(1)}, bf16[192,256]{1,0:T(8,128)(2,1)S(1)}, u32[]{:S(2)}, u32[]{:S(2)}) collective-permute-start(bf16[192,256]{1,0:T(8,128)(2,1)S(1)} %shard_map.127.after_ref.refs_0_.q_ref), channel_id=1, source_target_pairs={{0,6},{2,0},{4,2},{6,4},{1,7},{3,1},{5,3},{7,5},{8,14},{10,8},{12,... | collective-permute-start | bytes 294920 | tf_op jit(solution)/shard_map/ppermute | solution.py:536
  6.2 1.3 %collective-permute-start.1 = (bf16[192,256]{1,0:T(8,128)(2,1)S(1)}, bf16[192,256]{1,0:T(8,128)(2,1)S(1)}, u32[]{:S(2)}, u32[]{:S(2)}) collective-permute-start(bf16[192,256]{1,0:T(8,128)(2,1)S(1)} %shard_map.127.after_ref.refs_0_.q_ref), channel_id=1, source_target_pairs={{0,2},{2,4},{4,6},{6,0},{1,3},{3,5},{5,7},{7,1},{8,10},{10,12},{12... | collective-permute-start | bytes 294920 | tf_op jit(solution)/shard_map/ppermute | solution.py:536
  7.5 0.0 collective-permute-start
  7.5 3.5 %shard_map.128 = (bf16[4,256,2048]{2,1,0:T(8,128)(2,1)S(1)}, bf16[4,256,2048]{2,1,0:T(8,128)(2,1)S(1)}) custom-call(bf16[4,256,2048]{2,1,0:T(8,128)(2,1)} %k_hbm.1, bf16[4,256,2048]{2,1,0:T(8,128)(2,1)} %v_hbm.1, bf16[192,256]{1,0:T(8,128)(2,1)S(1)} %shard_map.127.after_ref.refs_0_.q_ref), custom_call_target="tpu_custom_call" | custom-call | bytes 8388608 | tf_op jit(solution)/shard_map/pallas_call | solution.py:543
  10.9 0.0 collective-permute-done.3.refs_3_
  11.0 2.1 %collective-permute-done.2.refs_2_ = bf16[192,256]{1,0:T(8,128)(2,1)S(1)} collective-permute-done((bf16[192,256]{1,0:T(8,128)(2,1)S(1)}, bf16[192,256]{1,0:T(8,128)(2,1)S(1)}, u32[]{:S(2)}, u32[]{:S(2)}) %collective-permute-start.2) | collective-permute-done | bytes 98336 | tf_op jit(solution)/shard_map/ppermute | solution.py:536
  13.1 0.7 collective-permute-done.1.refs_1_
  13.8 0.0 collective-permute-start.4
  13.8 0.5 collective-permute-start.5
  14.3 0.0 collective-permute-start.6
  14.3 0.0 collective-permute-done.refs_0_
  14.3 0.8 collective-permute-done.4.refs_1_
  15.1 0.2 collective-permute-done.5.refs_2_
  15.2 0.4 collective-permute-done.6.refs_3_
  15.6 2.8 %shard_map.129.refs_6_ = bf16[9,192,128]{2,1,0:T(8,128)(2,1)S(1)} custom-call(s32[4]{0:T(128)S(1)} %copy-done.6, bf16[192,256]{1,0:T(8,128)(2,1)S(1)} %collective-permute-done.refs_0_, bf16[192,256]{1,0:T(8,128)(2,1)S(1)} %collective-permute-done.4.refs_1_, bf16[192,256]{1,0:T(8,128)(2,1)S(1)} %collective-permute-done.5.refs_2_, ...), custom_call_target="tpu_custom_call" | custom-call | flops 201326592 | bytes 4194304 | tf_op jit(solution)/shard_map/pallas_call | solution.py:559
  18.4 0.0 copy-start
  18.4 0.0 copy-start.2
  18.4 0.0 copy-start.5
  18.4 0.1 collective-permute-start.7
  18.5 2.7 %shard_map.130 = (f32[8,192,128]{2,1,0:T(8,128)S(1)}, f32[192,128]{1,0:T(8,128)S(1)}) custom-call(s32[4]{0:T(128)S(1)} %copy-done.6, bf16[192,256]{1,0:T(8,128)(2,1)S(1)} %shard_map.127.after_ref.refs_0_.q_ref, bf16[192,256]{1,0:T(8,128)(2,1)S(1)} %collective-permute-done.1.refs_1_, bf16[192,256]{1,0:T(8,128)(2,1)S(1)} %collective-permute-done.2.refs_2_, ...), custom_call_target="tpu_custom_call" | custom-call | flops 201326592 | bytes 4194304 | tf_op jit(solution)/shard_map/pallas_call | solution.py:569
  21.2 0.0 copy-start.1
  21.2 0.0 copy-start.4
  21.3 0.7 shard_map.131
  22.0 0.1 collective-permute-start.8
  22.1 0.1 collective-permute-start.9
  22.2 1.9 %collective-permute-start.10 = (bf16[200,256]{1,0:T(8,128)(2,1)S(1)}, bf16[200,256]{1,0:T(8,128)(2,1)S(1)}, u32[]{:S(2)}, u32[]{:S(2)}) collective-permute-start(bf16[200,256]{1,0:T(8,128)(2,1)S(1)} %get-tuple-element.50), channel_id=1, source_target_pairs={{0,2},{2,4},{4,6},{6,0},{1,3},{3,5},{5,7},{7,1},{8,10},{10,12},{12... | collective-permute-start | bytes 307208 | tf_op jit(solution)/shard_map/ppermute | solution.py:536
  24.1 3.8 %shard_map.132 = (f32[192,256]{1,0:T(8,128)S(1)}, f32[8,256]{1,0:T(8,128)S(1)}) custom-call(bf16[192,2048]{1,0:T(8,128)(2,1)S(1)} %copy-done, bf16[2048]{0:T(1024)(128)(2,1)S(1)} %copy-done.2, bf16[3,2048,256]{2,1,0:T(8,128)(2,1)} %bitcast.17, bf16[192,256]{1,0:T(8,128)(2,1)S(1)} %shard_map.127.after_ref.refs_0_.q_ref, s32[4,48]{1,0:T(4,128)S(1)} %copy-done.5, ...), custom_call_target="tpu_custom_call" | custom-call | flops 402653184 | bytes 2883584 | tf_op jit(solution)/shard_map/pallas_call | solution.py:587
  27.9 0.0 collective-permute-done.8.refs_1_
  27.9 1.3 %collective-permute-done.9.refs_2_ = bf16[200,256]{1,0:T(8,128)(2,1)S(1)} collective-permute-done((bf16[200,256]{1,0:T(8,128)(2,1)S(1)}, bf16[200,256]{1,0:T(8,128)(2,1)S(1)}, u32[]{:S(2)}, u32[]{:S(2)}) %collective-permute-start.9) | collective-permute-done | bytes 102432 | tf_op jit(solution)/shard_map/ppermute | solution.py:536
  29.3 0.6 collective-permute-done.10.refs_3_
  29.9 0.9 shard_map.133
  30.8 0.0 copy-start.3
  30.8 0.1 collective-permute-start.11
  30.9 1.7 %collective-permute-done.11.theirs_ref = bf16[96,2048]{1,0:T(8,128)(2,1)S(1)} collective-permute-done((bf16[96,2048]{1,0:T(8,128)(2,1)S(1)}, bf16[96,2048]{1,0:T(8,128)(2,1)S(1)}, u32[]{:S(2)}, u32[]{:S(2)}) %collective-permute-start.11) | collective-permute-done | bytes 393248 | tf_op jit(solution)/shard_map/ppermute | solution.py:539
  32.6 0.1 shard_map.134
  32.7 1.6 %collective-permute-start.12 = (bf16[24,2048]{1,0:T(8,128)(2,1)S(1)}, bf16[24,2048]{1,0:T(8,128)(2,1)S(1)}, u32[]{:S(2)}, u32[]{:S(2)}) collective-permute-start(bf16[24,2048]{1,0:T(8,128)(2,1)S(1)} %get-tuple-element.56), channel_id=1, source_target_pairs={{0,6},{2,0},{4,2},{6,4},{1,7},{3,1},{5,3},{7,5},{8,14},{10,8},{12,... | collective-permute-start | bytes 294920 | tf_op jit(solution)/shard_map/ppermute | solution.py:536
  34.3 0.9 collective-permute-start.13
  35.2 1.2 %collective-permute-start.14 = (bf16[24,2048]{1,0:T(8,128)(2,1)S(1)}, bf16[24,2048]{1,0:T(8,128)(2,1)S(1)}, u32[]{:S(2)}, u32[]{:S(2)}) collective-permute-start(bf16[24,2048]{1,0:T(8,128)(2,1)S(1)} %get-tuple-element.58), channel_id=1, source_target_pairs={{0,2},{2,4},{4,6},{6,0},{1,3},{3,5},{5,7},{7,1},{8,10},{10,12},{12... | collective-permute-start | bytes 294920 | tf_op jit(solution)/shard_map/ppermute | solution.py:536
  36.4 3.2 %shard_map.135 = (bf16[3,512,48]{2,1,0:T(8,128)(2,1)S(1)}, bf16[4,192,256]{2,1,0:T(8,128)(2,1)S(1)}, bf16[3,256,384]{2,1,0:T(8,128)(2,1)S(1)}, bf16[3072,1024]{1,0:T(8,128)(2,1)S(1)}) custom-call(s32[8,24]{1,0:T(8,128)S(1)} %bitcast.13, bf16[2048,1024]{1,0:T(8,128)(2,1)} %bitcast.18, bf16[512,2048]{1,0:T(8,128)(2,1)} %bitcast.19, ...), custom_call_target="tpu_custom_call" | custom-call | flops 16777216 | bytes 8388608 | tf_op jit(solution)/shard_map/pallas_call | solution.py:617
  39.7 1.7 %collective-permute-done.13.refs_2_ = bf16[24,2048]{1,0:T(8,128)(2,1)S(1)} collective-permute-done((bf16[24,2048]{1,0:T(8,128)(2,1)S(1)}, bf16[24,2048]{1,0:T(8,128)(2,1)S(1)}, u32[]{:S(2)}, u32[]{:S(2)}) %collective-permute-start.13) | collective-permute-done | bytes 98336 | tf_op jit(solution)/shard_map/ppermute | solution.py:536
  41.4 1.0 collective-permute-done.14.refs_3_
  42.5 0.7 shard_map.136
  43.2 33.1 %all_to_all.10 = bf16[64,8,1536]{2,1,0:T(8,128)(2,1)S(1)} all-to-all(bf16[64,8,1536]{2,1,0:T(8,128)(2,1)S(1)} %bitcast.11), channel_id=1, replica_groups=mesh['req'=16,'z'=4,'core'=2] {'req','z'}, dimensions={0} | all-to-all | bytes 3145728 | tf_op jit(solution)/shard_map/all_to_all | solution.py:650
  76.3 7.3 %shard_map.137 = (bf16[512,1536]{1,0:T(8,128)(2,1)S(1)}, bf16[3,96,512]{2,1,0:T(8,128)(2,1)S(1)}) custom-call(bf16[512,1536]{1,0:T(8,128)(2,1)S(1)} %bitcast.10, bf16[3072,1024]{1,0:T(8,128)(2,1)S(1)} %get-tuple-element.66.weights_ref, bf16[3072,1024]{1,0:T(8,128)(2,1)S(1)} %collective-permute-done.15.other_ref, ...), custom_call_target="tpu_custom_call" | custom-call | flops 4831838208 | bytes 12582912 | tf_op jit(solution)/shard_map/pallas_call | solution.py:658
  83.6 28.6 %all_to_all.11 = bf16[64,8,1536]{2,1,0:T(8,128)(2,1)S(1)} all-to-all(bf16[64,8,1536]{2,1,0:T(8,128)(2,1)S(1)} %bitcast.12), channel_id=1, replica_groups=mesh['req'=16,'z'=4,'core'=2] {'req','z'}, dimensions={0} | all-to-all | bytes 3145728 | tf_op jit(solution)/shard_map/all_to_all | solution.py:678
  112.3 1.0 shard_map.138
  (14 shorter events, 0.0 us)
Async XLA Ops:
  2.0 13.6 %copy-start.6 = (s32[4]{0:T(128)S(1)}, s32[4]{0:T(128)}, u32[]{:S(2)}) copy-start(s32[4]{0:T(128)} %lengths_ref.3) | copy-start | bytes 52
  2.0 8.9 %collective-permute-start.3 = (bf16[192,256]{1,0:T(8,128)(2,1)S(1)}, bf16[192,256]{1,0:T(8,128)(2,1)S(1)}, u32[]{:S(2)}, u32[]{:S(2)}) collective-permute-start(bf16[192,256]{1,0:T(8,128)(2,1)S(1)} %shard_map.127.after_ref.refs_0_.q_ref), channel_id=1, source_target_pairs={{0,6},{2,0},{4,2},{6,4},{1,7},{3,1},{5,3},{7,5},{8,14},{10,8},{12,... | collective-permute-start | bytes 294920 | tf_op jit(solution)/shard_map/ppermute | solution.py:536
  6.2 6.9 %collective-permute-start.2 = (bf16[192,256]{1,0:T(8,128)(2,1)S(1)}, bf16[192,256]{1,0:T(8,128)(2,1)S(1)}, u32[]{:S(2)}, u32[]{:S(2)}) collective-permute-start(bf16[192,256]{1,0:T(8,128)(2,1)S(1)} %shard_map.127.after_ref.refs_0_.q_ref), channel_id=1, source_target_pairs={{0,4},{2,6},{4,0},{6,2},{1,5},{3,7},{5,1},{7,3},{8,12},{10,14},{12... | collective-permute-start | bytes 294920 | tf_op jit(solution)/shard_map/ppermute | solution.py:536
  6.2 7.6 %collective-permute-start.1 = (bf16[192,256]{1,0:T(8,128)(2,1)S(1)}, bf16[192,256]{1,0:T(8,128)(2,1)S(1)}, u32[]{:S(2)}, u32[]{:S(2)}) collective-permute-start(bf16[192,256]{1,0:T(8,128)(2,1)S(1)} %shard_map.127.after_ref.refs_0_.q_ref), channel_id=1, source_target_pairs={{0,2},{2,4},{4,6},{6,0},{1,3},{3,5},{5,7},{7,1},{8,10},{10,12},{12... | collective-permute-start | bytes 294920 | tf_op jit(solution)/shard_map/ppermute | solution.py:536
  7.5 6.8 %collective-permute-start = (bf16[192,256]{1,0:T(8,128)(2,1)S(1)}, bf16[192,256]{1,0:T(8,128)(2,1)S(1)}, u32[]{:S(2)}, u32[]{:S(2)}) collective-permute-start(bf16[192,256]{1,0:T(8,128)(2,1)S(1)} %shard_map.127.after_ref.refs_0_.q_ref), channel_id=1, source_target_pairs={{0,1},{1,0},{2,3},{3,2},{4,5},{5,4},{6,7},{7,6},{8,9},{9,8},{10,11... | collective-permute-start | bytes 294920 | tf_op jit(solution)/shard_map/ppermute | solution.py:539
  13.8 1.3 %collective-permute-start.4 = (bf16[192,256]{1,0:T(8,128)(2,1)S(1)}, bf16[192,256]{1,0:T(8,128)(2,1)S(1)}, u32[]{:S(2)}, u32[]{:S(2)}) collective-permute-start(bf16[192,256]{1,0:T(8,128)(2,1)S(1)} %collective-permute-done.1.refs_1_), channel_id=1, source_target_pairs={{0,1},{1,0},{2,3},{3,2},{4,5},{5,4},{6,7},{7,6},{8,9},{9,8},{10,11... | collective-permute-start | bytes 294920 | tf_op jit(solution)/shard_map/ppermute | solution.py:539
  13.8 1.5 %collective-permute-start.5 = (bf16[192,256]{1,0:T(8,128)(2,1)S(1)}, bf16[192,256]{1,0:T(8,128)(2,1)S(1)}, u32[]{:S(2)}, u32[]{:S(2)}) collective-permute-start(bf16[192,256]{1,0:T(8,128)(2,1)S(1)} %collective-permute-done.2.refs_2_), channel_id=1, source_target_pairs={{0,1},{1,0},{2,3},{3,2},{4,5},{5,4},{6,7},{7,6},{8,9},{9,8},{10,11... | collective-permute-start | bytes 294920 | tf_op jit(solution)/shard_map/ppermute | solution.py:539
  14.3 1.3 %collective-permute-start.6 = (bf16[192,256]{1,0:T(8,128)(2,1)S(1)}, bf16[192,256]{1,0:T(8,128)(2,1)S(1)}, u32[]{:S(2)}, u32[]{:S(2)}) collective-permute-start(bf16[192,256]{1,0:T(8,128)(2,1)S(1)} %collective-permute-done.3.refs_3_), channel_id=1, source_target_pairs={{0,1},{1,0},{2,3},{3,2},{4,5},{5,4},{6,7},{7,6},{8,9},{9,8},{10,11... | collective-permute-start | bytes 294920 | tf_op jit(solution)/shard_map/ppermute | solution.py:539
  18.4 5.7 %copy-start = (bf16[192,2048]{1,0:T(8,128)(2,1)S(1)}, bf16[192,2048]{1,0:T(8,128)(2,1)}, u32[]{:S(2)}) copy-start(bf16[192,2048]{1,0:T(8,128)(2,1)} %refs_4_.1) | copy-start | bytes 2359300
  18.4 5.7 %copy-start.2 = (bf16[2048]{0:T(1024)(128)(2,1)S(1)}, bf16[2048]{0:T(1024)(128)(2,1)}, u32[]{:S(2)}) copy-start(bf16[2048]{0:T(1024)(128)(2,1)} %g_ref.1) | copy-start | bytes 12292
  18.4 5.7 %copy-start.5 = (s32[4,48]{1,0:T(4,128)S(1)}, s32[4,48]{1,0:T(4,128)}, u32[]{:S(2)}) copy-start(s32[4,48]{1,0:T(4,128)} %up_ref.1) | copy-start | bytes 2308
  18.4 2.9 %collective-permute-start.7 = (bf16[9,192,128]{2,1,0:T(8,128)(2,1)S(1)}, bf16[9,192,128]{2,1,0:T(8,128)(2,1)S(1)}, u32[]{:S(2)}, u32[]{:S(2)}) collective-permute-start(bf16[9,192,128]{2,1,0:T(8,128)(2,1)S(1)} %shard_map.129.refs_6_), channel_id=1, source_target_pairs={{0,1},{1,0},{2,3},{3,2},{4,5},{5,4},{6,7},{7,6},{8,9},{9,8},{10,11... | collective-permute-start | bytes 1327112 | tf_op jit(solution)/shard_map/ppermute | solution.py:539
  21.2 8.6 %copy-start.1 = (bf16[256,2048]{1,0:T(8,128)(2,1)S(1)}, bf16[256,2048]{1,0:T(8,128)(2,1)}, u32[]{:S(2)}) copy-start(bf16[256,2048]{1,0:T(8,128)(2,1)} %refs_6_.1) | copy-start | bytes 3145732
  21.2 15.2 %copy-start.4 = (s32[24,8]{0,1:T(8,128)S(1)}, s32[24,8]{0,1:T(8,128)}, u32[]{:S(2)}) copy-start(s32[24,8]{0,1:T(8,128)} %param.23) | copy-start | bytes 2308
  22.0 5.9 %collective-permute-start.8 = (bf16[200,256]{1,0:T(8,128)(2,1)S(1)}, bf16[200,256]{1,0:T(8,128)(2,1)S(1)}, u32[]{:S(2)}, u32[]{:S(2)}) collective-permute-start(bf16[200,256]{1,0:T(8,128)(2,1)S(1)} %get-tuple-element.48), channel_id=1, source_target_pairs={{0,6},{2,0},{4,2},{6,4},{1,7},{3,1},{5,3},{7,5},{8,14},{10,8},{12,... | collective-permute-start | bytes 307208 | tf_op jit(solution)/shard_map/ppermute | solution.py:536
  22.1 7.2 %collective-permute-start.9 = (bf16[200,256]{1,0:T(8,128)(2,1)S(1)}, bf16[200,256]{1,0:T(8,128)(2,1)S(1)}, u32[]{:S(2)}, u32[]{:S(2)}) collective-permute-start(bf16[200,256]{1,0:T(8,128)(2,1)S(1)} %get-tuple-element.49), channel_id=1, source_target_pairs={{0,4},{2,6},{4,0},{6,2},{1,5},{3,7},{5,1},{7,3},{8,12},{10,14},{12... | collective-permute-start | bytes 307208 | tf_op jit(solution)/shard_map/ppermute | solution.py:536
  22.2 7.7 %collective-permute-start.10 = (bf16[200,256]{1,0:T(8,128)(2,1)S(1)}, bf16[200,256]{1,0:T(8,128)(2,1)S(1)}, u32[]{:S(2)}, u32[]{:S(2)}) collective-permute-start(bf16[200,256]{1,0:T(8,128)(2,1)S(1)} %get-tuple-element.50), channel_id=1, source_target_pairs={{0,2},{2,4},{4,6},{6,0},{1,3},{3,5},{5,7},{7,1},{8,10},{10,12},{12... | collective-permute-start | bytes 307208 | tf_op jit(solution)/shard_map/ppermute | solution.py:536
  30.8 11.7 %copy-start.3 = (bf16[2048]{0:T(1024)(128)(2,1)S(1)}, bf16[2048]{0:T(1024)(128)(2,1)}, u32[]{:S(2)}) copy-start(bf16[2048]{0:T(1024)(128)(2,1)} %refs_5_.1) | copy-start | bytes 12292
  30.8 1.8 %collective-permute-start.11 = (bf16[96,2048]{1,0:T(8,128)(2,1)S(1)}, bf16[96,2048]{1,0:T(8,128)(2,1)S(1)}, u32[]{:S(2)}, u32[]{:S(2)}) collective-permute-start(bf16[96,2048]{1,0:T(8,128)(2,1)S(1)} %get-tuple-element.54), channel_id=1, source_target_pairs={{0,1},{1,0},{2,3},{3,2},{4,5},{5,4},{6,7},{7,6},{8,9},{9,8},{10,11... | collective-permute-start | bytes 1179656 | tf_op jit(solution)/shard_map/ppermute | solution.py:539
  32.7 7.0 %collective-permute-start.12 = (bf16[24,2048]{1,0:T(8,128)(2,1)S(1)}, bf16[24,2048]{1,0:T(8,128)(2,1)S(1)}, u32[]{:S(2)}, u32[]{:S(2)}) collective-permute-start(bf16[24,2048]{1,0:T(8,128)(2,1)S(1)} %get-tuple-element.56), channel_id=1, source_target_pairs={{0,6},{2,0},{4,2},{6,4},{1,7},{3,1},{5,3},{7,5},{8,14},{10,8},{12,... | collective-permute-start | bytes 294920 | tf_op jit(solution)/shard_map/ppermute | solution.py:536
  34.3 7.1 %collective-permute-start.13 = (bf16[24,2048]{1,0:T(8,128)(2,1)S(1)}, bf16[24,2048]{1,0:T(8,128)(2,1)S(1)}, u32[]{:S(2)}, u32[]{:S(2)}) collective-permute-start(bf16[24,2048]{1,0:T(8,128)(2,1)S(1)} %get-tuple-element.57), channel_id=1, source_target_pairs={{0,4},{2,6},{4,0},{6,2},{1,5},{3,7},{5,1},{7,3},{8,12},{10,14},{12... | collective-permute-start | bytes 294920 | tf_op jit(solution)/shard_map/ppermute | solution.py:536
  35.2 7.3 %collective-permute-start.14 = (bf16[24,2048]{1,0:T(8,128)(2,1)S(1)}, bf16[24,2048]{1,0:T(8,128)(2,1)S(1)}, u32[]{:S(2)}, u32[]{:S(2)}) collective-permute-start(bf16[24,2048]{1,0:T(8,128)(2,1)S(1)} %get-tuple-element.58), channel_id=1, source_target_pairs={{0,2},{2,4},{4,6},{6,0},{1,3},{3,5},{5,7},{7,1},{8,10},{10,12},{12... | collective-permute-start | bytes 294920 | tf_op jit(solution)/shard_map/ppermute | solution.py:536
  36.4 39.9 %copy-start.7 = (bf16[2048,64]{0,1:T(8,128)(2,1)S(1)}, bf16[2048,64]{0,1:T(8,128)(2,1)}, u32[]{:S(2)}) copy-start(bf16[2048,64]{0,1:T(8,128)(2,1)} %param.22) | copy-start | bytes 786436
  42.5 33.8 %collective-permute-start.15 = (bf16[3072,1024]{1,0:T(8,128)(2,1)S(1)}, bf16[3072,1024]{1,0:T(8,128)(2,1)S(1)}, u32[]{:S(2)}, u32[]{:S(2)}) collective-permute-start(bf16[3072,1024]{1,0:T(8,128)(2,1)S(1)} %get-tuple-element.66.weights_ref), channel_id=1, source_target_pairs={{0,1},{1,0},{2,3},{3,2},{4,5},{5,4},{6,7},{7,6},{8,9},{9,8},{10,11... | collective-permute-start | bytes 18874376 | tf_op jit(solution)/shard_map/ppermute | solution.py:539

commit v7 on v6

--- a/solution.py
+++ b/solution.py
@@ -67,27 +67,17 @@
 
 
 def query_kernel(x_hbm, g_hbm, w_hbm, q_ref, x_ref, g_ref, w_ref, sems):
-    half = x_ref.shape[0] // 2
-    rows = [slice(0, half), slice(half, 2 * half)]
-    g_copy = pltpu.make_async_copy(g_hbm, g_ref, sems.at[0])
-    x_copies = [
-        pltpu.make_async_copy(x_hbm.at[rows[i]], x_ref.at[rows[i]], sems.at[1 + i])
-        for i in range(2)
-    ]
-    w_copy = pltpu.make_async_copy(w_hbm.at[0], w_ref, sems.at[3])
+    x_copy = pltpu.make_async_copy(x_hbm, x_ref, sems.at[0])
+    w_copy = pltpu.make_async_copy(w_hbm.at[0], w_ref, sems.at[1])
+    g_copy = pltpu.make_async_copy(g_hbm, g_ref, sems.at[2])
+    x_copy.start()
     g_copy.start()
-    for copy in x_copies:
-        copy.start()
     w_copy.start()
     g_copy.wait()
-    gain = g_ref[...].astype(F32).reshape(1, -1)
-    normed = []
-    for copy, cut in zip(x_copies, rows):
-        copy.wait()
-        normed.append(normed_rows(x_ref[cut, :].astype(F32), gain))
+    x_copy.wait()
+    normed = normed_rows(x_ref[...].astype(F32), g_ref[...].astype(F32).reshape(1, -1))
     w_copy.wait()
-    for values, cut in zip(normed, rows):
-        q_ref[cut, :] = dot(values, w_ref[...]).astype(BF16)
+    q_ref[...] = dot(normed, w_ref[...]).astype(BF16)
 
 
 def load_kernel(k_hbm, v_hbm, after_ref, k_ref, v_ref, sems):
@@ -156,61 +146,50 @@
     wide = iota((tree, width), 1) < HEAD_DIM
     owners = homes(len(pieces), not kept)
     start = (lax.axis_index("z") * CORES + lax.axis_index("core")) * page
+    lives = lengths_ref[...] - start
 
     def columns(i):
         return pl.ds(pl.multiple_of(owners[i] * width, width), width)
 
     for r in range(requests):
         rows = slice(r * tree, (r + 1) * tree)
-        live = lengths_ref[r] - start
-
-        @pl.when(live > 0)
-        def _():
-            for i, piece in enumerate(pieces):
-                query = piece[rows, :]
-                zero = jnp.zeros_like(query)
-                both = jnp.concatenate(
-                    [jnp.where(wide, query, zero), jnp.where(wide, zero, query)], axis=0
-                )
-                s_all[i * pair : (i + 1) * pair, :] = dot_t(both, k_ref[r, :, columns(i)])
-            scores = s_all[...] * scale
-            scores = jnp.where(iota(scores.shape, 1) < live, scores, NEGATIVE)
-            high = jnp.max(scores, axis=-1, keepdims=True)
-            weights = jnp.exp(scores - high)
-            total = jnp.sum(weights, axis=-1, keepdims=True)
-            p_all[...] = weights.astype(BF16)
-            inverse = 1.0 / total
-            lse = high + jnp.log(total)
-            first = lse.astype(BF16).astype(F32)
-            second = (lse - first).astype(BF16).astype(F32)
-            third = lse - first - second
-            stats = jnp.zeros((tree, 128), F32)
-            for i in range(len(pieces)):
-                summed = dot(p_all[i * pair : (i + 1) * pair, :], v_ref[r, :, columns(i)])
-                for h in range(2):
-                    own = slice(i * pair + h * tree, i * pair + (h + 1) * tree)
-                    cut = slice(h * HEAD_DIM, (h + 1) * HEAD_DIM)
-                    value = summed[h * tree : (h + 1) * tree, cut] * inverse[own]
-                    out_ref[2 * i + h, rows, :] = value.astype(out_ref.dtype)
-                    if kept:
-                        stats = jnp.where(lane == i * 8 + h, lse[own], stats)
-                    else:
-                        for j, part in enumerate((first, second, third)):
-                            stats = jnp.where(lane == i * 8 + 2 * j + h, part[own], stats)
-            if kept:
-                outs[1][rows, :] = stats
-            else:
-                out_ref[8, rows, :] = stats.astype(BF16)
-
-        @pl.when(live <= 0)
-        def _():
-            for i in range(8):
-                out_ref[i, rows, :] = jnp.zeros((tree, HEAD_DIM), out_ref.dtype)
-            empty = jnp.where(lane % 8 < 2, NEGATIVE, 0.0)
-            if kept:
-                outs[1][rows, :] = empty
-            else:
-                out_ref[8, rows, :] = empty.astype(BF16)
+        for i, piece in enumerate(pieces):
+            query = piece[rows, :]
+            zero = jnp.zeros_like(query)
+            both = jnp.concatenate(
+                [jnp.where(wide, query, zero), jnp.where(wide, zero, query)], axis=0
+            )
+            s_all[r, i * pair : (i + 1) * pair, :] = dot_t(both, k_ref[r, :, columns(i)])
+    for r in range(requests):
+        rows = slice(r * tree, (r + 1) * tree)
+        scores = s_all[r] * scale
+        scores = jnp.where(iota(scores.shape, 1) < lives[:, r : r + 1], scores, NEGATIVE)
+        high = jnp.max(scores, axis=-1, keepdims=True)
+        weights = jnp.exp(scores - high)
+        total = jnp.sum(weights, axis=-1, keepdims=True)
+        p_all[r] = weights.astype(BF16)
+        inverse = 1.0 / total
+        lse = high + jnp.log(total)
+        first = lse.astype(BF16).astype(F32)
+        second = (lse - first).astype(BF16).astype(F32)
+        third = lse - first - second
+        stats = jnp.zeros((tree, 128), F32)
+        for i in range(len(pieces)):
+            summed = dot(p_all[r, i * pair : (i + 1) * pair, :], v_ref[r, :, columns(i)])
+            for h in range(2):
+                own = slice(i * pair + h * tree, i * pair + (h + 1) * tree)
+                cut = slice(h * HEAD_DIM, (h + 1) * HEAD_DIM)
+                value = summed[h * tree : (h + 1) * tree, cut] * inverse[own]
+                out_ref[2 * i + h, rows, :] = value.astype(out_ref.dtype)
+                if kept:
+                    stats = jnp.where(lane == i * 8 + h, lse[own], stats)
+                else:
+                    for j, part in enumerate((first, second, third)):
+                        stats = jnp.where(lane == i * 8 + 2 * j + h, part[own], stats)
+        if kept:
+            outs[1][rows, :] = stats
+        else:
+            out_ref[8, rows, :] = stats.astype(BF16)
 
 
 def merge_kernel(other_ref, kept_ref, lse_ref, *refs):
@@ -522,7 +501,7 @@
             pltpu.VMEM((tokens, width), BF16),
             pltpu.VMEM((width,), BF16),
             pltpu.VMEM((width, local_width), BF16),
-            pltpu.SemaphoreType.DMA((4,)),
+            pltpu.SemaphoreType.DMA((3,)),
         ],
         flops=2 * tokens * width * local_width,
         bytes_accessed=2 * width * (tokens + local_width),
@@ -548,33 +527,34 @@
         bytes_accessed=4 * requests * page * width,
         vmem=16 << 20,
     )(cache_keys, cache_values, query)
-    pieces[1:], keys = lax.optimization_barrier((pieces[1:], keys))
+    pieces[0], keys = lax.optimization_barrier((pieces[0], keys))
     other_pieces = [over_core(piece) for piece in pieces]
 
     scratch = [
-        pltpu.VMEM((z_count * 2 * tree, page), F32),
-        pltpu.VMEM((z_count * 2 * tree, page), BF16),
+        pltpu.VMEM((requests, z_count * 2 * tree, page), F32),
+        pltpu.VMEM((requests, z_count * 2 * tree, page), BF16),
     ]
     heads = 2 * z_count
+    lengths = cache_lengths.reshape(1, requests)
     for_other = call(
         functools.partial(page_kernel, scale, tree, False),
         sds((heads + 1, tokens, HEAD_DIM), BF16),
-        [SMEM] + [VMEM] * 6,
+        [VMEM] * 7,
         scratch,
         flops=2 * tokens * page * width,
         bytes_accessed=2 * requests * page * width,
         vmem=20 << 20,
-    )(cache_lengths, *other_pieces, keys, values)
+    )(lengths, *other_pieces, keys, values)
     from_other = over_core(for_other)
     kept, kept_lse = call(
         functools.partial(page_kernel, scale, tree, True),
         (sds((heads, tokens, HEAD_DIM), F32), sds((tokens, 128), F32)),
-        [SMEM] + [VMEM] * 6 + [pl.ANY],
+        [VMEM] * 7 + [pl.ANY],
         scratch,
         flops=2 * tokens * page * width,
         bytes_accessed=2 * requests * page * width,
         vmem=20 << 20,
-    )(cache_lengths, *pieces, keys, values, for_other)
+    )(lengths, *pieces, keys, values, for_other)
     merged = call(
         merge_kernel,
         tuple(sds((padded, local_width), BF16) for _ in range(z_count)),

time: 114 us -> 112 us (0.982)
  Pallas kernels: 28.9 us -> 26.1 us
    pallas_call x1, Pallas kernels: 2.73 us -> 1.38 us  [per_device(): call(functools.partial(page_kernel, scale, tree, True), (sds((heads, toke...]
    pallas_call x1, Pallas kernels: 2.76 us -> 1.46 us  [per_device(): call(functools.partial(page_kernel, scale, tree, False), sds((heads + 1,...]
  transfers between devices with their start and end apart: 16 -> 16, of which waited for: 10 -> 10; matrix products, arithmetic and copies ran while one was open for 0% -> 0% of each run, Pallas kernels for 12% -> 11%
where the time goes in v7:
time: 112 us; the launch traced here: 111 us
  blocking collectives  62.2 us (56%)
  Pallas kernels  26.1 us (23%)
  starting transfers between devices  11.6 us (10%)
  waiting for transfers between devices  11.2 us (10%)
    all_to_all x1, blocking collectives, per_device(): lax.all_to_all(outgoing.reshape(experts, SLOTS, packed), ('req', 'z'), sp...  33.5 us
    all_to_all x1, blocking collectives, per_device(): lax.all_to_all(summed.reshape(experts, SLOTS, packed), ('req', 'z'), spli...  28.6 us
    ppermute x9, starting transfers between devices, over_z(): lax.ppermute(value, 'z', [(i, (i + step) % z_count) for i in range(z_coun...  10.7 us
    ppermute x9, waiting for transfers between devices, over_z(): lax.ppermute(value, 'z', [(i, (i + step) % z_count) for i in range(z_coun...  7.96 us
    pallas_call x1, Pallas kernels, per_device(): call(expert_kernel, (sds((experts * SLOTS, packed), BF16), sds((chunks, 4...  7.35 us
    pallas_call x1, Pallas kernels, per_device(): call(functools.partial(tree_kernel, scale), (sds((tokens, local_width), F...  3.83 us
    pallas_call x1, Pallas kernels, per_device(): call(load_kernel, (sds(cache_keys.shape, BF16), sds(cache_values.shape, B...  3.48 us
    ppermute x7, waiting for transfers between devices, over_core(): return lax.ppermute(value, 'core', [(0, 1), (1, 0)])  3.27 us
  transfers between devices with their start and end apart: 16, of which 10 were waited for; matrix products, arithmetic and copies ran while one was open for 0% of the time, Pallas kernels for 11%

profile of v7, /device:TPU:0, one launch (start us, length us, event | category | flops | bytes accessed | tf_op | source)
XLA Modules:
  0.0 111.3 jit_solution(12631296618238188108)
XLA Ops:
  0.0 1.9 %shard_map.127.after_ref.refs_0_.q_ref = bf16[192,256]{1,0:T(8,128)(2,1)S(1)} custom-call(bf16[192,2048]{1,0:T(8,128)(2,1)} %refs_4_.1, bf16[2048]{0:T(1024)(128)(2,1)} %g_ref.1, bf16[3,2048,256]{2,1,0:T(8,128)(2,1)} %bitcast.19), custom_call_target="tpu_custom_call" | custom-call | flops 201326592 | bytes 1835008 | tf_op jit(solution)/shard_map/pallas_call | solution.py:496
  1.9 0.0 copy-start.6
  1.9 4.2 %collective-permute-start.5 = (bf16[192,256]{1,0:T(8,128)(2,1)S(1)}, bf16[192,256]{1,0:T(8,128)(2,1)S(1)}, u32[]{:S(2)}, u32[]{:S(2)}) collective-permute-start(bf16[192,256]{1,0:T(8,128)(2,1)S(1)} %shard_map.127.after_ref.refs_0_.q_ref), channel_id=1, source_target_pairs={{0,6},{2,0},{4,2},{6,4},{1,7},{3,1},{5,3},{7,5},{8,14},{10,8},{12,... | collective-permute-start | bytes 294920 | tf_op jit(solution)/shard_map/ppermute | solution.py:515
  6.1 0.0 collective-permute-start.3
  6.1 1.3 %collective-permute-start.1 = (bf16[192,256]{1,0:T(8,128)(2,1)S(1)}, bf16[192,256]{1,0:T(8,128)(2,1)S(1)}, u32[]{:S(2)}, u32[]{:S(2)}) collective-permute-start(bf16[192,256]{1,0:T(8,128)(2,1)S(1)} %shard_map.127.after_ref.refs_0_.q_ref), channel_id=1, source_target_pairs={{0,2},{2,4},{4,6},{6,0},{1,3},{3,5},{5,7},{7,1},{8,10},{10,12},{12... | collective-permute-start | bytes 294920 | tf_op jit(solution)/shard_map/ppermute | solution.py:515
  7.4 3.5 %shard_map.128 = (bf16[4,256,2048]{2,1,0:T(8,128)(2,1)S(1)}, bf16[4,256,2048]{2,1,0:T(8,128)(2,1)S(1)}) custom-call(bf16[4,256,2048]{2,1,0:T(8,128)(2,1)} %k_hbm.1, bf16[4,256,2048]{2,1,0:T(8,128)(2,1)} %v_hbm.1, bf16[192,256]{1,0:T(8,128)(2,1)S(1)} %shard_map.127.after_ref.refs_0_.q_ref), custom_call_target="tpu_custom_call" | custom-call | bytes 8388608 | tf_op jit(solution)/shard_map/pallas_call | solution.py:522
  10.8 0.1 collective-permute-start
  10.9 0.0 collective-permute-done.5.refs_3_
  11.0 0.5 collective-permute-start.6
  11.4 1.5 %collective-permute-done.3.refs_2_ = bf16[192,256]{1,0:T(8,128)(2,1)S(1)} collective-permute-done((bf16[192,256]{1,0:T(8,128)(2,1)S(1)}, bf16[192,256]{1,0:T(8,128)(2,1)S(1)}, u32[]{:S(2)}, u32[]{:S(2)}) %collective-permute-start.3) | collective-permute-done | bytes 98336 | tf_op jit(solution)/shard_map/ppermute | solution.py:515
  13.0 0.0 collective-permute-start.4
  13.0 0.7 collective-permute-done.1.refs_1_
  13.7 0.6 collective-permute-done.4.refs_2_
  14.3 0.7 collective-permute-done.2.refs_1_
  15.0 1.5 %shard_map.129.refs_6_ = bf16[9,192,128]{2,1,0:T(8,128)(2,1)S(1)} custom-call(s32[1,4]{1,0:T(1,128)S(1)} %bitcast.16, bf16[192,256]{1,0:T(8,128)(2,1)S(1)} %collective-permute-done.refs_0_, bf16[192,256]{1,0:T(8,128)(2,1)S(1)} %collective-permute-done.2.refs_1_, bf16[192,256]{1,0:T(8,128)(2,1)S(1)} %collective-permute-done.4.refs_2_, ...), custom_call_target="tpu_custom_call" | custom-call | flops 201326592 | bytes 4194304 | tf_op jit(solution)/shard_map/pallas_call | solution.py:539
  16.4 0.0 copy-start
  16.4 0.0 copy-start.2
  16.5 0.0 copy-start.5
  16.5 0.2 collective-permute-start.7
  16.7 1.4 %shard_map.130 = (f32[8,192,128]{2,1,0:T(8,128)S(1)}, f32[192,128]{1,0:T(8,128)S(1)}) custom-call(s32[1,4]{1,0:T(1,128)S(1)} %bitcast.17, bf16[192,256]{1,0:T(8,128)(2,1)S(1)} %shard_map.127.after_ref.refs_0_.q_ref, bf16[192,256]{1,0:T(8,128)(2,1)S(1)} %collective-permute-done.1.refs_1_, bf16[192,256]{1,0:T(8,128)(2,1)S(1)} %collective-permute-done.3.refs_2_, ...), custom_call_target="tpu_custom_call" | custom-call | flops 201326592 | bytes 4194304 | tf_op jit(solution)/shard_map/pallas_call | solution.py:549
  18.1 0.0 copy-start.1
  18.1 0.0 copy-start.4
  18.1 0.3 collective-permute-done.7.other_ref
  18.3 0.7 shard_map.131
  19.1 1.0 collective-permute-start.8
  20.0 1.3 %collective-permute-start.9 = (bf16[200,256]{1,0:T(8,128)(2,1)S(1)}, bf16[200,256]{1,0:T(8,128)(2,1)S(1)}, u32[]{:S(2)}, u32[]{:S(2)}) collective-permute-start(bf16[200,256]{1,0:T(8,128)(2,1)S(1)} %get-tuple-element.45), channel_id=1, source_target_pairs={{0,4},{2,6},{4,0},{6,2},{1,5},{3,7},{5,1},{7,3},{8,12},{10,14},{12... | collective-permute-start | bytes 307208 | tf_op jit(solution)/shard_map/ppermute | solution.py:515
  21.4 0.0 collective-permute-start.10
  21.4 3.8 %shard_map.132 = (f32[192,256]{1,0:T(8,128)S(1)}, f32[8,256]{1,0:T(8,128)S(1)}) custom-call(bf16[192,2048]{1,0:T(8,128)(2,1)S(1)} %copy-done, bf16[2048]{0:T(1024)(128)(2,1)S(1)} %copy-done.2, bf16[3,2048,256]{2,1,0:T(8,128)(2,1)} %bitcast.20, bf16[192,256]{1,0:T(8,128)(2,1)S(1)} %shard_map.127.after_ref.refs_0_.q_ref, s32[4,48]{1,0:T(4,128)S(1)} %copy-done.5, ...), custom_call_target="tpu_custom_call" | custom-call | flops 402653184 | bytes 2883584 | tf_op jit(solution)/shard_map/pallas_call | solution.py:567
  25.2 0.0 collective-permute-done.8.refs_1_
  25.2 1.8 %collective-permute-done.9.refs_2_ = bf16[200,256]{1,0:T(8,128)(2,1)S(1)} collective-permute-done((bf16[200,256]{1,0:T(8,128)(2,1)S(1)}, bf16[200,256]{1,0:T(8,128)(2,1)S(1)}, u32[]{:S(2)}, u32[]{:S(2)}) %collective-permute-start.9) | collective-permute-done | bytes 102432 | tf_op jit(solution)/shard_map/ppermute | solution.py:515
  27.0 1.4 %collective-permute-done.10.refs_3_ = bf16[200,256]{1,0:T(8,128)(2,1)S(1)} collective-permute-done((bf16[200,256]{1,0:T(8,128)(2,1)S(1)}, bf16[200,256]{1,0:T(8,128)(2,1)S(1)}, u32[]{:S(2)}, u32[]{:S(2)}) %collective-permute-start.10) | collective-permute-done | bytes 102432 | tf_op jit(solution)/shard_map/ppermute | solution.py:515
  28.4 0.9 shard_map.133
  29.4 0.1 collective-permute-start.11
  29.4 1.7 %collective-permute-done.11.theirs_ref = bf16[96,2048]{1,0:T(8,128)(2,1)S(1)} collective-permute-done((bf16[96,2048]{1,0:T(8,128)(2,1)S(1)}, bf16[96,2048]{1,0:T(8,128)(2,1)S(1)}, u32[]{:S(2)}, u32[]{:S(2)}) %collective-permute-start.11) | collective-permute-done | bytes 393248 | tf_op jit(solution)/shard_map/ppermute | solution.py:518
  31.2 0.1 shard_map.134
  31.2 0.6 collective-permute-start.12
  31.9 1.5 %collective-permute-start.13 = (bf16[24,2048]{1,0:T(8,128)(2,1)S(1)}, bf16[24,2048]{1,0:T(8,128)(2,1)S(1)}, u32[]{:S(2)}, u32[]{:S(2)}) collective-permute-start(bf16[24,2048]{1,0:T(8,128)(2,1)S(1)} %get-tuple-element.53), channel_id=1, source_target_pairs={{0,4},{2,6},{4,0},{6,2},{1,5},{3,7},{5,1},{7,3},{8,12},{10,14},{12... | collective-permute-start | bytes 294920 | tf_op jit(solution)/shard_map/ppermute | solution.py:515
  33.4 0.9 collective-permute-start.14
  34.2 3.2 %shard_map.135 = (bf16[3,512,48]{2,1,0:T(8,128)(2,1)S(1)}, bf16[4,192,256]{2,1,0:T(8,128)(2,1)S(1)}, bf16[3,256,384]{2,1,0:T(8,128)(2,1)S(1)}, bf16[3072,1024]{1,0:T(8,128)(2,1)S(1)}) custom-call(s32[8,24]{1,0:T(8,128)S(1)} %bitcast.14, bf16[2048,1024]{1,0:T(8,128)(2,1)} %bitcast.21, bf16[512,2048]{1,0:T(8,128)(2,1)} %bitcast.22, ...), custom_call_target="tpu_custom_call" | custom-call | flops 16777216 | bytes 8388608 | tf_op jit(solution)/shard_map/pallas_call | solution.py:597
  37.5 0.9 collective-permute-done.13.refs_2_
  38.4 1.6 %collective-permute-done.14.refs_3_ = bf16[24,2048]{1,0:T(8,128)(2,1)S(1)} collective-permute-done((bf16[24,2048]{1,0:T(8,128)(2,1)S(1)}, bf16[24,2048]{1,0:T(8,128)(2,1)S(1)}, u32[]{:S(2)}, u32[]{:S(2)}) %collective-permute-start.14) | collective-permute-done | bytes 98336 | tf_op jit(solution)/shard_map/ppermute | solution.py:515
  40.1 0.0 collective-permute-start.15
  40.1 0.7 shard_map.136
  40.8 33.5 %all_to_all.10 = bf16[64,8,1536]{2,1,0:T(8,128)(2,1)S(1)} all-to-all(bf16[64,8,1536]{2,1,0:T(8,128)(2,1)S(1)} %bitcast.12), channel_id=1, replica_groups=mesh['req'=16,'z'=4,'core'=2] {'req','z'}, dimensions={0} | all-to-all | bytes 3145728 | tf_op jit(solution)/shard_map/all_to_all | solution.py:630
  74.3 0.0 collective-permute-done.15.other_ref
  74.3 7.3 %shard_map.137 = (bf16[512,1536]{1,0:T(8,128)(2,1)S(1)}, bf16[3,96,512]{2,1,0:T(8,128)(2,1)S(1)}) custom-call(bf16[512,1536]{1,0:T(8,128)(2,1)S(1)} %bitcast.11, bf16[3072,1024]{1,0:T(8,128)(2,1)S(1)} %get-tuple-element.62.weights_ref, bf16[3072,1024]{1,0:T(8,128)(2,1)S(1)} %collective-permute-done.15.other_ref, ...), custom_call_target="tpu_custom_call" | custom-call | flops 4831838208 | bytes 12582912 | tf_op jit(solution)/shard_map/pallas_call | solution.py:638
  81.6 28.6 %all_to_all.11 = bf16[64,8,1536]{2,1,0:T(8,128)(2,1)S(1)} all-to-all(bf16[64,8,1536]{2,1,0:T(8,128)(2,1)S(1)} %bitcast.13), channel_id=1, replica_groups=mesh['req'=16,'z'=4,'core'=2] {'req','z'}, dimensions={0} | all-to-all | bytes 3145728 | tf_op jit(solution)/shard_map/all_to_all | solution.py:658
  110.3 1.0 shard_map.138
  (14 shorter events, 0.0 us)
Async XLA Ops:
  1.9 13.1 %copy-start.6 = (s32[4]{0:T(128)S(1)}, s32[4]{0:T(128)}, u32[]{:S(2)}) copy-start(s32[4]{0:T(128)} %param.19) | copy-start | bytes 52
  1.9 9.0 %collective-permute-start.5 = (bf16[192,256]{1,0:T(8,128)(2,1)S(1)}, bf16[192,256]{1,0:T(8,128)(2,1)S(1)}, u32[]{:S(2)}, u32[]{:S(2)}) collective-permute-start(bf16[192,256]{1,0:T(8,128)(2,1)S(1)} %shard_map.127.after_ref.refs_0_.q_ref), channel_id=1, source_target_pairs={{0,6},{2,0},{4,2},{6,4},{1,7},{3,1},{5,3},{7,5},{8,14},{10,8},{12,... | collective-permute-start | bytes 294920 | tf_op jit(solution)/shard_map/ppermute | solution.py:515
  6.1 6.9 %collective-permute-start.3 = (bf16[192,256]{1,0:T(8,128)(2,1)S(1)}, bf16[192,256]{1,0:T(8,128)(2,1)S(1)}, u32[]{:S(2)}, u32[]{:S(2)}) collective-permute-start(bf16[192,256]{1,0:T(8,128)(2,1)S(1)} %shard_map.127.after_ref.refs_0_.q_ref), channel_id=1, source_target_pairs={{0,4},{2,6},{4,0},{6,2},{1,5},{3,7},{5,1},{7,3},{8,12},{10,14},{12... | collective-permute-start | bytes 294920 | tf_op jit(solution)/shard_map/ppermute | solution.py:515
  6.1 7.6 %collective-permute-start.1 = (bf16[192,256]{1,0:T(8,128)(2,1)S(1)}, bf16[192,256]{1,0:T(8,128)(2,1)S(1)}, u32[]{:S(2)}, u32[]{:S(2)}) collective-permute-start(bf16[192,256]{1,0:T(8,128)(2,1)S(1)} %shard_map.127.after_ref.refs_0_.q_ref), channel_id=1, source_target_pairs={{0,2},{2,4},{4,6},{6,0},{1,3},{3,5},{5,7},{7,1},{8,10},{10,12},{12... | collective-permute-start | bytes 294920 | tf_op jit(solution)/shard_map/ppermute | solution.py:515
  10.8 2.8 %collective-permute-start = (bf16[192,256]{1,0:T(8,128)(2,1)S(1)}, bf16[192,256]{1,0:T(8,128)(2,1)S(1)}, u32[]{:S(2)}, u32[]{:S(2)}) collective-permute-start(bf16[192,256]{1,0:T(8,128)(2,1)S(1)} %shard_map.127.after_ref.refs_0_.q_ref), channel_id=1, source_target_pairs={{0,1},{1,0},{2,3},{3,2},{4,5},{5,4},{6,7},{7,6},{8,9},{9,8},{10,11... | collective-permute-start | bytes 294920 | tf_op jit(solution)/shard_map/ppermute | solution.py:518
  11.0 2.7 %collective-permute-start.6 = (bf16[192,256]{1,0:T(8,128)(2,1)S(1)}, bf16[192,256]{1,0:T(8,128)(2,1)S(1)}, u32[]{:S(2)}, u32[]{:S(2)}) collective-permute-start(bf16[192,256]{1,0:T(8,128)(2,1)S(1)} %collective-permute-done.5.refs_3_), channel_id=1, source_target_pairs={{0,1},{1,0},{2,3},{3,2},{4,5},{5,4},{6,7},{7,6},{8,9},{9,8},{10,11... | collective-permute-start | bytes 294920 | tf_op jit(solution)/shard_map/ppermute | solution.py:518
  13.0 1.3 %collective-permute-start.4 = (bf16[192,256]{1,0:T(8,128)(2,1)S(1)}, bf16[192,256]{1,0:T(8,128)(2,1)S(1)}, u32[]{:S(2)}, u32[]{:S(2)}) collective-permute-start(bf16[192,256]{1,0:T(8,128)(2,1)S(1)} %collective-permute-done.3.refs_2_), channel_id=1, source_target_pairs={{0,1},{1,0},{2,3},{3,2},{4,5},{5,4},{6,7},{7,6},{8,9},{9,8},{10,11... | collective-permute-start | bytes 294920 | tf_op jit(solution)/shard_map/ppermute | solution.py:518
  13.7 1.3 %collective-permute-start.2 = (bf16[192,256]{1,0:T(8,128)(2,1)S(1)}, bf16[192,256]{1,0:T(8,128)(2,1)S(1)}, u32[]{:S(2)}, u32[]{:S(2)}) collective-permute-start(bf16[192,256]{1,0:T(8,128)(2,1)S(1)} %collective-permute-done.1.refs_1_), channel_id=1, source_target_pairs={{0,1},{1,0},{2,3},{3,2},{4,5},{5,4},{6,7},{7,6},{8,9},{9,8},{10,11... | collective-permute-start | bytes 294920 | tf_op jit(solution)/shard_map/ppermute | solution.py:518
  16.4 4.9 %copy-start = (bf16[192,2048]{1,0:T(8,128)(2,1)S(1)}, bf16[192,2048]{1,0:T(8,128)(2,1)}, u32[]{:S(2)}) copy-start(bf16[192,2048]{1,0:T(8,128)(2,1)} %refs_4_.1) | copy-start | bytes 2359300
  16.4 4.9 %copy-start.2 = (bf16[2048]{0:T(1024)(128)(2,1)S(1)}, bf16[2048]{0:T(1024)(128)(2,1)}, u32[]{:S(2)}) copy-start(bf16[2048]{0:T(1024)(128)(2,1)} %g_ref.1) | copy-start | bytes 12292
  16.5 4.9 %copy-start.5 = (s32[4,48]{1,0:T(4,128)S(1)}, s32[4,48]{1,0:T(4,128)}, u32[]{:S(2)}) copy-start(s32[4,48]{1,0:T(4,128)} %up_ref.1) | copy-start | bytes 2308
  16.5 1.9 %collective-permute-start.7 = (bf16[9,192,128]{2,1,0:T(8,128)(2,1)S(1)}, bf16[9,192,128]{2,1,0:T(8,128)(2,1)S(1)}, u32[]{:S(2)}, u32[]{:S(2)}) collective-permute-start(bf16[9,192,128]{2,1,0:T(8,128)(2,1)S(1)} %shard_map.129.refs_6_), channel_id=1, source_target_pairs={{0,1},{1,0},{2,3},{3,2},{4,5},{5,4},{6,7},{7,6},{8,9},{9,8},{10,11... | collective-permute-start | bytes 1327112 | tf_op jit(solution)/shard_map/ppermute | solution.py:518
  18.1 10.4 %copy-start.1 = (bf16[256,2048]{1,0:T(8,128)(2,1)S(1)}, bf16[256,2048]{1,0:T(8,128)(2,1)}, u32[]{:S(2)}) copy-start(bf16[256,2048]{1,0:T(8,128)(2,1)} %refs_6_.1) | copy-start | bytes 3145732
  18.1 16.2 %copy-start.4 = (s32[24,8]{0,1:T(8,128)S(1)}, s32[24,8]{0,1:T(8,128)}, u32[]{:S(2)}) copy-start(s32[24,8]{0,1:T(8,128)} %param.23) | copy-start | bytes 2308
  19.1 6.2 %collective-permute-start.8 = (bf16[200,256]{1,0:T(8,128)(2,1)S(1)}, bf16[200,256]{1,0:T(8,128)(2,1)S(1)}, u32[]{:S(2)}, u32[]{:S(2)}) collective-permute-start(bf16[200,256]{1,0:T(8,128)(2,1)S(1)} %get-tuple-element.44), channel_id=1, source_target_pairs={{0,6},{2,0},{4,2},{6,4},{1,7},{3,1},{5,3},{7,5},{8,14},{10,8},{12,... | collective-permute-start | bytes 307208 | tf_op jit(solution)/shard_map/ppermute | solution.py:515
  20.0 7.0 %collective-permute-start.9 = (bf16[200,256]{1,0:T(8,128)(2,1)S(1)}, bf16[200,256]{1,0:T(8,128)(2,1)S(1)}, u32[]{:S(2)}, u32[]{:S(2)}) collective-permute-start(bf16[200,256]{1,0:T(8,128)(2,1)S(1)} %get-tuple-element.45), channel_id=1, source_target_pairs={{0,4},{2,6},{4,0},{6,2},{1,5},{3,7},{5,1},{7,3},{8,12},{10,14},{12... | collective-permute-start | bytes 307208 | tf_op jit(solution)/shard_map/ppermute | solution.py:515
  21.4 7.0 %collective-permute-start.10 = (bf16[200,256]{1,0:T(8,128)(2,1)S(1)}, bf16[200,256]{1,0:T(8,128)(2,1)S(1)}, u32[]{:S(2)}, u32[]{:S(2)}) collective-permute-start(bf16[200,256]{1,0:T(8,128)(2,1)S(1)} %get-tuple-element.46), channel_id=1, source_target_pairs={{0,2},{2,4},{4,6},{6,0},{1,3},{3,5},{5,7},{7,1},{8,10},{10,12},{12... | collective-permute-start | bytes 307208 | tf_op jit(solution)/shard_map/ppermute | solution.py:515
  29.3 10.7 %copy-start.3 = (bf16[2048]{0:T(1024)(128)(2,1)S(1)}, bf16[2048]{0:T(1024)(128)(2,1)}, u32[]{:S(2)}) copy-start(bf16[2048]{0:T(1024)(128)(2,1)} %refs_5_.1) | copy-start | bytes 12292
  29.4 1.8 %collective-permute-start.11 = (bf16[96,2048]{1,0:T(8,128)(2,1)S(1)}, bf16[96,2048]{1,0:T(8,128)(2,1)S(1)}, u32[]{:S(2)}, u32[]{:S(2)}) collective-permute-start(bf16[96,2048]{1,0:T(8,128)(2,1)S(1)} %get-tuple-element.50), channel_id=1, source_target_pairs={{0,1},{1,0},{2,3},{3,2},{4,5},{5,4},{6,7},{7,6},{8,9},{9,8},{10,11... | collective-permute-start | bytes 1179656 | tf_op jit(solution)/shard_map/ppermute | solution.py:518
  31.2 6.2 %collective-permute-start.12 = (bf16[24,2048]{1,0:T(8,128)(2,1)S(1)}, bf16[24,2048]{1,0:T(8,128)(2,1)S(1)}, u32[]{:S(2)}, u32[]{:S(2)}) collective-permute-start(bf16[24,2048]{1,0:T(8,128)(2,1)S(1)} %get-tuple-element.52), channel_id=1, source_target_pairs={{0,6},{2,0},{4,2},{6,4},{1,7},{3,1},{5,3},{7,5},{8,14},{10,8},{12,... | collective-permute-start | bytes 294920 | tf_op jit(solution)/shard_map/ppermute | solution.py:515
  31.9 6.6 %collective-permute-start.13 = (bf16[24,2048]{1,0:T(8,128)(2,1)S(1)}, bf16[24,2048]{1,0:T(8,128)(2,1)S(1)}, u32[]{:S(2)}, u32[]{:S(2)}) collective-permute-start(bf16[24,2048]{1,0:T(8,128)(2,1)S(1)} %get-tuple-element.53), channel_id=1, source_target_pairs={{0,4},{2,6},{4,0},{6,2},{1,5},{3,7},{5,1},{7,3},{8,12},{10,14},{12... | collective-permute-start | bytes 294920 | tf_op jit(solution)/shard_map/ppermute | solution.py:515
  33.4 6.7 %collective-permute-start.14 = (bf16[24,2048]{1,0:T(8,128)(2,1)S(1)}, bf16[24,2048]{1,0:T(8,128)(2,1)S(1)}, u32[]{:S(2)}, u32[]{:S(2)}) collective-permute-start(bf16[24,2048]{1,0:T(8,128)(2,1)S(1)} %get-tuple-element.54), channel_id=1, source_target_pairs={{0,2},{2,4},{4,6},{6,0},{1,3},{3,5},{5,7},{7,1},{8,10},{10,12},{12... | collective-permute-start | bytes 294920 | tf_op jit(solution)/shard_map/ppermute | solution.py:515
  34.2 40.1 %copy-start.7 = (bf16[2048,64]{0,1:T(8,128)(2,1)S(1)}, bf16[2048,64]{0,1:T(8,128)(2,1)}, u32[]{:S(2)}) copy-start(bf16[2048,64]{0,1:T(8,128)(2,1)} %param.22) | copy-start | bytes 786436
  40.1 34.2 %collective-permute-start.15 = (bf16[3072,1024]{1,0:T(8,128)(2,1)S(1)}, bf16[3072,1024]{1,0:T(8,128)(2,1)S(1)}, u32[]{:S(2)}, u32[]{:S(2)}) collective-permute-start(bf16[3072,1024]{1,0:T(8,128)(2,1)S(1)} %get-tuple-element.62.weights_ref), channel_id=1, source_target_pairs={{0,1},{1,0},{2,3},{3,2},{4,5},{5,4},{6,7},{7,6},{8,9},{9,8},{10,11... | collective-permute-start | bytes 18874376 | tf_op jit(solution)/shard_map/ppermute | solution.py:518

commit v8 on v7

--- a/solution.py
+++ b/solution.py
@@ -67,24 +67,33 @@
 
 
 def query_kernel(x_hbm, g_hbm, w_hbm, q_ref, x_ref, g_ref, w_ref, sems):
-    x_copy = pltpu.make_async_copy(x_hbm, x_ref, sems.at[0])
-    w_copy = pltpu.make_async_copy(w_hbm.at[0], w_ref, sems.at[1])
-    g_copy = pltpu.make_async_copy(g_hbm, g_ref, sems.at[2])
-    x_copy.start()
+    half = x_ref.shape[0] // 2
+    rows = [slice(0, half), slice(half, 2 * half)]
+    g_copy = pltpu.make_async_copy(g_hbm, g_ref, sems.at[0])
+    x_copies = [
+        pltpu.make_async_copy(x_hbm.at[rows[i]], x_ref.at[rows[i]], sems.at[1 + i])
+        for i in range(2)
+    ]
+    w_copy = pltpu.make_async_copy(w_hbm.at[0], w_ref, sems.at[3])
     g_copy.start()
+    for copy in x_copies:
+        copy.start()
+    g_copy.wait()
+    gain = g_ref[...].astype(F32).reshape(1, -1)
+    x_copies[0].wait()
     w_copy.start()
-    g_copy.wait()
-    x_copy.wait()
-    normed = normed_rows(x_ref[...].astype(F32), g_ref[...].astype(F32).reshape(1, -1))
+    first = normed_rows(x_ref[rows[0], :].astype(F32), gain)
+    x_copies[1].wait()
+    second = normed_rows(x_ref[rows[1], :].astype(F32), gain)
     w_copy.wait()
-    q_ref[...] = dot(normed, w_ref[...]).astype(BF16)
-
-
-def load_kernel(k_hbm, v_hbm, after_ref, k_ref, v_ref, sems):
+    q_ref[...] = dot(jnp.concatenate([first, second], axis=0), w_ref[...]).astype(BF16)
+
+
+def load_kernel(source_hbm, after_ref, target_ref, sems):
     del after_ref
     copies = [
-        pltpu.make_async_copy(k_hbm, k_ref, sems.at[0]),
-        pltpu.make_async_copy(v_hbm, v_ref, sems.at[1]),
+        pltpu.make_async_copy(source_hbm.at[r], target_ref.at[r], sems.at[r])
+        for r in range(source_hbm.shape[0])
     ]
     for copy in copies:
         copy.start()
@@ -269,7 +278,7 @@
 
 
 def table_kernel(routes_ref, up_hbm, down_hbm, after_ref, *refs):
-    place_refs, (weights_ref, sems) = refs[:3], refs[3:]
+    place_refs, (weights_ref, sems) = refs[:4], refs[4:]
     del after_ref
     depth, both = up_hbm.shape
     units = down_hbm.shape[0]
@@ -290,7 +299,7 @@
         copy.wait()
 
 
-def place_kernel(routes_ref, place_ref, gather_ref, scatter_ref):
+def place_kernel(routes_ref, place_ref, gather_ref, compact_ref, scatter_ref):
     chunks = place_ref.shape[0]
     _, real, block = gather_ref.shape
     row, column = iota((real, block), 0), iota((real, block), 1)
@@ -299,14 +308,18 @@
     for k in range(chunks):
         hit = (column == base + CAP + slot // chunks) & (slot % chunks == k)
         gather_ref[1 + k] = jnp.where(hit, 1.0, 0.0).astype(BF16)
-    row, column = iota((block, 2 * real), 0), iota((block, 2 * real), 1)
-    is_tail = column >= real
-    column = column - jnp.where(is_tail, real, 0)
-    base, slot = column // CAP * SLOTS, column % CAP
+    spare = SLOTS - CAP
+    compact = compact_ref.shape[1]
+    row, column = iota((compact, real), 0), iota((compact, real), 1)
+    slot = column % CAP
     for k in range(chunks):
-        main = (row == base + slot) & jnp.logical_not(is_tail)
-        tail = (row == base + CAP + slot // chunks) & (slot % chunks == k) & is_tail
-        scatter_ref[k] = jnp.where(main | tail, 1.0, 0.0).astype(BF16)
+        hit = (column // CAP == row // spare) & (slot == row % spare * chunks + k)
+        compact_ref[k] = jnp.where(hit, 1.0, 0.0).astype(BF16)
+    row, column = iota((block, real + compact), 0), iota((block, real + compact), 1)
+    main = (column < real) & (row == column // CAP * SLOTS + column % CAP)
+    column = column - real
+    tail = (column >= 0) & (row == column // spare * SLOTS + CAP + column % spare)
+    scatter_ref[...] = jnp.where(main | tail, 1.0, 0.0).astype(BF16)
     top, tokens = routes_ref.shape
     chunks, rows, _ = place_ref.shape
     experts = rows // SLOTS
@@ -393,6 +406,7 @@
     weights_ref,
     other_ref,
     gather_ref,
+    compact_ref,
     scatter_ref,
     normed_ref,
     router_ref,
@@ -441,24 +455,33 @@
         value = result(k)
         for i in range(rows // block):
             own = slice(i * real, (i + 1) * real)
-            pair = jnp.concatenate([value[own], last[own]], axis=0)
-            out_ref[i * block : (i + 1) * block, columns] = dot(scatter_ref[k], pair).astype(
+            tail = dot(compact_ref[k], last[own]).astype(BF16)
+            pair = jnp.concatenate([value[own], tail], axis=0)
+            out_ref[i * block : (i + 1) * block, columns] = dot(scatter_ref[...], pair).astype(
                 BF16
             )
 
 
-def final_kernel(back_ref, table_ref, res_ref, out_ref):
+def final_kernel(back_ref, table_ref, res_ref, out_hbm, out_ref, sems):
     tokens, width = res_ref.shape
     chunks = table_ref.shape[0]
     cut = width // (chunks + 1)
-    tail = res_ref[:, chunks * cut :]
+    spans = [slice(j * cut, (j + 1) * cut) for j in range(chunks + 1)]
+    copies = [
+        pltpu.make_async_copy(out_ref.at[:, span], out_hbm.at[:, span], sems.at[j])
+        for j, span in enumerate(spans)
+    ]
+    tail = res_ref[:, spans[-1]]
     for j in range(chunks):
-        span = slice(j * cut, (j + 1) * cut)
-        sums = dot(table_ref[j], back_ref[:, span])
+        sums = dot(table_ref[j], back_ref[:, spans[j]])
         main = sums[0:tokens] + sums[tokens : 2 * tokens]
-        out_ref[:, span] = (res_ref[:, span] + main).astype(BF16)
+        out_ref[:, spans[j]] = (res_ref[:, spans[j]] + main).astype(BF16)
+        copies[j].start()
         tail = tail + (sums[2 * tokens : 3 * tokens] + sums[3 * tokens :])
-    out_ref[:, chunks * cut :] = tail.astype(BF16)
+    out_ref[:, spans[-1]] = tail.astype(BF16)
+    copies[-1].start()
+    for copy in copies:
+        copy.wait()
 
 
 def per_device(
@@ -501,7 +524,7 @@
             pltpu.VMEM((tokens, width), BF16),
             pltpu.VMEM((width,), BF16),
             pltpu.VMEM((width, local_width), BF16),
-            pltpu.SemaphoreType.DMA((3,)),
+            pltpu.SemaphoreType.DMA((4,)),
         ],
         flops=2 * tokens * width * local_width,
         bytes_accessed=2 * width * (tokens + local_width),
@@ -519,14 +542,14 @@
 
     steps = range(1, z_count)
     pieces = [query] + [over_z(query, step) for step in steps]
-    keys, values = call(
+    load = call(
         load_kernel,
-        (sds(cache_keys.shape, BF16), sds(cache_values.shape, BF16)),
-        [HBM, HBM, pl.ANY],
-        [pltpu.SemaphoreType.DMA((2,))],
-        bytes_accessed=4 * requests * page * width,
-        vmem=16 << 20,
-    )(cache_keys, cache_values, query)
+        sds(cache_keys.shape, BF16),
+        [HBM, pl.ANY],
+        [pltpu.SemaphoreType.DMA((requests,))],
+        bytes_accessed=2 * requests * page * width,
+    )
+    keys, values = load(cache_keys, query), load(cache_values, query)
     pieces[0], keys = lax.optimization_barrier((pieces[0], keys))
     other_pieces = [over_core(piece) for piece in pieces]
 
@@ -594,12 +617,13 @@
     block = experts * SLOTS // 2
     real = block // SLOTS * CAP
     weight_rows = width + width * w_down.shape[1] // w_gate_up.shape[2]
-    place, gather, scatter, weights = call(
+    place, gather, compact, scatter, weights = call(
         table_kernel,
         (
             sds((chunks, experts * SLOTS, 2 * own), BF16),
             sds((1 + chunks, real, block), BF16),
-            sds((chunks, block, 2 * real), BF16),
+            sds((chunks, block - real, real), BF16),
+            sds((block, block), BF16),
             sds((weight_rows, w_gate_up.shape[2]), BF16),
         ),
         [VMEM, HBM, HBM, pl.ANY],
@@ -641,7 +665,7 @@
             sds((experts * SLOTS, packed), BF16),
             sds((chunks, 4 * own, experts * SLOTS), BF16),
         ),
-        [VMEM] * 8,
+        [VMEM] * 9,
         flops=12 * experts * CAP * width * w_down.shape[1],
         bytes_accessed=12 * width * w_down.shape[1],
         vmem=24 << 20,
@@ -650,6 +674,7 @@
         weights,
         other_weights,
         gather,
+        compact,
         scatter,
         normed,
         w_router.T,
@@ -662,12 +687,16 @@
         concat_axis=0,
         tiled=True,
     ).reshape(experts * SLOTS, packed)
-    return call(
+    return pl.pallas_call(
         final_kernel,
-        sds((own, width), BF16),
-        [VMEM] * 3,
-        flops=1 << 27,
-        bytes_accessed=1 << 22,
+        out_shape=sds((own, width), BF16),
+        in_specs=[pl.BlockSpec(memory_space=VMEM)] * 3,
+        out_specs=pl.BlockSpec(memory_space=HBM),
+        scratch_shapes=[
+            pltpu.VMEM((own, width), BF16),
+            pltpu.SemaphoreType.DMA((chunks + 1,)),
+        ],
+        compiler_params=pltpu.CompilerParams(vmem_limit_bytes=10 << 20),
     )(back, table, residual)
 
 

time: 112 us -> 113 us (level)
  waiting for transfers between devices: 11.2 us -> 12.9 us
  Pallas kernels: 26.1 us -> 27.6 us
    ppermute x9, waiting for transfers between devices: 7.96 us -> 11.2 us  [over_z(): lax.ppermute(value, 'z', [(i, (i + step) % z_count) for i in range(z_coun...]
    ppermute x7, waiting for transfers between devices: 3.27 us -> 1.73 us  [over_core(): return lax.ppermute(value, 'core', [(0, 1), (1, 0)])]
    pallas_call x2 -> x3, Pallas kernels: 4.52 us -> 5.45 us  [the longest x2 4.41 us: per_device(): keys, values = (load(cache_keys, query), load(cache_values, query))]
  transfers between devices with their start and end apart: 16 -> 16, of which waited for: 10 -> 9; matrix products, arithmetic and copies ran while one was open for 0% -> 0% of each run, Pallas kernels for 11% -> 12%
where the time goes in v8:
time: 113 us
  blocking collectives  61.5 us (54%)
  Pallas kernels  27.6 us (24%)
  waiting for transfers between devices  12.9 us (11%)
  starting transfers between devices  10.6 us (9%)
    all_to_all x1, blocking collectives, per_device(): lax.all_to_all(outgoing.reshape(experts, SLOTS, packed), ('req', 'z'), sp...  32.9 us
    all_to_all x1, blocking collectives, per_device(): lax.all_to_all(summed.reshape(experts, SLOTS, packed), ('req', 'z'), spli...  28.6 us
    ppermute x9, waiting for transfers between devices, over_z(): lax.ppermute(value, 'z', [(i, (i + step) % z_count) for i in range(z_coun...  11.2 us
    ppermute x9, starting transfers between devices, over_z(): lax.ppermute(value, 'z', [(i, (i + step) % z_count) for i in range(z_coun...  9.87 us
    pallas_call x1, Pallas kernels, per_device(): call(expert_kernel, (sds((experts * SLOTS, packed), BF16), sds((chunks, 4...  7.47 us
    pallas_call x2, Pallas kernels, per_device(): keys, values = (load(cache_keys, query), load(cache_values, query))  4.41 us
    pallas_call x1, Pallas kernels, per_device(): call(functools.partial(tree_kernel, scale), (sds((tokens, local_width), F...  3.83 us
    pallas_call x1, Pallas kernels, per_device(): call(table_kernel, (sds((chunks, experts * SLOTS, 2 * own), BF16), sds((1...  2.87 us
  transfers between devices with their start and end apart: 16, of which 9 were waited for; matrix products, arithmetic and copies ran while one was open for 0% of the time, Pallas kernels for 12%

profile of v8, /device:TPU:0, one launch (start us, length us, event | category | flops | bytes accessed | tf_op | source)
XLA Modules:
  0.0 113.1 jit_solution(12473329613145296628)
XLA Ops:
  0.0 2.7 %shard_map.127.after_ref.refs_0_.q_ref = bf16[192,256]{1,0:T(8,128)(2,1)S(1)} custom-call(bf16[192,2048]{1,0:T(8,128)(2,1)} %refs_4_.1, bf16[2048]{0:T(1024)(128)(2,1)} %g_ref.1, bf16[3,2048,256]{2,1,0:T(8,128)(2,1)} %bitcast.19), custom_call_target="tpu_custom_call" | custom-call | flops 201326592 | bytes 1835008 | tf_op jit(solution)/shard_map/pallas_call | solution.py:519
  2.7 4.2 %collective-permute-start.5 = (bf16[192,256]{1,0:T(8,128)(2,1)S(1)}, bf16[192,256]{1,0:T(8,128)(2,1)S(1)}, u32[]{:S(2)}, u32[]{:S(2)}) collective-permute-start(bf16[192,256]{1,0:T(8,128)(2,1)S(1)} %shard_map.127.after_ref.refs_0_.q_ref), channel_id=1, source_target_pairs={{0,6},{2,0},{4,2},{6,4},{1,7},{3,1},{5,3},{7,5},{8,14},{10,8},{12,... | collective-permute-start | bytes 294920 | tf_op jit(solution)/shard_map/ppermute | solution.py:538
  6.9 1.3 %collective-permute-start.1 = (bf16[192,256]{1,0:T(8,128)(2,1)S(1)}, bf16[192,256]{1,0:T(8,128)(2,1)S(1)}, u32[]{:S(2)}, u32[]{:S(2)}) collective-permute-start(bf16[192,256]{1,0:T(8,128)(2,1)S(1)} %shard_map.127.after_ref.refs_0_.q_ref), channel_id=1, source_target_pairs={{0,2},{2,4},{4,6},{6,0},{1,3},{3,5},{5,7},{7,1},{8,10},{10,12},{12... | collective-permute-start | bytes 294920 | tf_op jit(solution)/shard_map/ppermute | solution.py:538
  8.1 2.2 %shard_map.128.refs_4_ = bf16[4,256,2048]{2,1,0:T(8,128)(2,1)S(1)} custom-call(bf16[4,256,2048]{2,1,0:T(8,128)(2,1)} %source_hbm.2, bf16[192,256]{1,0:T(8,128)(2,1)S(1)} %shard_map.127.after_ref.refs_0_.q_ref), custom_call_target="tpu_custom_call" | custom-call | bytes 4194304 | tf_op jit(solution)/shard_map/pallas_call | solution.py:552
  10.4 0.0 copy-start.6
  10.4 0.1 collective-permute-start
  10.5 0.6 collective-permute-done.5.refs_3_
  11.0 0.0 collective-permute-start.6
  11.1 2.7 %collective-permute-done.3.refs_2_ = bf16[192,256]{1,0:T(8,128)(2,1)S(1)} collective-permute-done((bf16[192,256]{1,0:T(8,128)(2,1)S(1)}, bf16[192,256]{1,0:T(8,128)(2,1)S(1)}, u32[]{:S(2)}, u32[]{:S(2)}) %collective-permute-start.3) | collective-permute-done | bytes 98336 | tf_op jit(solution)/shard_map/ppermute | solution.py:538
  13.8 0.0 collective-permute-start.4
  13.8 0.7 collective-permute-done.1.refs_1_
  14.5 0.0 collective-permute-start.2
  14.5 2.2 %shard_map.129.refs_5_ = bf16[4,256,2048]{2,1,0:T(8,128)(2,1)S(1)} custom-call(bf16[4,256,2048]{2,1,0:T(8,128)(2,1)} %source_hbm.3, bf16[192,256]{1,0:T(8,128)(2,1)S(1)} %shard_map.127.after_ref.refs_0_.q_ref), custom_call_target="tpu_custom_call" | custom-call | bytes 4194304 | tf_op jit(solution)/shard_map/pallas_call | solution.py:552
  16.7 0.0 collective-permute-done.refs_0_
  16.7 1.5 %shard_map.130.refs_6_ = bf16[9,192,128]{2,1,0:T(8,128)(2,1)S(1)} custom-call(s32[1,4]{1,0:T(1,128)S(1)} %bitcast.16, bf16[192,256]{1,0:T(8,128)(2,1)S(1)} %collective-permute-done.refs_0_, bf16[192,256]{1,0:T(8,128)(2,1)S(1)} %collective-permute-done.2.refs_1_, bf16[192,256]{1,0:T(8,128)(2,1)S(1)} %collective-permute-done.4.refs_2_, ...), custom_call_target="tpu_custom_call" | custom-call | flops 201326592 | bytes 4194304 | tf_op jit(solution)/shard_map/pallas_call | solution.py:562
  18.2 0.0 copy-start
  18.2 0.0 copy-start.2
  18.2 0.0 copy-start.5
  18.2 0.6 collective-permute-start.7
  18.8 1.4 %shard_map.131 = (f32[8,192,128]{2,1,0:T(8,128)S(1)}, f32[192,128]{1,0:T(8,128)S(1)}) custom-call(s32[1,4]{1,0:T(1,128)S(1)} %bitcast.17, bf16[192,256]{1,0:T(8,128)(2,1)S(1)} %shard_map.127.after_ref.refs_0_.q_ref, bf16[192,256]{1,0:T(8,128)(2,1)S(1)} %collective-permute-done.1.refs_1_, bf16[192,256]{1,0:T(8,128)(2,1)S(1)} %collective-permute-done.3.refs_2_, ...), custom_call_target="tpu_custom_call" | custom-call | flops 201326592 | bytes 4194304 | tf_op jit(solution)/shard_map/pallas_call | solution.py:572
  20.2 0.0 copy-start.1
  20.2 0.0 copy-start.4
  20.2 0.0 collective-permute-done.7.other_ref
  20.2 0.7 shard_map.132
  20.9 1.0 collective-permute-start.8
  21.9 0.3 collective-permute-start.9
  22.2 1.0 collective-permute-start.10
  23.3 3.8 %shard_map.133 = (f32[192,256]{1,0:T(8,128)S(1)}, f32[8,256]{1,0:T(8,128)S(1)}) custom-call(bf16[192,2048]{1,0:T(8,128)(2,1)S(1)} %copy-done, bf16[2048]{0:T(1024)(128)(2,1)S(1)} %copy-done.2, bf16[3,2048,256]{2,1,0:T(8,128)(2,1)} %bitcast.20, bf16[192,256]{1,0:T(8,128)(2,1)S(1)} %shard_map.127.after_ref.refs_0_.q_ref, s32[4,48]{1,0:T(4,128)S(1)} %copy-done.5, ...), custom_call_target="tpu_custom_call" | custom-call | flops 402653184 | bytes 2883584 | tf_op jit(solution)/shard_map/pallas_call | solution.py:590
  27.1 2.0 %collective-permute-done.9.refs_2_ = bf16[200,256]{1,0:T(8,128)(2,1)S(1)} collective-permute-done((bf16[200,256]{1,0:T(8,128)(2,1)S(1)}, bf16[200,256]{1,0:T(8,128)(2,1)S(1)}, u32[]{:S(2)}, u32[]{:S(2)}) %collective-permute-start.9) | collective-permute-done | bytes 102432 | tf_op jit(solution)/shard_map/ppermute | solution.py:538
  29.1 1.4 %collective-permute-done.10.refs_3_ = bf16[200,256]{1,0:T(8,128)(2,1)S(1)} collective-permute-done((bf16[200,256]{1,0:T(8,128)(2,1)S(1)}, bf16[200,256]{1,0:T(8,128)(2,1)S(1)}, u32[]{:S(2)}, u32[]{:S(2)}) %collective-permute-start.10) | collective-permute-done | bytes 102432 | tf_op jit(solution)/shard_map/ppermute | solution.py:538
  30.5 0.9 shard_map.134
  31.4 0.0 copy-start.3
  31.4 0.1 collective-permute-start.11
  31.5 1.7 %collective-permute-done.11.theirs_ref = bf16[96,2048]{1,0:T(8,128)(2,1)S(1)} collective-permute-done((bf16[96,2048]{1,0:T(8,128)(2,1)S(1)}, bf16[96,2048]{1,0:T(8,128)(2,1)S(1)}, u32[]{:S(2)}, u32[]{:S(2)}) %collective-permute-start.11) | collective-permute-done | bytes 393248 | tf_op jit(solution)/shard_map/ppermute | solution.py:541
  33.2 0.1 shard_map.135
  33.3 0.6 collective-permute-start.12
  34.0 0.4 collective-permute-start.13
  34.4 1.0 collective-permute-start.14
  35.4 2.9 %shard_map.136 = (bf16[3,512,48]{2,1,0:T(8,128)(2,1)S(1)}, bf16[4,192,256]{2,1,0:T(8,128)(2,1)S(1)}, bf16[3,64,192]{2,1,0:T(8,128)(2,1)S(1)}, bf16[256,256]{1,0:T(8,128)(2,1)S(1)}, bf16[3072,1024]{1,0:T(8,128)(2,1)S(1)}) custom-call(s32[8,24]{1,0:T(8,128)S(1)} %bitcast.14, bf16[2048,1024]{1,0:T(8,128)(2,1)} %bitcast.21, bf16[512,2048]{1,0:T(8,128)(2,1)} %bitcast.22, ...), custom_call_target="tpu_custom_call" | custom-call | flops 16777216 | bytes 8388608 | tf_op jit(solution)/shard_map/pallas_call | solution.py:620
  38.3 0.7 collective-permute-done.12.refs_1_
  39.0 1.5 %collective-permute-done.13.refs_2_ = bf16[24,2048]{1,0:T(8,128)(2,1)S(1)} collective-permute-done((bf16[24,2048]{1,0:T(8,128)(2,1)S(1)}, bf16[24,2048]{1,0:T(8,128)(2,1)S(1)}, u32[]{:S(2)}, u32[]{:S(2)}) %collective-permute-start.13) | collective-permute-done | bytes 98336 | tf_op jit(solution)/shard_map/ppermute | solution.py:538
  40.5 1.6 %collective-permute-done.14.refs_3_ = bf16[24,2048]{1,0:T(8,128)(2,1)S(1)} collective-permute-done((bf16[24,2048]{1,0:T(8,128)(2,1)S(1)}, bf16[24,2048]{1,0:T(8,128)(2,1)S(1)}, u32[]{:S(2)}, u32[]{:S(2)}) %collective-permute-start.14) | collective-permute-done | bytes 98336 | tf_op jit(solution)/shard_map/ppermute | solution.py:538
  42.1 0.0 collective-permute-start.15
  42.1 0.7 shard_map.137
  42.9 32.9 %all_to_all.10 = bf16[64,8,1536]{2,1,0:T(8,128)(2,1)S(1)} all-to-all(bf16[64,8,1536]{2,1,0:T(8,128)(2,1)S(1)} %bitcast.13), channel_id=1, replica_groups=mesh['req'=16,'z'=4,'core'=2] {'req','z'}, dimensions={0} | all-to-all | bytes 3145728 | tf_op jit(solution)/shard_map/all_to_all | solution.py:654
  75.8 7.5 %shard_map.138 = (bf16[512,1536]{1,0:T(8,128)(2,1)S(1)}, bf16[3,96,512]{2,1,0:T(8,128)(2,1)S(1)}) custom-call(bf16[512,1536]{1,0:T(8,128)(2,1)S(1)} %bitcast.11, bf16[3072,1024]{1,0:T(8,128)(2,1)S(1)} %get-tuple-element.59.weights_ref, bf16[3072,1024]{1,0:T(8,128)(2,1)S(1)} %collective-permute-done.15.other_ref, ...), custom_call_target="tpu_custom_call" | custom-call | flops 4831838208 | bytes 12582912 | tf_op jit(solution)/shard_map/pallas_call | solution.py:662
  83.3 28.6 %all_to_all.11 = bf16[64,8,1536]{2,1,0:T(8,128)(2,1)S(1)} all-to-all(bf16[64,8,1536]{2,1,0:T(8,128)(2,1)S(1)} %bitcast.12), channel_id=1, replica_groups=mesh['req'=16,'z'=4,'core'=2] {'req','z'}, dimensions={0} | all-to-all | bytes 3145728 | tf_op jit(solution)/shard_map/all_to_all | solution.py:683
  111.9 1.0 shard_map.139
  (15 shorter events, 0.0 us)
Async XLA Ops:
  2.7 8.3 %collective-permute-start.5 = (bf16[192,256]{1,0:T(8,128)(2,1)S(1)}, bf16[192,256]{1,0:T(8,128)(2,1)S(1)}, u32[]{:S(2)}, u32[]{:S(2)}) collective-permute-start(bf16[192,256]{1,0:T(8,128)(2,1)S(1)} %shard_map.127.after_ref.refs_0_.q_ref), channel_id=1, source_target_pairs={{0,6},{2,0},{4,2},{6,4},{1,7},{3,1},{5,3},{7,5},{8,14},{10,8},{12,... | collective-permute-start | bytes 294920 | tf_op jit(solution)/shard_map/ppermute | solution.py:538
  6.9 6.9 %collective-permute-start.3 = (bf16[192,256]{1,0:T(8,128)(2,1)S(1)}, bf16[192,256]{1,0:T(8,128)(2,1)S(1)}, u32[]{:S(2)}, u32[]{:S(2)}) collective-permute-start(bf16[192,256]{1,0:T(8,128)(2,1)S(1)} %shard_map.127.after_ref.refs_0_.q_ref), channel_id=1, source_target_pairs={{0,4},{2,6},{4,0},{6,2},{1,5},{3,7},{5,1},{7,3},{8,12},{10,14},{12... | collective-permute-start | bytes 294920 | tf_op jit(solution)/shard_map/ppermute | solution.py:538
  6.9 7.6 %collective-permute-start.1 = (bf16[192,256]{1,0:T(8,128)(2,1)S(1)}, bf16[192,256]{1,0:T(8,128)(2,1)S(1)}, u32[]{:S(2)}, u32[]{:S(2)}) collective-permute-start(bf16[192,256]{1,0:T(8,128)(2,1)S(1)} %shard_map.127.after_ref.refs_0_.q_ref), channel_id=1, source_target_pairs={{0,2},{2,4},{4,6},{6,0},{1,3},{3,5},{5,7},{7,1},{8,10},{10,12},{12... | collective-permute-start | bytes 294920 | tf_op jit(solution)/shard_map/ppermute | solution.py:538
  10.4 6.4 %copy-start.6 = (s32[4]{0:T(128)S(1)}, s32[4]{0:T(128)}, u32[]{:S(2)}) copy-start(s32[4]{0:T(128)} %param.19) | copy-start | bytes 52
  10.4 6.3 %collective-permute-start = (bf16[192,256]{1,0:T(8,128)(2,1)S(1)}, bf16[192,256]{1,0:T(8,128)(2,1)S(1)}, u32[]{:S(2)}, u32[]{:S(2)}) collective-permute-start(bf16[192,256]{1,0:T(8,128)(2,1)S(1)} %shard_map.127.after_ref.refs_0_.q_ref), channel_id=1, source_target_pairs={{0,1},{1,0},{2,3},{3,2},{4,5},{5,4},{6,7},{7,6},{8,9},{9,8},{10,11... | collective-permute-start | bytes 294920 | tf_op jit(solution)/shard_map/ppermute | solution.py:541
  11.0 5.6 %collective-permute-start.6 = (bf16[192,256]{1,0:T(8,128)(2,1)S(1)}, bf16[192,256]{1,0:T(8,128)(2,1)S(1)}, u32[]{:S(2)}, u32[]{:S(2)}) collective-permute-start(bf16[192,256]{1,0:T(8,128)(2,1)S(1)} %collective-permute-done.5.refs_3_), channel_id=1, source_target_pairs={{0,1},{1,0},{2,3},{3,2},{4,5},{5,4},{6,7},{7,6},{8,9},{9,8},{10,11... | collective-permute-start | bytes 294920 | tf_op jit(solution)/shard_map/ppermute | solution.py:541
  13.8 2.9 %collective-permute-start.4 = (bf16[192,256]{1,0:T(8,128)(2,1)S(1)}, bf16[192,256]{1,0:T(8,128)(2,1)S(1)}, u32[]{:S(2)}, u32[]{:S(2)}) collective-permute-start(bf16[192,256]{1,0:T(8,128)(2,1)S(1)} %collective-permute-done.3.refs_2_), channel_id=1, source_target_pairs={{0,1},{1,0},{2,3},{3,2},{4,5},{5,4},{6,7},{7,6},{8,9},{9,8},{10,11... | collective-permute-start | bytes 294920 | tf_op jit(solution)/shard_map/ppermute | solution.py:541
  14.5 2.3 %collective-permute-start.2 = (bf16[192,256]{1,0:T(8,128)(2,1)S(1)}, bf16[192,256]{1,0:T(8,128)(2,1)S(1)}, u32[]{:S(2)}, u32[]{:S(2)}) collective-permute-start(bf16[192,256]{1,0:T(8,128)(2,1)S(1)} %collective-permute-done.1.refs_1_), channel_id=1, source_target_pairs={{0,1},{1,0},{2,3},{3,2},{4,5},{5,4},{6,7},{7,6},{8,9},{9,8},{10,11... | collective-permute-start | bytes 294920 | tf_op jit(solution)/shard_map/ppermute | solution.py:541
  18.2 5.1 %copy-start = (bf16[192,2048]{1,0:T(8,128)(2,1)S(1)}, bf16[192,2048]{1,0:T(8,128)(2,1)}, u32[]{:S(2)}) copy-start(bf16[192,2048]{1,0:T(8,128)(2,1)} %refs_4_.1) | copy-start | bytes 2359300
  18.2 5.1 %copy-start.2 = (bf16[2048]{0:T(1024)(128)(2,1)S(1)}, bf16[2048]{0:T(1024)(128)(2,1)}, u32[]{:S(2)}) copy-start(bf16[2048]{0:T(1024)(128)(2,1)} %g_ref.1) | copy-start | bytes 12292
  18.2 5.0 %copy-start.5 = (s32[4,48]{1,0:T(4,128)S(1)}, s32[4,48]{1,0:T(4,128)}, u32[]{:S(2)}) copy-start(s32[4,48]{1,0:T(4,128)} %up_ref.1) | copy-start | bytes 2308
  18.2 2.0 %collective-permute-start.7 = (bf16[9,192,128]{2,1,0:T(8,128)(2,1)S(1)}, bf16[9,192,128]{2,1,0:T(8,128)(2,1)S(1)}, u32[]{:S(2)}, u32[]{:S(2)}) collective-permute-start(bf16[9,192,128]{2,1,0:T(8,128)(2,1)S(1)} %shard_map.130.refs_6_), channel_id=1, source_target_pairs={{0,1},{1,0},{2,3},{3,2},{4,5},{5,4},{6,7},{7,6},{8,9},{9,8},{10,11... | collective-permute-start | bytes 1327112 | tf_op jit(solution)/shard_map/ppermute | solution.py:541
  20.2 10.3 %copy-start.1 = (bf16[256,2048]{1,0:T(8,128)(2,1)S(1)}, bf16[256,2048]{1,0:T(8,128)(2,1)}, u32[]{:S(2)}) copy-start(bf16[256,2048]{1,0:T(8,128)(2,1)} %refs_6_.1) | copy-start | bytes 3145732
  20.2 15.2 %copy-start.4 = (s32[24,8]{0,1:T(8,128)S(1)}, s32[24,8]{0,1:T(8,128)}, u32[]{:S(2)}) copy-start(s32[24,8]{0,1:T(8,128)} %param.23) | copy-start | bytes 2308
  20.9 6.2 %collective-permute-start.8 = (bf16[200,256]{1,0:T(8,128)(2,1)S(1)}, bf16[200,256]{1,0:T(8,128)(2,1)S(1)}, u32[]{:S(2)}, u32[]{:S(2)}) collective-permute-start(bf16[200,256]{1,0:T(8,128)(2,1)S(1)} %get-tuple-element.41), channel_id=1, source_target_pairs={{0,6},{2,0},{4,2},{6,4},{1,7},{3,1},{5,3},{7,5},{8,14},{10,8},{12,... | collective-permute-start | bytes 307208 | tf_op jit(solution)/shard_map/ppermute | solution.py:538
  21.9 7.2 %collective-permute-start.9 = (bf16[200,256]{1,0:T(8,128)(2,1)S(1)}, bf16[200,256]{1,0:T(8,128)(2,1)S(1)}, u32[]{:S(2)}, u32[]{:S(2)}) collective-permute-start(bf16[200,256]{1,0:T(8,128)(2,1)S(1)} %get-tuple-element.42), channel_id=1, source_target_pairs={{0,4},{2,6},{4,0},{6,2},{1,5},{3,7},{5,1},{7,3},{8,12},{10,14},{12... | collective-permute-start | bytes 307208 | tf_op jit(solution)/shard_map/ppermute | solution.py:538
  22.2 8.3 %collective-permute-start.10 = (bf16[200,256]{1,0:T(8,128)(2,1)S(1)}, bf16[200,256]{1,0:T(8,128)(2,1)S(1)}, u32[]{:S(2)}, u32[]{:S(2)}) collective-permute-start(bf16[200,256]{1,0:T(8,128)(2,1)S(1)} %get-tuple-element.43), channel_id=1, source_target_pairs={{0,2},{2,4},{4,6},{6,0},{1,3},{3,5},{5,7},{7,1},{8,10},{10,12},{12... | collective-permute-start | bytes 307208 | tf_op jit(solution)/shard_map/ppermute | solution.py:538
  31.4 10.7 %copy-start.3 = (bf16[2048]{0:T(1024)(128)(2,1)S(1)}, bf16[2048]{0:T(1024)(128)(2,1)}, u32[]{:S(2)}) copy-start(bf16[2048]{0:T(1024)(128)(2,1)} %refs_5_.1) | copy-start | bytes 12292
  31.4 1.8 %collective-permute-start.11 = (bf16[96,2048]{1,0:T(8,128)(2,1)S(1)}, bf16[96,2048]{1,0:T(8,128)(2,1)S(1)}, u32[]{:S(2)}, u32[]{:S(2)}) collective-permute-start(bf16[96,2048]{1,0:T(8,128)(2,1)S(1)} %get-tuple-element.47), channel_id=1, source_target_pairs={{0,1},{1,0},{2,3},{3,2},{4,5},{5,4},{6,7},{7,6},{8,9},{9,8},{10,11... | collective-permute-start | bytes 1179656 | tf_op jit(solution)/shard_map/ppermute | solution.py:541
  33.3 5.7 %collective-permute-start.12 = (bf16[24,2048]{1,0:T(8,128)(2,1)S(1)}, bf16[24,2048]{1,0:T(8,128)(2,1)S(1)}, u32[]{:S(2)}, u32[]{:S(2)}) collective-permute-start(bf16[24,2048]{1,0:T(8,128)(2,1)S(1)} %get-tuple-element.49), channel_id=1, source_target_pairs={{0,6},{2,0},{4,2},{6,4},{1,7},{3,1},{5,3},{7,5},{8,14},{10,8},{12,... | collective-permute-start | bytes 294920 | tf_op jit(solution)/shard_map/ppermute | solution.py:538
  34.0 6.5 %collective-permute-start.13 = (bf16[24,2048]{1,0:T(8,128)(2,1)S(1)}, bf16[24,2048]{1,0:T(8,128)(2,1)S(1)}, u32[]{:S(2)}, u32[]{:S(2)}) collective-permute-start(bf16[24,2048]{1,0:T(8,128)(2,1)S(1)} %get-tuple-element.50), channel_id=1, source_target_pairs={{0,4},{2,6},{4,0},{6,2},{1,5},{3,7},{5,1},{7,3},{8,12},{10,14},{12... | collective-permute-start | bytes 294920 | tf_op jit(solution)/shard_map/ppermute | solution.py:538
  34.4 7.7 %collective-permute-start.14 = (bf16[24,2048]{1,0:T(8,128)(2,1)S(1)}, bf16[24,2048]{1,0:T(8,128)(2,1)S(1)}, u32[]{:S(2)}, u32[]{:S(2)}) collective-permute-start(bf16[24,2048]{1,0:T(8,128)(2,1)S(1)} %get-tuple-element.51), channel_id=1, source_target_pairs={{0,2},{2,4},{4,6},{6,0},{1,3},{3,5},{5,7},{7,1},{8,10},{10,12},{12... | collective-permute-start | bytes 294920 | tf_op jit(solution)/shard_map/ppermute | solution.py:538
  35.4 40.4 %copy-start.7 = (bf16[2048,64]{0,1:T(8,128)(2,1)S(1)}, bf16[2048,64]{0,1:T(8,128)(2,1)}, u32[]{:S(2)}) copy-start(bf16[2048,64]{0,1:T(8,128)(2,1)} %param.22) | copy-start | bytes 786436
  42.1 33.7 %collective-permute-start.15 = (bf16[3072,1024]{1,0:T(8,128)(2,1)S(1)}, bf16[3072,1024]{1,0:T(8,128)(2,1)S(1)}, u32[]{:S(2)}, u32[]{:S(2)}) collective-permute-start(bf16[3072,1024]{1,0:T(8,128)(2,1)S(1)} %get-tuple-element.59.weights_ref), channel_id=1, source_target_pairs={{0,1},{1,0},{2,3},{3,2},{4,5},{5,4},{6,7},{7,6},{8,9},{9,8},{10,11... | collective-permute-start | bytes 18874376 | tf_op jit(solution)/shard_map/ppermute | solution.py:541

commit v9 on v7

--- a/solution.py
+++ b/solution.py
@@ -66,7 +66,7 @@
     return (values * inverse * gain).astype(BF16)
 
 
-def query_kernel(x_hbm, g_hbm, w_hbm, q_ref, x_ref, g_ref, w_ref, sems):
+def query_kernel(x_hbm, g_hbm, w_hbm, q_ref, normed_ref, x_ref, g_ref, w_ref, sems):
     x_copy = pltpu.make_async_copy(x_hbm, x_ref, sems.at[0])
     w_copy = pltpu.make_async_copy(w_hbm.at[0], w_ref, sems.at[1])
     g_copy = pltpu.make_async_copy(g_hbm, g_ref, sems.at[2])
@@ -75,38 +75,33 @@
     w_copy.start()
     g_copy.wait()
     x_copy.wait()
-    normed = normed_rows(x_ref[...].astype(F32), g_ref[...].astype(F32).reshape(1, -1))
+    gain = g_ref[...].astype(F32).reshape(1, -1)
+    normed_ref[...] = normed_rows(x_ref[...].astype(F32), gain)
     w_copy.wait()
-    q_ref[...] = dot(normed, w_ref[...]).astype(BF16)
-
-
-def load_kernel(k_hbm, v_hbm, after_ref, k_ref, v_ref, sems):
+    q_ref[...] = dot(normed_ref[...], w_ref[...]).astype(BF16)
+
+
+def load_kernel(
+    k_hbm, v_hbm, up_hbm, after_ref, k_ref, v_ref, visible_ref, up_ref, sems
+):
     del after_ref
+    up_copy = pltpu.make_async_copy(up_hbm, up_ref, sems.at[2])
+    up_copy.start()
     copies = [
         pltpu.make_async_copy(k_hbm, k_ref, sems.at[0]),
         pltpu.make_async_copy(v_hbm, v_ref, sems.at[1]),
     ]
     for copy in copies:
         copy.start()
+    up_copy.wait()
+    visible_ref[...] = ancestors(up_ref)
     for copy in copies:
         copy.wait()
 
 
-def tree_kernel(scale, x_ref, g_ref, w_hbm, q_ref, up_ref, after_ref, *refs):
-    o_ref, lse_ref, turn, w_ref, sems = refs
-    del after_ref
-    tokens, width = q_ref.shape
-    w_copies = [
-        pltpu.make_async_copy(w_hbm.at[i + 1], w_ref.at[i], sems.at[i]) for i in range(2)
-    ]
-    for w_copy in w_copies:
-        w_copy.start()
-    normed = normed_rows(x_ref[...].astype(F32), g_ref[...].astype(F32).reshape(1, -1))
-    w_copies[0].wait()
-    keys = dot(normed, w_ref[0]).astype(BF16)
-    w_copies[1].wait()
-    values = dot(normed, w_ref[1]).astype(BF16)
+def ancestors(up_ref):
     requests, tree = up_ref.shape
+    tokens = requests * tree
     spread = iota((tree, tokens), 0) == iota((tree, tokens), 1) % tree
     wide = dot(up_ref[...].astype(BF16), jnp.where(spread, 1.0, 0.0).astype(BF16))
     home = iota((requests, tokens), 1) // tree
@@ -115,10 +110,20 @@
     row = iota((tokens, tokens), 0)
     same = row == iota((tokens, tokens), 1)
     reach = jnp.where(same | (row.astype(F32) == parent), 1.0, 0.0)
-    for _ in range(6):
+    for _ in range((tree - 1).bit_length()):
         half = reach.astype(BF16)
         reach = jnp.minimum(dot(half, half), 1.0)
-    visible = dot_t(jnp.where(same, 1.0, 0.0).astype(BF16), reach.astype(BF16)) > 0.5
+    return dot_t(jnp.where(same, 1.0, 0.0).astype(BF16), reach.astype(BF16))
+
+
+def tree_kernel(
+    scale, normed_ref, w_ref, q_ref, visible_ref, after_ref, o_ref, lse_ref, turn
+):
+    del after_ref
+    tokens, width = q_ref.shape
+    keys = dot(normed_ref[...], w_ref[0]).astype(BF16)
+    values = dot(normed_ref[...], w_ref[1]).astype(BF16)
+    visible = visible_ref[...] > 0.5
     lane = iota((tokens, 128), 1)
     stats = jnp.zeros((tokens, 128), F32)
     for h in range(width // HEAD_DIM):
@@ -136,9 +141,17 @@
 
 def page_kernel(scale, tree, kept, lengths_ref, *refs):
     pieces, (k_ref, v_ref) = refs[:4], refs[4:6]
-    outs = refs[7:-2] if kept else refs[6:-2]
-    s_all, p_all = refs[-2:]
+    outs = refs[7:-2] if kept else refs[7:-3]
+    s_all, p_all = refs[-2:] if kept else refs[-3:-1]
     out_ref = outs[0]
+    w_copies = []
+    if not kept:
+        w_hbm, sems = refs[6], refs[-1]
+        for i in range(2):
+            w_copies.append(
+                pltpu.make_async_copy(w_hbm.at[i + 1], outs[1].at[i], sems.at[i])
+            )
+            w_copies[i].start()
     requests, page = k_ref.shape[0], k_ref.shape[1]
     width = pieces[0].shape[1]
     pair = 2 * tree
@@ -190,6 +203,8 @@
             outs[1][rows, :] = stats
         else:
             out_ref[8, rows, :] = stats.astype(BF16)
+    for w_copy in w_copies:
+        w_copy.wait()
 
 
 def merge_kernel(other_ref, kept_ref, lse_ref, *refs):
@@ -493,9 +508,9 @@
     cache_keys = pltpu.with_memory_space_constraint(cache_keys, HBM)
     cache_values = pltpu.with_memory_space_constraint(cache_values, HBM)
 
-    query = call(
+    query, normed_attn = call(
         query_kernel,
-        sds((tokens, local_width), BF16),
+        (sds((tokens, local_width), BF16), sds((tokens, width), BF16)),
         [HBM, HBM, HBM],
         [
             pltpu.VMEM((tokens, width), BF16),
@@ -519,14 +534,23 @@
 
     steps = range(1, z_count)
     pieces = [query] + [over_z(query, step) for step in steps]
-    keys, values = call(
+    keys, values, visible = call(
         load_kernel,
-        (sds(cache_keys.shape, BF16), sds(cache_values.shape, BF16)),
-        [HBM, HBM, pl.ANY],
-        [pltpu.SemaphoreType.DMA((2,))],
+        (
+            sds(cache_keys.shape, BF16),
+            sds(cache_values.shape, BF16),
+            sds((tokens, tokens), F32),
+        ),
+        [HBM, HBM, HBM, pl.ANY],
+        [pltpu.VMEM(parents.shape, jnp.int32), pltpu.SemaphoreType.DMA((3,))],
         bytes_accessed=4 * requests * page * width,
         vmem=16 << 20,
-    )(cache_keys, cache_values, query)
+    )(
+        cache_keys,
+        cache_values,
+        pltpu.with_memory_space_constraint(parents, HBM),
+        query,
+    )
     pieces[0], keys = lax.optimization_barrier((pieces[0], keys))
     other_pieces = [over_core(piece) for piece in pieces]
 
@@ -536,15 +560,15 @@
     ]
     heads = 2 * z_count
     lengths = cache_lengths.reshape(1, requests)
-    for_other = call(
+    for_other, w_pair = call(
         functools.partial(page_kernel, scale, tree, False),
-        sds((heads + 1, tokens, HEAD_DIM), BF16),
-        [VMEM] * 7,
-        scratch,
+        (sds((heads + 1, tokens, HEAD_DIM), BF16), sds((2, width, local_width), BF16)),
+        [VMEM] * 7 + [HBM],
+        scratch + [pltpu.SemaphoreType.DMA((2,))],
         flops=2 * tokens * page * width,
         bytes_accessed=2 * requests * page * width,
         vmem=20 << 20,
-    )(lengths, *other_pieces, keys, values)
+    )(lengths, *other_pieces, keys, values, w_three)
     from_other = over_core(for_other)
     kept, kept_lse = call(
         functools.partial(page_kernel, scale, tree, True),
@@ -567,15 +591,11 @@
     tree_o, tree_lse = call(
         functools.partial(tree_kernel, scale),
         (sds((tokens, local_width), F32), sds((8, 256), F32)),
-        [VMEM, VMEM, HBM, VMEM, VMEM, pl.ANY],
-        [
-            pltpu.VMEM((256, 128), F32),
-            pltpu.VMEM((2, width, local_width), BF16),
-            pltpu.SemaphoreType.DMA((2,)),
-        ],
+        [VMEM] * 4 + [pl.ANY],
+        [pltpu.VMEM((256, 128), F32)],
         flops=4 * tokens * width * local_width,
         bytes_accessed=2 * width * (tokens + 2 * local_width),
-    )(hidden, gain_attn, w_three, query, parents, merged[0])
+    )(normed_attn, w_pair, query, visible, merged[0])
     theirs, ours = call(
         out_kernel,
         (sds((z_count * own, width), BF16), sds((z_count * own, width), F32)),

time: 112 us -> 112 us (level)
  waiting for transfers between devices: 11.2 us -> 13.9 us
  Pallas kernels: 26.1 us -> 23.9 us
    pallas_call x1, Pallas kernels: 3.83 us -> 1.02 us  [per_device(): call(functools.partial(tree_kernel, scale), (sds((tokens, local_width), F...]
    ppermute x9, waiting for transfers between devices: 7.96 us -> 10.7 us  [over_z(): lax.ppermute(value, 'z', [(i, (i + step) % z_count) for i in range(z_coun...]
  transfers between devices with their start and end apart: 16 -> 16, of which waited for: 10 -> 11; matrix products, arithmetic and copies ran while one was open for 0% -> 0% of each run, Pallas kernels for 11% -> 9%
where the time goes in v9:
time: 112 us
  blocking collectives  62.3 us (56%)
  Pallas kernels  23.9 us (21%)
  waiting for transfers between devices  13.9 us (12%)
  starting transfers between devices  11.7 us (10%)
    all_to_all x1, blocking collectives, per_device(): lax.all_to_all(outgoing.reshape(experts, SLOTS, packed), ('req', 'z'), sp...  33.7 us
    all_to_all x1, blocking collectives, per_device(): lax.all_to_all(summed.reshape(experts, SLOTS, packed), ('req', 'z'), spli...  28.6 us
    ppermute x9, starting transfers between devices, over_z(): lax.ppermute(value, 'z', [(i, (i + step) % z_count) for i in range(z_coun...  10.8 us
    ppermute x9, waiting for transfers between devices, over_z(): lax.ppermute(value, 'z', [(i, (i + step) % z_count) for i in range(z_coun...  10.7 us
    pallas_call x1, Pallas kernels, per_device(): call(expert_kernel, (sds((experts * SLOTS, packed), BF16), sds((chunks, 4...  7.36 us
    pallas_call x1, Pallas kernels, per_device(): call(load_kernel, (sds(cache_keys.shape, BF16), sds(cache_values.shape, B...  3.5 us
    pallas_call x1, Pallas kernels, per_device(): call(table_kernel, (sds((chunks, experts * SLOTS, 2 * own), BF16), sds((1...  3.24 us
    ppermute x7, waiting for transfers between devices, over_core(): return lax.ppermute(value, 'core', [(0, 1), (1, 0)])  3.23 us
  transfers between devices with their start and end apart: 16, of which 11 were waited for; matrix products, arithmetic and copies ran while one was open for 0% of the time, Pallas kernels for 9%

profile of v9, /device:TPU:0, one launch (start us, length us, event | category | flops | bytes accessed | tf_op | source)
XLA Modules:
  0.0 112.1 jit_solution(13918427100899598123)
XLA Ops:
  0.0 1.9 %shard_map.127 = (bf16[192,256]{1,0:T(8,128)(2,1)S(1)}, bf16[192,2048]{1,0:T(8,128)(2,1)S(1)}) custom-call(bf16[192,2048]{1,0:T(8,128)(2,1)} %refs_4_.1, bf16[2048]{0:T(1024)(128)(2,1)} %g_hbm.1, bf16[3,2048,256]{2,1,0:T(8,128)(2,1)} %bitcast.19), custom_call_target="tpu_custom_call" | custom-call | flops 201326592 | bytes 1835008 | tf_op jit(solution)/shard_map/pallas_call | solution.py:511
  1.9 0.0 copy-start.4
  1.9 4.2 %collective-permute-start.5 = (bf16[192,256]{1,0:T(8,128)(2,1)S(1)}, bf16[192,256]{1,0:T(8,128)(2,1)S(1)}, u32[]{:S(2)}, u32[]{:S(2)}) collective-permute-start(bf16[192,256]{1,0:T(8,128)(2,1)S(1)} %get-tuple-element.44.after_ref.refs_0_.q_ref), channel_id=1, source_target_pairs={{0,6},{2,0},{4,2},{6,4},{1,7},{3,1},{5,3},{7,5},{8,14},{10,8},{12,... | collective-permute-start | bytes 294920 | tf_op jit(solution)/shard_map/ppermute | solution.py:530
  6.1 0.0 collective-permute-start.3
  6.1 1.3 %collective-permute-start.1 = (bf16[192,256]{1,0:T(8,128)(2,1)S(1)}, bf16[192,256]{1,0:T(8,128)(2,1)S(1)}, u32[]{:S(2)}, u32[]{:S(2)}) collective-permute-start(bf16[192,256]{1,0:T(8,128)(2,1)S(1)} %get-tuple-element.44.after_ref.refs_0_.q_ref), channel_id=1, source_target_pairs={{0,2},{2,4},{4,6},{6,0},{1,3},{3,5},{5,7},{7,1},{8,10},{10,12},{12... | collective-permute-start | bytes 294920 | tf_op jit(solution)/shard_map/ppermute | solution.py:530
  7.4 3.5 %shard_map.128 = (bf16[4,256,2048]{2,1,0:T(8,128)(2,1)S(1)}, bf16[4,256,2048]{2,1,0:T(8,128)(2,1)S(1)}, f32[192,192]{1,0:T(8,128)S(1)}) custom-call(bf16[4,256,2048]{2,1,0:T(8,128)(2,1)} %k_hbm.1, bf16[4,256,2048]{2,1,0:T(8,128)(2,1)} %v_hbm.1, s32[4,48]{1,0:T(4,128)} %up_hbm.1, bf16[192,256]{1,0:T(8,128)(2,1)S(1)} %get-tuple-element.44.after_ref.refs_0_.q_ref), custom_call_target="tpu_custom_call" | custom-call | bytes 8388608 | tf_op jit(solution)/shard_map/pallas_call | solution.py:537
  10.9 0.1 collective-permute-start
  11.0 0.5 collective-permute-start.6
  11.5 1.5 %collective-permute-done.3.refs_2_ = bf16[192,256]{1,0:T(8,128)(2,1)S(1)} collective-permute-done((bf16[192,256]{1,0:T(8,128)(2,1)S(1)}, bf16[192,256]{1,0:T(8,128)(2,1)S(1)}, u32[]{:S(2)}, u32[]{:S(2)}) %collective-permute-start.3) | collective-permute-done | bytes 98336 | tf_op jit(solution)/shard_map/ppermute | solution.py:530
  13.0 0.0 collective-permute-start.4
  13.0 0.7 collective-permute-done.1.refs_1_
  13.7 0.0 collective-permute-start.2
  13.7 0.0 collective-permute-done.refs_0_
  13.7 0.0 collective-permute-done.6.refs_3_
  13.7 0.6 collective-permute-done.4.refs_2_
  14.3 0.7 collective-permute-done.2.refs_1_
  15.0 2.0 %shard_map.129 = (bf16[9,192,128]{2,1,0:T(8,128)(2,1)S(1)}, bf16[2,2048,256]{2,1,0:T(8,128)(2,1)S(1)}) custom-call(s32[1,4]{1,0:T(1,128)S(1)} %bitcast.16, bf16[192,256]{1,0:T(8,128)(2,1)S(1)} %collective-permute-done.refs_0_, bf16[192,256]{1,0:T(8,128)(2,1)S(1)} %collective-permute-done.2.refs_1_, bf16[192,256]{1,0:T(8,128)(2,1)S(1)} %collective-permute-done.4.refs_2_, ...), custom_call_target="tpu_custom_call" | custom-call | flops 201326592 | bytes 4194304 | tf_op jit(solution)/shard_map/pallas_call | solution.py:563
  17.0 0.2 collective-permute-start.7
  17.2 1.4 %shard_map.130 = (f32[8,192,128]{2,1,0:T(8,128)S(1)}, f32[192,128]{1,0:T(8,128)S(1)}) custom-call(s32[1,4]{1,0:T(1,128)S(1)} %bitcast.17, bf16[192,256]{1,0:T(8,128)(2,1)S(1)} %get-tuple-element.44.after_ref.refs_0_.q_ref, bf16[192,256]{1,0:T(8,128)(2,1)S(1)} %collective-permute-done.1.refs_1_, bf16[192,256]{1,0:T(8,128)(2,1)S(1)} %collective-permute-done.3.refs_2_, ...), custom_call_target="tpu_custom_call" | custom-call | flops 201326592 | bytes 4194304 | tf_op jit(solution)/shard_map/pallas_call | solution.py:573
  18.6 0.0 copy-start.1
  18.6 0.0 copy-start.3
  18.6 0.2 collective-permute-done.7.other_ref
  18.8 0.7 shard_map.131
  19.6 1.0 collective-permute-start.8
  20.5 1.4 %collective-permute-start.9 = (bf16[200,256]{1,0:T(8,128)(2,1)S(1)}, bf16[200,256]{1,0:T(8,128)(2,1)S(1)}, u32[]{:S(2)}, u32[]{:S(2)}) collective-permute-start(bf16[200,256]{1,0:T(8,128)(2,1)S(1)} %get-tuple-element.52), channel_id=1, source_target_pairs={{0,4},{2,6},{4,0},{6,2},{1,5},{3,7},{5,1},{7,3},{8,12},{10,14},{12... | collective-permute-start | bytes 307208 | tf_op jit(solution)/shard_map/ppermute | solution.py:530
  21.9 0.0 collective-permute-start.10
  21.9 1.0 shard_map.132
  22.9 2.4 %collective-permute-done.8.refs_1_ = bf16[200,256]{1,0:T(8,128)(2,1)S(1)} collective-permute-done((bf16[200,256]{1,0:T(8,128)(2,1)S(1)}, bf16[200,256]{1,0:T(8,128)(2,1)S(1)}, u32[]{:S(2)}, u32[]{:S(2)}) %collective-permute-start.8) | collective-permute-done | bytes 102432 | tf_op jit(solution)/shard_map/ppermute | solution.py:530
  25.4 2.2 %collective-permute-done.9.refs_2_ = bf16[200,256]{1,0:T(8,128)(2,1)S(1)} collective-permute-done((bf16[200,256]{1,0:T(8,128)(2,1)S(1)}, bf16[200,256]{1,0:T(8,128)(2,1)S(1)}, u32[]{:S(2)}, u32[]{:S(2)}) %collective-permute-start.9) | collective-permute-done | bytes 102432 | tf_op jit(solution)/shard_map/ppermute | solution.py:530
  27.5 1.4 %collective-permute-done.10.refs_3_ = bf16[200,256]{1,0:T(8,128)(2,1)S(1)} collective-permute-done((bf16[200,256]{1,0:T(8,128)(2,1)S(1)}, bf16[200,256]{1,0:T(8,128)(2,1)S(1)}, u32[]{:S(2)}, u32[]{:S(2)}) %collective-permute-start.10) | collective-permute-done | bytes 102432 | tf_op jit(solution)/shard_map/ppermute | solution.py:530
  28.9 0.9 shard_map.133
  29.8 0.0 copy-start
  29.8 0.0 copy-start.2
  29.9 0.1 collective-permute-start.11
  29.9 1.7 %collective-permute-done.11.theirs_ref = bf16[96,2048]{1,0:T(8,128)(2,1)S(1)} collective-permute-done((bf16[96,2048]{1,0:T(8,128)(2,1)S(1)}, bf16[96,2048]{1,0:T(8,128)(2,1)S(1)}, u32[]{:S(2)}, u32[]{:S(2)}) %collective-permute-start.11) | collective-permute-done | bytes 393248 | tf_op jit(solution)/shard_map/ppermute | solution.py:533
  31.7 0.1 shard_map.134
  31.8 0.6 collective-permute-start.12
  32.4 1.5 %collective-permute-start.13 = (bf16[24,2048]{1,0:T(8,128)(2,1)S(1)}, bf16[24,2048]{1,0:T(8,128)(2,1)S(1)}, u32[]{:S(2)}, u32[]{:S(2)}) collective-permute-start(bf16[24,2048]{1,0:T(8,128)(2,1)S(1)} %get-tuple-element.63), channel_id=1, source_target_pairs={{0,4},{2,6},{4,0},{6,2},{1,5},{3,7},{5,1},{7,3},{8,12},{10,14},{12... | collective-permute-start | bytes 294920 | tf_op jit(solution)/shard_map/ppermute | solution.py:530
  33.9 0.9 collective-permute-start.14
  34.8 3.2 %shard_map.135 = (bf16[3,512,48]{2,1,0:T(8,128)(2,1)S(1)}, bf16[4,192,256]{2,1,0:T(8,128)(2,1)S(1)}, bf16[3,256,384]{2,1,0:T(8,128)(2,1)S(1)}, bf16[3072,1024]{1,0:T(8,128)(2,1)S(1)}) custom-call(s32[8,24]{1,0:T(8,128)S(1)} %bitcast.14, bf16[2048,1024]{1,0:T(8,128)(2,1)} %bitcast.21, bf16[512,2048]{1,0:T(8,128)(2,1)} %bitcast.22, ...), custom_call_target="tpu_custom_call" | custom-call | flops 16777216 | bytes 8388608 | tf_op jit(solution)/shard_map/pallas_call | solution.py:617
  38.0 0.0 collective-permute-done.12.refs_1_
  38.1 0.9 collective-permute-done.13.refs_2_
  38.9 1.6 %collective-permute-done.14.refs_3_ = bf16[24,2048]{1,0:T(8,128)(2,1)S(1)} collective-permute-done((bf16[24,2048]{1,0:T(8,128)(2,1)S(1)}, bf16[24,2048]{1,0:T(8,128)(2,1)S(1)}, u32[]{:S(2)}, u32[]{:S(2)}) %collective-permute-start.14) | collective-permute-done | bytes 98336 | tf_op jit(solution)/shard_map/ppermute | solution.py:530
  40.6 0.7 shard_map.136
  41.3 33.7 %all_to_all.10 = bf16[64,8,1536]{2,1,0:T(8,128)(2,1)S(1)} all-to-all(bf16[64,8,1536]{2,1,0:T(8,128)(2,1)S(1)} %bitcast.12), channel_id=1, replica_groups=mesh['req'=16,'z'=4,'core'=2] {'req','z'}, dimensions={0} | all-to-all | bytes 3145728 | tf_op jit(solution)/shard_map/all_to_all | solution.py:650
  75.0 7.4 %shard_map.137 = (bf16[512,1536]{1,0:T(8,128)(2,1)S(1)}, bf16[3,96,512]{2,1,0:T(8,128)(2,1)S(1)}) custom-call(bf16[512,1536]{1,0:T(8,128)(2,1)S(1)} %bitcast.11, bf16[3072,1024]{1,0:T(8,128)(2,1)S(1)} %get-tuple-element.72.weights_ref, bf16[3072,1024]{1,0:T(8,128)(2,1)S(1)} %collective-permute-done.15.other_ref, ...), custom_call_target="tpu_custom_call" | custom-call | flops 4831838208 | bytes 12582912 | tf_op jit(solution)/shard_map/pallas_call | solution.py:658
  82.4 28.6 %all_to_all.11 = bf16[64,8,1536]{2,1,0:T(8,128)(2,1)S(1)} all-to-all(bf16[64,8,1536]{2,1,0:T(8,128)(2,1)S(1)} %bitcast.13), channel_id=1, replica_groups=mesh['req'=16,'z'=4,'core'=2] {'req','z'}, dimensions={0} | all-to-all | bytes 3145728 | tf_op jit(solution)/shard_map/all_to_all | solution.py:678
  111.0 1.0 shard_map.138
  (10 shorter events, 0.0 us)
Async XLA Ops:
  1.9 13.1 %copy-start.4 = (s32[4]{0:T(128)S(1)}, s32[4]{0:T(128)}, u32[]{:S(2)}) copy-start(s32[4]{0:T(128)} %param.19) | copy-start | bytes 52
  1.9 9.1 %collective-permute-start.5 = (bf16[192,256]{1,0:T(8,128)(2,1)S(1)}, bf16[192,256]{1,0:T(8,128)(2,1)S(1)}, u32[]{:S(2)}, u32[]{:S(2)}) collective-permute-start(bf16[192,256]{1,0:T(8,128)(2,1)S(1)} %get-tuple-element.44.after_ref.refs_0_.q_ref), channel_id=1, source_target_pairs={{0,6},{2,0},{4,2},{6,4},{1,7},{3,1},{5,3},{7,5},{8,14},{10,8},{12,... | collective-permute-start | bytes 294920 | tf_op jit(solution)/shard_map/ppermute | solution.py:530
  6.1 6.9 %collective-permute-start.3 = (bf16[192,256]{1,0:T(8,128)(2,1)S(1)}, bf16[192,256]{1,0:T(8,128)(2,1)S(1)}, u32[]{:S(2)}, u32[]{:S(2)}) collective-permute-start(bf16[192,256]{1,0:T(8,128)(2,1)S(1)} %get-tuple-element.44.after_ref.refs_0_.q_ref), channel_id=1, source_target_pairs={{0,4},{2,6},{4,0},{6,2},{1,5},{3,7},{5,1},{7,3},{8,12},{10,14},{12... | collective-permute-start | bytes 294920 | tf_op jit(solution)/shard_map/ppermute | solution.py:530
  6.1 7.6 %collective-permute-start.1 = (bf16[192,256]{1,0:T(8,128)(2,1)S(1)}, bf16[192,256]{1,0:T(8,128)(2,1)S(1)}, u32[]{:S(2)}, u32[]{:S(2)}) collective-permute-start(bf16[192,256]{1,0:T(8,128)(2,1)S(1)} %get-tuple-element.44.after_ref.refs_0_.q_ref), channel_id=1, source_target_pairs={{0,2},{2,4},{4,6},{6,0},{1,3},{3,5},{5,7},{7,1},{8,10},{10,12},{12... | collective-permute-start | bytes 294920 | tf_op jit(solution)/shard_map/ppermute | solution.py:530
  10.9 2.8 %collective-permute-start = (bf16[192,256]{1,0:T(8,128)(2,1)S(1)}, bf16[192,256]{1,0:T(8,128)(2,1)S(1)}, u32[]{:S(2)}, u32[]{:S(2)}) collective-permute-start(bf16[192,256]{1,0:T(8,128)(2,1)S(1)} %get-tuple-element.44.after_ref.refs_0_.q_ref), channel_id=1, source_target_pairs={{0,1},{1,0},{2,3},{3,2},{4,5},{5,4},{6,7},{7,6},{8,9},{9,8},{10,11... | collective-permute-start | bytes 294920 | tf_op jit(solution)/shard_map/ppermute | solution.py:533
  11.0 2.7 %collective-permute-start.6 = (bf16[192,256]{1,0:T(8,128)(2,1)S(1)}, bf16[192,256]{1,0:T(8,128)(2,1)S(1)}, u32[]{:S(2)}, u32[]{:S(2)}) collective-permute-start(bf16[192,256]{1,0:T(8,128)(2,1)S(1)} %collective-permute-done.5.refs_3_), channel_id=1, source_target_pairs={{0,1},{1,0},{2,3},{3,2},{4,5},{5,4},{6,7},{7,6},{8,9},{9,8},{10,11... | collective-permute-start | bytes 294920 | tf_op jit(solution)/shard_map/ppermute | solution.py:533
  13.0 1.3 %collective-permute-start.4 = (bf16[192,256]{1,0:T(8,128)(2,1)S(1)}, bf16[192,256]{1,0:T(8,128)(2,1)S(1)}, u32[]{:S(2)}, u32[]{:S(2)}) collective-permute-start(bf16[192,256]{1,0:T(8,128)(2,1)S(1)} %collective-permute-done.3.refs_2_), channel_id=1, source_target_pairs={{0,1},{1,0},{2,3},{3,2},{4,5},{5,4},{6,7},{7,6},{8,9},{9,8},{10,11... | collective-permute-start | bytes 294920 | tf_op jit(solution)/shard_map/ppermute | solution.py:533
  13.7 1.3 %collective-permute-start.2 = (bf16[192,256]{1,0:T(8,128)(2,1)S(1)}, bf16[192,256]{1,0:T(8,128)(2,1)S(1)}, u32[]{:S(2)}, u32[]{:S(2)}) collective-permute-start(bf16[192,256]{1,0:T(8,128)(2,1)S(1)} %collective-permute-done.1.refs_1_), channel_id=1, source_target_pairs={{0,1},{1,0},{2,3},{3,2},{4,5},{5,4},{6,7},{7,6},{8,9},{9,8},{10,11... | collective-permute-start | bytes 294920 | tf_op jit(solution)/shard_map/ppermute | solution.py:533
  17.0 1.9 %collective-permute-start.7 = (bf16[9,192,128]{2,1,0:T(8,128)(2,1)S(1)}, bf16[9,192,128]{2,1,0:T(8,128)(2,1)S(1)}, u32[]{:S(2)}, u32[]{:S(2)}) collective-permute-start(bf16[9,192,128]{2,1,0:T(8,128)(2,1)S(1)} %get-tuple-element.47.refs_6_), channel_id=1, source_target_pairs={{0,1},{1,0},{2,3},{3,2},{4,5},{5,4},{6,7},{7,6},{8,9},{9,8},{10,11... | collective-permute-start | bytes 1327112 | tf_op jit(solution)/shard_map/ppermute | solution.py:533
  18.6 10.3 %copy-start.1 = (bf16[256,2048]{1,0:T(8,128)(2,1)S(1)}, bf16[256,2048]{1,0:T(8,128)(2,1)}, u32[]{:S(2)}) copy-start(bf16[256,2048]{1,0:T(8,128)(2,1)} %refs_6_.1) | copy-start | bytes 3145732
  18.6 16.2 %copy-start.3 = (s32[24,8]{0,1:T(8,128)S(1)}, s32[24,8]{0,1:T(8,128)}, u32[]{:S(2)}) copy-start(s32[24,8]{0,1:T(8,128)} %param.23) | copy-start | bytes 2308
  19.6 5.8 %collective-permute-start.8 = (bf16[200,256]{1,0:T(8,128)(2,1)S(1)}, bf16[200,256]{1,0:T(8,128)(2,1)S(1)}, u32[]{:S(2)}, u32[]{:S(2)}) collective-permute-start(bf16[200,256]{1,0:T(8,128)(2,1)S(1)} %get-tuple-element.51), channel_id=1, source_target_pairs={{0,6},{2,0},{4,2},{6,4},{1,7},{3,1},{5,3},{7,5},{8,14},{10,8},{12,... | collective-permute-start | bytes 307208 | tf_op jit(solution)/shard_map/ppermute | solution.py:530
  20.5 7.0 %collective-permute-start.9 = (bf16[200,256]{1,0:T(8,128)(2,1)S(1)}, bf16[200,256]{1,0:T(8,128)(2,1)S(1)}, u32[]{:S(2)}, u32[]{:S(2)}) collective-permute-start(bf16[200,256]{1,0:T(8,128)(2,1)S(1)} %get-tuple-element.52), channel_id=1, source_target_pairs={{0,4},{2,6},{4,0},{6,2},{1,5},{3,7},{5,1},{7,3},{8,12},{10,14},{12... | collective-permute-start | bytes 307208 | tf_op jit(solution)/shard_map/ppermute | solution.py:530
  21.9 7.0 %collective-permute-start.10 = (bf16[200,256]{1,0:T(8,128)(2,1)S(1)}, bf16[200,256]{1,0:T(8,128)(2,1)S(1)}, u32[]{:S(2)}, u32[]{:S(2)}) collective-permute-start(bf16[200,256]{1,0:T(8,128)(2,1)S(1)} %get-tuple-element.53), channel_id=1, source_target_pairs={{0,2},{2,4},{4,6},{6,0},{1,3},{3,5},{5,7},{7,1},{8,10},{10,12},{12... | collective-permute-start | bytes 307208 | tf_op jit(solution)/shard_map/ppermute | solution.py:530
  29.8 10.7 %copy-start = (bf16[192,2048]{1,0:T(8,128)(2,1)S(1)}, bf16[192,2048]{1,0:T(8,128)(2,1)}, u32[]{:S(2)}) copy-start(bf16[192,2048]{1,0:T(8,128)(2,1)} %refs_4_.1) | copy-start | bytes 2359300
  29.8 10.7 %copy-start.2 = (bf16[2048]{0:T(1024)(128)(2,1)S(1)}, bf16[2048]{0:T(1024)(128)(2,1)}, u32[]{:S(2)}) copy-start(bf16[2048]{0:T(1024)(128)(2,1)} %refs_5_.1) | copy-start | bytes 12292
  29.9 1.8 %collective-permute-start.11 = (bf16[96,2048]{1,0:T(8,128)(2,1)S(1)}, bf16[96,2048]{1,0:T(8,128)(2,1)S(1)}, u32[]{:S(2)}, u32[]{:S(2)}) collective-permute-start(bf16[96,2048]{1,0:T(8,128)(2,1)S(1)} %get-tuple-element.60), channel_id=1, source_target_pairs={{0,1},{1,0},{2,3},{3,2},{4,5},{5,4},{6,7},{7,6},{8,9},{9,8},{10,11... | collective-permute-start | bytes 1179656 | tf_op jit(solution)/shard_map/ppermute | solution.py:533
  31.8 6.3 %collective-permute-start.12 = (bf16[24,2048]{1,0:T(8,128)(2,1)S(1)}, bf16[24,2048]{1,0:T(8,128)(2,1)S(1)}, u32[]{:S(2)}, u32[]{:S(2)}) collective-permute-start(bf16[24,2048]{1,0:T(8,128)(2,1)S(1)} %get-tuple-element.62), channel_id=1, source_target_pairs={{0,6},{2,0},{4,2},{6,4},{1,7},{3,1},{5,3},{7,5},{8,14},{10,8},{12,... | collective-permute-start | bytes 294920 | tf_op jit(solution)/shard_map/ppermute | solution.py:530
  32.4 6.6 %collective-permute-start.13 = (bf16[24,2048]{1,0:T(8,128)(2,1)S(1)}, bf16[24,2048]{1,0:T(8,128)(2,1)S(1)}, u32[]{:S(2)}, u32[]{:S(2)}) collective-permute-start(bf16[24,2048]{1,0:T(8,128)(2,1)S(1)} %get-tuple-element.63), channel_id=1, source_target_pairs={{0,4},{2,6},{4,0},{6,2},{1,5},{3,7},{5,1},{7,3},{8,12},{10,14},{12... | collective-permute-start | bytes 294920 | tf_op jit(solution)/shard_map/ppermute | solution.py:530
  33.9 6.6 %collective-permute-start.14 = (bf16[24,2048]{1,0:T(8,128)(2,1)S(1)}, bf16[24,2048]{1,0:T(8,128)(2,1)S(1)}, u32[]{:S(2)}, u32[]{:S(2)}) collective-permute-start(bf16[24,2048]{1,0:T(8,128)(2,1)S(1)} %get-tuple-element.64), channel_id=1, source_target_pairs={{0,2},{2,4},{4,6},{6,0},{1,3},{3,5},{5,7},{7,1},{8,10},{10,12},{12... | collective-permute-start | bytes 294920 | tf_op jit(solution)/shard_map/ppermute | solution.py:530
  34.8 40.2 %copy-start.5 = (bf16[2048,64]{0,1:T(8,128)(2,1)S(1)}, bf16[2048,64]{0,1:T(8,128)(2,1)}, u32[]{:S(2)}) copy-start(bf16[2048,64]{0,1:T(8,128)(2,1)} %param.22) | copy-start | bytes 786436
  40.6 34.5 %collective-permute-start.15 = (bf16[3072,1024]{1,0:T(8,128)(2,1)S(1)}, bf16[3072,1024]{1,0:T(8,128)(2,1)S(1)}, u32[]{:S(2)}, u32[]{:S(2)}) collective-permute-start(bf16[3072,1024]{1,0:T(8,128)(2,1)S(1)} %get-tuple-element.72.weights_ref), channel_id=1, source_target_pairs={{0,1},{1,0},{2,3},{3,2},{4,5},{5,4},{6,7},{7,6},{8,9},{9,8},{10,11... | collective-permute-start | bytes 18874376 | tf_op jit(solution)/shard_map/ppermute | solution.py:533

commit v10 on v7

--- a/solution.py
+++ b/solution.py
@@ -517,8 +517,9 @@
     def over_core(value):
         return lax.ppermute(value, "core", [(0, 1), (1, 0)])
 
-    steps = range(1, z_count)
-    pieces = [query] + [over_z(query, step) for step in steps]
+    steps = sorted(range(1, z_count), key=lambda step: -min(step, z_count - step))
+
+    pieces = [query] + [over_z(query, step) for step in range(1, z_count)]
     keys, values = call(
         load_kernel,
         (sds(cache_keys.shape, BF16), sds(cache_values.shape, BF16)),

time: 112 us -> 110 us (0.982)
  no operation moved by 1% of the time
where the time goes in v10:
time: 110 us
  blocking collectives  61.6 us (56%)
  Pallas kernels  26.1 us (24%)
  starting transfers between devices  12 us (11%)
  waiting for transfers between devices  10.4 us (9%)
    all_to_all x1, blocking collectives, per_device(): lax.all_to_all(outgoing.reshape(experts, SLOTS, packed), ('req', 'z'), sp...  33 us
    all_to_all x1, blocking collectives, per_device(): lax.all_to_all(summed.reshape(experts, SLOTS, packed), ('req', 'z'), spli...  28.6 us
    ppermute x9, starting transfers between devices, over_z(): lax.ppermute(value, 'z', [(i, (i + step) % z_count) for i in range(z_coun...  11.1 us
    pallas_call x1, Pallas kernels, per_device(): call(expert_kernel, (sds((experts * SLOTS, packed), BF16), sds((chunks, 4...  7.35 us
    ppermute x9, waiting for transfers between devices, over_z(): lax.ppermute(value, 'z', [(i, (i + step) % z_count) for i in range(z_coun...  7.11 us
    pallas_call x1, Pallas kernels, per_device(): call(functools.partial(tree_kernel, scale), (sds((tokens, local_width), F...  3.83 us
    pallas_call x1, Pallas kernels, per_device(): call(load_kernel, (sds(cache_keys.shape, BF16), sds(cache_values.shape, B...  3.48 us
    ppermute x7, waiting for transfers between devices, over_core(): return lax.ppermute(value, 'core', [(0, 1), (1, 0)])  3.27 us
  transfers between devices with their start and end apart: 16, of which 10 were waited for; matrix products, arithmetic and copies ran while one was open for 0% of the time, Pallas kernels for 11%

profile of v10, /device:TPU:0, one launch (start us, length us, event | category | flops | bytes accessed | tf_op | source)
XLA Modules:
  0.0 110.2 jit_solution(7549343414388648644)
XLA Ops:
  0.0 1.9 %shard_map.127.after_ref.refs_0_.q_ref = bf16[192,256]{1,0:T(8,128)(2,1)S(1)} custom-call(bf16[192,2048]{1,0:T(8,128)(2,1)} %refs_4_.1, bf16[2048]{0:T(1024)(128)(2,1)} %g_ref.1, bf16[3,2048,256]{2,1,0:T(8,128)(2,1)} %bitcast.19), custom_call_target="tpu_custom_call" | custom-call | flops 201326592 | bytes 1835008 | tf_op jit(solution)/shard_map/pallas_call | solution.py:496
  1.9 0.0 copy-start.6
  1.9 4.2 %collective-permute-start.5 = (bf16[192,256]{1,0:T(8,128)(2,1)S(1)}, bf16[192,256]{1,0:T(8,128)(2,1)S(1)}, u32[]{:S(2)}, u32[]{:S(2)}) collective-permute-start(bf16[192,256]{1,0:T(8,128)(2,1)S(1)} %shard_map.127.after_ref.refs_0_.q_ref), channel_id=1, source_target_pairs={{0,6},{2,0},{4,2},{6,4},{1,7},{3,1},{5,3},{7,5},{8,14},{10,8},{12,... | collective-permute-start | bytes 294920 | tf_op jit(solution)/shard_map/ppermute | solution.py:515
  6.1 0.0 collective-permute-start.3
  6.1 1.3 %collective-permute-start.1 = (bf16[192,256]{1,0:T(8,128)(2,1)S(1)}, bf16[192,256]{1,0:T(8,128)(2,1)S(1)}, u32[]{:S(2)}, u32[]{:S(2)}) collective-permute-start(bf16[192,256]{1,0:T(8,128)(2,1)S(1)} %shard_map.127.after_ref.refs_0_.q_ref), channel_id=1, source_target_pairs={{0,2},{2,4},{4,6},{6,0},{1,3},{3,5},{5,7},{7,1},{8,10},{10,12},{12... | collective-permute-start | bytes 294920 | tf_op jit(solution)/shard_map/ppermute | solution.py:515
  7.4 3.5 %shard_map.128 = (bf16[4,256,2048]{2,1,0:T(8,128)(2,1)S(1)}, bf16[4,256,2048]{2,1,0:T(8,128)(2,1)S(1)}) custom-call(bf16[4,256,2048]{2,1,0:T(8,128)(2,1)} %k_hbm.1, bf16[4,256,2048]{2,1,0:T(8,128)(2,1)} %v_hbm.1, bf16[192,256]{1,0:T(8,128)(2,1)S(1)} %shard_map.127.after_ref.refs_0_.q_ref), custom_call_target="tpu_custom_call" | custom-call | bytes 8388608 | tf_op jit(solution)/shard_map/pallas_call | solution.py:523
  10.8 0.1 collective-permute-start
  10.9 0.0 collective-permute-done.5.refs_3_
  11.0 0.5 collective-permute-start.6
  11.4 1.5 %collective-permute-done.3.refs_2_ = bf16[192,256]{1,0:T(8,128)(2,1)S(1)} collective-permute-done((bf16[192,256]{1,0:T(8,128)(2,1)S(1)}, bf16[192,256]{1,0:T(8,128)(2,1)S(1)}, u32[]{:S(2)}, u32[]{:S(2)}) %collective-permute-start.3) | collective-permute-done | bytes 98336 | tf_op jit(solution)/shard_map/ppermute | solution.py:515
  13.0 0.0 collective-permute-start.4
  13.0 0.7 collective-permute-done.1.refs_1_
  13.7 0.6 collective-permute-done.4.refs_2_
  14.3 0.7 collective-permute-done.2.refs_1_
  15.0 1.5 %shard_map.129.refs_6_ = bf16[9,192,128]{2,1,0:T(8,128)(2,1)S(1)} custom-call(s32[1,4]{1,0:T(1,128)S(1)} %bitcast.16, bf16[192,256]{1,0:T(8,128)(2,1)S(1)} %collective-permute-done.refs_0_, bf16[192,256]{1,0:T(8,128)(2,1)S(1)} %collective-permute-done.2.refs_1_, bf16[192,256]{1,0:T(8,128)(2,1)S(1)} %collective-permute-done.4.refs_2_, ...), custom_call_target="tpu_custom_call" | custom-call | flops 201326592 | bytes 4194304 | tf_op jit(solution)/shard_map/pallas_call | solution.py:540
  16.4 0.0 copy-start
  16.4 0.0 copy-start.2
  16.5 0.0 copy-start.5
  16.5 0.2 collective-permute-start.7
  16.7 1.4 %shard_map.130 = (f32[8,192,128]{2,1,0:T(8,128)S(1)}, f32[192,128]{1,0:T(8,128)S(1)}) custom-call(s32[1,4]{1,0:T(1,128)S(1)} %bitcast.17, bf16[192,256]{1,0:T(8,128)(2,1)S(1)} %shard_map.127.after_ref.refs_0_.q_ref, bf16[192,256]{1,0:T(8,128)(2,1)S(1)} %collective-permute-done.1.refs_1_, bf16[192,256]{1,0:T(8,128)(2,1)S(1)} %collective-permute-done.3.refs_2_, ...), custom_call_target="tpu_custom_call" | custom-call | flops 201326592 | bytes 4194304 | tf_op jit(solution)/shard_map/pallas_call | solution.py:550
  18.1 0.0 copy-start.1
  18.1 0.0 copy-start.4
  18.1 0.3 collective-permute-done.7.other_ref
  18.3 0.7 shard_map.131
  19.1 0.9 collective-permute-start.8
  20.0 2.0 %collective-permute-start.9 = (bf16[200,256]{1,0:T(8,128)(2,1)S(1)}, bf16[200,256]{1,0:T(8,128)(2,1)S(1)}, u32[]{:S(2)}, u32[]{:S(2)}) collective-permute-start(bf16[200,256]{1,0:T(8,128)(2,1)S(1)} %get-tuple-element.45), channel_id=1, source_target_pairs={{0,6},{2,0},{4,2},{6,4},{1,7},{3,1},{5,3},{7,5},{8,14},{10,8},{12,... | collective-permute-start | bytes 307208 | tf_op jit(solution)/shard_map/ppermute | solution.py:515
  22.0 0.0 collective-permute-start.10
  22.0 3.8 %shard_map.132 = (f32[192,256]{1,0:T(8,128)S(1)}, f32[8,256]{1,0:T(8,128)S(1)}) custom-call(bf16[192,2048]{1,0:T(8,128)(2,1)S(1)} %copy-done, bf16[2048]{0:T(1024)(128)(2,1)S(1)} %copy-done.2, bf16[3,2048,256]{2,1,0:T(8,128)(2,1)} %bitcast.20, bf16[192,256]{1,0:T(8,128)(2,1)S(1)} %shard_map.127.after_ref.refs_0_.q_ref, s32[4,48]{1,0:T(4,128)S(1)} %copy-done.5, ...), custom_call_target="tpu_custom_call" | custom-call | flops 402653184 | bytes 2883584 | tf_op jit(solution)/shard_map/pallas_call | solution.py:568
  25.8 0.6 collective-permute-done.8.refs_1_
  26.4 1.8 %collective-permute-done.10.refs_3_ = bf16[200,256]{1,0:T(8,128)(2,1)S(1)} collective-permute-done((bf16[200,256]{1,0:T(8,128)(2,1)S(1)}, bf16[200,256]{1,0:T(8,128)(2,1)S(1)}, u32[]{:S(2)}, u32[]{:S(2)}) %collective-permute-start.10) | collective-permute-done | bytes 102432 | tf_op jit(solution)/shard_map/ppermute | solution.py:515
  28.2 0.9 shard_map.133
  29.1 0.0 copy-start.3
  29.1 0.1 collective-permute-start.11
  29.2 1.7 %collective-permute-done.11.theirs_ref = bf16[96,2048]{1,0:T(8,128)(2,1)S(1)} collective-permute-done((bf16[96,2048]{1,0:T(8,128)(2,1)S(1)}, bf16[96,2048]{1,0:T(8,128)(2,1)S(1)}, u32[]{:S(2)}, u32[]{:S(2)}) %collective-permute-start.11) | collective-permute-done | bytes 393248 | tf_op jit(solution)/shard_map/ppermute | solution.py:518
  30.9 0.1 shard_map.134
  31.0 0.7 collective-permute-start.12
  31.7 1.7 %collective-permute-start.13 = (bf16[24,2048]{1,0:T(8,128)(2,1)S(1)}, bf16[24,2048]{1,0:T(8,128)(2,1)S(1)}, u32[]{:S(2)}, u32[]{:S(2)}) collective-permute-start(bf16[24,2048]{1,0:T(8,128)(2,1)S(1)} %get-tuple-element.53), channel_id=1, source_target_pairs={{0,6},{2,0},{4,2},{6,4},{1,7},{3,1},{5,3},{7,5},{8,14},{10,8},{12,... | collective-permute-start | bytes 294920 | tf_op jit(solution)/shard_map/ppermute | solution.py:515
  33.4 0.4 collective-permute-start.14
  33.7 3.2 %shard_map.135 = (bf16[3,512,48]{2,1,0:T(8,128)(2,1)S(1)}, bf16[4,192,256]{2,1,0:T(8,128)(2,1)S(1)}, bf16[3,256,384]{2,1,0:T(8,128)(2,1)S(1)}, bf16[3072,1024]{1,0:T(8,128)(2,1)S(1)}) custom-call(s32[8,24]{1,0:T(8,128)S(1)} %bitcast.14, bf16[2048,1024]{1,0:T(8,128)(2,1)} %bitcast.21, bf16[512,2048]{1,0:T(8,128)(2,1)} %bitcast.22, ...), custom_call_target="tpu_custom_call" | custom-call | flops 16777216 | bytes 8388608 | tf_op jit(solution)/shard_map/pallas_call | solution.py:598
  37.0 1.1 %collective-permute-done.12.refs_1_ = bf16[24,2048]{1,0:T(8,128)(2,1)S(1)} collective-permute-done((bf16[24,2048]{1,0:T(8,128)(2,1)S(1)}, bf16[24,2048]{1,0:T(8,128)(2,1)S(1)}, u32[]{:S(2)}, u32[]{:S(2)}) %collective-permute-start.12) | collective-permute-done | bytes 98336 | tf_op jit(solution)/shard_map/ppermute | solution.py:515
  38.1 1.4 %collective-permute-done.14.refs_3_ = bf16[24,2048]{1,0:T(8,128)(2,1)S(1)} collective-permute-done((bf16[24,2048]{1,0:T(8,128)(2,1)S(1)}, bf16[24,2048]{1,0:T(8,128)(2,1)S(1)}, u32[]{:S(2)}, u32[]{:S(2)}) %collective-permute-start.14) | collective-permute-done | bytes 98336 | tf_op jit(solution)/shard_map/ppermute | solution.py:515
  39.5 0.0 collective-permute-start.15
  39.5 0.7 shard_map.136
  40.3 33.0 %all_to_all.10 = bf16[64,8,1536]{2,1,0:T(8,128)(2,1)S(1)} all-to-all(bf16[64,8,1536]{2,1,0:T(8,128)(2,1)S(1)} %bitcast.12), channel_id=1, replica_groups=mesh['req'=16,'z'=4,'core'=2] {'req','z'}, dimensions={0} | all-to-all | bytes 3145728 | tf_op jit(solution)/shard_map/all_to_all | solution.py:631
  73.2 0.0 collective-permute-done.15.other_ref
  73.2 7.3 %shard_map.137 = (bf16[512,1536]{1,0:T(8,128)(2,1)S(1)}, bf16[3,96,512]{2,1,0:T(8,128)(2,1)S(1)}) custom-call(bf16[512,1536]{1,0:T(8,128)(2,1)S(1)} %bitcast.11, bf16[3072,1024]{1,0:T(8,128)(2,1)S(1)} %get-tuple-element.62.weights_ref, bf16[3072,1024]{1,0:T(8,128)(2,1)S(1)} %collective-permute-done.15.other_ref, ...), custom_call_target="tpu_custom_call" | custom-call | flops 4831838208 | bytes 12582912 | tf_op jit(solution)/shard_map/pallas_call | solution.py:639
  80.6 28.6 %all_to_all.11 = bf16[64,8,1536]{2,1,0:T(8,128)(2,1)S(1)} all-to-all(bf16[64,8,1536]{2,1,0:T(8,128)(2,1)S(1)} %bitcast.13), channel_id=1, replica_groups=mesh['req'=16,'z'=4,'core'=2] {'req','z'}, dimensions={0} | all-to-all | bytes 3145728 | tf_op jit(solution)/shard_map/all_to_all | solution.py:659
  109.2 1.0 shard_map.138
  (14 shorter events, 0.0 us)
Async XLA Ops:
  1.9 13.1 %copy-start.6 = (s32[4]{0:T(128)S(1)}, s32[4]{0:T(128)}, u32[]{:S(2)}) copy-start(s32[4]{0:T(128)} %param.19) | copy-start | bytes 52
  1.9 9.0 %collective-permute-start.5 = (bf16[192,256]{1,0:T(8,128)(2,1)S(1)}, bf16[192,256]{1,0:T(8,128)(2,1)S(1)}, u32[]{:S(2)}, u32[]{:S(2)}) collective-permute-start(bf16[192,256]{1,0:T(8,128)(2,1)S(1)} %shard_map.127.after_ref.refs_0_.q_ref), channel_id=1, source_target_pairs={{0,6},{2,0},{4,2},{6,4},{1,7},{3,1},{5,3},{7,5},{8,14},{10,8},{12,... | collective-permute-start | bytes 294920 | tf_op jit(solution)/shard_map/ppermute | solution.py:515
  6.1 6.9 %collective-permute-start.3 = (bf16[192,256]{1,0:T(8,128)(2,1)S(1)}, bf16[192,256]{1,0:T(8,128)(2,1)S(1)}, u32[]{:S(2)}, u32[]{:S(2)}) collective-permute-start(bf16[192,256]{1,0:T(8,128)(2,1)S(1)} %shard_map.127.after_ref.refs_0_.q_ref), channel_id=1, source_target_pairs={{0,4},{2,6},{4,0},{6,2},{1,5},{3,7},{5,1},{7,3},{8,12},{10,14},{12... | collective-permute-start | bytes 294920 | tf_op jit(solution)/shard_map/ppermute | solution.py:515
  6.1 7.6 %collective-permute-start.1 = (bf16[192,256]{1,0:T(8,128)(2,1)S(1)}, bf16[192,256]{1,0:T(8,128)(2,1)S(1)}, u32[]{:S(2)}, u32[]{:S(2)}) collective-permute-start(bf16[192,256]{1,0:T(8,128)(2,1)S(1)} %shard_map.127.after_ref.refs_0_.q_ref), channel_id=1, source_target_pairs={{0,2},{2,4},{4,6},{6,0},{1,3},{3,5},{5,7},{7,1},{8,10},{10,12},{12... | collective-permute-start | bytes 294920 | tf_op jit(solution)/shard_map/ppermute | solution.py:515
  10.8 2.8 %collective-permute-start = (bf16[192,256]{1,0:T(8,128)(2,1)S(1)}, bf16[192,256]{1,0:T(8,128)(2,1)S(1)}, u32[]{:S(2)}, u32[]{:S(2)}) collective-permute-start(bf16[192,256]{1,0:T(8,128)(2,1)S(1)} %shard_map.127.after_ref.refs_0_.q_ref), channel_id=1, source_target_pairs={{0,1},{1,0},{2,3},{3,2},{4,5},{5,4},{6,7},{7,6},{8,9},{9,8},{10,11... | collective-permute-start | bytes 294920 | tf_op jit(solution)/shard_map/ppermute | solution.py:518
  11.0 2.7 %collective-permute-start.6 = (bf16[192,256]{1,0:T(8,128)(2,1)S(1)}, bf16[192,256]{1,0:T(8,128)(2,1)S(1)}, u32[]{:S(2)}, u32[]{:S(2)}) collective-permute-start(bf16[192,256]{1,0:T(8,128)(2,1)S(1)} %collective-permute-done.5.refs_3_), channel_id=1, source_target_pairs={{0,1},{1,0},{2,3},{3,2},{4,5},{5,4},{6,7},{7,6},{8,9},{9,8},{10,11... | collective-permute-start | bytes 294920 | tf_op jit(solution)/shard_map/ppermute | solution.py:518
  13.0 1.3 %collective-permute-start.4 = (bf16[192,256]{1,0:T(8,128)(2,1)S(1)}, bf16[192,256]{1,0:T(8,128)(2,1)S(1)}, u32[]{:S(2)}, u32[]{:S(2)}) collective-permute-start(bf16[192,256]{1,0:T(8,128)(2,1)S(1)} %collective-permute-done.3.refs_2_), channel_id=1, source_target_pairs={{0,1},{1,0},{2,3},{3,2},{4,5},{5,4},{6,7},{7,6},{8,9},{9,8},{10,11... | collective-permute-start | bytes 294920 | tf_op jit(solution)/shard_map/ppermute | solution.py:518
  13.7 1.3 %collective-permute-start.2 = (bf16[192,256]{1,0:T(8,128)(2,1)S(1)}, bf16[192,256]{1,0:T(8,128)(2,1)S(1)}, u32[]{:S(2)}, u32[]{:S(2)}) collective-permute-start(bf16[192,256]{1,0:T(8,128)(2,1)S(1)} %collective-permute-done.1.refs_1_), channel_id=1, source_target_pairs={{0,1},{1,0},{2,3},{3,2},{4,5},{5,4},{6,7},{7,6},{8,9},{9,8},{10,11... | collective-permute-start | bytes 294920 | tf_op jit(solution)/shard_map/ppermute | solution.py:518
  16.4 5.6 %copy-start = (bf16[192,2048]{1,0:T(8,128)(2,1)S(1)}, bf16[192,2048]{1,0:T(8,128)(2,1)}, u32[]{:S(2)}) copy-start(bf16[192,2048]{1,0:T(8,128)(2,1)} %refs_4_.1) | copy-start | bytes 2359300
  16.4 5.5 %copy-start.2 = (bf16[2048]{0:T(1024)(128)(2,1)S(1)}, bf16[2048]{0:T(1024)(128)(2,1)}, u32[]{:S(2)}) copy-start(bf16[2048]{0:T(1024)(128)(2,1)} %g_ref.1) | copy-start | bytes 12292
  16.5 5.5 %copy-start.5 = (s32[4,48]{1,0:T(4,128)S(1)}, s32[4,48]{1,0:T(4,128)}, u32[]{:S(2)}) copy-start(s32[4,48]{1,0:T(4,128)} %up_ref.1) | copy-start | bytes 2308
  16.5 1.9 %collective-permute-start.7 = (bf16[9,192,128]{2,1,0:T(8,128)(2,1)S(1)}, bf16[9,192,128]{2,1,0:T(8,128)(2,1)S(1)}, u32[]{:S(2)}, u32[]{:S(2)}) collective-permute-start(bf16[9,192,128]{2,1,0:T(8,128)(2,1)S(1)} %shard_map.129.refs_6_), channel_id=1, source_target_pairs={{0,1},{1,0},{2,3},{3,2},{4,5},{5,4},{6,7},{7,6},{8,9},{9,8},{10,11... | collective-permute-start | bytes 1327112 | tf_op jit(solution)/shard_map/ppermute | solution.py:518
  18.1 10.1 %copy-start.1 = (bf16[256,2048]{1,0:T(8,128)(2,1)S(1)}, bf16[256,2048]{1,0:T(8,128)(2,1)}, u32[]{:S(2)}) copy-start(bf16[256,2048]{1,0:T(8,128)(2,1)} %refs_6_.1) | copy-start | bytes 3145732
  18.1 15.7 %copy-start.4 = (s32[24,8]{0,1:T(8,128)S(1)}, s32[24,8]{0,1:T(8,128)}, u32[]{:S(2)}) copy-start(s32[24,8]{0,1:T(8,128)} %param.23) | copy-start | bytes 2308
  19.1 7.3 %collective-permute-start.8 = (bf16[200,256]{1,0:T(8,128)(2,1)S(1)}, bf16[200,256]{1,0:T(8,128)(2,1)S(1)}, u32[]{:S(2)}, u32[]{:S(2)}) collective-permute-start(bf16[200,256]{1,0:T(8,128)(2,1)S(1)} %get-tuple-element.44), channel_id=1, source_target_pairs={{0,4},{2,6},{4,0},{6,2},{1,5},{3,7},{5,1},{7,3},{8,12},{10,14},{12... | collective-permute-start | bytes 307208 | tf_op jit(solution)/shard_map/ppermute | solution.py:515
  20.0 6.4 %collective-permute-start.9 = (bf16[200,256]{1,0:T(8,128)(2,1)S(1)}, bf16[200,256]{1,0:T(8,128)(2,1)S(1)}, u32[]{:S(2)}, u32[]{:S(2)}) collective-permute-start(bf16[200,256]{1,0:T(8,128)(2,1)S(1)} %get-tuple-element.45), channel_id=1, source_target_pairs={{0,6},{2,0},{4,2},{6,4},{1,7},{3,1},{5,3},{7,5},{8,14},{10,8},{12,... | collective-permute-start | bytes 307208 | tf_op jit(solution)/shard_map/ppermute | solution.py:515
  22.0 6.2 %collective-permute-start.10 = (bf16[200,256]{1,0:T(8,128)(2,1)S(1)}, bf16[200,256]{1,0:T(8,128)(2,1)S(1)}, u32[]{:S(2)}, u32[]{:S(2)}) collective-permute-start(bf16[200,256]{1,0:T(8,128)(2,1)S(1)} %get-tuple-element.46), channel_id=1, source_target_pairs={{0,2},{2,4},{4,6},{6,0},{1,3},{3,5},{5,7},{7,1},{8,10},{10,12},{12... | collective-permute-start | bytes 307208 | tf_op jit(solution)/shard_map/ppermute | solution.py:515
  29.1 10.4 %copy-start.3 = (bf16[2048]{0:T(1024)(128)(2,1)S(1)}, bf16[2048]{0:T(1024)(128)(2,1)}, u32[]{:S(2)}) copy-start(bf16[2048]{0:T(1024)(128)(2,1)} %refs_5_.1) | copy-start | bytes 12292
  29.1 1.8 %collective-permute-start.11 = (bf16[96,2048]{1,0:T(8,128)(2,1)S(1)}, bf16[96,2048]{1,0:T(8,128)(2,1)S(1)}, u32[]{:S(2)}, u32[]{:S(2)}) collective-permute-start(bf16[96,2048]{1,0:T(8,128)(2,1)S(1)} %get-tuple-element.50), channel_id=1, source_target_pairs={{0,1},{1,0},{2,3},{3,2},{4,5},{5,4},{6,7},{7,6},{8,9},{9,8},{10,11... | collective-permute-start | bytes 1179656 | tf_op jit(solution)/shard_map/ppermute | solution.py:518
  31.0 7.1 %collective-permute-start.12 = (bf16[24,2048]{1,0:T(8,128)(2,1)S(1)}, bf16[24,2048]{1,0:T(8,128)(2,1)S(1)}, u32[]{:S(2)}, u32[]{:S(2)}) collective-permute-start(bf16[24,2048]{1,0:T(8,128)(2,1)S(1)} %get-tuple-element.52), channel_id=1, source_target_pairs={{0,4},{2,6},{4,0},{6,2},{1,5},{3,7},{5,1},{7,3},{8,12},{10,14},{12... | collective-permute-start | bytes 294920 | tf_op jit(solution)/shard_map/ppermute | solution.py:515
  31.7 6.4 %collective-permute-start.13 = (bf16[24,2048]{1,0:T(8,128)(2,1)S(1)}, bf16[24,2048]{1,0:T(8,128)(2,1)S(1)}, u32[]{:S(2)}, u32[]{:S(2)}) collective-permute-start(bf16[24,2048]{1,0:T(8,128)(2,1)S(1)} %get-tuple-element.53), channel_id=1, source_target_pairs={{0,6},{2,0},{4,2},{6,4},{1,7},{3,1},{5,3},{7,5},{8,14},{10,8},{12,... | collective-permute-start | bytes 294920 | tf_op jit(solution)/shard_map/ppermute | solution.py:515
  33.4 6.2 %collective-permute-start.14 = (bf16[24,2048]{1,0:T(8,128)(2,1)S(1)}, bf16[24,2048]{1,0:T(8,128)(2,1)S(1)}, u32[]{:S(2)}, u32[]{:S(2)}) collective-permute-start(bf16[24,2048]{1,0:T(8,128)(2,1)S(1)} %get-tuple-element.54), channel_id=1, source_target_pairs={{0,2},{2,4},{4,6},{6,0},{1,3},{3,5},{5,7},{7,1},{8,10},{10,12},{12... | collective-permute-start | bytes 294920 | tf_op jit(solution)/shard_map/ppermute | solution.py:515
  33.7 39.5 %copy-start.7 = (bf16[2048,64]{0,1:T(8,128)(2,1)S(1)}, bf16[2048,64]{0,1:T(8,128)(2,1)}, u32[]{:S(2)}) copy-start(bf16[2048,64]{0,1:T(8,128)(2,1)} %param.22) | copy-start | bytes 786436
  39.5 33.7 %collective-permute-start.15 = (bf16[3072,1024]{1,0:T(8,128)(2,1)S(1)}, bf16[3072,1024]{1,0:T(8,128)(2,1)S(1)}, u32[]{:S(2)}, u32[]{:S(2)}) collective-permute-start(bf16[3072,1024]{1,0:T(8,128)(2,1)S(1)} %get-tuple-element.62.weights_ref), channel_id=1, source_target_pairs={{0,1},{1,0},{2,3},{3,2},{4,5},{5,4},{6,7},{7,6},{8,9},{9,8},{10,11... | collective-permute-start | bytes 18874376 | tf_op jit(solution)/shard_map/ppermute | solution.py:518

commit v11 on v9

--- a/solution.py
+++ b/solution.py
@@ -55,10 +55,14 @@
     return jax.ShapeDtypeStruct(shape, dtype)
 
 
-def homes(count, other):
+def homes(count, other, order=None):
     z, core = lax.axis_index("z"), lax.axis_index("core")
     core = 1 - core if other else core
-    return [lax.rem(z + count - i, count) * CORES + core for i in range(count)]
+    return [lax.rem(z + count - i, count) * CORES + core for i in order or range(count)]
+
+
+def far_last(count):
+    return sorted(range(count), key=lambda step: min(step, count - step))
 
 
 def normed_rows(values, gain):
@@ -116,12 +120,18 @@
     return dot_t(jnp.where(same, 1.0, 0.0).astype(BF16), reach.astype(BF16))
 
 
-def tree_kernel(
-    scale, normed_ref, w_ref, q_ref, visible_ref, after_ref, o_ref, lse_ref, turn
-):
+def tree_kernel(scale, normed_ref, w_hbm, q_ref, visible_ref, after_ref, *refs):
+    o_ref, lse_ref, turn, w_ref, sems = refs
     del after_ref
     tokens, width = q_ref.shape
+    w_copies = [
+        pltpu.make_async_copy(w_hbm.at[i + 1], w_ref.at[i], sems.at[i]) for i in range(2)
+    ]
+    for w_copy in w_copies:
+        w_copy.start()
+    w_copies[0].wait()
     keys = dot(normed_ref[...], w_ref[0]).astype(BF16)
+    w_copies[1].wait()
     values = dot(normed_ref[...], w_ref[1]).astype(BF16)
     visible = visible_ref[...] > 0.5
     lane = iota((tokens, 128), 1)
@@ -141,23 +151,15 @@
 
 def page_kernel(scale, tree, kept, lengths_ref, *refs):
     pieces, (k_ref, v_ref) = refs[:4], refs[4:6]
-    outs = refs[7:-2] if kept else refs[7:-3]
-    s_all, p_all = refs[-2:] if kept else refs[-3:-1]
+    outs = refs[7:-2] if kept else refs[6:-2]
+    s_all, p_all = refs[-2:]
     out_ref = outs[0]
-    w_copies = []
-    if not kept:
-        w_hbm, sems = refs[6], refs[-1]
-        for i in range(2):
-            w_copies.append(
-                pltpu.make_async_copy(w_hbm.at[i + 1], outs[1].at[i], sems.at[i])
-            )
-            w_copies[i].start()
     requests, page = k_ref.shape[0], k_ref.shape[1]
     width = pieces[0].shape[1]
     pair = 2 * tree
     lane = iota((tree, 128), 1)
     wide = iota((tree, width), 1) < HEAD_DIM
-    owners = homes(len(pieces), not kept)
+    owners = homes(len(pieces), not kept, far_last(len(pieces)))
     start = (lax.axis_index("z") * CORES + lax.axis_index("core")) * page
     lives = lengths_ref[...] - start
 
@@ -203,8 +205,6 @@
             outs[1][rows, :] = stats
         else:
             out_ref[8, rows, :] = stats.astype(BF16)
-    for w_copy in w_copies:
-        w_copy.wait()
 
 
 def merge_kernel(other_ref, kept_ref, lse_ref, *refs):
@@ -532,8 +532,10 @@
     def over_core(value):
         return lax.ppermute(value, "core", [(0, 1), (1, 0)])
 
-    steps = range(1, z_count)
-    pieces = [query] + [over_z(query, step) for step in steps]
+    steps = sorted(range(1, z_count), key=lambda step: -min(step, z_count - step))
+
+    order = far_last(z_count)
+    pieces = [over_z(query, step) if step else query for step in order]
     keys, values, visible = call(
         load_kernel,
         (
@@ -560,15 +562,15 @@
     ]
     heads = 2 * z_count
     lengths = cache_lengths.reshape(1, requests)
-    for_other, w_pair = call(
+    for_other = call(
         functools.partial(page_kernel, scale, tree, False),
-        (sds((heads + 1, tokens, HEAD_DIM), BF16), sds((2, width, local_width), BF16)),
-        [VMEM] * 7 + [HBM],
-        scratch + [pltpu.SemaphoreType.DMA((2,))],
+        sds((heads + 1, tokens, HEAD_DIM), BF16),
+        [VMEM] * 7,
+        scratch,
         flops=2 * tokens * page * width,
         bytes_accessed=2 * requests * page * width,
         vmem=20 << 20,
-    )(lengths, *other_pieces, keys, values, w_three)
+    )(lengths, *other_pieces, keys, values)
     from_other = over_core(for_other)
     kept, kept_lse = call(
         functools.partial(page_kernel, scale, tree, True),
@@ -586,16 +588,20 @@
         [pltpu.VMEM((256, 128), F32)],
         bytes_accessed=1 << 20,
     )(from_other, kept, kept_lse)
-    arrived = [merged[0]] + [over_z(merged[step], -step) for step in steps]
+    arrived = [merged[0]] + [over_z(merged[order.index(step)], -step) for step in steps]
 
     tree_o, tree_lse = call(
         functools.partial(tree_kernel, scale),
         (sds((tokens, local_width), F32), sds((8, 256), F32)),
-        [VMEM] * 4 + [pl.ANY],
-        [pltpu.VMEM((256, 128), F32)],
+        [VMEM, HBM, VMEM, VMEM, pl.ANY],
+        [
+            pltpu.VMEM((256, 128), F32),
+            pltpu.VMEM((2, width, local_width), BF16),
+            pltpu.SemaphoreType.DMA((2,)),
+        ],
         flops=4 * tokens * width * local_width,
         bytes_accessed=2 * width * (tokens + 2 * local_width),
-    )(normed_attn, w_pair, query, visible, merged[0])
+    )(normed_attn, w_three, query, visible, merged[0])
     theirs, ours = call(
         out_kernel,
         (sds((z_count * own, width), BF16), sds((z_count * own, width), F32)),

time: 112 us -> 110 us (0.982)
  waiting for transfers between devices: 13.9 us -> 9.13 us
  starting transfers between devices: 11.7 us -> 13.9 us
    ppermute x9, waiting for transfers between devices: 10.7 us -> 5.96 us  [over_z(): lax.ppermute(value, 'z', [(i, (i + step) % z_count) for i in range(z_coun...]
    ppermute x9, starting transfers between devices: 10.8 us -> 12.8 us  [over_z(): lax.ppermute(value, 'z', [(i, (i + step) % z_count) for i in range(z_coun...]
    pallas_call x1, Pallas kernels: 1.02 us -> 2.58 us  [per_device(): call(functools.partial(tree_kernel, scale), (sds((tokens, local_width), F...]
  transfers between devices with their start and end apart: 16 -> 16, of which waited for: 11 -> 13; matrix products, arithmetic and copies ran while one was open for 0% -> 0% of each run, Pallas kernels for 9% -> 10%
where the time goes in v11:
time: 110 us
  blocking collectives  61.7 us (56%)
  Pallas kernels  24.9 us (23%)
  starting transfers between devices  13.9 us (13%)
  waiting for transfers between devices  9.13 us (8%)
    all_to_all x1, blocking collectives, per_device(): lax.all_to_all(outgoing.reshape(experts, SLOTS, packed), ('req', 'z'), sp...  33.1 us
    all_to_all x1, blocking collectives, per_device(): lax.all_to_all(summed.reshape(experts, SLOTS, packed), ('req', 'z'), spli...  28.6 us
    ppermute x9, starting transfers between devices, over_z(): lax.ppermute(value, 'z', [(i, (i + step) % z_count) for i in range(z_coun...  12.8 us
    pallas_call x1, Pallas kernels, per_device(): call(expert_kernel, (sds((experts * SLOTS, packed), BF16), sds((chunks, 4...  7.36 us
    ppermute x9, waiting for transfers between devices, over_z(): lax.ppermute(value, 'z', [(i, (i + step) % z_count) for i in range(z_coun...  5.96 us
    pallas_call x1, Pallas kernels, per_device(): call(load_kernel, (sds(cache_keys.shape, BF16), sds(cache_values.shape, B...  3.5 us
    pallas_call x1, Pallas kernels, per_device(): call(table_kernel, (sds((chunks, experts * SLOTS, 2 * own), BF16), sds((1...  3.24 us
    ppermute x7, waiting for transfers between devices, over_core(): return lax.ppermute(value, 'core', [(0, 1), (1, 0)])  3.17 us
  transfers between devices with their start and end apart: 16, of which 13 were waited for; matrix products, arithmetic and copies ran while one was open for 0% of the time, Pallas kernels for 10%

profile of v11, /device:TPU:0, one launch (start us, length us, event | category | flops | bytes accessed | tf_op | source)
XLA Modules:
  0.0 109.8 jit_solution(4697360786656863345)
XLA Ops:
  0.0 1.9 %shard_map.127 = (bf16[192,256]{1,0:T(8,128)(2,1)S(1)}, bf16[192,2048]{1,0:T(8,128)(2,1)S(1)}) custom-call(bf16[192,2048]{1,0:T(8,128)(2,1)} %refs_4_.1, bf16[2048]{0:T(1024)(128)(2,1)} %g_hbm.1, bf16[3,2048,256]{2,1,0:T(8,128)(2,1)} %bitcast.19), custom_call_target="tpu_custom_call" | custom-call | flops 201326592 | bytes 1835008 | tf_op jit(solution)/shard_map/pallas_call | solution.py:511
  1.9 0.0 copy-start.4
  1.9 4.0 %collective-permute-start.5 = (bf16[192,256]{1,0:T(8,128)(2,1)S(1)}, bf16[192,256]{1,0:T(8,128)(2,1)S(1)}, u32[]{:S(2)}, u32[]{:S(2)}) collective-permute-start(bf16[192,256]{1,0:T(8,128)(2,1)S(1)} %get-tuple-element.42.after_ref.refs_0_.q_ref), channel_id=1, source_target_pairs={{0,4},{2,6},{4,0},{6,2},{1,5},{3,7},{5,1},{7,3},{8,12},{10,14},{12... | collective-permute-start | bytes 294920 | tf_op jit(solution)/shard_map/ppermute | solution.py:530
  5.9 0.7 collective-permute-start.3
  6.7 1.3 %collective-permute-start.1 = (bf16[192,256]{1,0:T(8,128)(2,1)S(1)}, bf16[192,256]{1,0:T(8,128)(2,1)S(1)}, u32[]{:S(2)}, u32[]{:S(2)}) collective-permute-start(bf16[192,256]{1,0:T(8,128)(2,1)S(1)} %get-tuple-element.42.after_ref.refs_0_.q_ref), channel_id=1, source_target_pairs={{0,2},{2,4},{4,6},{6,0},{1,3},{3,5},{5,7},{7,1},{8,10},{10,12},{12... | collective-permute-start | bytes 294920 | tf_op jit(solution)/shard_map/ppermute | solution.py:530
  8.0 3.5 %shard_map.128 = (bf16[4,256,2048]{2,1,0:T(8,128)(2,1)S(1)}, bf16[4,256,2048]{2,1,0:T(8,128)(2,1)S(1)}, f32[192,192]{1,0:T(8,128)S(1)}) custom-call(bf16[4,256,2048]{2,1,0:T(8,128)(2,1)} %k_hbm.1, bf16[4,256,2048]{2,1,0:T(8,128)(2,1)} %v_hbm.1, s32[4,48]{1,0:T(4,128)} %up_hbm.1, bf16[192,256]{1,0:T(8,128)(2,1)S(1)} %get-tuple-element.42.after_ref.refs_0_.q_ref), custom_call_target="tpu_custom_call" | custom-call | bytes 8388608 | tf_op jit(solution)/shard_map/pallas_call | solution.py:539
  11.5 0.1 collective-permute-start
  11.6 0.5 collective-permute-start.6
  12.1 0.0 collective-permute-done.3.refs_2_
  12.1 0.1 collective-permute-start.4
  12.2 0.3 collective-permute-done.1.refs_1_
  12.5 0.1 collective-permute-start.2
  12.6 0.3 collective-permute-done.refs_0_
  12.9 0.2 collective-permute-done.6.refs_3_
  13.0 0.4 collective-permute-done.4.refs_2_
  13.4 0.4 collective-permute-done.2.refs_1_
  13.8 1.5 %shard_map.129.refs_6_ = bf16[9,192,128]{2,1,0:T(8,128)(2,1)S(1)} custom-call(s32[1,4]{1,0:T(1,128)S(1)} %bitcast.16, bf16[192,256]{1,0:T(8,128)(2,1)S(1)} %collective-permute-done.refs_0_, bf16[192,256]{1,0:T(8,128)(2,1)S(1)} %collective-permute-done.2.refs_1_, bf16[192,256]{1,0:T(8,128)(2,1)S(1)} %collective-permute-done.4.refs_2_, ...), custom_call_target="tpu_custom_call" | custom-call | flops 201326592 | bytes 4194304 | tf_op jit(solution)/shard_map/pallas_call | solution.py:565
  15.3 0.2 collective-permute-start.7
  15.5 1.4 %shard_map.130 = (f32[8,192,128]{2,1,0:T(8,128)S(1)}, f32[192,128]{1,0:T(8,128)S(1)}) custom-call(s32[1,4]{1,0:T(1,128)S(1)} %bitcast.17, bf16[192,256]{1,0:T(8,128)(2,1)S(1)} %get-tuple-element.42.after_ref.refs_0_.q_ref, bf16[192,256]{1,0:T(8,128)(2,1)S(1)} %collective-permute-done.1.refs_1_, bf16[192,256]{1,0:T(8,128)(2,1)S(1)} %collective-permute-done.3.refs_2_, ...), custom_call_target="tpu_custom_call" | custom-call | flops 201326592 | bytes 4194304 | tf_op jit(solution)/shard_map/pallas_call | solution.py:575
  16.9 0.0 copy-start.1
  16.9 0.3 collective-permute-done.7.other_ref
  17.1 0.7 shard_map.131
  17.9 1.7 %collective-permute-start.8 = (bf16[200,256]{1,0:T(8,128)(2,1)S(1)}, bf16[200,256]{1,0:T(8,128)(2,1)S(1)}, u32[]{:S(2)}, u32[]{:S(2)}) collective-permute-start(bf16[200,256]{1,0:T(8,128)(2,1)S(1)} %get-tuple-element.48), channel_id=1, source_target_pairs={{0,4},{2,6},{4,0},{6,2},{1,5},{3,7},{5,1},{7,3},{8,12},{10,14},{12... | collective-permute-start | bytes 307208 | tf_op jit(solution)/shard_map/ppermute | solution.py:530
  19.5 1.8 %collective-permute-start.9 = (bf16[200,256]{1,0:T(8,128)(2,1)S(1)}, bf16[200,256]{1,0:T(8,128)(2,1)S(1)}, u32[]{:S(2)}, u32[]{:S(2)}) collective-permute-start(bf16[200,256]{1,0:T(8,128)(2,1)S(1)} %get-tuple-element.49), channel_id=1, source_target_pairs={{0,6},{2,0},{4,2},{6,4},{1,7},{3,1},{5,3},{7,5},{8,14},{10,8},{12,... | collective-permute-start | bytes 307208 | tf_op jit(solution)/shard_map/ppermute | solution.py:530
  21.4 0.2 collective-permute-start.10
  21.6 2.6 %shard_map.132 = (f32[192,256]{1,0:T(8,128)S(1)}, f32[8,256]{1,0:T(8,128)S(1)}) custom-call(bf16[192,2048]{1,0:T(8,128)(2,1)S(1)} %get-tuple-element.51.normed_ref, bf16[3,2048,256]{2,1,0:T(8,128)(2,1)} %bitcast.20, bf16[192,256]{1,0:T(8,128)(2,1)S(1)} %get-tuple-element.42.after_ref.refs_0_.q_ref, f32[192,192]{1,0:T(8,128)S(1)} %get-tuple-element.52.visible_ref, ...), custom_call_target="tpu_custom_call" | custom-call | flops 402653184 | bytes 2883584 | tf_op jit(solution)/shard_map/pallas_call | solution.py:593
  24.2 1.0 collective-permute-done.8.refs_1_
  25.2 0.8 collective-permute-done.9.refs_2_
  26.0 1.3 %collective-permute-done.10.refs_3_ = bf16[200,256]{1,0:T(8,128)(2,1)S(1)} collective-permute-done((bf16[200,256]{1,0:T(8,128)(2,1)S(1)}, bf16[200,256]{1,0:T(8,128)(2,1)S(1)}, u32[]{:S(2)}, u32[]{:S(2)}) %collective-permute-start.10) | collective-permute-done | bytes 102432 | tf_op jit(solution)/shard_map/ppermute | solution.py:530
  27.3 0.9 shard_map.133
  28.2 0.0 copy-start.2
  28.2 0.1 collective-permute-start.11
  28.3 1.7 %collective-permute-done.11.theirs_ref = bf16[96,2048]{1,0:T(8,128)(2,1)S(1)} collective-permute-done((bf16[96,2048]{1,0:T(8,128)(2,1)S(1)}, bf16[96,2048]{1,0:T(8,128)(2,1)S(1)}, u32[]{:S(2)}, u32[]{:S(2)}) %collective-permute-start.11) | collective-permute-done | bytes 393248 | tf_op jit(solution)/shard_map/ppermute | solution.py:533
  30.0 0.1 shard_map.134
  30.1 1.0 collective-permute-start.12
  31.1 2.0 %collective-permute-start.13 = (bf16[24,2048]{1,0:T(8,128)(2,1)S(1)}, bf16[24,2048]{1,0:T(8,128)(2,1)S(1)}, u32[]{:S(2)}, u32[]{:S(2)}) collective-permute-start(bf16[24,2048]{1,0:T(8,128)(2,1)S(1)} %get-tuple-element.59), channel_id=1, source_target_pairs={{0,6},{2,0},{4,2},{6,4},{1,7},{3,1},{5,3},{7,5},{8,14},{10,8},{12,... | collective-permute-start | bytes 294920 | tf_op jit(solution)/shard_map/ppermute | solution.py:530
  33.1 0.0 collective-permute-start.14
  33.2 3.2 %shard_map.135 = (bf16[3,512,48]{2,1,0:T(8,128)(2,1)S(1)}, bf16[4,192,256]{2,1,0:T(8,128)(2,1)S(1)}, bf16[3,256,384]{2,1,0:T(8,128)(2,1)S(1)}, bf16[3072,1024]{1,0:T(8,128)(2,1)S(1)}) custom-call(s32[8,24]{1,0:T(8,128)S(1)} %bitcast.14, bf16[2048,1024]{1,0:T(8,128)(2,1)} %bitcast.21, bf16[512,2048]{1,0:T(8,128)(2,1)} %bitcast.22, ...), custom_call_target="tpu_custom_call" | custom-call | flops 16777216 | bytes 8388608 | tf_op jit(solution)/shard_map/pallas_call | solution.py:623
  36.4 0.8 collective-permute-done.12.refs_1_
  37.2 0.1 collective-permute-done.13.refs_2_
  37.4 1.6 %collective-permute-done.14.refs_3_ = bf16[24,2048]{1,0:T(8,128)(2,1)S(1)} collective-permute-done((bf16[24,2048]{1,0:T(8,128)(2,1)S(1)}, bf16[24,2048]{1,0:T(8,128)(2,1)S(1)}, u32[]{:S(2)}, u32[]{:S(2)}) %collective-permute-start.14) | collective-permute-done | bytes 98336 | tf_op jit(solution)/shard_map/ppermute | solution.py:530
  39.0 0.0 collective-permute-start.15
  39.0 0.7 shard_map.136
  39.7 33.1 %all_to_all.10 = bf16[64,8,1536]{2,1,0:T(8,128)(2,1)S(1)} all-to-all(bf16[64,8,1536]{2,1,0:T(8,128)(2,1)S(1)} %bitcast.12), channel_id=1, replica_groups=mesh['req'=16,'z'=4,'core'=2] {'req','z'}, dimensions={0} | all-to-all | bytes 3145728 | tf_op jit(solution)/shard_map/all_to_all | solution.py:656
  72.8 0.0 collective-permute-done.15.other_ref
  72.8 7.4 %shard_map.137 = (bf16[512,1536]{1,0:T(8,128)(2,1)S(1)}, bf16[3,96,512]{2,1,0:T(8,128)(2,1)S(1)}) custom-call(bf16[512,1536]{1,0:T(8,128)(2,1)S(1)} %bitcast.11, bf16[3072,1024]{1,0:T(8,128)(2,1)S(1)} %get-tuple-element.68.weights_ref, bf16[3072,1024]{1,0:T(8,128)(2,1)S(1)} %collective-permute-done.15.other_ref, ...), custom_call_target="tpu_custom_call" | custom-call | flops 4831838208 | bytes 12582912 | tf_op jit(solution)/shard_map/pallas_call | solution.py:664
  80.2 28.6 %all_to_all.11 = bf16[64,8,1536]{2,1,0:T(8,128)(2,1)S(1)} all-to-all(bf16[64,8,1536]{2,1,0:T(8,128)(2,1)S(1)} %bitcast.13), channel_id=1, replica_groups=mesh['req'=16,'z'=4,'core'=2] {'req','z'}, dimensions={0} | all-to-all | bytes 3145728 | tf_op jit(solution)/shard_map/all_to_all | solution.py:684
  108.8 1.0 shard_map.138
  (10 shorter events, 0.0 us)
Async XLA Ops:
  1.9 11.9 %copy-start.4 = (s32[4]{0:T(128)S(1)}, s32[4]{0:T(128)}, u32[]{:S(2)}) copy-start(s32[4]{0:T(128)} %param.19) | copy-start | bytes 52
  1.9 9.7 %collective-permute-start.5 = (bf16[192,256]{1,0:T(8,128)(2,1)S(1)}, bf16[192,256]{1,0:T(8,128)(2,1)S(1)}, u32[]{:S(2)}, u32[]{:S(2)}) collective-permute-start(bf16[192,256]{1,0:T(8,128)(2,1)S(1)} %get-tuple-element.42.after_ref.refs_0_.q_ref), channel_id=1, source_target_pairs={{0,4},{2,6},{4,0},{6,2},{1,5},{3,7},{5,1},{7,3},{8,12},{10,14},{12... | collective-permute-start | bytes 294920 | tf_op jit(solution)/shard_map/ppermute | solution.py:530
  5.9 6.1 %collective-permute-start.3 = (bf16[192,256]{1,0:T(8,128)(2,1)S(1)}, bf16[192,256]{1,0:T(8,128)(2,1)S(1)}, u32[]{:S(2)}, u32[]{:S(2)}) collective-permute-start(bf16[192,256]{1,0:T(8,128)(2,1)S(1)} %get-tuple-element.42.after_ref.refs_0_.q_ref), channel_id=1, source_target_pairs={{0,6},{2,0},{4,2},{6,4},{1,7},{3,1},{5,3},{7,5},{8,14},{10,8},{12,... | collective-permute-start | bytes 294920 | tf_op jit(solution)/shard_map/ppermute | solution.py:530
  6.7 5.8 %collective-permute-start.1 = (bf16[192,256]{1,0:T(8,128)(2,1)S(1)}, bf16[192,256]{1,0:T(8,128)(2,1)S(1)}, u32[]{:S(2)}, u32[]{:S(2)}) collective-permute-start(bf16[192,256]{1,0:T(8,128)(2,1)S(1)} %get-tuple-element.42.after_ref.refs_0_.q_ref), channel_id=1, source_target_pairs={{0,2},{2,4},{4,6},{6,0},{1,3},{3,5},{5,7},{7,1},{8,10},{10,12},{12... | collective-permute-start | bytes 294920 | tf_op jit(solution)/shard_map/ppermute | solution.py:530
  11.5 1.4 %collective-permute-start = (bf16[192,256]{1,0:T(8,128)(2,1)S(1)}, bf16[192,256]{1,0:T(8,128)(2,1)S(1)}, u32[]{:S(2)}, u32[]{:S(2)}) collective-permute-start(bf16[192,256]{1,0:T(8,128)(2,1)S(1)} %get-tuple-element.42.after_ref.refs_0_.q_ref), channel_id=1, source_target_pairs={{0,1},{1,0},{2,3},{3,2},{4,5},{5,4},{6,7},{7,6},{8,9},{9,8},{10,11... | collective-permute-start | bytes 294920 | tf_op jit(solution)/shard_map/ppermute | solution.py:533
  11.6 1.4 %collective-permute-start.6 = (bf16[192,256]{1,0:T(8,128)(2,1)S(1)}, bf16[192,256]{1,0:T(8,128)(2,1)S(1)}, u32[]{:S(2)}, u32[]{:S(2)}) collective-permute-start(bf16[192,256]{1,0:T(8,128)(2,1)S(1)} %collective-permute-done.5.refs_3_), channel_id=1, source_target_pairs={{0,1},{1,0},{2,3},{3,2},{4,5},{5,4},{6,7},{7,6},{8,9},{9,8},{10,11... | collective-permute-start | bytes 294920 | tf_op jit(solution)/shard_map/ppermute | solution.py:533
  12.1 1.3 %collective-permute-start.4 = (bf16[192,256]{1,0:T(8,128)(2,1)S(1)}, bf16[192,256]{1,0:T(8,128)(2,1)S(1)}, u32[]{:S(2)}, u32[]{:S(2)}) collective-permute-start(bf16[192,256]{1,0:T(8,128)(2,1)S(1)} %collective-permute-done.3.refs_2_), channel_id=1, source_target_pairs={{0,1},{1,0},{2,3},{3,2},{4,5},{5,4},{6,7},{7,6},{8,9},{9,8},{10,11... | collective-permute-start | bytes 294920 | tf_op jit(solution)/shard_map/ppermute | solution.py:533
  12.5 1.3 %collective-permute-start.2 = (bf16[192,256]{1,0:T(8,128)(2,1)S(1)}, bf16[192,256]{1,0:T(8,128)(2,1)S(1)}, u32[]{:S(2)}, u32[]{:S(2)}) collective-permute-start(bf16[192,256]{1,0:T(8,128)(2,1)S(1)} %collective-permute-done.1.refs_1_), channel_id=1, source_target_pairs={{0,1},{1,0},{2,3},{3,2},{4,5},{5,4},{6,7},{7,6},{8,9},{9,8},{10,11... | collective-permute-start | bytes 294920 | tf_op jit(solution)/shard_map/ppermute | solution.py:533
  15.3 1.9 %collective-permute-start.7 = (bf16[9,192,128]{2,1,0:T(8,128)(2,1)S(1)}, bf16[9,192,128]{2,1,0:T(8,128)(2,1)S(1)}, u32[]{:S(2)}, u32[]{:S(2)}) collective-permute-start(bf16[9,192,128]{2,1,0:T(8,128)(2,1)S(1)} %shard_map.129.refs_6_), channel_id=1, source_target_pairs={{0,1},{1,0},{2,3},{3,2},{4,5},{5,4},{6,7},{7,6},{8,9},{9,8},{10,11... | collective-permute-start | bytes 1327112 | tf_op jit(solution)/shard_map/ppermute | solution.py:533
  16.9 10.4 %copy-start.1 = (bf16[256,2048]{1,0:T(8,128)(2,1)S(1)}, bf16[256,2048]{1,0:T(8,128)(2,1)}, u32[]{:S(2)}) copy-start(bf16[256,2048]{1,0:T(8,128)(2,1)} %refs_6_.1) | copy-start | bytes 3145732
  17.1 16.0 %copy-start.3 = (s32[24,8]{0,1:T(8,128)S(1)}, s32[24,8]{0,1:T(8,128)}, u32[]{:S(2)}) copy-start(s32[24,8]{0,1:T(8,128)} %param.23) | copy-start | bytes 2308
  17.9 7.3 %collective-permute-start.8 = (bf16[200,256]{1,0:T(8,128)(2,1)S(1)}, bf16[200,256]{1,0:T(8,128)(2,1)S(1)}, u32[]{:S(2)}, u32[]{:S(2)}) collective-permute-start(bf16[200,256]{1,0:T(8,128)(2,1)S(1)} %get-tuple-element.48), channel_id=1, source_target_pairs={{0,4},{2,6},{4,0},{6,2},{1,5},{3,7},{5,1},{7,3},{8,12},{10,14},{12... | collective-permute-start | bytes 307208 | tf_op jit(solution)/shard_map/ppermute | solution.py:530
  19.5 6.4 %collective-permute-start.9 = (bf16[200,256]{1,0:T(8,128)(2,1)S(1)}, bf16[200,256]{1,0:T(8,128)(2,1)S(1)}, u32[]{:S(2)}, u32[]{:S(2)}) collective-permute-start(bf16[200,256]{1,0:T(8,128)(2,1)S(1)} %get-tuple-element.49), channel_id=1, source_target_pairs={{0,6},{2,0},{4,2},{6,4},{1,7},{3,1},{5,3},{7,5},{8,14},{10,8},{12,... | collective-permute-start | bytes 307208 | tf_op jit(solution)/shard_map/ppermute | solution.py:530
  21.4 5.9 %collective-permute-start.10 = (bf16[200,256]{1,0:T(8,128)(2,1)S(1)}, bf16[200,256]{1,0:T(8,128)(2,1)S(1)}, u32[]{:S(2)}, u32[]{:S(2)}) collective-permute-start(bf16[200,256]{1,0:T(8,128)(2,1)S(1)} %get-tuple-element.50), channel_id=1, source_target_pairs={{0,2},{2,4},{4,6},{6,0},{1,3},{3,5},{5,7},{7,1},{8,10},{10,12},{12... | collective-permute-start | bytes 307208 | tf_op jit(solution)/shard_map/ppermute | solution.py:530
  28.2 10.8 %copy-start = (bf16[192,2048]{1,0:T(8,128)(2,1)S(1)}, bf16[192,2048]{1,0:T(8,128)(2,1)}, u32[]{:S(2)}) copy-start(bf16[192,2048]{1,0:T(8,128)(2,1)} %refs_4_.1) | copy-start | bytes 2359300
  28.2 10.8 %copy-start.2 = (bf16[2048]{0:T(1024)(128)(2,1)S(1)}, bf16[2048]{0:T(1024)(128)(2,1)}, u32[]{:S(2)}) copy-start(bf16[2048]{0:T(1024)(128)(2,1)} %refs_5_.1) | copy-start | bytes 12292
  28.2 1.8 %collective-permute-start.11 = (bf16[96,2048]{1,0:T(8,128)(2,1)S(1)}, bf16[96,2048]{1,0:T(8,128)(2,1)S(1)}, u32[]{:S(2)}, u32[]{:S(2)}) collective-permute-start(bf16[96,2048]{1,0:T(8,128)(2,1)S(1)} %get-tuple-element.56), channel_id=1, source_target_pairs={{0,1},{1,0},{2,3},{3,2},{4,5},{5,4},{6,7},{7,6},{8,9},{9,8},{10,11... | collective-permute-start | bytes 1179656 | tf_op jit(solution)/shard_map/ppermute | solution.py:533
  30.1 7.1 %collective-permute-start.12 = (bf16[24,2048]{1,0:T(8,128)(2,1)S(1)}, bf16[24,2048]{1,0:T(8,128)(2,1)S(1)}, u32[]{:S(2)}, u32[]{:S(2)}) collective-permute-start(bf16[24,2048]{1,0:T(8,128)(2,1)S(1)} %get-tuple-element.58), channel_id=1, source_target_pairs={{0,4},{2,6},{4,0},{6,2},{1,5},{3,7},{5,1},{7,3},{8,12},{10,14},{12... | collective-permute-start | bytes 294920 | tf_op jit(solution)/shard_map/ppermute | solution.py:530
  31.1 6.2 %collective-permute-start.13 = (bf16[24,2048]{1,0:T(8,128)(2,1)S(1)}, bf16[24,2048]{1,0:T(8,128)(2,1)S(1)}, u32[]{:S(2)}, u32[]{:S(2)}) collective-permute-start(bf16[24,2048]{1,0:T(8,128)(2,1)S(1)} %get-tuple-element.59), channel_id=1, source_target_pairs={{0,6},{2,0},{4,2},{6,4},{1,7},{3,1},{5,3},{7,5},{8,14},{10,8},{12,... | collective-permute-start | bytes 294920 | tf_op jit(solution)/shard_map/ppermute | solution.py:530
  33.1 5.8 %collective-permute-start.14 = (bf16[24,2048]{1,0:T(8,128)(2,1)S(1)}, bf16[24,2048]{1,0:T(8,128)(2,1)S(1)}, u32[]{:S(2)}, u32[]{:S(2)}) collective-permute-start(bf16[24,2048]{1,0:T(8,128)(2,1)S(1)} %get-tuple-element.60), channel_id=1, source_target_pairs={{0,2},{2,4},{4,6},{6,0},{1,3},{3,5},{5,7},{7,1},{8,10},{10,12},{12... | collective-permute-start | bytes 294920 | tf_op jit(solution)/shard_map/ppermute | solution.py:530
  33.2 39.7 %copy-start.5 = (bf16[2048,64]{0,1:T(8,128)(2,1)S(1)}, bf16[2048,64]{0,1:T(8,128)(2,1)}, u32[]{:S(2)}) copy-start(bf16[2048,64]{0,1:T(8,128)(2,1)} %param.22) | copy-start | bytes 786436
  39.0 33.8 %collective-permute-start.15 = (bf16[3072,1024]{1,0:T(8,128)(2,1)S(1)}, bf16[3072,1024]{1,0:T(8,128)(2,1)S(1)}, u32[]{:S(2)}, u32[]{:S(2)}) collective-permute-start(bf16[3072,1024]{1,0:T(8,128)(2,1)S(1)} %get-tuple-element.68.weights_ref), channel_id=1, source_target_pairs={{0,1},{1,0},{2,3},{3,2},{4,5},{5,4},{6,7},{7,6},{8,9},{9,8},{10,11... | collective-permute-start | bytes 18874376 | tf_op jit(solution)/shard_map/ppermute | solution.py:533

commit v12 on v11

--- a/solution.py
+++ b/solution.py
@@ -85,22 +85,15 @@
     q_ref[...] = dot(normed_ref[...], w_ref[...]).astype(BF16)
 
 
-def load_kernel(
-    k_hbm, v_hbm, up_hbm, after_ref, k_ref, v_ref, visible_ref, up_ref, sems
-):
+def load_kernel(v_hbm, up_hbm, after_ref, v_ref, visible_ref, up_ref, sems):
     del after_ref
-    up_copy = pltpu.make_async_copy(up_hbm, up_ref, sems.at[2])
+    up_copy = pltpu.make_async_copy(up_hbm, up_ref, sems.at[0])
+    v_copy = pltpu.make_async_copy(v_hbm, v_ref, sems.at[1])
     up_copy.start()
-    copies = [
-        pltpu.make_async_copy(k_hbm, k_ref, sems.at[0]),
-        pltpu.make_async_copy(v_hbm, v_ref, sems.at[1]),
-    ]
-    for copy in copies:
-        copy.start()
+    v_copy.start()
     up_copy.wait()
     visible_ref[...] = ancestors(up_ref)
-    for copy in copies:
-        copy.wait()
+    v_copy.wait()
 
 
 def ancestors(up_ref):
@@ -505,7 +498,6 @@
     padded = tokens + 8
 
     w_three = pltpu.with_memory_space_constraint(jnp.transpose(w_qkv, (1, 0, 2)), HBM)
-    cache_keys = pltpu.with_memory_space_constraint(cache_keys, HBM)
     cache_values = pltpu.with_memory_space_constraint(cache_values, HBM)
 
     query, normed_attn = call(
@@ -536,24 +528,16 @@
 
     order = far_last(z_count)
     pieces = [over_z(query, step) if step else query for step in order]
-    keys, values, visible = call(
+    keys = pltpu.with_memory_space_constraint(cache_keys, VMEM)
+    values, visible = call(
         load_kernel,
-        (
-            sds(cache_keys.shape, BF16),
-            sds(cache_values.shape, BF16),
-            sds((tokens, tokens), F32),
-        ),
-        [HBM, HBM, HBM, pl.ANY],
-        [pltpu.VMEM(parents.shape, jnp.int32), pltpu.SemaphoreType.DMA((3,))],
-        bytes_accessed=4 * requests * page * width,
+        (sds(cache_values.shape, BF16), sds((tokens, tokens), F32)),
+        [HBM, HBM, pl.ANY],
+        [pltpu.VMEM(parents.shape, jnp.int32), pltpu.SemaphoreType.DMA((2,))],
+        bytes_accessed=2 * requests * page * width,
         vmem=16 << 20,
-    )(
-        cache_keys,
-        cache_values,
-        pltpu.with_memory_space_constraint(parents, HBM),
-        query,
-    )
-    pieces[0], keys = lax.optimization_barrier((pieces[0], keys))
+    )(cache_values, pltpu.with_memory_space_constraint(parents, HBM), query)
+    pieces[0], values = lax.optimization_barrier((pieces[0], values))
     other_pieces = [over_core(piece) for piece in pieces]
 
     scratch = [

time: 110 us -> 110 us (level)
    pallas_call x1, Pallas kernels: 3.5 us -> 2.22 us  [per_device(): call(load_kernel, (sds(cache_values.shape, BF16), sds((tokens, tokens), F...]
  transfers between devices with their start and end apart: 16 -> 16, of which waited for: 13 -> 12; matrix products, arithmetic and copies ran while one was open for 0% -> 0% of each run, Pallas kernels for 10% -> 9%
where the time goes in v12:
time: 110 us
  blocking collectives  62.3 us (57%)
  Pallas kernels  23.8 us (22%)
  starting transfers between devices  14.2 us (13%)
  waiting for transfers between devices  9.57 us (9%)
    all_to_all x1, blocking collectives, per_device(): lax.all_to_all(outgoing.reshape(experts, SLOTS, packed), ('req', 'z'), sp...  33.7 us
    all_to_all x1, blocking collectives, per_device(): lax.all_to_all(summed.reshape(experts, SLOTS, packed), ('req', 'z'), spli...  28.6 us
    ppermute x9, starting transfers between devices, over_z(): lax.ppermute(value, 'z', [(i, (i + step) % z_count) for i in range(z_coun...  13.2 us
    pallas_call x1, Pallas kernels, per_device(): call(expert_kernel, (sds((experts * SLOTS, packed), BF16), sds((chunks, 4...  7.36 us
    ppermute x9, waiting for transfers between devices, over_z(): lax.ppermute(value, 'z', [(i, (i + step) % z_count) for i in range(z_coun...  6.43 us
    pallas_call x1, Pallas kernels, per_device(): call(table_kernel, (sds((chunks, experts * SLOTS, 2 * own), BF16), sds((1...  3.24 us
    ppermute x7, waiting for transfers between devices, over_core(): return lax.ppermute(value, 'core', [(0, 1), (1, 0)])  3.14 us
    pallas_call x1, Pallas kernels, per_device(): call(functools.partial(tree_kernel, scale), (sds((tokens, local_width), F...  2.58 us
  transfers between devices with their start and end apart: 16, of which 12 were waited for; matrix products, arithmetic and copies ran while one was open for 0% of the time, Pallas kernels for 9%

profile of v12, /device:TPU:0, one launch (start us, length us, event | category | flops | bytes accessed | tf_op | source)
XLA Modules:
  0.0 110.0 jit_solution(6597040657371387341)
XLA Ops:
  0.0 2.0 %shard_map.127 = (bf16[192,256]{1,0:T(8,128)(2,1)S(1)}, bf16[192,2048]{1,0:T(8,128)(2,1)S(1)}) custom-call(bf16[192,2048]{1,0:T(8,128)(2,1)} %refs_4_.5, bf16[2048]{0:T(1024)(128)(2,1)} %g_hbm.1, bf16[3,2048,256]{2,1,0:T(8,128)(2,1)} %bitcast.19), custom_call_target="tpu_custom_call" | custom-call | flops 201326592 | bytes 1835008 | tf_op jit(solution)/shard_map/pallas_call | solution.py:503
  2.0 4.0 %collective-permute-start.5 = (bf16[192,256]{1,0:T(8,128)(2,1)S(1)}, bf16[192,256]{1,0:T(8,128)(2,1)S(1)}, u32[]{:S(2)}, u32[]{:S(2)}) collective-permute-start(bf16[192,256]{1,0:T(8,128)(2,1)S(1)} %get-tuple-element.41.after_ref.refs_0_.q_ref), channel_id=1, source_target_pairs={{0,4},{2,6},{4,0},{6,2},{1,5},{3,7},{5,1},{7,3},{8,12},{10,14},{12... | collective-permute-start | bytes 294920 | tf_op jit(solution)/shard_map/ppermute | solution.py:522
  6.1 0.7 collective-permute-start.3
  6.8 1.3 %collective-permute-start.1 = (bf16[192,256]{1,0:T(8,128)(2,1)S(1)}, bf16[192,256]{1,0:T(8,128)(2,1)S(1)}, u32[]{:S(2)}, u32[]{:S(2)}) collective-permute-start(bf16[192,256]{1,0:T(8,128)(2,1)S(1)} %get-tuple-element.41.after_ref.refs_0_.q_ref), channel_id=1, source_target_pairs={{0,2},{2,4},{4,6},{6,0},{1,3},{3,5},{5,7},{7,1},{8,10},{10,12},{12... | collective-permute-start | bytes 294920 | tf_op jit(solution)/shard_map/ppermute | solution.py:522
  8.1 2.2 %shard_map.128 = (bf16[4,256,2048]{2,1,0:T(8,128)(2,1)S(1)}, f32[192,192]{1,0:T(8,128)S(1)}) custom-call(bf16[4,256,2048]{2,1,0:T(8,128)(2,1)} %v_hbm.1, s32[4,48]{1,0:T(4,128)} %up_hbm.1, bf16[192,256]{1,0:T(8,128)(2,1)S(1)} %get-tuple-element.41.after_ref.refs_0_.q_ref), custom_call_target="tpu_custom_call" | custom-call | bytes 4194304 | tf_op jit(solution)/shard_map/pallas_call | solution.py:532
  10.3 0.1 collective-permute-start
  10.4 0.0 collective-permute-done.5.refs_3_
  10.4 0.5 collective-permute-start.6
  10.9 0.8 collective-permute-done.3.refs_2_
  11.8 0.0 collective-permute-start.4
  11.8 0.9 collective-permute-done.1.refs_1_
  12.6 0.0 collective-permute-start.2
  12.6 0.0 collective-permute-done.6.refs_3_
  12.6 0.4 collective-permute-done.4.refs_2_
  13.1 0.9 collective-permute-done.2.refs_1_
  13.9 1.4 %shard_map.129.refs_6_ = bf16[9,192,128]{2,1,0:T(8,128)(2,1)S(1)} custom-call(s32[1,4]{1,0:T(1,128)S(1)} %bitcast.16, bf16[192,256]{1,0:T(8,128)(2,1)S(1)} %collective-permute-done.refs_0_, bf16[192,256]{1,0:T(8,128)(2,1)S(1)} %collective-permute-done.2.refs_1_, bf16[192,256]{1,0:T(8,128)(2,1)S(1)} %collective-permute-done.4.refs_2_, ...), custom_call_target="tpu_custom_call" | custom-call | flops 201326592 | bytes 4194304 | tf_op jit(solution)/shard_map/pallas_call | solution.py:549
  15.4 0.3 collective-permute-start.7
  15.6 1.4 %shard_map.130 = (f32[8,192,128]{2,1,0:T(8,128)S(1)}, f32[192,128]{1,0:T(8,128)S(1)}) custom-call(s32[1,4]{1,0:T(1,128)S(1)} %bitcast.17, bf16[192,256]{1,0:T(8,128)(2,1)S(1)} %get-tuple-element.41.after_ref.refs_0_.q_ref, bf16[192,256]{1,0:T(8,128)(2,1)S(1)} %collective-permute-done.1.refs_1_, bf16[192,256]{1,0:T(8,128)(2,1)S(1)} %collective-permute-done.3.refs_2_, ...), custom_call_target="tpu_custom_call" | custom-call | flops 201326592 | bytes 4194304 | tf_op jit(solution)/shard_map/pallas_call | solution.py:559
  17.1 0.0 copy-start.2
  17.1 0.1 collective-permute-done.7.other_ref
  17.2 0.7 shard_map.131
  18.0 1.7 %collective-permute-start.8 = (bf16[200,256]{1,0:T(8,128)(2,1)S(1)}, bf16[200,256]{1,0:T(8,128)(2,1)S(1)}, u32[]{:S(2)}, u32[]{:S(2)}) collective-permute-start(bf16[200,256]{1,0:T(8,128)(2,1)S(1)} %get-tuple-element.46), channel_id=1, source_target_pairs={{0,4},{2,6},{4,0},{6,2},{1,5},{3,7},{5,1},{7,3},{8,12},{10,14},{12... | collective-permute-start | bytes 307208 | tf_op jit(solution)/shard_map/ppermute | solution.py:522
  19.6 1.3 %collective-permute-start.9 = (bf16[200,256]{1,0:T(8,128)(2,1)S(1)}, bf16[200,256]{1,0:T(8,128)(2,1)S(1)}, u32[]{:S(2)}, u32[]{:S(2)}) collective-permute-start(bf16[200,256]{1,0:T(8,128)(2,1)S(1)} %get-tuple-element.47), channel_id=1, source_target_pairs={{0,6},{2,0},{4,2},{6,4},{1,7},{3,1},{5,3},{7,5},{8,14},{10,8},{12,... | collective-permute-start | bytes 307208 | tf_op jit(solution)/shard_map/ppermute | solution.py:522
  20.9 0.8 collective-permute-start.10
  21.7 2.6 %shard_map.132 = (f32[192,256]{1,0:T(8,128)S(1)}, f32[8,256]{1,0:T(8,128)S(1)}) custom-call(bf16[192,2048]{1,0:T(8,128)(2,1)S(1)} %get-tuple-element.49.normed_ref, bf16[3,2048,256]{2,1,0:T(8,128)(2,1)} %bitcast.20, bf16[192,256]{1,0:T(8,128)(2,1)S(1)} %get-tuple-element.41.after_ref.refs_0_.q_ref, f32[192,192]{1,0:T(8,128)S(1)} %get-tuple-element.50.visible_ref, ...), custom_call_target="tpu_custom_call" | custom-call | flops 402653184 | bytes 2883584 | tf_op jit(solution)/shard_map/pallas_call | solution.py:577
  24.3 1.0 collective-permute-done.8.refs_1_
  25.3 0.8 collective-permute-done.9.refs_2_
  26.1 0.9 collective-permute-done.10.refs_3_
  27.0 0.9 shard_map.133
  28.0 0.0 copy-start.1
  28.0 0.0 copy-start.3
  28.0 0.1 collective-permute-start.11
  28.1 1.7 %collective-permute-done.11.theirs_ref = bf16[96,2048]{1,0:T(8,128)(2,1)S(1)} collective-permute-done((bf16[96,2048]{1,0:T(8,128)(2,1)S(1)}, bf16[96,2048]{1,0:T(8,128)(2,1)S(1)}, u32[]{:S(2)}, u32[]{:S(2)}) %collective-permute-start.11) | collective-permute-done | bytes 393248 | tf_op jit(solution)/shard_map/ppermute | solution.py:525
  29.8 0.1 shard_map.134
  29.9 1.4 %collective-permute-start.12 = (bf16[24,2048]{1,0:T(8,128)(2,1)S(1)}, bf16[24,2048]{1,0:T(8,128)(2,1)S(1)}, u32[]{:S(2)}, u32[]{:S(2)}) collective-permute-start(bf16[24,2048]{1,0:T(8,128)(2,1)S(1)} %get-tuple-element.56), channel_id=1, source_target_pairs={{0,4},{2,6},{4,0},{6,2},{1,5},{3,7},{5,1},{7,3},{8,12},{10,14},{12... | collective-permute-start | bytes 294920 | tf_op jit(solution)/shard_map/ppermute | solution.py:522
  31.3 1.2 %collective-permute-start.13 = (bf16[24,2048]{1,0:T(8,128)(2,1)S(1)}, bf16[24,2048]{1,0:T(8,128)(2,1)S(1)}, u32[]{:S(2)}, u32[]{:S(2)}) collective-permute-start(bf16[24,2048]{1,0:T(8,128)(2,1)S(1)} %get-tuple-element.57), channel_id=1, source_target_pairs={{0,6},{2,0},{4,2},{6,4},{1,7},{3,1},{5,3},{7,5},{8,14},{10,8},{12,... | collective-permute-start | bytes 294920 | tf_op jit(solution)/shard_map/ppermute | solution.py:522
  32.5 0.8 collective-permute-start.14
  33.3 3.2 %shard_map.135 = (bf16[3,512,48]{2,1,0:T(8,128)(2,1)S(1)}, bf16[4,192,256]{2,1,0:T(8,128)(2,1)S(1)}, bf16[3,256,384]{2,1,0:T(8,128)(2,1)S(1)}, bf16[3072,1024]{1,0:T(8,128)(2,1)S(1)}) custom-call(s32[8,24]{1,0:T(8,128)S(1)} %bitcast.14, bf16[2048,1024]{1,0:T(8,128)(2,1)} %bitcast.21, bf16[512,2048]{1,0:T(8,128)(2,1)} %bitcast.22, ...), custom_call_target="tpu_custom_call" | custom-call | flops 16777216 | bytes 8388608 | tf_op jit(solution)/shard_map/pallas_call | solution.py:607
  36.6 0.4 collective-permute-done.12.refs_1_
  37.0 0.5 collective-permute-done.13.refs_2_
  37.5 1.0 collective-permute-done.14.refs_3_
  38.5 0.0 collective-permute-start.15
  38.6 0.7 shard_map.136
  39.3 33.7 %all_to_all.10 = bf16[64,8,1536]{2,1,0:T(8,128)(2,1)S(1)} all-to-all(bf16[64,8,1536]{2,1,0:T(8,128)(2,1)S(1)} %bitcast.12), channel_id=1, replica_groups=mesh['req'=16,'z'=4,'core'=2] {'req','z'}, dimensions={0} | all-to-all | bytes 3145728 | tf_op jit(solution)/shard_map/all_to_all | solution.py:640
  73.0 0.0 collective-permute-done.15.other_ref
  73.0 7.4 %shard_map.137 = (bf16[512,1536]{1,0:T(8,128)(2,1)S(1)}, bf16[3,96,512]{2,1,0:T(8,128)(2,1)S(1)}) custom-call(bf16[512,1536]{1,0:T(8,128)(2,1)S(1)} %bitcast.11, bf16[3072,1024]{1,0:T(8,128)(2,1)S(1)} %get-tuple-element.66.weights_ref, bf16[3072,1024]{1,0:T(8,128)(2,1)S(1)} %collective-permute-done.15.other_ref, ...), custom_call_target="tpu_custom_call" | custom-call | flops 4831838208 | bytes 12582912 | tf_op jit(solution)/shard_map/pallas_call | solution.py:648
  80.4 28.6 %all_to_all.11 = bf16[64,8,1536]{2,1,0:T(8,128)(2,1)S(1)} all-to-all(bf16[64,8,1536]{2,1,0:T(8,128)(2,1)S(1)} %bitcast.13), channel_id=1, replica_groups=mesh['req'=16,'z'=4,'core'=2] {'req','z'}, dimensions={0} | all-to-all | bytes 3145728 | tf_op jit(solution)/shard_map/all_to_all | solution.py:668
  109.0 1.0 shard_map.138
  (12 shorter events, 0.0 us)
Async XLA Ops:
  0.0 13.9 %copy-start = (bf16[4,256,2048]{2,1,0:T(8,128)(2,1)S(1)}, bf16[4,256,2048]{2,1,0:T(8,128)(2,1)}, u32[]{:S(2)}) copy-start(bf16[4,256,2048]{2,1,0:T(8,128)(2,1)} %refs_4_.4) | copy-start | bytes 12582916
  0.0 13.9 %copy-start.5 = (s32[4]{0:T(128)S(1)}, s32[4]{0:T(128)}, u32[]{:S(2)}) copy-start(s32[4]{0:T(128)} %param.19) | copy-start | bytes 52
  2.0 8.4 %collective-permute-start.5 = (bf16[192,256]{1,0:T(8,128)(2,1)S(1)}, bf16[192,256]{1,0:T(8,128)(2,1)S(1)}, u32[]{:S(2)}, u32[]{:S(2)}) collective-permute-start(bf16[192,256]{1,0:T(8,128)(2,1)S(1)} %get-tuple-element.41.after_ref.refs_0_.q_ref), channel_id=1, source_target_pairs={{0,4},{2,6},{4,0},{6,2},{1,5},{3,7},{5,1},{7,3},{8,12},{10,14},{12... | collective-permute-start | bytes 294920 | tf_op jit(solution)/shard_map/ppermute | solution.py:522
  6.1 5.7 %collective-permute-start.3 = (bf16[192,256]{1,0:T(8,128)(2,1)S(1)}, bf16[192,256]{1,0:T(8,128)(2,1)S(1)}, u32[]{:S(2)}, u32[]{:S(2)}) collective-permute-start(bf16[192,256]{1,0:T(8,128)(2,1)S(1)} %get-tuple-element.41.after_ref.refs_0_.q_ref), channel_id=1, source_target_pairs={{0,6},{2,0},{4,2},{6,4},{1,7},{3,1},{5,3},{7,5},{8,14},{10,8},{12,... | collective-permute-start | bytes 294920 | tf_op jit(solution)/shard_map/ppermute | solution.py:522
  6.8 5.8 %collective-permute-start.1 = (bf16[192,256]{1,0:T(8,128)(2,1)S(1)}, bf16[192,256]{1,0:T(8,128)(2,1)S(1)}, u32[]{:S(2)}, u32[]{:S(2)}) collective-permute-start(bf16[192,256]{1,0:T(8,128)(2,1)S(1)} %get-tuple-element.41.after_ref.refs_0_.q_ref), channel_id=1, source_target_pairs={{0,2},{2,4},{4,6},{6,0},{1,3},{3,5},{5,7},{7,1},{8,10},{10,12},{12... | collective-permute-start | bytes 294920 | tf_op jit(solution)/shard_map/ppermute | solution.py:522
  10.3 2.3 %collective-permute-start = (bf16[192,256]{1,0:T(8,128)(2,1)S(1)}, bf16[192,256]{1,0:T(8,128)(2,1)S(1)}, u32[]{:S(2)}, u32[]{:S(2)}) collective-permute-start(bf16[192,256]{1,0:T(8,128)(2,1)S(1)} %get-tuple-element.41.after_ref.refs_0_.q_ref), channel_id=1, source_target_pairs={{0,1},{1,0},{2,3},{3,2},{4,5},{5,4},{6,7},{7,6},{8,9},{9,8},{10,11... | collective-permute-start | bytes 294920 | tf_op jit(solution)/shard_map/ppermute | solution.py:525
  10.4 2.2 %collective-permute-start.6 = (bf16[192,256]{1,0:T(8,128)(2,1)S(1)}, bf16[192,256]{1,0:T(8,128)(2,1)S(1)}, u32[]{:S(2)}, u32[]{:S(2)}) collective-permute-start(bf16[192,256]{1,0:T(8,128)(2,1)S(1)} %collective-permute-done.5.refs_3_), channel_id=1, source_target_pairs={{0,1},{1,0},{2,3},{3,2},{4,5},{5,4},{6,7},{7,6},{8,9},{9,8},{10,11... | collective-permute-start | bytes 294920 | tf_op jit(solution)/shard_map/ppermute | solution.py:525
  11.8 1.3 %collective-permute-start.4 = (bf16[192,256]{1,0:T(8,128)(2,1)S(1)}, bf16[192,256]{1,0:T(8,128)(2,1)S(1)}, u32[]{:S(2)}, u32[]{:S(2)}) collective-permute-start(bf16[192,256]{1,0:T(8,128)(2,1)S(1)} %collective-permute-done.3.refs_2_), channel_id=1, source_target_pairs={{0,1},{1,0},{2,3},{3,2},{4,5},{5,4},{6,7},{7,6},{8,9},{9,8},{10,11... | collective-permute-start | bytes 294920 | tf_op jit(solution)/shard_map/ppermute | solution.py:525
  12.6 1.3 %collective-permute-start.2 = (bf16[192,256]{1,0:T(8,128)(2,1)S(1)}, bf16[192,256]{1,0:T(8,128)(2,1)S(1)}, u32[]{:S(2)}, u32[]{:S(2)}) collective-permute-start(bf16[192,256]{1,0:T(8,128)(2,1)S(1)} %collective-permute-done.1.refs_1_), channel_id=1, source_target_pairs={{0,1},{1,0},{2,3},{3,2},{4,5},{5,4},{6,7},{7,6},{8,9},{9,8},{10,11... | collective-permute-start | bytes 294920 | tf_op jit(solution)/shard_map/ppermute | solution.py:525
  15.4 1.9 %collective-permute-start.7 = (bf16[9,192,128]{2,1,0:T(8,128)(2,1)S(1)}, bf16[9,192,128]{2,1,0:T(8,128)(2,1)S(1)}, u32[]{:S(2)}, u32[]{:S(2)}) collective-permute-start(bf16[9,192,128]{2,1,0:T(8,128)(2,1)S(1)} %shard_map.129.refs_6_), channel_id=1, source_target_pairs={{0,1},{1,0},{2,3},{3,2},{4,5},{5,4},{6,7},{7,6},{8,9},{9,8},{10,11... | collective-permute-start | bytes 1327112 | tf_op jit(solution)/shard_map/ppermute | solution.py:525
  17.1 9.9 %copy-start.2 = (bf16[256,2048]{1,0:T(8,128)(2,1)S(1)}, bf16[256,2048]{1,0:T(8,128)(2,1)}, u32[]{:S(2)}) copy-start(bf16[256,2048]{1,0:T(8,128)(2,1)} %refs_6_.1) | copy-start | bytes 3145732
  17.2 16.1 %copy-start.4 = (s32[24,8]{0,1:T(8,128)S(1)}, s32[24,8]{0,1:T(8,128)}, u32[]{:S(2)}) copy-start(s32[24,8]{0,1:T(8,128)} %param.23) | copy-start | bytes 2308
  18.0 7.3 %collective-permute-start.8 = (bf16[200,256]{1,0:T(8,128)(2,1)S(1)}, bf16[200,256]{1,0:T(8,128)(2,1)S(1)}, u32[]{:S(2)}, u32[]{:S(2)}) collective-permute-start(bf16[200,256]{1,0:T(8,128)(2,1)S(1)} %get-tuple-element.46), channel_id=1, source_target_pairs={{0,4},{2,6},{4,0},{6,2},{1,5},{3,7},{5,1},{7,3},{8,12},{10,14},{12... | collective-permute-start | bytes 307208 | tf_op jit(solution)/shard_map/ppermute | solution.py:522
  19.6 6.5 %collective-permute-start.9 = (bf16[200,256]{1,0:T(8,128)(2,1)S(1)}, bf16[200,256]{1,0:T(8,128)(2,1)S(1)}, u32[]{:S(2)}, u32[]{:S(2)}) collective-permute-start(bf16[200,256]{1,0:T(8,128)(2,1)S(1)} %get-tuple-element.47), channel_id=1, source_target_pairs={{0,6},{2,0},{4,2},{6,4},{1,7},{3,1},{5,3},{7,5},{8,14},{10,8},{12,... | collective-permute-start | bytes 307208 | tf_op jit(solution)/shard_map/ppermute | solution.py:522
  20.9 6.1 %collective-permute-start.10 = (bf16[200,256]{1,0:T(8,128)(2,1)S(1)}, bf16[200,256]{1,0:T(8,128)(2,1)S(1)}, u32[]{:S(2)}, u32[]{:S(2)}) collective-permute-start(bf16[200,256]{1,0:T(8,128)(2,1)S(1)} %get-tuple-element.48), channel_id=1, source_target_pairs={{0,2},{2,4},{4,6},{6,0},{1,3},{3,5},{5,7},{7,1},{8,10},{10,12},{12... | collective-permute-start | bytes 307208 | tf_op jit(solution)/shard_map/ppermute | solution.py:522
  28.0 10.6 %copy-start.1 = (bf16[192,2048]{1,0:T(8,128)(2,1)S(1)}, bf16[192,2048]{1,0:T(8,128)(2,1)}, u32[]{:S(2)}) copy-start(bf16[192,2048]{1,0:T(8,128)(2,1)} %refs_4_.5) | copy-start | bytes 2359300
  28.0 10.6 %copy-start.3 = (bf16[2048]{0:T(1024)(128)(2,1)S(1)}, bf16[2048]{0:T(1024)(128)(2,1)}, u32[]{:S(2)}) copy-start(bf16[2048]{0:T(1024)(128)(2,1)} %refs_5_.1) | copy-start | bytes 12292
  28.0 1.8 %collective-permute-start.11 = (bf16[96,2048]{1,0:T(8,128)(2,1)S(1)}, bf16[96,2048]{1,0:T(8,128)(2,1)S(1)}, u32[]{:S(2)}, u32[]{:S(2)}) collective-permute-start(bf16[96,2048]{1,0:T(8,128)(2,1)S(1)} %get-tuple-element.54), channel_id=1, source_target_pairs={{0,1},{1,0},{2,3},{3,2},{4,5},{5,4},{6,7},{7,6},{8,9},{9,8},{10,11... | collective-permute-start | bytes 1179656 | tf_op jit(solution)/shard_map/ppermute | solution.py:525
  29.9 7.1 %collective-permute-start.12 = (bf16[24,2048]{1,0:T(8,128)(2,1)S(1)}, bf16[24,2048]{1,0:T(8,128)(2,1)S(1)}, u32[]{:S(2)}, u32[]{:S(2)}) collective-permute-start(bf16[24,2048]{1,0:T(8,128)(2,1)S(1)} %get-tuple-element.56), channel_id=1, source_target_pairs={{0,4},{2,6},{4,0},{6,2},{1,5},{3,7},{5,1},{7,3},{8,12},{10,14},{12... | collective-permute-start | bytes 294920 | tf_op jit(solution)/shard_map/ppermute | solution.py:522
  31.3 6.3 %collective-permute-start.13 = (bf16[24,2048]{1,0:T(8,128)(2,1)S(1)}, bf16[24,2048]{1,0:T(8,128)(2,1)S(1)}, u32[]{:S(2)}, u32[]{:S(2)}) collective-permute-start(bf16[24,2048]{1,0:T(8,128)(2,1)S(1)} %get-tuple-element.57), channel_id=1, source_target_pairs={{0,6},{2,0},{4,2},{6,4},{1,7},{3,1},{5,3},{7,5},{8,14},{10,8},{12,... | collective-permute-start | bytes 294920 | tf_op jit(solution)/shard_map/ppermute | solution.py:522
  32.5 6.0 %collective-permute-start.14 = (bf16[24,2048]{1,0:T(8,128)(2,1)S(1)}, bf16[24,2048]{1,0:T(8,128)(2,1)S(1)}, u32[]{:S(2)}, u32[]{:S(2)}) collective-permute-start(bf16[24,2048]{1,0:T(8,128)(2,1)S(1)} %get-tuple-element.58), channel_id=1, source_target_pairs={{0,2},{2,4},{4,6},{6,0},{1,3},{3,5},{5,7},{7,1},{8,10},{10,12},{12... | collective-permute-start | bytes 294920 | tf_op jit(solution)/shard_map/ppermute | solution.py:522
  33.3 39.7 %copy-start.6 = (bf16[2048,64]{0,1:T(8,128)(2,1)S(1)}, bf16[2048,64]{0,1:T(8,128)(2,1)}, u32[]{:S(2)}) copy-start(bf16[2048,64]{0,1:T(8,128)(2,1)} %param.22) | copy-start | bytes 786436
  38.5 34.4 %collective-permute-start.15 = (bf16[3072,1024]{1,0:T(8,128)(2,1)S(1)}, bf16[3072,1024]{1,0:T(8,128)(2,1)S(1)}, u32[]{:S(2)}, u32[]{:S(2)}) collective-permute-start(bf16[3072,1024]{1,0:T(8,128)(2,1)S(1)} %get-tuple-element.66.weights_ref), channel_id=1, source_target_pairs={{0,1},{1,0},{2,3},{3,2},{4,5},{5,4},{6,7},{7,6},{8,9},{9,8},{10,11... | collective-permute-start | bytes 18874376 | tf_op jit(solution)/shard_map/ppermute | solution.py:525

commit v13 on v12

--- a/solution.py
+++ b/solution.py
@@ -408,7 +408,6 @@
     out_ref,
     table_ref,
 ):
-    gate_kernel(normed_ref, router_ref, routes_ref, table_ref)
     rows, packed = x_ref.shape
     width = normed_ref.shape[1]
     both = weights_ref.shape[1]
@@ -453,6 +452,7 @@
             out_ref[i * block : (i + 1) * block, columns] = dot(scatter_ref[k], pair).astype(
                 BF16
             )
+    gate_kernel(normed_ref, router_ref, routes_ref, table_ref)
 
 
 def final_kernel(back_ref, table_ref, res_ref, out_ref):

time: 110 us -> 110 us (level)
  no operation moved by 1% of the time
where the time goes in v13:
time: 110 us
  blocking collectives  62.3 us (57%)
  Pallas kernels  23.8 us (22%)
  starting transfers between devices  14.2 us (13%)
  waiting for transfers between devices  9.57 us (9%)
    all_to_all x1, blocking collectives, per_device(): lax.all_to_all(outgoing.reshape(experts, SLOTS, packed), ('req', 'z'), sp...  33.7 us
    all_to_all x1, blocking collectives, per_device(): lax.all_to_all(summed.reshape(experts, SLOTS, packed), ('req', 'z'), spli...  28.6 us
    ppermute x9, starting transfers between devices, over_z(): lax.ppermute(value, 'z', [(i, (i + step) % z_count) for i in range(z_coun...  13.2 us
    pallas_call x1, Pallas kernels, per_device(): call(expert_kernel, (sds((experts * SLOTS, packed), BF16), sds((chunks, 4...  7.32 us
    ppermute x9, waiting for transfers between devices, over_z(): lax.ppermute(value, 'z', [(i, (i + step) % z_count) for i in range(z_coun...  6.43 us
    pallas_call x1, Pallas kernels, per_device(): call(table_kernel, (sds((chunks, experts * SLOTS, 2 * own), BF16), sds((1...  3.24 us
    ppermute x7, waiting for transfers between devices, over_core(): return lax.ppermute(value, 'core', [(0, 1), (1, 0)])  3.14 us
    pallas_call x1, Pallas kernels, per_device(): call(functools.partial(tree_kernel, scale), (sds((tokens, local_width), F...  2.58 us
  transfers between devices with their start and end apart: 16, of which 12 were waited for; matrix products, arithmetic and copies ran while one was open for 0% of the time, Pallas kernels for 9%

profile of v13, /device:TPU:0, one launch (start us, length us, event | category | flops | bytes accessed | tf_op | source)
XLA Modules:
  0.0 110.0 jit_solution(12050038593898743917)
XLA Ops:
  0.0 2.0 %shard_map.127 = (bf16[192,256]{1,0:T(8,128)(2,1)S(1)}, bf16[192,2048]{1,0:T(8,128)(2,1)S(1)}) custom-call(bf16[192,2048]{1,0:T(8,128)(2,1)} %refs_4_.5, bf16[2048]{0:T(1024)(128)(2,1)} %g_hbm.1, bf16[3,2048,256]{2,1,0:T(8,128)(2,1)} %bitcast.19), custom_call_target="tpu_custom_call" | custom-call | flops 201326592 | bytes 1835008 | tf_op jit(solution)/shard_map/pallas_call | solution.py:503
  2.0 4.0 %collective-permute-start.5 = (bf16[192,256]{1,0:T(8,128)(2,1)S(1)}, bf16[192,256]{1,0:T(8,128)(2,1)S(1)}, u32[]{:S(2)}, u32[]{:S(2)}) collective-permute-start(bf16[192,256]{1,0:T(8,128)(2,1)S(1)} %get-tuple-element.41.after_ref.refs_0_.q_ref), channel_id=1, source_target_pairs={{0,4},{2,6},{4,0},{6,2},{1,5},{3,7},{5,1},{7,3},{8,12},{10,14},{12... | collective-permute-start | bytes 294920 | tf_op jit(solution)/shard_map/ppermute | solution.py:522
  6.1 0.7 collective-permute-start.3
  6.8 1.3 %collective-permute-start.1 = (bf16[192,256]{1,0:T(8,128)(2,1)S(1)}, bf16[192,256]{1,0:T(8,128)(2,1)S(1)}, u32[]{:S(2)}, u32[]{:S(2)}) collective-permute-start(bf16[192,256]{1,0:T(8,128)(2,1)S(1)} %get-tuple-element.41.after_ref.refs_0_.q_ref), channel_id=1, source_target_pairs={{0,2},{2,4},{4,6},{6,0},{1,3},{3,5},{5,7},{7,1},{8,10},{10,12},{12... | collective-permute-start | bytes 294920 | tf_op jit(solution)/shard_map/ppermute | solution.py:522
  8.1 2.2 %shard_map.128 = (bf16[4,256,2048]{2,1,0:T(8,128)(2,1)S(1)}, f32[192,192]{1,0:T(8,128)S(1)}) custom-call(bf16[4,256,2048]{2,1,0:T(8,128)(2,1)} %v_hbm.1, s32[4,48]{1,0:T(4,128)} %up_hbm.1, bf16[192,256]{1,0:T(8,128)(2,1)S(1)} %get-tuple-element.41.after_ref.refs_0_.q_ref), custom_call_target="tpu_custom_call" | custom-call | bytes 4194304 | tf_op jit(solution)/shard_map/pallas_call | solution.py:532
  10.3 0.1 collective-permute-start
  10.4 0.0 collective-permute-done.5.refs_3_
  10.4 0.5 collective-permute-start.6
  10.9 0.8 collective-permute-done.3.refs_2_
  11.8 0.0 collective-permute-start.4
  11.8 0.9 collective-permute-done.1.refs_1_
  12.6 0.0 collective-permute-start.2
  12.6 0.0 collective-permute-done.6.refs_3_
  12.6 0.4 collective-permute-done.4.refs_2_
  13.1 0.9 collective-permute-done.2.refs_1_
  13.9 1.4 %shard_map.129.refs_6_ = bf16[9,192,128]{2,1,0:T(8,128)(2,1)S(1)} custom-call(s32[1,4]{1,0:T(1,128)S(1)} %bitcast.16, bf16[192,256]{1,0:T(8,128)(2,1)S(1)} %collective-permute-done.refs_0_, bf16[192,256]{1,0:T(8,128)(2,1)S(1)} %collective-permute-done.2.refs_1_, bf16[192,256]{1,0:T(8,128)(2,1)S(1)} %collective-permute-done.4.refs_2_, ...), custom_call_target="tpu_custom_call" | custom-call | flops 201326592 | bytes 4194304 | tf_op jit(solution)/shard_map/pallas_call | solution.py:549
  15.4 0.3 collective-permute-start.7
  15.6 1.4 %shard_map.130 = (f32[8,192,128]{2,1,0:T(8,128)S(1)}, f32[192,128]{1,0:T(8,128)S(1)}) custom-call(s32[1,4]{1,0:T(1,128)S(1)} %bitcast.17, bf16[192,256]{1,0:T(8,128)(2,1)S(1)} %get-tuple-element.41.after_ref.refs_0_.q_ref, bf16[192,256]{1,0:T(8,128)(2,1)S(1)} %collective-permute-done.1.refs_1_, bf16[192,256]{1,0:T(8,128)(2,1)S(1)} %collective-permute-done.3.refs_2_, ...), custom_call_target="tpu_custom_call" | custom-call | flops 201326592 | bytes 4194304 | tf_op jit(solution)/shard_map/pallas_call | solution.py:559
  17.1 0.0 copy-start.2
  17.1 0.1 collective-permute-done.7.other_ref
  17.2 0.7 shard_map.131
  18.0 1.7 %collective-permute-start.8 = (bf16[200,256]{1,0:T(8,128)(2,1)S(1)}, bf16[200,256]{1,0:T(8,128)(2,1)S(1)}, u32[]{:S(2)}, u32[]{:S(2)}) collective-permute-start(bf16[200,256]{1,0:T(8,128)(2,1)S(1)} %get-tuple-element.46), channel_id=1, source_target_pairs={{0,4},{2,6},{4,0},{6,2},{1,5},{3,7},{5,1},{7,3},{8,12},{10,14},{12... | collective-permute-start | bytes 307208 | tf_op jit(solution)/shard_map/ppermute | solution.py:522
  19.6 1.3 %collective-permute-start.9 = (bf16[200,256]{1,0:T(8,128)(2,1)S(1)}, bf16[200,256]{1,0:T(8,128)(2,1)S(1)}, u32[]{:S(2)}, u32[]{:S(2)}) collective-permute-start(bf16[200,256]{1,0:T(8,128)(2,1)S(1)} %get-tuple-element.47), channel_id=1, source_target_pairs={{0,6},{2,0},{4,2},{6,4},{1,7},{3,1},{5,3},{7,5},{8,14},{10,8},{12,... | collective-permute-start | bytes 307208 | tf_op jit(solution)/shard_map/ppermute | solution.py:522
  20.9 0.8 collective-permute-start.10
  21.7 2.6 %shard_map.132 = (f32[192,256]{1,0:T(8,128)S(1)}, f32[8,256]{1,0:T(8,128)S(1)}) custom-call(bf16[192,2048]{1,0:T(8,128)(2,1)S(1)} %get-tuple-element.49.normed_ref, bf16[3,2048,256]{2,1,0:T(8,128)(2,1)} %bitcast.20, bf16[192,256]{1,0:T(8,128)(2,1)S(1)} %get-tuple-element.41.after_ref.refs_0_.q_ref, f32[192,192]{1,0:T(8,128)S(1)} %get-tuple-element.50.visible_ref, ...), custom_call_target="tpu_custom_call" | custom-call | flops 402653184 | bytes 2883584 | tf_op jit(solution)/shard_map/pallas_call | solution.py:577
  24.3 1.0 collective-permute-done.8.refs_1_
  25.3 0.8 collective-permute-done.9.refs_2_
  26.1 0.9 collective-permute-done.10.refs_3_
  27.0 0.9 shard_map.133
  28.0 0.0 copy-start.1
  28.0 0.0 copy-start.3
  28.0 0.1 collective-permute-start.11
  28.1 1.7 %collective-permute-done.11.theirs_ref = bf16[96,2048]{1,0:T(8,128)(2,1)S(1)} collective-permute-done((bf16[96,2048]{1,0:T(8,128)(2,1)S(1)}, bf16[96,2048]{1,0:T(8,128)(2,1)S(1)}, u32[]{:S(2)}, u32[]{:S(2)}) %collective-permute-start.11) | collective-permute-done | bytes 393248 | tf_op jit(solution)/shard_map/ppermute | solution.py:525
  29.8 0.1 shard_map.134
  29.9 1.4 %collective-permute-start.12 = (bf16[24,2048]{1,0:T(8,128)(2,1)S(1)}, bf16[24,2048]{1,0:T(8,128)(2,1)S(1)}, u32[]{:S(2)}, u32[]{:S(2)}) collective-permute-start(bf16[24,2048]{1,0:T(8,128)(2,1)S(1)} %get-tuple-element.56), channel_id=1, source_target_pairs={{0,4},{2,6},{4,0},{6,2},{1,5},{3,7},{5,1},{7,3},{8,12},{10,14},{12... | collective-permute-start | bytes 294920 | tf_op jit(solution)/shard_map/ppermute | solution.py:522
  31.3 1.2 %collective-permute-start.13 = (bf16[24,2048]{1,0:T(8,128)(2,1)S(1)}, bf16[24,2048]{1,0:T(8,128)(2,1)S(1)}, u32[]{:S(2)}, u32[]{:S(2)}) collective-permute-start(bf16[24,2048]{1,0:T(8,128)(2,1)S(1)} %get-tuple-element.57), channel_id=1, source_target_pairs={{0,6},{2,0},{4,2},{6,4},{1,7},{3,1},{5,3},{7,5},{8,14},{10,8},{12,... | collective-permute-start | bytes 294920 | tf_op jit(solution)/shard_map/ppermute | solution.py:522
  32.5 0.8 collective-permute-start.14
  33.3 3.2 %shard_map.135 = (bf16[3,512,48]{2,1,0:T(8,128)(2,1)S(1)}, bf16[4,192,256]{2,1,0:T(8,128)(2,1)S(1)}, bf16[3,256,384]{2,1,0:T(8,128)(2,1)S(1)}, bf16[3072,1024]{1,0:T(8,128)(2,1)S(1)}) custom-call(s32[8,24]{1,0:T(8,128)S(1)} %bitcast.14, bf16[2048,1024]{1,0:T(8,128)(2,1)} %bitcast.21, bf16[512,2048]{1,0:T(8,128)(2,1)} %bitcast.22, ...), custom_call_target="tpu_custom_call" | custom-call | flops 16777216 | bytes 8388608 | tf_op jit(solution)/shard_map/pallas_call | solution.py:607
  36.6 0.4 collective-permute-done.12.refs_1_
  37.0 0.5 collective-permute-done.13.refs_2_
  37.5 1.0 collective-permute-done.14.refs_3_
  38.5 0.0 collective-permute-start.15
  38.6 0.7 shard_map.136
  39.3 33.7 %all_to_all.10 = bf16[64,8,1536]{2,1,0:T(8,128)(2,1)S(1)} all-to-all(bf16[64,8,1536]{2,1,0:T(8,128)(2,1)S(1)} %bitcast.12), channel_id=1, replica_groups=mesh['req'=16,'z'=4,'core'=2] {'req','z'}, dimensions={0} | all-to-all | bytes 3145728 | tf_op jit(solution)/shard_map/all_to_all | solution.py:640
  73.0 0.0 collective-permute-done.15.other_ref
  73.0 7.3 %shard_map.137 = (bf16[512,1536]{1,0:T(8,128)(2,1)S(1)}, bf16[3,96,512]{2,1,0:T(8,128)(2,1)S(1)}) custom-call(bf16[512,1536]{1,0:T(8,128)(2,1)S(1)} %bitcast.11, bf16[3072,1024]{1,0:T(8,128)(2,1)S(1)} %get-tuple-element.66.weights_ref, bf16[3072,1024]{1,0:T(8,128)(2,1)S(1)} %collective-permute-done.15.other_ref, ...), custom_call_target="tpu_custom_call" | custom-call | flops 4831838208 | bytes 12582912 | tf_op jit(solution)/shard_map/pallas_call | solution.py:648
  80.3 28.6 %all_to_all.11 = bf16[64,8,1536]{2,1,0:T(8,128)(2,1)S(1)} all-to-all(bf16[64,8,1536]{2,1,0:T(8,128)(2,1)S(1)} %bitcast.13), channel_id=1, replica_groups=mesh['req'=16,'z'=4,'core'=2] {'req','z'}, dimensions={0} | all-to-all | bytes 3145728 | tf_op jit(solution)/shard_map/all_to_all | solution.py:668
  108.9 1.0 shard_map.138
  (12 shorter events, 0.0 us)
Async XLA Ops:
  0.0 13.9 %copy-start = (bf16[4,256,2048]{2,1,0:T(8,128)(2,1)S(1)}, bf16[4,256,2048]{2,1,0:T(8,128)(2,1)}, u32[]{:S(2)}) copy-start(bf16[4,256,2048]{2,1,0:T(8,128)(2,1)} %refs_4_.4) | copy-start | bytes 12582916
  0.0 13.9 %copy-start.5 = (s32[4]{0:T(128)S(1)}, s32[4]{0:T(128)}, u32[]{:S(2)}) copy-start(s32[4]{0:T(128)} %param.19) | copy-start | bytes 52
  2.0 8.4 %collective-permute-start.5 = (bf16[192,256]{1,0:T(8,128)(2,1)S(1)}, bf16[192,256]{1,0:T(8,128)(2,1)S(1)}, u32[]{:S(2)}, u32[]{:S(2)}) collective-permute-start(bf16[192,256]{1,0:T(8,128)(2,1)S(1)} %get-tuple-element.41.after_ref.refs_0_.q_ref), channel_id=1, source_target_pairs={{0,4},{2,6},{4,0},{6,2},{1,5},{3,7},{5,1},{7,3},{8,12},{10,14},{12... | collective-permute-start | bytes 294920 | tf_op jit(solution)/shard_map/ppermute | solution.py:522
  6.1 5.7 %collective-permute-start.3 = (bf16[192,256]{1,0:T(8,128)(2,1)S(1)}, bf16[192,256]{1,0:T(8,128)(2,1)S(1)}, u32[]{:S(2)}, u32[]{:S(2)}) collective-permute-start(bf16[192,256]{1,0:T(8,128)(2,1)S(1)} %get-tuple-element.41.after_ref.refs_0_.q_ref), channel_id=1, source_target_pairs={{0,6},{2,0},{4,2},{6,4},{1,7},{3,1},{5,3},{7,5},{8,14},{10,8},{12,... | collective-permute-start | bytes 294920 | tf_op jit(solution)/shard_map/ppermute | solution.py:522
  6.8 5.8 %collective-permute-start.1 = (bf16[192,256]{1,0:T(8,128)(2,1)S(1)}, bf16[192,256]{1,0:T(8,128)(2,1)S(1)}, u32[]{:S(2)}, u32[]{:S(2)}) collective-permute-start(bf16[192,256]{1,0:T(8,128)(2,1)S(1)} %get-tuple-element.41.after_ref.refs_0_.q_ref), channel_id=1, source_target_pairs={{0,2},{2,4},{4,6},{6,0},{1,3},{3,5},{5,7},{7,1},{8,10},{10,12},{12... | collective-permute-start | bytes 294920 | tf_op jit(solution)/shard_map/ppermute | solution.py:522
  10.3 2.3 %collective-permute-start = (bf16[192,256]{1,0:T(8,128)(2,1)S(1)}, bf16[192,256]{1,0:T(8,128)(2,1)S(1)}, u32[]{:S(2)}, u32[]{:S(2)}) collective-permute-start(bf16[192,256]{1,0:T(8,128)(2,1)S(1)} %get-tuple-element.41.after_ref.refs_0_.q_ref), channel_id=1, source_target_pairs={{0,1},{1,0},{2,3},{3,2},{4,5},{5,4},{6,7},{7,6},{8,9},{9,8},{10,11... | collective-permute-start | bytes 294920 | tf_op jit(solution)/shard_map/ppermute | solution.py:525
  10.4 2.2 %collective-permute-start.6 = (bf16[192,256]{1,0:T(8,128)(2,1)S(1)}, bf16[192,256]{1,0:T(8,128)(2,1)S(1)}, u32[]{:S(2)}, u32[]{:S(2)}) collective-permute-start(bf16[192,256]{1,0:T(8,128)(2,1)S(1)} %collective-permute-done.5.refs_3_), channel_id=1, source_target_pairs={{0,1},{1,0},{2,3},{3,2},{4,5},{5,4},{6,7},{7,6},{8,9},{9,8},{10,11... | collective-permute-start | bytes 294920 | tf_op jit(solution)/shard_map/ppermute | solution.py:525
  11.8 1.3 %collective-permute-start.4 = (bf16[192,256]{1,0:T(8,128)(2,1)S(1)}, bf16[192,256]{1,0:T(8,128)(2,1)S(1)}, u32[]{:S(2)}, u32[]{:S(2)}) collective-permute-start(bf16[192,256]{1,0:T(8,128)(2,1)S(1)} %collective-permute-done.3.refs_2_), channel_id=1, source_target_pairs={{0,1},{1,0},{2,3},{3,2},{4,5},{5,4},{6,7},{7,6},{8,9},{9,8},{10,11... | collective-permute-start | bytes 294920 | tf_op jit(solution)/shard_map/ppermute | solution.py:525
  12.6 1.3 %collective-permute-start.2 = (bf16[192,256]{1,0:T(8,128)(2,1)S(1)}, bf16[192,256]{1,0:T(8,128)(2,1)S(1)}, u32[]{:S(2)}, u32[]{:S(2)}) collective-permute-start(bf16[192,256]{1,0:T(8,128)(2,1)S(1)} %collective-permute-done.1.refs_1_), channel_id=1, source_target_pairs={{0,1},{1,0},{2,3},{3,2},{4,5},{5,4},{6,7},{7,6},{8,9},{9,8},{10,11... | collective-permute-start | bytes 294920 | tf_op jit(solution)/shard_map/ppermute | solution.py:525
  15.4 1.9 %collective-permute-start.7 = (bf16[9,192,128]{2,1,0:T(8,128)(2,1)S(1)}, bf16[9,192,128]{2,1,0:T(8,128)(2,1)S(1)}, u32[]{:S(2)}, u32[]{:S(2)}) collective-permute-start(bf16[9,192,128]{2,1,0:T(8,128)(2,1)S(1)} %shard_map.129.refs_6_), channel_id=1, source_target_pairs={{0,1},{1,0},{2,3},{3,2},{4,5},{5,4},{6,7},{7,6},{8,9},{9,8},{10,11... | collective-permute-start | bytes 1327112 | tf_op jit(solution)/shard_map/ppermute | solution.py:525
  17.1 9.9 %copy-start.2 = (bf16[256,2048]{1,0:T(8,128)(2,1)S(1)}, bf16[256,2048]{1,0:T(8,128)(2,1)}, u32[]{:S(2)}) copy-start(bf16[256,2048]{1,0:T(8,128)(2,1)} %refs_6_.1) | copy-start | bytes 3145732
  17.2 16.1 %copy-start.4 = (s32[24,8]{0,1:T(8,128)S(1)}, s32[24,8]{0,1:T(8,128)}, u32[]{:S(2)}) copy-start(s32[24,8]{0,1:T(8,128)} %param.23) | copy-start | bytes 2308
  18.0 7.3 %collective-permute-start.8 = (bf16[200,256]{1,0:T(8,128)(2,1)S(1)}, bf16[200,256]{1,0:T(8,128)(2,1)S(1)}, u32[]{:S(2)}, u32[]{:S(2)}) collective-permute-start(bf16[200,256]{1,0:T(8,128)(2,1)S(1)} %get-tuple-element.46), channel_id=1, source_target_pairs={{0,4},{2,6},{4,0},{6,2},{1,5},{3,7},{5,1},{7,3},{8,12},{10,14},{12... | collective-permute-start | bytes 307208 | tf_op jit(solution)/shard_map/ppermute | solution.py:522
  19.6 6.5 %collective-permute-start.9 = (bf16[200,256]{1,0:T(8,128)(2,1)S(1)}, bf16[200,256]{1,0:T(8,128)(2,1)S(1)}, u32[]{:S(2)}, u32[]{:S(2)}) collective-permute-start(bf16[200,256]{1,0:T(8,128)(2,1)S(1)} %get-tuple-element.47), channel_id=1, source_target_pairs={{0,6},{2,0},{4,2},{6,4},{1,7},{3,1},{5,3},{7,5},{8,14},{10,8},{12,... | collective-permute-start | bytes 307208 | tf_op jit(solution)/shard_map/ppermute | solution.py:522
  20.9 6.1 %collective-permute-start.10 = (bf16[200,256]{1,0:T(8,128)(2,1)S(1)}, bf16[200,256]{1,0:T(8,128)(2,1)S(1)}, u32[]{:S(2)}, u32[]{:S(2)}) collective-permute-start(bf16[200,256]{1,0:T(8,128)(2,1)S(1)} %get-tuple-element.48), channel_id=1, source_target_pairs={{0,2},{2,4},{4,6},{6,0},{1,3},{3,5},{5,7},{7,1},{8,10},{10,12},{12... | collective-permute-start | bytes 307208 | tf_op jit(solution)/shard_map/ppermute | solution.py:522
  28.0 10.6 %copy-start.1 = (bf16[192,2048]{1,0:T(8,128)(2,1)S(1)}, bf16[192,2048]{1,0:T(8,128)(2,1)}, u32[]{:S(2)}) copy-start(bf16[192,2048]{1,0:T(8,128)(2,1)} %refs_4_.5) | copy-start | bytes 2359300
  28.0 10.6 %copy-start.3 = (bf16[2048]{0:T(1024)(128)(2,1)S(1)}, bf16[2048]{0:T(1024)(128)(2,1)}, u32[]{:S(2)}) copy-start(bf16[2048]{0:T(1024)(128)(2,1)} %refs_5_.1) | copy-start | bytes 12292
  28.0 1.8 %collective-permute-start.11 = (bf16[96,2048]{1,0:T(8,128)(2,1)S(1)}, bf16[96,2048]{1,0:T(8,128)(2,1)S(1)}, u32[]{:S(2)}, u32[]{:S(2)}) collective-permute-start(bf16[96,2048]{1,0:T(8,128)(2,1)S(1)} %get-tuple-element.54), channel_id=1, source_target_pairs={{0,1},{1,0},{2,3},{3,2},{4,5},{5,4},{6,7},{7,6},{8,9},{9,8},{10,11... | collective-permute-start | bytes 1179656 | tf_op jit(solution)/shard_map/ppermute | solution.py:525
  29.9 7.1 %collective-permute-start.12 = (bf16[24,2048]{1,0:T(8,128)(2,1)S(1)}, bf16[24,2048]{1,0:T(8,128)(2,1)S(1)}, u32[]{:S(2)}, u32[]{:S(2)}) collective-permute-start(bf16[24,2048]{1,0:T(8,128)(2,1)S(1)} %get-tuple-element.56), channel_id=1, source_target_pairs={{0,4},{2,6},{4,0},{6,2},{1,5},{3,7},{5,1},{7,3},{8,12},{10,14},{12... | collective-permute-start | bytes 294920 | tf_op jit(solution)/shard_map/ppermute | solution.py:522
  31.3 6.3 %collective-permute-start.13 = (bf16[24,2048]{1,0:T(8,128)(2,1)S(1)}, bf16[24,2048]{1,0:T(8,128)(2,1)S(1)}, u32[]{:S(2)}, u32[]{:S(2)}) collective-permute-start(bf16[24,2048]{1,0:T(8,128)(2,1)S(1)} %get-tuple-element.57), channel_id=1, source_target_pairs={{0,6},{2,0},{4,2},{6,4},{1,7},{3,1},{5,3},{7,5},{8,14},{10,8},{12,... | collective-permute-start | bytes 294920 | tf_op jit(solution)/shard_map/ppermute | solution.py:522
  32.5 6.0 %collective-permute-start.14 = (bf16[24,2048]{1,0:T(8,128)(2,1)S(1)}, bf16[24,2048]{1,0:T(8,128)(2,1)S(1)}, u32[]{:S(2)}, u32[]{:S(2)}) collective-permute-start(bf16[24,2048]{1,0:T(8,128)(2,1)S(1)} %get-tuple-element.58), channel_id=1, source_target_pairs={{0,2},{2,4},{4,6},{6,0},{1,3},{3,5},{5,7},{7,1},{8,10},{10,12},{12... | collective-permute-start | bytes 294920 | tf_op jit(solution)/shard_map/ppermute | solution.py:522
  33.3 39.7 %copy-start.6 = (bf16[2048,64]{0,1:T(8,128)(2,1)S(1)}, bf16[2048,64]{0,1:T(8,128)(2,1)}, u32[]{:S(2)}) copy-start(bf16[2048,64]{0,1:T(8,128)(2,1)} %param.22) | copy-start | bytes 786436
  38.5 34.4 %collective-permute-start.15 = (bf16[3072,1024]{1,0:T(8,128)(2,1)S(1)}, bf16[3072,1024]{1,0:T(8,128)(2,1)S(1)}, u32[]{:S(2)}, u32[]{:S(2)}) collective-permute-start(bf16[3072,1024]{1,0:T(8,128)(2,1)S(1)} %get-tuple-element.66.weights_ref), channel_id=1, source_target_pairs={{0,1},{1,0},{2,3},{3,2},{4,5},{5,4},{6,7},{7,6},{8,9},{9,8},{10,11... | collective-permute-start | bytes 18874376 | tf_op jit(solution)/shard_map/ppermute | solution.py:525
